TPU v7x, 32 devices: a whole 2x2x4 slice. The times are simulated.
32 devices in a mesh: dp: 8 (over z, x), tp: 4 (over y, core).
Axes of the slice: x: 2, y: 2, z: 4, core: 2. Of those that a mesh axis runs over, the one named last changes fastest.
Arguments:
- layer_input: bfloat16 [4096, 768], P('dp'), may hold values from -6 to 6
- pair_lengths: int32 [16], P('dp'), may hold values from 32 to 256, as said below
- query_weight: bfloat16 [768, 768], P('dp', 'tp'), may hold values from -0.21875 to 0.21875
- query_bias: float32 [768], P('tp'), may hold values from -3 to 3
- key_weight: bfloat16 [768, 768], P('dp', 'tp'), may hold values from -0.21875 to 0.21875
- value_weight: bfloat16 [768, 768], P('dp', 'tp'), may hold values from -0.21875 to 0.21875
- value_bias: float32 [768], P('tp'), may hold values from -3 to 3
- out_weight: bfloat16 [768, 768], P('tp', 'dp'), may hold values from -1.5 to 1.5
- out_bias: float32 [768], replicated, may hold values from -3 to 3
- first_gain: float32 [768], replicated, may hold values from 0.5 to 1.5
- first_shift: float32 [768], replicated, may hold values from -2 to 2
- up_weight: bfloat16 [768, 3072], P('dp', 'tp'), may hold values from -0.21875 to 0.21875
- up_bias: float32 [3072], P('tp'), may hold values from -3 to 3
- down_weight: bfloat16 [3072, 768], P('tp', 'dp'), may hold values from -0.21875 to 0.21875
- down_bias: float32 [768], replicated, may hold values from -3 to 3
- second_gain: float32 [768], replicated, may hold values from 0.5 to 1.5
- second_shift: float32 [768], replicated, may hold values from -2 to 2
- out_grad: bfloat16 [4096, 768], P('dp'), may hold values from -6 to 6
- query_tangent: bfloat16 [768, 768], P('dp', 'tp'), may hold values from -0.21875 to 0.21875
- key_tangent: bfloat16 [768, 768], P('dp', 'tp'), may hold values from -0.21875 to 0.21875
- value_tangent: bfloat16 [768, 768], P('dp', 'tp'), may hold values from -0.21875 to 0.21875
- out_tangent: bfloat16 [768, 768], P('tp', 'dp'), may hold values from -1.5 to 1.5
- up_tangent: bfloat16 [768, 3072], P('dp', 'tp'), may hold values from -0.21875 to 0.21875
- down_tangent: bfloat16 [3072, 768], P('tp', 'dp'), may hold values from -0.21875 to 0.21875
Outputs:
- layer_output: bfloat16 [4096, 768], P('dp')
- input_grad: bfloat16 [4096, 768], P('dp')
- layer_output_jvp: bfloat16 [4096, 768], P('dp')
- query_weight_grad: float32 [768, 768], P('dp', 'tp')
- query_bias_grad: float32 [768], P('tp')
- key_weight_grad: float32 [768, 768], P('dp', 'tp')
- value_weight_grad: float32 [768, 768], P('dp', 'tp')
- value_bias_grad: float32 [768], P('tp')
- out_weight_grad: float32 [768, 768], P('tp', 'dp')
- out_bias_grad: float32 [768], replicated
- first_gain_grad: float32 [768], replicated
- first_shift_grad: float32 [768], replicated
- up_weight_grad: float32 [768, 3072], P('dp', 'tp')
- up_bias_grad: float32 [3072], P('tp')
- down_weight_grad: float32 [3072, 768], P('tp', 'dp')
- down_bias_grad: float32 [768], replicated
- second_gain_grad: float32 [768], replicated
- second_shift_grad: float32 [768], replicated
Inputs may be any that keep to these rules, and one draw needn't show every extreme that they name: Slots 0 to pair_lengths[p] - 1 of pair p hold tokens, the rest are padding; some pair has length 256.
All inputs are finite; a program needn't handle non-finite values.
Results may differ from a plain program's by a relative error of at most 0.024.
Values may be sent and summed in bfloat16 or wider, within the bound.
No kernel may reach another device: no remote copies, remote signals or barrier semaphores. Data moves between devices by JAX's collectives and lax.ppermute only.
A program may use at most 128 MiB of HBM per device.

v0:
```python
import jax
import jax.numpy as jnp
from jax import lax
from jax.sharding import PartitionSpec as P

D = 768
HEAD = 64
SEQ = 256
MICRO = 2


EPSILON = 1e-06


def norm_apply(resid, gain, shift):
    center = resid - jnp.mean(resid, axis=-1, keepdims=True)
    spread = jnp.mean(center * center, axis=-1, keepdims=True)
    return center * lax.rsqrt(spread + EPSILON) * gain + shift


def gelu_exact(value):
    return jax.nn.gelu(value, approximate=False)


def per_device(
    layer_input,
    pair_lengths,
    query_weight,
    query_bias,
    key_weight,
    value_weight,
    value_bias,
    out_weight,
    out_bias,
    first_gain,
    first_shift,
    up_weight,
    up_bias,
    down_weight,
    down_bias,
    second_gain,
    second_shift,
    out_grad,
    query_tangent,
    key_tangent,
    value_tangent,
    out_tangent,
    up_tangent,
    down_tangent,
):
    total_rows = layer_input.shape[0]
    step_rows = total_rows // MICRO
    step_pairs = step_rows // SEQ
    local_width = query_weight.shape[1]
    local_hidden = up_weight.shape[1]
    local_heads = local_width // HEAD
    scale = HEAD ** (-0.5)
    shape_heads = (step_pairs, SEQ, local_heads, HEAD)

    def zeros_of(shape):
        return jnp.zeros(shape, jnp.float32)

    zero_width = zeros_of((D,))
    own_query = zeros_of(query_weight.shape)
    own_key = zeros_of(key_weight.shape)
    own_value = zeros_of(value_weight.shape)
    own_out = zeros_of(out_weight.shape)
    own_up = zeros_of(up_weight.shape)
    own_down = zeros_of(down_weight.shape)
    sum_qbias = zeros_of((local_width,))
    sum_vbias = zeros_of((local_width,))
    sum_obias = zeros_of((D,))
    sum_gain_one = zeros_of((D,))
    sum_shift_one = zeros_of((D,))
    sum_ubias = zeros_of((local_hidden,))
    sum_dbias = zeros_of((D,))
    sum_gain_two = zeros_of((D,))
    sum_shift_two = zeros_of((D,))
    output_blocks = []
    grad_blocks = []
    along_blocks = []
    for index in range(MICRO):
        start = index * step_rows
        rows_in = layer_input[start : start + step_rows]
        lengths = pair_lengths[index * step_pairs : (index + 1) * step_pairs]
        upstream = out_grad[start : start + step_rows].astype(jnp.float32)
        (
            query_full,
            key_full,
            value_full,
            out_full,
            up_full,
            down_full,
            tquery_full,
            tkey_full,
            tvalue_full,
            tout_full,
            tup_full,
            tdown_full,
        ) = (
            lax.all_gather(query_weight, "dp", axis=0, tiled=True),
            lax.all_gather(key_weight, "dp", axis=0, tiled=True),
            lax.all_gather(value_weight, "dp", axis=0, tiled=True),
            lax.all_gather(out_weight, "dp", axis=1, tiled=True),
            lax.all_gather(up_weight, "dp", axis=0, tiled=True),
            lax.all_gather(down_weight, "dp", axis=1, tiled=True),
            lax.all_gather(query_tangent, "dp", axis=0, tiled=True),
            lax.all_gather(key_tangent, "dp", axis=0, tiled=True),
            lax.all_gather(value_tangent, "dp", axis=0, tiled=True),
            lax.all_gather(out_tangent, "dp", axis=1, tiled=True),
            lax.all_gather(up_tangent, "dp", axis=0, tiled=True),
            lax.all_gather(down_tangent, "dp", axis=1, tiled=True),
        )
        queries = (
            jnp.dot(rows_in, query_full, preferred_element_type=jnp.float32) + query_bias
        ).astype(jnp.bfloat16)
        keys = jnp.dot(rows_in, key_full, preferred_element_type=jnp.float32).astype(jnp.bfloat16)
        values = (
            jnp.dot(rows_in, value_full, preferred_element_type=jnp.float32) + value_bias
        ).astype(jnp.bfloat16)
        query_heads = queries.reshape(shape_heads)
        key_heads = keys.reshape(shape_heads)
        value_heads = values.reshape(shape_heads)
        tquery_heads = (
            jnp.dot(rows_in, tquery_full, preferred_element_type=jnp.float32)
            .astype(jnp.bfloat16)
            .reshape(shape_heads)
        )
        tkey_heads = (
            jnp.dot(rows_in, tkey_full, preferred_element_type=jnp.float32)
            .astype(jnp.bfloat16)
            .reshape(shape_heads)
        )
        tvalue_heads = (
            jnp.dot(rows_in, tvalue_full, preferred_element_type=jnp.float32)
            .astype(jnp.bfloat16)
            .reshape(shape_heads)
        )
        valid = (
            lax.broadcasted_iota(jnp.int32, (step_pairs, 1, 1, SEQ), 3)
            < lengths[:, None, None, None]
        )

        def scores_of():
            raw = (
                jnp.einsum(
                    "pqhd,pkhd->phqk", query_heads, key_heads, preferred_element_type=jnp.float32
                )
                * scale
            )
            return jnp.where(valid, raw, jnp.float32(-1e30))

        scores = scores_of()
        top = jnp.max(scores, axis=-1, keepdims=True)
        expo = jnp.exp(scores - top)
        totals = jnp.sum(expo, axis=-1, keepdims=True)
        log_total = top + jnp.log(totals)
        probs_full = expo / totals
        probs_low = probs_full.astype(jnp.bfloat16)
        context = jnp.einsum(
            "phqk,pkhd->pqhd", probs_low, value_heads, preferred_element_type=jnp.float32
        )
        context_low = context.reshape(step_rows, local_width).astype(jnp.bfloat16)
        attn_part = jnp.dot(context_low, out_full, preferred_element_type=jnp.float32)
        tscores = jnp.einsum(
            "pqhd,pkhd->phqk", tquery_heads, key_heads, preferred_element_type=jnp.float32
        )
        tscores = tscores + jnp.einsum(
            "pqhd,pkhd->phqk", query_heads, tkey_heads, preferred_element_type=jnp.float32
        )
        tscores = jnp.where(valid, tscores * scale, jnp.float32(0.0))
        tprobs = probs_full * (tscores - jnp.sum(tscores * probs_full, axis=-1, keepdims=True))
        tprobs_low = tprobs.astype(jnp.bfloat16)
        tcontext = jnp.einsum(
            "phqk,pkhd->pqhd", tprobs_low, value_heads, preferred_element_type=jnp.float32
        )
        tcontext = tcontext + jnp.einsum(
            "phqk,pkhd->pqhd", probs_low, tvalue_heads, preferred_element_type=jnp.float32
        )
        tcontext_low = tcontext.reshape(step_rows, local_width).astype(jnp.bfloat16)
        tattn_part = jnp.dot(tcontext_low, out_full, preferred_element_type=jnp.float32)
        tattn_part = tattn_part + jnp.dot(
            context_low, tout_full, preferred_element_type=jnp.float32
        )
        attended, tattended = (
            lax.psum(attn_part.astype(jnp.bfloat16), "tp").astype(jnp.float32),
            lax.psum(tattn_part.astype(jnp.bfloat16), "tp").astype(jnp.float32),
        )
        resid_one = rows_in.astype(jnp.float32) + attended + out_bias
        first, first_pull = jax.vjp(norm_apply, resid_one, first_gain, first_shift)
        _, tfirst = jax.jvp(
            norm_apply, (resid_one, first_gain, first_shift), (tattended, zero_width, zero_width)
        )
        first_low = first.astype(jnp.bfloat16)
        tfirst_low = tfirst.astype(jnp.bfloat16)
        upper = jnp.dot(first_low, up_full, preferred_element_type=jnp.float32) + up_bias
        tupper = jnp.dot(tfirst_low, up_full, preferred_element_type=jnp.float32)
        tupper = tupper + jnp.dot(first_low, tup_full, preferred_element_type=jnp.float32)
        active, gelu_pull = jax.vjp(gelu_exact, upper)
        _, tactive = jax.jvp(gelu_exact, (upper,), (tupper,))
        active_low = active.astype(jnp.bfloat16)
        tactive_low = tactive.astype(jnp.bfloat16)
        down_part = jnp.dot(active_low, down_full, preferred_element_type=jnp.float32)
        tdown_part = jnp.dot(tactive_low, down_full, preferred_element_type=jnp.float32)
        tdown_part = tdown_part + jnp.dot(
            active_low, tdown_full, preferred_element_type=jnp.float32
        )
        lowered, tlowered = (
            lax.psum(down_part.astype(jnp.bfloat16), "tp").astype(jnp.float32),
            lax.psum(tdown_part.astype(jnp.bfloat16), "tp").astype(jnp.float32),
        )
        resid_two = first + lowered + down_bias
        result, second_pull = jax.vjp(norm_apply, resid_two, second_gain, second_shift)
        _, tresult = jax.jvp(
            norm_apply,
            (resid_two, second_gain, second_shift),
            (tfirst + tlowered, zero_width, zero_width),
        )
        output_blocks.append(result.astype(jnp.bfloat16))
        along_blocks.append(tresult.astype(jnp.bfloat16))
        query_full, key_full, value_full, out_full, up_full, down_full = (
            lax.all_gather(query_weight, "dp", axis=0, tiled=True),
            lax.all_gather(key_weight, "dp", axis=0, tiled=True),
            lax.all_gather(value_weight, "dp", axis=0, tiled=True),
            lax.all_gather(out_weight, "dp", axis=1, tiled=True),
            lax.all_gather(up_weight, "dp", axis=0, tiled=True),
            lax.all_gather(down_weight, "dp", axis=1, tiled=True),
        )
        grad_two, gain_two, shift_two = second_pull(upstream)
        grad_down_low = grad_two.astype(jnp.bfloat16)
        step_down = jnp.einsum(
            "rf,rd->fd", active_low, grad_down_low, preferred_element_type=jnp.float32
        )
        grad_active = jnp.einsum(
            "rd,fd->rf", grad_down_low, down_full, preferred_element_type=jnp.float32
        )
        (grad_upper,) = gelu_pull(grad_active)
        grad_upper_low = grad_upper.astype(jnp.bfloat16)
        step_up = jnp.einsum(
            "rd,rf->df", first_low, grad_upper_low, preferred_element_type=jnp.float32
        )
        first_part = jnp.einsum(
            "rf,df->rd", grad_upper_low, up_full, preferred_element_type=jnp.float32
        )
        grad_first = lax.psum(first_part.astype(jnp.bfloat16), "tp").astype(jnp.float32) + grad_two
        grad_one, gain_one, shift_one = first_pull(grad_first)
        grad_attn_low = grad_one.astype(jnp.bfloat16)
        step_out = jnp.einsum(
            "rc,rd->cd", context_low, grad_attn_low, preferred_element_type=jnp.float32
        )
        grad_context = jnp.einsum(
            "rd,cd->rc", grad_attn_low, out_full, preferred_element_type=jnp.float32
        )
        grad_context_heads = grad_context.astype(jnp.bfloat16).reshape(shape_heads)
        probs = jnp.exp(scores_of() - log_total)
        again_low = probs.astype(jnp.bfloat16)
        grad_values = jnp.einsum(
            "phqk,pqhd->pkhd", again_low, grad_context_heads, preferred_element_type=jnp.float32
        )
        grad_values_low = grad_values.astype(jnp.bfloat16).reshape(step_rows, local_width)
        grad_probs = jnp.einsum(
            "pqhd,pkhd->phqk", grad_context_heads, value_heads, preferred_element_type=jnp.float32
        )
        grad_scores = probs * (grad_probs - jnp.sum(grad_probs * probs, axis=-1, keepdims=True))
        grad_scores_low = grad_scores.astype(jnp.bfloat16)
        grad_queries = (
            jnp.einsum(
                "phqk,pkhd->pqhd", grad_scores_low, key_heads, preferred_element_type=jnp.float32
            )
            * scale
        )
        grad_keys = (
            jnp.einsum(
                "phqk,pqhd->pkhd", grad_scores_low, query_heads, preferred_element_type=jnp.float32
            )
            * scale
        )
        grad_queries_low = grad_queries.astype(jnp.bfloat16).reshape(step_rows, local_width)
        grad_keys_low = grad_keys.astype(jnp.bfloat16).reshape(step_rows, local_width)
        step_query = jnp.einsum(
            "rd,rc->dc", rows_in, grad_queries_low, preferred_element_type=jnp.float32
        )
        step_key = jnp.einsum(
            "rd,rc->dc", rows_in, grad_keys_low, preferred_element_type=jnp.float32
        )
        step_value = jnp.einsum(
            "rd,rc->dc", rows_in, grad_values_low, preferred_element_type=jnp.float32
        )
        input_part = jnp.einsum(
            "rc,dc->rd", grad_queries_low, query_full, preferred_element_type=jnp.float32
        )
        input_part = input_part + jnp.einsum(
            "rc,dc->rd", grad_keys_low, key_full, preferred_element_type=jnp.float32
        )
        input_part = input_part + jnp.einsum(
            "rc,dc->rd", grad_values_low, value_full, preferred_element_type=jnp.float32
        )
        grad_input = lax.psum(input_part.astype(jnp.bfloat16), "tp").astype(jnp.float32) + grad_one
        grad_blocks.append(grad_input.astype(jnp.bfloat16))
        sum_qbias = sum_qbias + jnp.sum(grad_queries_low.astype(jnp.float32), axis=0)
        sum_vbias = sum_vbias + jnp.sum(grad_values_low.astype(jnp.float32), axis=0)
        sum_obias = sum_obias + jnp.sum(grad_one, axis=0)
        sum_gain_one = sum_gain_one + gain_one
        sum_shift_one = sum_shift_one + shift_one
        sum_ubias = sum_ubias + jnp.sum(grad_upper, axis=0)
        sum_dbias = sum_dbias + jnp.sum(grad_two, axis=0)
        sum_gain_two = sum_gain_two + gain_two
        sum_shift_two = sum_shift_two + shift_two
        piece_query, piece_key, piece_value, piece_out, piece_up, piece_down = (
            lax.psum_scatter(
                step_query.astype(jnp.bfloat16), "dp", scatter_dimension=0, tiled=True
            ).astype(jnp.float32),
            lax.psum_scatter(
                step_key.astype(jnp.bfloat16), "dp", scatter_dimension=0, tiled=True
            ).astype(jnp.float32),
            lax.psum_scatter(
                step_value.astype(jnp.bfloat16), "dp", scatter_dimension=0, tiled=True
            ).astype(jnp.float32),
            lax.psum_scatter(
                step_out.astype(jnp.bfloat16), "dp", scatter_dimension=1, tiled=True
            ).astype(jnp.float32),
            lax.psum_scatter(
                step_up.astype(jnp.bfloat16), "dp", scatter_dimension=0, tiled=True
            ).astype(jnp.float32),
            lax.psum_scatter(
                step_down.astype(jnp.bfloat16), "dp", scatter_dimension=1, tiled=True
            ).astype(jnp.float32),
        )
        own_query = own_query + piece_query
        own_key = own_key + piece_key
        own_value = own_value + piece_value
        own_out = own_out + piece_out
        own_up = own_up + piece_up
        own_down = own_down + piece_down
    small_sums = lax.psum(
        (
            sum_qbias,
            sum_vbias,
            sum_obias,
            sum_gain_one,
            sum_shift_one,
            sum_ubias,
            sum_dbias,
            sum_gain_two,
            sum_shift_two,
        ),
        "dp",
    )
    return (
        jnp.concatenate(output_blocks, axis=0),
        jnp.concatenate(grad_blocks, axis=0),
        jnp.concatenate(along_blocks, axis=0),
        own_query,
        small_sums[0],
        own_key,
        own_value,
        small_sums[1],
        own_out,
        small_sums[2],
        small_sums[3],
        small_sums[4],
        own_up,
        small_sums[5],
        own_down,
        small_sums[6],
        small_sums[7],
        small_sums[8],
    )


def solution(mesh):
    placed = (
        P("dp", None),
        P("dp"),
        P("dp", "tp"),
        P("tp"),
        P("dp", "tp"),
        P("dp", "tp"),
        P("tp"),
        P("tp", "dp"),
        P(),
        P(),
        P(),
        P("dp", "tp"),
        P("tp"),
        P("tp", "dp"),
        P(),
        P(),
        P(),
        P("dp", None),
        P("dp", "tp"),
        P("dp", "tp"),
        P("dp", "tp"),
        P("tp", "dp"),
        P("dp", "tp"),
        P("tp", "dp"),
    )
    return jax.shard_map(
        per_device,
        mesh=mesh,
        in_specs=placed,
        out_specs=(
            P("dp", None),
            P("dp", None),
            P("dp", None),
            P("dp", "tp"),
            P("tp"),
            P("dp", "tp"),
            P("dp", "tp"),
            P("tp"),
            P("tp", "dp"),
            P(),
            P(),
            P(),
            P("dp", "tp"),
            P("tp"),
            P("tp", "dp"),
            P(),
            P(),
            P(),
        ),
        check_vma=False,
    )
```

profile of v0, /device:TPU:0, one launch (start us, length us, event | category | flops | bytes accessed | tf_op | source)
XLA Modules:
  0.0 1256.8 jit_solution(17693199640528512861)
XLA Ops:
  11.0 32.7 %all_gather.27 = bf16[192,768]{0,1:T(8,128)(2,1)S(1)} all-gather(bf16[192,96]{0,1:T(8,128)(2,1)S(1)} %copy.58), channel_id=1, replica_groups=mesh['dp'=8,'tp'=4] {'dp'}, dimensions={1}, use_global_device_ids=true | all-gather | bytes 331776 | tf_op jit(solution)/shard_map/all_gather | solution.py:104
  43.7 31.5 %all_gather.25 = bf16[768,192]{1,0:T(8,128)(2,1)S(1)} all-gather(bf16[96,192]{1,0:T(8,128)(2,1)} %param.26), channel_id=1, replica_groups=mesh['dp'=8,'tp'=4] {'dp'}, dimensions={0}, use_global_device_ids=true | all-gather | bytes 331776 | tf_op jit(solution)/shard_map/all_gather | solution.py:101
  75.2 31.2 %all_gather.26 = bf16[768,192]{1,0:T(8,128)(2,1)S(1)} all-gather(bf16[96,192]{1,0:T(8,128)(2,1)} %param.28), channel_id=1, replica_groups=mesh['dp'=8,'tp'=4] {'dp'}, dimensions={0}, use_global_device_ids=true | all-gather | bytes 331776 | tf_op jit(solution)/shard_map/all_gather | solution.py:102
  106.4 31.0 %all_gather.24 = bf16[768,192]{1,0:T(8,128)(2,1)S(1)} all-gather(bf16[96,192]{1,0:T(8,128)(2,1)S(1)} %copy-done.85), channel_id=1, replica_groups=mesh['dp'=8,'tp'=4] {'dp'}, dimensions={0}, use_global_device_ids=true | all-gather | bytes 331776 | tf_op jit(solution)/shard_map/all_gather | solution.py:103
  145.8 31.4 %all_gather.30 = bf16[768,192]{1,0:T(8,128)(2,1)S(1)} all-gather(bf16[96,192]{1,0:T(8,128)(2,1)S(1)} %copy-done.86), channel_id=1, replica_groups=mesh['dp'=8,'tp'=4] {'dp'}, dimensions={0}, use_global_device_ids=true | all-gather | bytes 331776 | tf_op jit(solution)/shard_map/all_gather | solution.py:107
  177.6 31.6 %all_gather.31 = bf16[768,192]{1,0:T(8,128)(2,1)S(1)} all-gather(bf16[96,192]{1,0:T(8,128)(2,1)S(1)} %copy-done.87), channel_id=1, replica_groups=mesh['dp'=8,'tp'=4] {'dp'}, dimensions={0}, use_global_device_ids=true | all-gather | bytes 331776 | tf_op jit(solution)/shard_map/all_gather | solution.py:108
  209.5 31.5 %all_gather.32 = bf16[768,192]{1,0:T(8,128)(2,1)S(1)} all-gather(bf16[96,192]{1,0:T(8,128)(2,1)S(1)} %copy-done.88), channel_id=1, replica_groups=mesh['dp'=8,'tp'=4] {'dp'}, dimensions={0}, use_global_device_ids=true | all-gather | bytes 331776 | tf_op jit(solution)/shard_map/all_gather | solution.py:109
  244.7 31.3 %all_gather.33 = bf16[192,768]{0,1:T(8,128)(2,1)S(1)} all-gather(bf16[192,96]{0,1:T(8,128)(2,1)S(1)} %copy-done.82), channel_id=1, replica_groups=mesh['dp'=8,'tp'=4] {'dp'}, dimensions={1}, use_global_device_ids=true | all-gather | bytes 331776 | tf_op jit(solution)/shard_map/all_gather | solution.py:110
  280.1 4.5 multiply_convert_fusion.5
  284.6 2.6 convolution_convert_fusion.8
  288.6 32.6 %all-reduce.13.cloned.1.call-done = bf16[256,768]{1,0:T(8,128)(2,1)} async-done(((bf16[256,768]{1,0:T(8,128)(2,1)}), bf16[256,768]{1,0:T(8,128)(2,1)}) %all-reduce.13.cloned.1.call-update) | async-done | bytes 393232 | tf_op jit(solution)/shard_map/psum | solution.py:209
  328.9 37.8 %all-reduce.21.cloned.1.call-done = (bf16[256,768]{1,0:T(8,128)(2,1)}, bf16[256,768]{1,0:T(8,128)(2,1)}, bf16[256,768]{1,0:T(8,128)(2,1)}) async-done(((bf16[256,768]{1,0:T(8,128)(2,1)}, bf16[256,768]{1,0:T(8,128)(2,1)}, bf16[256,768]{1,0:T(8,128)(2,1)}), (bf16[256,768]{1,0:T(8,128)(2,1)}, bf16[256,768]{1,0:T(8,128)(2,1)}, bf16[256,768]{1,0:T(8,128)(2,1)})) %all-reduce.21.cloned.1.call-update) | async-done | bytes 1179664 | tf_op jit(solution)/shard_map/psum | solution.py:245
  367.9 2.9 multiply_reduce_fusion.3
  371.0 3.5 fusion.156
  374.5 3.2 multiply_convert_fusion.4
  391.1 21.5 %all-reduce.15.cloned.1.call-done = bf16[256,768]{1,0:T(8,128)(2,1)} async-done(((bf16[256,768]{1,0:T(8,128)(2,1)}), bf16[256,768]{1,0:T(8,128)(2,1)}) %all-reduce.15.cloned.1.call-update) | async-done | bytes 393232 | tf_op jit(solution)/shard_map/psum | solution.py:209
  420.5 2.6 convert_reduce_fusion.5
  425.0 3.2 multiply_reduce_fusion.8
  439.6 2.0 fusion.23
  441.5 2.2 fusion.169
  450.4 2.9 fusion.89
  453.4 4.5 fusion.53
  457.9 8.9 all-gather.11.cloned.1.call-done
  466.8 2.9 fusion.9
  470.9 2.9 multiply_reduce_fusion.2
  479.4 2.2 convolution_convert_fusion.25
  484.9 2.7 multiply_reduce_fusion.6
  489.0 1.9 convert_reduce_fusion.6
  495.1 2.0 copy.92
  497.1 2.1 fusion.170
  499.2 2.7 fusion.86
  501.9 4.4 fusion.52
  511.8 2.8 convolution_convert_fusion.1
  515.6 2.8 convolution_convert_fusion
  519.4 2.7 convolution_convert_fusion.3
  526.1 2.7 convolution_convert_fusion.2
  531.4 63.2 %reduce-scatter.45.cloned.1.call-done = bf16[96,192]{1,0:T(8,128)(2,1)} async-done(((bf16[768,192]{1,0:T(8,128)(2,1)}), bf16[96,192]{1,0:T(8,128)(2,1)}) %reduce-scatter.45.cloned.1.call-update) | async-done | bytes 36880
  595.5 63.2 %reduce-scatter.37.cloned.1.call-done = bf16[96,192]{1,0:T(8,128)(2,1)} async-done(((bf16[768,192]{1,0:T(8,128)(2,1)}), bf16[96,192]{1,0:T(8,128)(2,1)}) %reduce-scatter.37.cloned.1.call-update) | async-done | bytes 36880
  659.6 63.1 %reduce-scatter.41.cloned.1.call-done = bf16[96,192]{1,0:T(8,128)(2,1)} async-done(((bf16[768,192]{1,0:T(8,128)(2,1)}), bf16[96,192]{1,0:T(8,128)(2,1)}) %reduce-scatter.41.cloned.1.call-update) | async-done | bytes 36880
  726.7 59.9 %reduce-scatter.51.cloned.1.call-done = bf16[96,192]{1,0:T(8,128)(2,1)} async-done(((bf16[768,192]{1,0:T(8,128)(2,1)}), bf16[96,192]{1,0:T(8,128)(2,1)}) %reduce-scatter.51.cloned.1.call-update) | async-done | bytes 36880
  787.6 63.3 %reduce-scatter.47.cloned.1.call-done = bf16[96,192]{1,0:T(8,128)(2,1)} async-done(((bf16[768,192]{1,0:T(8,128)(2,1)}), bf16[96,192]{1,0:T(8,128)(2,1)}) %reduce-scatter.47.cloned.1.call-update) | async-done | bytes 36880
  852.5 62.3 %reduce-scatter.39.cloned.1.call-done = bf16[96,192]{1,0:T(8,128)(2,1)} async-done(((bf16[768,192]{1,0:T(8,128)(2,1)}), bf16[96,192]{1,0:T(8,128)(2,1)}) %reduce-scatter.39.cloned.1.call-update) | async-done | bytes 36880
  916.5 62.5 %reduce-scatter.43.cloned.1.call-done = bf16[96,192]{1,0:T(8,128)(2,1)} async-done(((bf16[768,192]{1,0:T(8,128)(2,1)}), bf16[96,192]{1,0:T(8,128)(2,1)}) %reduce-scatter.43.cloned.1.call-update) | async-done | bytes 36880
  987.1 36.7 %all-reduce = (f32[192]{0:T(256)}, f32[192]{0:T(256)}, f32[768]{0:T(1024)}, f32[768]{0:T(1024)}, f32[768]{0:T(1024)}, /*index=5*/f32[768]{0:T(1024)}, f32[768]{0:T(1024)}, f32[768]{0:T(1024)}, f32[768]{0:T(1024)}) all-reduce(f32[192]{0:T(256)} %add.418, f32[192]{0:T(256)} %add.422, ...), channel_id=1, replica_groups=mesh['dp'=8,'tp'=4] {'dp'}, use_global_device_ids=true, to_apply=%region_48.49 | all-reduce | flops 5760 | bytes 46080 | tf_op jit(solution)/shard_map/psum | solution.py:335
  1030.3 15.7 %reduce-scatter.33.cloned.1.call-done = bf16[768,96]{0,1:T(8,128)(2,1)} async-done(((bf16[768,768]{0,1:T(8,128)(2,1)}), bf16[768,96]{0,1:T(8,128)(2,1)}) %reduce-scatter.33.cloned.1.call-update) | async-done | bytes 147472 | tf_op jit(solution)/shard_map/reduce_scatter | solution.py:325
  1046.0 67.0 %reduce-scatter.35.cloned.1.call-done = bf16[768,96]{0,1:T(8,128)(2,1)} async-done(((bf16[768,768]{0,1:T(8,128)(2,1)}), bf16[768,96]{0,1:T(8,128)(2,1)}) %reduce-scatter.35.cloned.1.call-update) | async-done | bytes 147472 | tf_op jit(solution)/shard_map/reduce_scatter | solution.py:325
  1114.7 65.4 %reduce-scatter.29.cloned.1.call-done = bf16[96,768]{1,0:T(8,128)(2,1)} async-done(((bf16[768,768]{1,0:T(8,128)(2,1)}), bf16[96,768]{1,0:T(8,128)(2,1)}) %reduce-scatter.29.cloned.1.call-update) | async-done | bytes 147472 | tf_op jit(solution)/shard_map/reduce_scatter | solution.py:322
  1180.1 66.9 %reduce-scatter.31.cloned.1.call-done = bf16[96,768]{1,0:T(8,128)(2,1)} async-done(((bf16[768,768]{1,0:T(8,128)(2,1)}), bf16[96,768]{1,0:T(8,128)(2,1)}) %reduce-scatter.31.cloned.1.call-update) | async-done | bytes 147472 | tf_op jit(solution)/shard_map/reduce_scatter | solution.py:322
  (504 shorter events, 127.5 us)
Async XLA Ops:
  8.0 98.4 %copy-start.85 = (bf16[96,192]{1,0:T(8,128)(2,1)S(1)}, bf16[96,192]{1,0:T(8,128)(2,1)}, u32[]{:S(2)}) copy-start(bf16[96,192]{1,0:T(8,128)(2,1)} %param.29) | copy-start | bytes 110596
  8.0 129.4 %copy-start = (bf16[512,768]{1,0:T(8,128)(2,1)S(1)}, bf16[512,768]{1,0:T(8,128)(2,1)}, u32[]{:S(2)}) copy-start(bf16[512,768]{1,0:T(8,128)(2,1)} %param.24) | copy-start | bytes 2359300
  8.0 269.4 %all-reduce.11.cloned.1.call-start = ((), (), s32[]{:S(2)}) async-start(), calls=%async_computation.12 | async-start | bytes 786432 | tf_op jit(solution)/shard_map/psum | solution.py:186
  10.1 128.4 %copy-start.147 = (pred[256]{0:T(512)(128)(4,1)}, pred[256]{0:T(512)(128)(4,1)S(1)}, u32[]{:S(2)}) copy-start(pred[256]{0:T(512)(128)(4,1)S(1)} %iota_compare_fusion.1) | copy-start | bytes 772
  43.7 94.0 %copy-start.142 = (f32[192]{0:T(256)S(1)}, f32[192]{0:T(256)}, u32[]{:S(2)}) copy-start(f32[192]{0:T(256)} %param.27) | copy-start | bytes 2308
  75.2 66.3 %copy-start.17 = (bf16[768,192]{1,0:T(8,128)(2,1)}, bf16[768,192]{1,0:T(8,128)(2,1)S(1)}, u32[]{:S(2)}) copy-start(bf16[768,192]{1,0:T(8,128)(2,1)S(1)} %all_gather.25) | copy-start | bytes 884740
  106.4 36.1 %copy-start.19 = (bf16[768,192]{1,0:T(8,128)(2,1)}, bf16[768,192]{1,0:T(8,128)(2,1)S(1)}, u32[]{:S(2)}) copy-start(bf16[768,192]{1,0:T(8,128)(2,1)S(1)} %all_gather.26) | copy-start | bytes 884740
  137.7 103.6 %copy-start.55 = (bf16[256,192]{0,1:T(8,128)(2,1)}, bf16[256,192]{0,1:T(8,128)(2,1)S(1)}, u32[]{:S(2)}) copy-start(bf16[256,192]{0,1:T(8,128)(2,1)S(1)} %convolution_convert_fusion.31) | copy-start | bytes 294916
  138.1 103.6 %copy-start.63 = (bf16[256,192]{0,1:T(8,128)(2,1)}, bf16[256,192]{0,1:T(8,128)(2,1)S(1)}, u32[]{:S(2)}) copy-start(bf16[256,192]{0,1:T(8,128)(2,1)S(1)} %fusion.19) | copy-start | bytes 294916
  138.4 103.7 %copy-start.78 = (bf16[256,192]{0,1:T(8,128)(2,1)}, bf16[256,192]{0,1:T(8,128)(2,1)S(1)}, u32[]{:S(2)}) copy-start(bf16[256,192]{0,1:T(8,128)(2,1)S(1)} %fusion.18) | copy-start | bytes 294916
  138.8 103.7 %copy-start.1 = (f32[3,256,256]{1,2,0:T(8,128)}, f32[3,256,256]{1,2,0:T(8,128)S(1)}, u32[]{:S(2)}) copy-start(f32[3,256,256]{1,2,0:T(8,128)S(1)} %get-tuple-element.131) | copy-start | bytes 2359300
  138.9 103.6 %copy-start.116 = (f32[3,256]{1,0:T(4,128)}, f32[3,256]{1,0:T(4,128)S(1)}, u32[]{:S(2)}) copy-start(f32[3,256]{1,0:T(4,128)S(1)} %fusion.65) | copy-start | bytes 9220
  140.3 139.8 %all-gather.5.cloned.1.call-start = ((), (), s32[]{:S(2)}) async-start(), calls=%async_computation.13 | async-start | bytes 1327104 | tf_op jit(solution)/shard_map/all_gather | solution.py:105
  140.9 143.8 %all-gather.7.cloned.1.call-start = ((), (), s32[]{:S(2)}) async-start(), calls=%async_computation.14 | async-start | bytes 1327104 | tf_op jit(solution)/shard_map/all_gather | solution.py:106
  141.4 179.7 %all-reduce.13.cloned.1.call-start = ((), (), s32[]{:S(2)}) async-start(), calls=%async_computation.15 | async-start | bytes 786432 | tf_op jit(solution)/shard_map/psum | solution.py:209
  145.1 97.7 %copy-start.145 = (pred[256]{0:T(512)(128)(4,1)}, pred[256]{0:T(512)(128)(4,1)S(1)}, u32[]{:S(2)}) copy-start(pred[256]{0:T(512)(128)(4,1)S(1)} %iota_compare_fusion) | copy-start | bytes 772
  177.2 63.8 %copy-start.33 = (bf16[768,192]{1,0:T(8,128)(2,1)}, bf16[768,192]{1,0:T(8,128)(2,1)S(1)}, u32[]{:S(2)}) copy-start(bf16[768,192]{1,0:T(8,128)(2,1)S(1)} %all_gather.30) | copy-start | bytes 884740
  244.7 42.8 %copy-start.64 = (bf16[3,64,256]{2,1,0:T(8,128)(2,1)}, bf16[3,64,256]{2,1,0:T(8,128)(2,1)S(1)}, u32[]{:S(2)}) copy-start(bf16[3,64,256]{2,1,0:T(8,128)(2,1)S(1)} %convolution_convert_fusion.28) | copy-start | bytes 294916
  287.3 79.4 %all-reduce.21.cloned.1.call-start = ((), (), s32[]{:S(2)}) async-start(), calls=%async_computation.33 | async-start | bytes 2359296 | tf_op jit(solution)/shard_map/psum | solution.py:245
  324.9 43.0 %copy-start.13 = (f32[256,768]{1,0:T(8,128)}, f32[256,768]{1,0:T(8,128)S(1)}, u32[]{:S(2)}) copy-start(f32[256,768]{1,0:T(8,128)S(1)} %get-tuple-element.108) | copy-start | bytes 2359300
  328.8 83.8 %all-reduce.15.cloned.1.call-start = ((), (), s32[]{:S(2)}) async-start(), calls=%async_computation.16 | async-start | bytes 786432 | tf_op jit(solution)/shard_map/psum | solution.py:209
  379.8 73.5 %all-gather.9.cloned.1.call-start = ((), (), s32[]{:S(2)}) async-start(), calls=%async_computation.17 | async-start | bytes 1327104 | tf_op jit(solution)/shard_map/all_gather | solution.py:111
  380.4 86.4 %all-gather.11.cloned.1.call-start = ((), (), s32[]{:S(2)}) async-start(), calls=%async_computation.18 | async-start | bytes 1327104 | tf_op jit(solution)/shard_map/all_gather | solution.py:112
  381.1 88.5 %all-reduce.19.cloned.1.call-start = ((), (), s32[]{:S(2)}) async-start(), calls=%async_computation.32 | async-start | bytes 1572864 | tf_op jit(solution)/shard_map/psum | solution.py:245
  420.4 110.0 %reduce-scatter.49.cloned.1.call-start = ((), (), s32[]{:S(2)}) async-start(), calls=%async_computation.29 | async-start | bytes 442368
  428.2 166.4 %reduce-scatter.45.cloned.1.call-start = ((), (), s32[]{:S(2)}) async-start(), calls=%async_computation.27 | async-start | bytes 442368
  435.8 222.8 %reduce-scatter.37.cloned.1.call-start = ((), (), s32[]{:S(2)}) async-start(), calls=%async_computation.23 | async-start | bytes 442368
  443.8 278.9 %reduce-scatter.41.cloned.1.call-start = ((), (), s32[]{:S(2)}) async-start(), calls=%async_computation.25 | async-start | bytes 442368
  450.4 336.3 %reduce-scatter.51.cloned.1.call-start = ((), (), s32[]{:S(2)}) async-start(), calls=%async_computation.30 | async-start | bytes 442368
  481.5 369.3 %reduce-scatter.47.cloned.1.call-start = ((), (), s32[]{:S(2)}) async-start(), calls=%async_computation.28 | async-start | bytes 442368
  487.6 427.2 %reduce-scatter.39.cloned.1.call-start = ((), (), s32[]{:S(2)}) async-start(), calls=%async_computation.24 | async-start | bytes 442368
  492.1 486.9 %reduce-scatter.43.cloned.1.call-start = ((), (), s32[]{:S(2)}) async-start(), calls=%async_computation.26 | async-start | bytes 442368
  499.2 482.2 %all-reduce.17.cloned.1.call-start = ((), (), s32[]{:S(2)}) async-start(), calls=%async_computation.31 | async-start | bytes 3145728 | tf_op jit(solution)/shard_map/psum | solution.py:298
  510.8 535.1 %reduce-scatter.33.cloned.1.call-start = ((), (), s32[]{:S(2)}) async-start(), calls=%async_computation.21 | async-start | bytes 1327104 | tf_op jit(solution)/shard_map/reduce_scatter | solution.py:325
  514.6 598.4 %reduce-scatter.35.cloned.1.call-start = ((), (), s32[]{:S(2)}) async-start(), calls=%async_computation.22 | async-start | bytes 1327104 | tf_op jit(solution)/shard_map/reduce_scatter | solution.py:325
  518.4 661.7 %reduce-scatter.29.cloned.1.call-start = ((), (), s32[]{:S(2)}) async-start(), calls=%async_computation.19 | async-start | bytes 1327104 | tf_op jit(solution)/shard_map/reduce_scatter | solution.py:322
  522.2 724.9 %reduce-scatter.31.cloned.1.call-start = ((), (), s32[]{:S(2)}) async-start(), calls=%async_computation.20 | async-start | bytes 1327104 | tf_op jit(solution)/shard_map/reduce_scatter | solution.py:322
  528.9 194.7 %copy-start.138 = (f32[3,64]{1,0:T(4,128)S(1)}, f32[3,64]{1,0:T(4,128)}, u32[]{:S(2)}) copy-start(f32[3,64]{1,0:T(4,128)} %get-tuple-element.148) | copy-start | bytes 2308
  528.9 194.7 %copy-start.140 = (f32[3,64]{1,0:T(4,128)S(1)}, f32[3,64]{1,0:T(4,128)}, u32[]{:S(2)}) copy-start(f32[3,64]{1,0:T(4,128)} %get-tuple-element.150) | copy-start | bytes 2308
  528.9 195.4 %copy-start.139 = (f32[3,64]{1,0:T(4,128)S(1)}, f32[3,64]{1,0:T(4,128)}, u32[]{:S(2)}) copy-start(f32[3,64]{1,0:T(4,128)} %get-tuple-element.144) | copy-start | bytes 2308
  528.9 195.4 %copy-start.141 = (f32[3,64]{1,0:T(4,128)S(1)}, f32[3,64]{1,0:T(4,128)}, u32[]{:S(2)}) copy-start(f32[3,64]{1,0:T(4,128)} %get-tuple-element.146) | copy-start | bytes 2308
  528.9 196.0 %copy-start.112 = (f32[768]{0:T(1024)S(1)}, f32[768]{0:T(1024)}, u32[]{:S(2)}) copy-start(f32[768]{0:T(1024)} %get-tuple-element.68) | copy-start | bytes 9220
  528.9 196.0 %copy-start.115 = (f32[768]{0:T(1024)S(1)}, f32[768]{0:T(1024)}, u32[]{:S(2)}) copy-start(f32[768]{0:T(1024)} %get-tuple-element.67) | copy-start | bytes 9220
  528.9 196.6 %copy-start.111 = (f32[768]{0:T(1024)S(1)}, f32[768]{0:T(1024)}, u32[]{:S(2)}) copy-start(f32[768]{0:T(1024)} %get-tuple-element.65) | copy-start | bytes 9220
  528.9 196.6 %copy-start.114 = (f32[768]{0:T(1024)S(1)}, f32[768]{0:T(1024)}, u32[]{:S(2)}) copy-start(f32[768]{0:T(1024)} %get-tuple-element.64) | copy-start | bytes 9220
  528.9 197.2 %copy-start.110 = (f32[768]{0:T(1024)S(1)}, f32[768]{0:T(1024)}, u32[]{:S(2)}) copy-start(f32[768]{0:T(1024)} %get-tuple-element.56) | copy-start | bytes 9220
  528.9 197.2 %copy-start.113 = (f32[768]{0:T(1024)S(1)}, f32[768]{0:T(1024)}, u32[]{:S(2)}) copy-start(f32[768]{0:T(1024)} %get-tuple-element.54) | copy-start | bytes 9220
  852.5 130.2 %copy-start.3 = (f32[256,768]{1,0:T(8,128)S(1)}, f32[256,768]{1,0:T(8,128)}, u32[]{:S(2)}) copy-start(f32[256,768]{1,0:T(8,128)} %get-tuple-element.115) | copy-start | bytes 2359300
  (129 other events, 520.4 us)
Sparse Core Ops, SparseCore 0:
  140.4 34.1 all-reduce.10
  287.4 33.6 all-reduce.12
  328.9 37.7 all-reduce.20
  380.0 32.6 all-reduce.14
  420.5 34.8 all-reduce.18
  511.0 41.9 all-reduce.16
Sparse Core Ops, SparseCore 1:
  143.2 44.4 all-gather.4
  190.0 42.3 all-gather.6
  382.7 41.5 all-gather.8
  426.7 40.0 all-gather.10
  470.4 60.0 reduce-scatter.48
  534.1 60.4 reduce-scatter.44
  598.0 60.6 reduce-scatter.36
  662.1 60.5 reduce-scatter.40
  726.1 60.4 reduce-scatter.50
  790.3 60.5 reduce-scatter.46
  854.4 60.4 reduce-scatter.38
  918.5 60.5 reduce-scatter.42
  982.6 63.3 reduce-scatter.32
  1049.8 63.2 reduce-scatter.34
  1116.8 63.3 reduce-scatter.28
  1183.9 63.1 reduce-scatter.30
where the time goes:
time: 1270 us; the launch traced here: 1260 us
  waiting for transfers between devices  758 us (60%)
  blocking collectives  289 us (23%)
  matrix products  102 us (8%)
  other arithmetic  49.7 us (4%)
  local copies, waits for them, and re-layouts  39.1 us (3%)
  between operations  18.2 us (1%)
    unnamed x30, waiting for transfers between devices  442 us
    reduce_scatter x2, waiting for transfers between devices, per_device(): lax.psum_scatter(step_up.astype(jnp.bfloat16), 'dp', scatter_dimension=0,...  132 us
    reduce_scatter x2, waiting for transfers between devices, per_device(): lax.psum_scatter(step_down.astype(jnp.bfloat16), 'dp', scatter_dimension=...  82.7 us
    psum x2, waiting for transfers between devices, per_device(): lax.psum(down_part.astype(jnp.bfloat16), 'tp').astype(jnp.float32)  54.1 us
    psum x2, waiting for transfers between devices, per_device(): lax.psum(first_part.astype(jnp.bfloat16), 'tp').astype(jnp.float32)  37.8 us
    psum x1, blocking collectives, per_device(): lax.psum((sum_qbias, sum_vbias, sum_obias, sum_gain_one, sum_shift_one, s...  36.7 us
    unnamed x331, local copies, waits for them, and re-layouts  36.5 us
    all_gather x1, blocking collectives, per_device(): lax.all_gather(out_weight, 'dp', axis=1, tiled=True)  32.7 us
  transfers between devices with their start and end apart: 22, of which 16 were waited for; matrix products, arithmetic and copies ran while one was open for 12% of the time, Pallas kernels for 0%

commit v1 on v0

v1 whole, which is shorter than its diff:
```python
import jax
import jax.numpy as jnp
from jax import lax
from jax.sharding import PartitionSpec as P

HEAD = 64
SEQ = 256
EPSILON = 1e-06
SNAKE = (0, 2, 4, 6, 7, 5, 3, 1)
BF = jnp.bfloat16
F32 = jnp.float32


def dot(left, right, dims):
    return lax.dot_general(left, right, (dims, ((), ())), preferred_element_type=F32)


NN = ((1,), (0,))
NT = ((1,), (1,))
TN = ((0,), (0,))


def xor_pairs(size, bit):
    return [(i, i ^ bit) for i in range(size)]


def gather_rows(shard, dp):
    if dp != len(SNAKE):
        return lax.all_gather(shard, "dp", axis=0, tiled=True)
    size = len(SNAKE)
    ahead = [(SNAKE[i], SNAKE[(i + 1) % size]) for i in range(size)]
    behind = [(b, a) for a, b in ahead]
    place = [0] * size
    for position, device in enumerate(SNAKE):
        place[device] = position
    me = lax.axis_index("dp")
    own_place = jnp.array(place, jnp.int32)[me]
    order = jnp.array(SNAKE, jnp.int32)
    rows = shard.shape[0]
    whole = jnp.zeros((size * rows, shard.shape[1]), shard.dtype)
    whole = lax.dynamic_update_slice(whole, shard, (me * rows, 0))
    one = two = shard
    for step in range(1, size // 2 + 1):
        one = lax.ppermute(one, "dp", ahead)
        owner = order[(own_place - step) % size]
        whole = lax.dynamic_update_slice(whole, one, (owner * rows, 0))
        if step < size // 2:
            two = lax.ppermute(two, "dp", behind)
            owner = order[(own_place + step) % size]
            whole = lax.dynamic_update_slice(whole, two, (owner * rows, 0))
    return whole


def scatter_sum(part, tp):
    count, rows, width = part.shape
    me = lax.axis_index("tp")
    rest = part.reshape(count, tp, rows // tp, width)
    size = tp
    bit = 1
    while bit < tp:
        size = size // 2
        split = rest.reshape(count, size, 2, rows // tp, width)
        mine = (me // bit) % 2
        keep = lax.dynamic_index_in_dim(split, mine, 2, keepdims=False)
        send = lax.dynamic_index_in_dim(split, 1 - mine, 2, keepdims=False)
        came = lax.ppermute(send.astype(BF), "tp", xor_pairs(tp, bit))
        rest = keep.astype(F32) + came.astype(F32)
        bit = bit * 2
        if bit < tp:
            rest = rest.astype(BF)
    return rest.reshape(count, rows // tp, width)


def norm_parts(resid):
    center = resid - jnp.mean(resid, axis=-1, keepdims=True)
    inverse = lax.rsqrt(jnp.mean(center * center, axis=-1, keepdims=True) + EPSILON)
    return center * inverse, inverse


def norm_along(unit, inverse, along):
    shifted = along - jnp.mean(along, axis=-1, keepdims=True)
    return inverse * (shifted - unit * jnp.mean(unit * shifted, axis=-1, keepdims=True))


def per_device(tp, dp, *arrays):
    (
        layer_input,
        pair_lengths,
        query_weight,
        query_bias,
        key_weight,
        value_weight,
        value_bias,
        out_weight,
        out_bias,
        first_gain,
        first_shift,
        up_weight,
        up_bias,
        down_weight,
        down_bias,
        second_gain,
        second_shift,
        out_grad,
        query_tangent,
        key_tangent,
        value_tangent,
        out_tangent,
        up_tangent,
        down_tangent,
    ) = arrays
    rows, width = layer_input.shape
    pairs = rows // SEQ
    cols = query_weight.shape[1]
    hidden = up_weight.shape[1]
    heads = cols // HEAD
    scale = HEAD ** (-0.5)
    me = lax.axis_index("tp")
    own_rows = rows // tp

    attn = gather_rows(
        jnp.concatenate(
            [query_weight, key_weight, value_weight, query_tangent, key_tangent, value_tangent], 1
        ),
        dp,
    )
    outs = gather_rows(jnp.concatenate([out_weight.T, out_tangent.T], 1), dp)
    ups = gather_rows(jnp.concatenate([up_weight, up_tangent], 1), dp)
    downs = gather_rows(jnp.concatenate([down_weight.T, down_tangent.T], 1), dp)
    out_full, tout_full = outs[:, :cols], outs[:, cols:]
    up_full, tup_full = ups[:, :hidden], ups[:, hidden:]
    down_full, tdown_full = downs[:, :hidden], downs[:, hidden:]

    rows_own = lax.dynamic_slice_in_dim(layer_input, me * own_rows, own_rows, 0).astype(F32)
    upstream = lax.dynamic_slice_in_dim(out_grad, me * own_rows, own_rows, 0).astype(F32)

    zeros = jnp.zeros((cols,), F32)
    shift_all = jnp.concatenate([query_bias, zeros, value_bias, zeros, zeros, zeros])
    mixed = (dot(layer_input, attn, NN) + shift_all).astype(BF)
    mixed = mixed.reshape(pairs, SEQ, 6, heads, HEAD)
    query, key, value, tquery, tkey, tvalue = [mixed[:, :, i] for i in range(6)]
    valid = (
        lax.broadcasted_iota(jnp.int32, (pairs, 1, 1, SEQ), 3) < pair_lengths[:, None, None, None]
    )

    def ein(text, left, right):
        return jnp.einsum(text, left, right, preferred_element_type=F32)

    scores = jnp.where(valid, ein("pqhd,pkhd->phqk", query, key) * scale, jnp.float32(-1e30))
    expo = jnp.exp(scores - jnp.max(scores, axis=-1, keepdims=True))
    probs = expo / jnp.sum(expo, axis=-1, keepdims=True)
    probs_low = probs.astype(BF)
    context = ein("phqk,pkhd->pqhd", probs_low, value).reshape(rows, cols).astype(BF)
    tscores = ein("pqhd,pkhd->phqk", tquery, key) + ein("pqhd,pkhd->phqk", query, tkey)
    tscores = jnp.where(valid, tscores * scale, jnp.float32(0.0))
    tprobs = probs * (tscores - jnp.sum(tscores * probs, axis=-1, keepdims=True))
    tcontext = ein("phqk,pkhd->pqhd", tprobs.astype(BF), value)
    tcontext = tcontext + ein("phqk,pkhd->pqhd", probs_low, tvalue)
    tcontext = tcontext.reshape(rows, cols).astype(BF)
    part = dot(context, out_full, NT).astype(BF)
    tpart = (dot(tcontext, out_full, NT) + dot(context, tout_full, NT)).astype(BF)
    attended, tattended = scatter_sum(jnp.stack([part, tpart]), tp)

    unit_one, inverse_one = norm_parts(rows_own + attended + out_bias)
    first = unit_one * first_gain + first_shift
    tfirst = norm_along(unit_one, inverse_one, tattended) * first_gain
    first_low = lax.all_gather(first.astype(BF), "tp", axis=0, tiled=True)
    tfirst_low = lax.all_gather(tfirst.astype(BF), "tp", axis=0, tiled=True)

    upper = dot(first_low, up_full, NN) + up_bias
    tupper = dot(tfirst_low, up_full, NN) + dot(first_low, tup_full, NN)
    half = 0.5 * (1.0 + lax.erf(upper * (2.0 ** -0.5)))
    active = (upper * half).astype(BF)
    slope = half + upper * (jnp.exp(-0.5 * upper * upper) * ((2.0 * jnp.pi) ** -0.5))
    tactive = (slope * tupper).astype(BF)
    part = dot(active, down_full, NT).astype(BF)
    tpart = (dot(tactive, down_full, NT) + dot(active, tdown_full, NT)).astype(BF)
    lowered, tlowered = scatter_sum(jnp.stack([part, tpart]), tp)

    unit_two, inverse_two = norm_parts(first + lowered + down_bias)
    result = (unit_two * second_gain + second_shift).astype(BF)
    tresult = (norm_along(unit_two, inverse_two, tfirst + tlowered) * second_gain).astype(BF)
    gain_two = jnp.sum(upstream * unit_two, axis=0)
    shift_two = jnp.sum(upstream, axis=0)
    grad_two = norm_along(unit_two, inverse_two, upstream * second_gain)
    bias_two = jnp.sum(grad_two, axis=0)
    grad_down = lax.all_gather(grad_two.astype(BF), "tp", axis=0, tiled=True)

    grad_active = dot(grad_down, down_full, NN)
    grad_upper = grad_active * slope
    bias_up = jnp.sum(grad_upper, axis=0)
    grad_upper_low = grad_upper.astype(BF)
    step_down = dot(grad_down, active, TN).astype(BF)
    step_up = dot(first_low, grad_upper_low, TN).astype(BF)
    part = dot(grad_upper_low, up_full, NT).astype(BF)
    (grad_first,) = scatter_sum(part[None], tp)
    grad_first = grad_first + grad_two

    gain_one = jnp.sum(grad_first * unit_one, axis=0)
    shift_one = jnp.sum(grad_first, axis=0)
    grad_one = norm_along(unit_one, inverse_one, grad_first * first_gain)
    bias_out = jnp.sum(grad_one, axis=0)
    grad_attn = lax.all_gather(grad_one.astype(BF), "tp", axis=0, tiled=True)

    step_out = dot(grad_attn, context, TN).astype(BF)
    grad_context = dot(grad_attn, out_full, NN).astype(BF).reshape(pairs, SEQ, heads, HEAD)
    grad_values = ein("phqk,pqhd->pkhd", probs_low, grad_context).astype(BF)
    grad_probs = ein("pqhd,pkhd->phqk", grad_context, value)
    grad_scores = probs * (grad_probs - jnp.sum(grad_probs * probs, axis=-1, keepdims=True))
    grad_scores = grad_scores.astype(BF)
    grad_queries = (ein("phqk,pkhd->pqhd", grad_scores, key) * scale).astype(BF)
    grad_keys = (ein("phqk,pqhd->pkhd", grad_scores, query) * scale).astype(BF)
    grad_mixed = jnp.concatenate(
        [g.reshape(rows, cols) for g in (grad_queries, grad_keys, grad_values)], 1
    )
    step_mixed = dot(layer_input, grad_mixed, TN).astype(BF)
    bias_mixed = jnp.sum(grad_mixed.astype(F32), axis=0)
    part = dot(grad_mixed, attn[:, : 3 * cols], NT).astype(BF)
    (grad_input,) = scatter_sum(part[None], tp)
    grad_input = (grad_input + grad_one).astype(BF)

    def spread(step):
        split = step.reshape(dp, step.shape[0] // dp, step.shape[1])
        came = lax.all_to_all(split, "dp", 0, 0, tiled=True)
        return jnp.sum(came.astype(F32), axis=0)

    own_down = spread(step_down).T
    own_up = spread(step_up)
    own_out = spread(step_out).T
    own_mixed = spread(step_mixed)
    small = jnp.concatenate(
        [bias_out, gain_one, shift_one, bias_two, gain_two, shift_two, bias_up, bias_mixed]
    )
    pad = -small.shape[0] % 128
    small = jnp.concatenate([small, jnp.zeros((pad,), F32)]).reshape(1, -1, 128)
    small = lax.all_to_all(jnp.broadcast_to(small, (dp,) + small.shape[1:]), "dp", 0, 0, tiled=True)
    small = jnp.sum(small, axis=0)
    shared = 6 * width // 128
    common = lax.all_gather(small[:shared], "tp", axis=0, tiled=False)
    common = jnp.sum(common, axis=0).reshape(6, width)
    small = small[shared:].reshape(-1)

    def all_rows(block):
        return lax.all_gather(block, "tp", axis=0, tiled=True)

    return (
        all_rows(result),
        all_rows(grad_input),
        all_rows(tresult),
        own_mixed[:, :cols],
        small[hidden : hidden + cols],
        own_mixed[:, cols : 2 * cols],
        own_mixed[:, 2 * cols :],
        small[hidden + 2 * cols : hidden + 3 * cols],
        own_out,
        common[0],
        common[1],
        common[2],
        own_up,
        small[:hidden],
        own_down,
        common[3],
        common[4],
        common[5],
    )


def solution(mesh):
    wide, tall, col, row, full = P("dp", "tp"), P("tp", "dp"), P("tp"), P("dp", None), P()
    placed = (
        (row, P("dp"), wide, col, wide, wide, col, tall, full, full, full, wide, col, tall)
        + (full, full, full, row, wide, wide, wide, tall, wide, tall)
    )
    results = (row, row, row, wide, col, wide, wide, col, tall, full, full, full)
    results = results + (wide, col, tall, full, full, full)
    tp, dp = mesh.shape["tp"], mesh.shape["dp"]

    def body(*arrays):
        return per_device(tp, dp, *arrays)

    return jax.shard_map(
        body, mesh=mesh, in_specs=placed, out_specs=results, check_vma=False
    )
```

time: 1270 us -> 349 us (0.27)
  waiting for transfers between devices: 758 us -> 98.1 us
  blocking collectives: 289 us -> 66.5 us
  starting transfers between devices: 1.58 us -> 61.3 us
  matrix products: 102 us -> 43.8 us
  other arithmetic: 49.7 us -> 8.69 us
  local copies, waits for them, and re-layouts: 39.1 us -> 57.4 us
    unnamed x30 -> x0, waiting for transfers between devices: 442 us -> none
    reduce_scatter x4 -> x0, waiting for transfers between devices: 215 us -> none  [the longest x2 132 us: per_device(): lax.psum_scatter(step_up.astype(jnp.bfloat16), 'dp', scatter_dimension=0,...]
    all_gather x8, blocking collectives: 252 us -> 66.5 us  [the longest x3 26.9 us: all_rows(): return lax.all_gather(block, 'tp', axis=0, tiled=True)]
    psum x6 -> x0, waiting for transfers between devices: 91.9 us -> none  [the longest x2 54.1 us: per_device(): lax.psum(down_part.astype(jnp.bfloat16), 'tp').astype(jnp.float32)]
    dot_general x72 -> x26, matrix products: 102 us -> 41.9 us  [the longest x17 35.7 us: dot(): lax.dot_general(left, right, (dims, ((), ())), preferred_element_type=F32)]
    ppermute x0 -> x36, waiting for transfers between devices: none -> 51 us  [the longest x8 27 us: scatter_sum(): came = lax.ppermute(send.astype(BF), 'tp', xor_pairs(tp, bit))]
    all_to_all x0 -> x5, waiting for transfers between devices: none -> 47 us  [the longest x4 40 us: spread(): came = lax.all_to_all(split, 'dp', 0, 0, tiled=True)]
    ppermute x0 -> x36, starting transfers between devices: none -> 41.4 us  [the longest x16 31.3 us: gather_rows(): one = lax.ppermute(one, 'dp', ahead)]
  transfers between devices with their start and end apart: 22 -> 41, of which waited for: 16 -> 17; matrix products, arithmetic and copies ran while one was open for 12% -> 20% of each run, Pallas kernels for 0% -> 0%
where the time goes in v1:
time: 349 us; the launch traced here: 347 us
  waiting for transfers between devices  98.1 us (28%)
  blocking collectives  66.5 us (19%)
  starting transfers between devices  61.3 us (18%)
  local copies, waits for them, and re-layouts  57.4 us (16%)
  matrix products  43.8 us (13%)
  between operations  11.3 us (3%)
  other arithmetic  8.69 us (2%)
    all_to_all x4, waiting for transfers between devices, spread(): came = lax.all_to_all(split, 'dp', 0, 0, tiled=True)  40 us
    dot_general x17, matrix products, dot(): lax.dot_general(left, right, (dims, ((), ())), preferred_element_type=F32)  35.7 us
    ppermute x16, starting transfers between devices, gather_rows(): one = lax.ppermute(one, 'dp', ahead)  31.3 us
    ppermute x8, waiting for transfers between devices, scatter_sum(): came = lax.ppermute(send.astype(BF), 'tp', xor_pairs(tp, bit))  27 us
    all_gather x3, blocking collectives, all_rows(): return lax.all_gather(block, 'tp', axis=0, tiled=True)  26.9 us
    ppermute x16, waiting for transfers between devices, gather_rows(): one = lax.ppermute(one, 'dp', ahead)  19.9 us
    all_to_all x4, starting transfers between devices, spread(): came = lax.all_to_all(split, 'dp', 0, 0, tiled=True)  16.4 us
    dynamic_update_slice x16, local copies, waits for them, and re-layouts, gather_rows(): whole = lax.dynamic_update_slice(whole, one, (owner * rows, 0))  16.2 us
  transfers between devices with their start and end apart: 41, of which 17 were waited for; matrix products, arithmetic and copies ran while one was open for 20% of the time, Pallas kernels for 0%

profile of v1, /device:TPU:0, one launch (start us, length us, event | category | flops | bytes accessed | tf_op | source)
XLA Modules:
  0.0 347.0 jit_solution(11669292654470791537)
XLA Ops:
  3.2 3.0 collective-permute-start.23
  6.2 2.1 collective-permute-start.7
  8.5 2.1 collective-permute-start
  13.1 3.0 collective-permute-done.7
  16.1 2.1 collective-permute-start.9
  37.4 2.1 collective-permute-start.11
  39.5 3.1 collective-permute-done.1
  43.6 2.3 collective-permute-start.17
  47.6 2.0 collective-permute-start.2
  53.0 2.0 collective-permute-start.13
  56.7 2.0 collective-permute-done.13
  71.8 3.5 %collective-permute-done.18 = bf16[96,1536]{1,0:T(8,128)(2,1)} collective-permute-done((bf16[96,1536]{1,0:T(8,128)(2,1)}, bf16[96,1536]{1,0:T(8,128)(2,1)}, u32[]{:S(2)}, u32[]{:S(2)}) %collective-permute-start.18) | collective-permute-done | bytes 294944 | tf_op jit(solution)/shard_map/ppermute | solution.py:44
  78.4 2.2 collective-permute-start.20
  84.7 6.0 %collective-permute-done.6 = bf16[96,1152]{1,0:T(8,128)(2,1)S(1)} collective-permute-done((bf16[96,1152]{1,0:T(8,128)(2,1)S(1)}, bf16[96,1152]{1,0:T(8,128)(2,1)S(1)}, u32[]{:S(2)}, u32[]{:S(2)}) %collective-permute-start.6) | collective-permute-done | bytes 221216 | tf_op jit(solution)/shard_map/ppermute | solution.py:44
  90.7 2.2 fusion.2
  92.9 2.9 reshape.362
  118.4 5.3 %collective-permute-done.22 = bf16[96,1536]{1,0:T(8,128)(2,1)S(1)} collective-permute-done((bf16[96,1536]{1,0:T(8,128)(2,1)}, bf16[96,1536]{1,0:T(8,128)(2,1)S(1)}, u32[]{:S(2)}, u32[]{:S(2)}) %collective-permute-start.22) | collective-permute-done | bytes 294944 | tf_op jit(solution)/shard_map/ppermute | solution.py:44
  125.3 2.6 collective-permute-done.15
  128.9 8.6 %all_gather.27 = bf16[512,768]{1,0:T(8,128)(2,1)S(1)} all-gather(bf16[128,768]{1,0:T(8,128)(2,1)S(1)} %get-tuple-element.46), channel_id=1, replica_groups=mesh['dp'=8,'tp'=4] {'tp'}, dimensions={0}, use_global_device_ids=true | all-gather | bytes 983040 | tf_op jit(solution)/shard_map/all_gather | solution.py:167
  137.5 3.5 %fusion.14 = f32[512,768]{1,0:T(8,128)} fusion(bf16[512,768]{1,0:T(8,128)(2,1)S(1)} %all_gather.27, bf16[768,1536]{1,0:T(8,128)(2,1)} %constant_dynamic-update-slice_fusion.13), kind=kOutput, calls=%fused_computation.53 | convolution fusion | flops 603979776 | bytes 3538944 | tf_op jit(solution)/shard_map/dot_general | solution.py:15
  141.0 3.3 multiply_convert_fusion.2
  144.3 3.6 %fusion.12 = f32[512,768]{1,0:T(8,128)} fusion(bf16[512,768]{1,0:T(8,128)(2,1)S(1)} %get-tuple-element.71, bf16[768,1536]{1,0:T(8,128)(2,1)} %constant_dynamic-update-slice_fusion.20), kind=kOutput, calls=%fused_computation.51 | convolution fusion | flops 603979776 | bytes 3538944 | tf_op jit(solution)/shard_map/dot_general | solution.py:15
  147.9 2.1 convolution_convert_fusion.4
  150.0 9.4 %all_gather.28 = bf16[512,768]{1,0:T(8,128)(2,1)} all-gather(bf16[128,768]{1,0:T(8,128)(2,1)S(1)} %get-tuple-element.33), channel_id=1, replica_groups=mesh['dp'=8,'tp'=4] {'tp'}, dimensions={0}, use_global_device_ids=true | all-gather | bytes 983040 | tf_op jit(solution)/shard_map/all_gather | solution.py:168
  159.4 4.9 %add_convert_fusion = bf16[512,768]{1,0:T(8,128)(2,1)S(1)} fusion(f32[512,768]{1,0:T(8,128)} %fusion.12, bf16[768,1536]{1,0:T(8,128)(2,1)} %constant_dynamic-update-slice_fusion.20, f32[512,768]{1,0:T(8,128)} %fusion.14, bf16[512,768]{1,0:T(8,128)(2,1)} %all_gather.28, bf16[768,1536]{1,0:T(8,128)(2,1)} %constant_dynamic-update-slice_fusion.13, ...), kind=kOutput, calls=%fused_computation.27 | convolution fusion | flops 1213071360 | bytes 8650752 | tf_op jit(solution)/shard_map/dot_general | solution.py:15
  167.7 10.7 %collective-permute-done.31 = bf16[2,1,128,768]{3,2,1,0:T(8,128)(2,1)S(1)} collective-permute-done((bf16[2,1,128,768]{3,2,1,0:T(8,128)(2,1)S(1)}, bf16[2,1,128,768]{3,2,1,0:T(8,128)(2,1)S(1)}, u32[]{:S(2)}, u32[]{:S(2)}) %collective-permute-start.31) | collective-permute-done | bytes 393248 | tf_op jit(solution)/shard_map/ppermute | solution.py:66
  179.7 8.0 %all_gather.30 = bf16[512,768]{1,0:T(8,128)(2,1)S(1)} all-gather(bf16[128,768]{1,0:T(8,128)(2,1)S(1)} %convert_element_type.267), channel_id=1, replica_groups=mesh['dp'=8,'tp'=4] {'tp'}, dimensions={0}, use_global_device_ids=true | all-gather | bytes 983040 | tf_op jit(solution)/shard_map/all_gather | solution.py:187
  187.7 2.6 fusion.92
  190.4 2.4 convolution_convert_fusion.3
  196.0 5.9 %collective-permute-done.33 = bf16[1,1,128,768]{3,2,1,0:T(8,128)(2,1)S(1)} collective-permute-done((bf16[1,1,128,768]{3,2,1,0:T(8,128)(2,1)S(1)}, bf16[1,1,128,768]{3,2,1,0:T(8,128)(2,1)S(1)}, u32[]{:S(2)}, u32[]{:S(2)}) %collective-permute-start.33) | collective-permute-done | bytes 196640 | tf_op jit(solution)/shard_map/ppermute | solution.py:66
  202.5 8.3 %all_gather.31 = bf16[512,768]{1,0:T(8,128)(2,1)S(1)} all-gather(bf16[128,768]{1,0:T(8,128)(2,1)S(1)} %convert_element_type.276), channel_id=1, replica_groups=mesh['dp'=8,'tp'=4] {'tp'}, dimensions={0}, use_global_device_ids=true | all-gather | bytes 983040 | tf_op jit(solution)/shard_map/all_gather | solution.py:203
  217.0 3.4 all-to-all-start.1
  222.1 7.1 %all-to-all-done.1 = f32[8,47,128]{2,1,0:T(8,128)S(1)} async-done(((f32[8,47,128]{2,1,0:T(8,128)}), f32[8,47,128]{2,1,0:T(8,128)S(1)}, u32[]{:S(2)}, u32[]{:S(2)}) %all-to-all-start.1) | async-done | bytes 192544 | tf_op jit(solution)/shard_map/all_to_all | solution.py:236
  229.1 3.5 all-to-all-start.2
  232.6 3.0 convolution_convert_fusion
  235.6 8.6 %all-to-all-done.2 = bf16[8,96,192]{1,2,0:T(8,128)(2,1)S(1)} async-done(((bf16[8,96,192]{1,2,0:T(8,128)(2,1)}), bf16[8,96,192]{1,2,0:T(8,128)(2,1)S(1)}, u32[]{:S(2)}, u32[]{:S(2)}) %all-to-all-start.2) | async-done | bytes 294944 | tf_op jit(solution)/shard_map/all_to_all | solution.py:224
  244.9 3.6 %all-to-all-start.4 = ((bf16[8,96,768]{2,1,0:T(8,128)(2,1)}), bf16[8,96,768]{2,1,0:T(8,128)(2,1)S(1)}, u32[]{:S(2)}, u32[]{:S(2)}) async-start(bf16[8,96,768]{2,1,0:T(8,128)(2,1)} %bitcast.61), calls=%async_computation.4 | async-start | bytes 2359296 | tf_op jit(solution)/shard_map/all_to_all | solution.py:224
  248.5 3.0 convolution_convert_fusion.1
  251.5 25.4 %all-to-all-done.4 = bf16[8,96,768]{2,1,0:T(8,128)(2,1)S(1)} async-done(((bf16[8,96,768]{2,1,0:T(8,128)(2,1)}), bf16[8,96,768]{2,1,0:T(8,128)(2,1)S(1)}, u32[]{:S(2)}, u32[]{:S(2)}) %all-to-all-start.4) | async-done | bytes 1179680 | tf_op jit(solution)/shard_map/all_to_all | solution.py:224
  276.9 3.6 %all-to-all-start.3 = ((bf16[8,96,768]{2,1,0:T(8,128)(2,1)}), bf16[8,96,768]{2,1,0:T(8,128)(2,1)S(1)}, u32[]{:S(2)}, u32[]{:S(2)}) async-start(bf16[8,96,768]{2,1,0:T(8,128)(2,1)} %bitcast.59), calls=%async_computation.3 | async-start | bytes 2359296 | tf_op jit(solution)/shard_map/all_to_all | solution.py:224
  280.5 8.7 %all_gather.29 = bf16[512,768]{1,0:T(8,128)(2,1)} all-gather(bf16[128,768]{1,0:T(8,128)(2,1)S(1)} %get-tuple-element.45), channel_id=1, replica_groups=mesh['dp'=8,'tp'=4] {'tp'}, dimensions={0}, use_global_device_ids=true | all-gather | bytes 983040 | tf_op jit(solution)/shard_map/all_gather | solution.py:244
  289.1 9.4 %all_gather.33 = bf16[512,768]{1,0:T(8,128)(2,1)} all-gather(bf16[128,768]{1,0:T(8,128)(2,1)S(1)} %get-tuple-element.44), channel_id=1, replica_groups=mesh['dp'=8,'tp'=4] {'tp'}, dimensions={0}, use_global_device_ids=true | all-gather | bytes 983040 | tf_op jit(solution)/shard_map/all_gather | solution.py:244
  303.9 2.2 copy.175
  306.2 5.3 %all-gather.1 = f32[4,36,128]{2,1,0:T(8,128)S(1)} all-gather(f32[1,36,128]{2,1,0:T(8,128)S(1)} %slice_bitcast_fusion.3), channel_id=2, replica_groups=mesh['dp'=8,'tp'=4] {'tp'}, dimensions={0}, use_global_device_ids=true | all-gather | bytes 92160 | tf_op jit(solution)/shard_map/all_gather | solution.py:239
  312.7 5.8 %all-to-all-start = ((bf16[8,96,576]{2,1,0:T(8,128)(2,1)}), bf16[8,96,576]{2,1,0:T(8,128)(2,1)S(1)}, u32[]{:S(2)}, u32[]{:S(2)}) async-start(bf16[8,96,576]{2,1,0:T(8,128)(2,1)} %bitcast.51), calls=%async_computation | async-start | bytes 1966080 | tf_op jit(solution)/shard_map/all_to_all | solution.py:224
  322.4 4.4 %collective-permute-done.35 = bf16[1,1,128,768]{3,2,1,0:T(8,128)(2,1)S(1)} collective-permute-done((bf16[1,1,128,768]{3,2,1,0:T(8,128)(2,1)S(1)}, bf16[1,1,128,768]{3,2,1,0:T(8,128)(2,1)S(1)}, u32[]{:S(2)}, u32[]{:S(2)}) %collective-permute-start.35) | collective-permute-done | bytes 196640 | tf_op jit(solution)/shard_map/ppermute | solution.py:66
  326.9 8.8 %all_gather.32 = bf16[512,768]{1,0:T(8,128)(2,1)} all-gather(bf16[128,768]{1,0:T(8,128)(2,1)S(1)} %fusion.57), channel_id=1, replica_groups=mesh['dp'=8,'tp'=4] {'tp'}, dimensions={0}, use_global_device_ids=true | all-gather | bytes 983040 | tf_op jit(solution)/shard_map/all_gather | solution.py:244
  337.4 6.0 %all-to-all-done = bf16[8,96,576]{2,1,0:T(8,128)(2,1)S(1)} async-done(((bf16[8,96,576]{2,1,0:T(8,128)(2,1)}), bf16[8,96,576]{2,1,0:T(8,128)(2,1)S(1)}, u32[]{:S(2)}, u32[]{:S(2)}) %all-to-all-start) | async-done | bytes 884768 | tf_op jit(solution)/shard_map/all_to_all | solution.py:224
  (304 shorter events, 100.2 us)
Async XLA Ops:
  3.2 48.0 %collective-permute-start.23 = (bf16[96,1536]{1,0:T(8,128)(2,1)S(1)}, bf16[96,1536]{1,0:T(8,128)(2,1)}, u32[]{:S(2)}, u32[]{:S(2)}) collective-permute-start(bf16[96,1536]{1,0:T(8,128)(2,1)S(1)} %get-tuple-element.47), channel_id=1, source_target_pairs={{0,8},{8,16},{16,24},{24,28},{28,20},{20,12},{12,4},{4,0},{1,9},{9... | collective-permute-start | bytes 884744 | tf_op jit(solution)/shard_map/ppermute | solution.py:44
  6.2 46.8 %collective-permute-start.24 = (bf16[96,1536]{1,0:T(8,128)(2,1)S(1)}, bf16[96,1536]{1,0:T(8,128)(2,1)}, u32[]{:S(2)}, u32[]{:S(2)}) collective-permute-start(bf16[96,1536]{1,0:T(8,128)(2,1)S(1)} %get-tuple-element.47), channel_id=1, source_target_pairs={{8,0},{16,8},{24,16},{28,24},{20,28},{12,20},{4,12},{0,4},{9,1},{1... | collective-permute-start | bytes 884744 | tf_op jit(solution)/shard_map/ppermute | solution.py:48
  6.2 9.9 %collective-permute-start.7 = (bf16[96,384]{0,1:T(8,128)(2,1)S(1)}, bf16[96,384]{0,1:T(8,128)(2,1)}, u32[]{:S(2)}, u32[]{:S(2)}) collective-permute-start(bf16[96,384]{0,1:T(8,128)(2,1)S(1)} %pad_maximum_fusion.1), channel_id=1, source_target_pairs={{0,8},{8,16},{16,24},{24,28},{28,20},{20,12},{12,4},{4,0},{1,9},{9... | collective-permute-start | bytes 221192 | tf_op jit(solution)/shard_map/ppermute | solution.py:44
  8.3 10.0 %collective-permute-start.8 = (bf16[96,384]{0,1:T(8,128)(2,1)S(1)}, bf16[96,384]{0,1:T(8,128)(2,1)}, u32[]{:S(2)}, u32[]{:S(2)}) collective-permute-start(bf16[96,384]{0,1:T(8,128)(2,1)S(1)} %pad_maximum_fusion.1), channel_id=1, source_target_pairs={{8,0},{16,8},{24,16},{28,24},{20,28},{12,20},{4,12},{0,4},{9,1},{1... | collective-permute-start | bytes 221192 | tf_op jit(solution)/shard_map/ppermute | solution.py:48
  8.5 28.9 %collective-permute-start = (bf16[96,1152]{1,0:T(8,128)(2,1)S(1)}, bf16[96,1152]{1,0:T(8,128)(2,1)S(1)}, u32[]{:S(2)}, u32[]{:S(2)}) collective-permute-start(bf16[96,1152]{1,0:T(8,128)(2,1)S(1)} %concatenate.26), channel_id=1, source_target_pairs={{0,8},{8,16},{16,24},{24,28},{28,20},{20,12},{12,4},{4,0},{1,9},{9... | collective-permute-start | bytes 663560 | tf_op jit(solution)/shard_map/ppermute | solution.py:44
  10.8 12.8 %copy-start.43 = (s32[8]{0:T(128)S(1)}, s32[8]{0:T(128)}, u32[]{:S(2)}) copy-start(s32[8]{0:T(128)} %constant.369.clone) | copy-start | bytes 100
  10.8 18.6 %copy-start.47 = (f32[192]{0:T(256)S(1)}, f32[192]{0:T(256)}, u32[]{:S(2)}) copy-start(f32[192]{0:T(256)} %param.35) | copy-start | bytes 2308
  10.8 18.6 %copy-start.48 = (f32[192]{0:T(256)S(1)}, f32[192]{0:T(256)}, u32[]{:S(2)}) copy-start(f32[192]{0:T(256)} %param.38) | copy-start | bytes 2308
  16.1 16.4 %collective-permute-start.9 = (bf16[96,384]{0,1:T(8,128)(2,1)}, bf16[96,384]{0,1:T(8,128)(2,1)}, u32[]{:S(2)}, u32[]{:S(2)}) collective-permute-start(bf16[96,384]{0,1:T(8,128)(2,1)} %collective-permute-done.7), channel_id=1, source_target_pairs={{0,8},{8,16},{16,24},{24,28},{28,20},{20,12},{12,4},{4,0},{1,9},{9... | collective-permute-start | bytes 221192 | tf_op jit(solution)/shard_map/ppermute | solution.py:44
  18.3 17.5 %collective-permute-start.10 = (bf16[96,384]{0,1:T(8,128)(2,1)}, bf16[96,384]{0,1:T(8,128)(2,1)}, u32[]{:S(2)}, u32[]{:S(2)}) collective-permute-start(bf16[96,384]{0,1:T(8,128)(2,1)} %collective-permute-done.8), channel_id=1, source_target_pairs={{8,0},{16,8},{24,16},{28,24},{20,28},{12,20},{4,12},{0,4},{9,1},{1... | collective-permute-start | bytes 221192 | tf_op jit(solution)/shard_map/ppermute | solution.py:48
  32.6 28.6 %collective-permute-start.16 = (bf16[96,1536]{1,0:T(8,128)(2,1)S(1)}, bf16[96,1536]{1,0:T(8,128)(2,1)}, u32[]{:S(2)}, u32[]{:S(2)}) collective-permute-start(bf16[96,1536]{1,0:T(8,128)(2,1)S(1)} %constant_dynamic-update-slice_fusion), channel_id=1, source_target_pairs={{0,8},{8,16},{16,24},{24,28},{28,20},{20,12},{12,4},{4,0},{1,9},{9... | collective-permute-start | bytes 884744 | tf_op jit(solution)/shard_map/ppermute | solution.py:44
  35.8 6.8 %collective-permute-start.1 = (bf16[96,1152]{1,0:T(8,128)(2,1)S(1)}, bf16[96,1152]{1,0:T(8,128)(2,1)}, u32[]{:S(2)}, u32[]{:S(2)}) collective-permute-start(bf16[96,1152]{1,0:T(8,128)(2,1)S(1)} %concatenate.26), channel_id=1, source_target_pairs={{8,0},{16,8},{24,16},{28,24},{20,28},{12,20},{4,12},{0,4},{9,1},{1... | collective-permute-start | bytes 663560 | tf_op jit(solution)/shard_map/ppermute | solution.py:48
  37.4 6.2 %collective-permute-start.11 = (bf16[96,384]{0,1:T(8,128)(2,1)}, bf16[96,384]{0,1:T(8,128)(2,1)S(1)}, u32[]{:S(2)}, u32[]{:S(2)}) collective-permute-start(bf16[96,384]{0,1:T(8,128)(2,1)} %collective-permute-done.9), channel_id=1, source_target_pairs={{0,8},{8,16},{16,24},{24,28},{28,20},{20,12},{12,4},{4,0},{1,9},{9... | collective-permute-start | bytes 221192 | tf_op jit(solution)/shard_map/ppermute | solution.py:44
  42.6 5.0 %collective-permute-start.12 = (bf16[96,384]{0,1:T(8,128)(2,1)}, bf16[96,384]{0,1:T(8,128)(2,1)}, u32[]{:S(2)}, u32[]{:S(2)}) collective-permute-start(bf16[96,384]{0,1:T(8,128)(2,1)} %collective-permute-done.10), channel_id=1, source_target_pairs={{8,0},{16,8},{24,16},{28,24},{20,28},{12,20},{4,12},{0,4},{9,1},{1... | collective-permute-start | bytes 221192 | tf_op jit(solution)/shard_map/ppermute | solution.py:48
  43.6 19.6 %collective-permute-start.17 = (bf16[96,1536]{1,0:T(8,128)(2,1)S(1)}, bf16[96,1536]{1,0:T(8,128)(2,1)}, u32[]{:S(2)}, u32[]{:S(2)}) collective-permute-start(bf16[96,1536]{1,0:T(8,128)(2,1)S(1)} %constant_dynamic-update-slice_fusion), channel_id=1, source_target_pairs={{8,0},{16,8},{24,16},{28,24},{20,28},{12,20},{4,12},{0,4},{9,1},{1... | collective-permute-start | bytes 884744 | tf_op jit(solution)/shard_map/ppermute | solution.py:48
  47.6 19.0 %collective-permute-start.2 = (bf16[96,1152]{1,0:T(8,128)(2,1)S(1)}, bf16[96,1152]{1,0:T(8,128)(2,1)S(1)}, u32[]{:S(2)}, u32[]{:S(2)}) collective-permute-start(bf16[96,1152]{1,0:T(8,128)(2,1)S(1)} %collective-permute-done), channel_id=1, source_target_pairs={{0,8},{8,16},{16,24},{24,28},{28,20},{20,12},{12,4},{4,0},{1,9},{9... | collective-permute-start | bytes 663560 | tf_op jit(solution)/shard_map/ppermute | solution.py:44
  51.2 15.8 %collective-permute-start.3 = (bf16[96,1152]{1,0:T(8,128)(2,1)}, bf16[96,1152]{1,0:T(8,128)(2,1)}, u32[]{:S(2)}, u32[]{:S(2)}) collective-permute-start(bf16[96,1152]{1,0:T(8,128)(2,1)} %collective-permute-done.1), channel_id=1, source_target_pairs={{8,0},{16,8},{24,16},{28,24},{20,28},{12,20},{4,12},{0,4},{9,1},{1... | collective-permute-start | bytes 663560 | tf_op jit(solution)/shard_map/ppermute | solution.py:48
  53.0 5.7 %collective-permute-start.13 = (bf16[96,384]{0,1:T(8,128)(2,1)S(1)}, bf16[96,384]{0,1:T(8,128)(2,1)S(1)}, u32[]{:S(2)}, u32[]{:S(2)}) collective-permute-start(bf16[96,384]{0,1:T(8,128)(2,1)S(1)} %collective-permute-done.11), channel_id=1, source_target_pairs={{0,8},{8,16},{16,24},{24,28},{28,20},{20,12},{12,4},{4,0},{1,9},{9... | collective-permute-start | bytes 221192 | tf_op jit(solution)/shard_map/ppermute | solution.py:44
  58.7 11.1 %collective-permute-start.25 = (bf16[96,1536]{1,0:T(8,128)(2,1)}, bf16[96,1536]{1,0:T(8,128)(2,1)}, u32[]{:S(2)}, u32[]{:S(2)}) collective-permute-start(bf16[96,1536]{1,0:T(8,128)(2,1)} %collective-permute-done.23), channel_id=1, source_target_pairs={{0,8},{8,16},{16,24},{24,28},{28,20},{20,12},{12,4},{4,0},{1,9},{9... | collective-permute-start | bytes 884744 | tf_op jit(solution)/shard_map/ppermute | solution.py:44
  61.2 17.3 %collective-permute-start.26 = (bf16[96,1536]{1,0:T(8,128)(2,1)}, bf16[96,1536]{1,0:T(8,128)(2,1)}, u32[]{:S(2)}, u32[]{:S(2)}) collective-permute-start(bf16[96,1536]{1,0:T(8,128)(2,1)} %collective-permute-done.24), channel_id=1, source_target_pairs={{8,0},{16,8},{24,16},{28,24},{20,28},{12,20},{4,12},{0,4},{9,1},{1... | collective-permute-start | bytes 884744 | tf_op jit(solution)/shard_map/ppermute | solution.py:48
  63.2 12.1 %collective-permute-start.18 = (bf16[96,1536]{1,0:T(8,128)(2,1)}, bf16[96,1536]{1,0:T(8,128)(2,1)}, u32[]{:S(2)}, u32[]{:S(2)}) collective-permute-start(bf16[96,1536]{1,0:T(8,128)(2,1)} %collective-permute-done.16), channel_id=1, source_target_pairs={{0,8},{8,16},{16,24},{24,28},{28,20},{20,12},{12,4},{4,0},{1,9},{9... | collective-permute-start | bytes 884744 | tf_op jit(solution)/shard_map/ppermute | solution.py:44
  66.7 15.7 %collective-permute-start.19 = (bf16[96,1536]{1,0:T(8,128)(2,1)}, bf16[96,1536]{1,0:T(8,128)(2,1)}, u32[]{:S(2)}, u32[]{:S(2)}) collective-permute-start(bf16[96,1536]{1,0:T(8,128)(2,1)} %collective-permute-done.17), channel_id=1, source_target_pairs={{8,0},{16,8},{24,16},{28,24},{20,28},{12,20},{4,12},{0,4},{9,1},{1... | collective-permute-start | bytes 884744 | tf_op jit(solution)/shard_map/ppermute | solution.py:48
  67.0 15.3 %collective-permute-start.4 = (bf16[96,1152]{1,0:T(8,128)(2,1)S(1)}, bf16[96,1152]{1,0:T(8,128)(2,1)S(1)}, u32[]{:S(2)}, u32[]{:S(2)}) collective-permute-start(bf16[96,1152]{1,0:T(8,128)(2,1)S(1)} %collective-permute-done.2), channel_id=1, source_target_pairs={{0,8},{8,16},{16,24},{24,28},{28,20},{20,12},{12,4},{4,0},{1,9},{9... | collective-permute-start | bytes 663560 | tf_op jit(solution)/shard_map/ppermute | solution.py:44
  69.7 21.0 %copy-start.19 = (bf16[512,768]{1,0:T(8,128)(2,1)S(1)}, bf16[512,768]{1,0:T(8,128)(2,1)}, u32[]{:S(2)}) copy-start(bf16[512,768]{1,0:T(8,128)(2,1)} %param.32) | copy-start | bytes 2359300
  69.7 13.0 %collective-permute-start.5 = (bf16[96,1152]{1,0:T(8,128)(2,1)}, bf16[96,1152]{1,0:T(8,128)(2,1)S(1)}, u32[]{:S(2)}, u32[]{:S(2)}) collective-permute-start(bf16[96,1152]{1,0:T(8,128)(2,1)} %collective-permute-done.3), channel_id=1, source_target_pairs={{8,0},{16,8},{24,16},{28,24},{20,28},{12,20},{4,12},{0,4},{9,1},{1... | collective-permute-start | bytes 663560 | tf_op jit(solution)/shard_map/ppermute | solution.py:48
  75.3 32.6 %collective-permute-start.27 = (bf16[96,1536]{1,0:T(8,128)(2,1)}, bf16[96,1536]{1,0:T(8,128)(2,1)}, u32[]{:S(2)}, u32[]{:S(2)}) collective-permute-start(bf16[96,1536]{1,0:T(8,128)(2,1)} %collective-permute-done.25), channel_id=1, source_target_pairs={{0,8},{8,16},{16,24},{24,28},{28,20},{20,12},{12,4},{4,0},{1,9},{9... | collective-permute-start | bytes 884744 | tf_op jit(solution)/shard_map/ppermute | solution.py:44
  78.4 32.5 %collective-permute-start.20 = (bf16[96,1536]{1,0:T(8,128)(2,1)}, bf16[96,1536]{1,0:T(8,128)(2,1)}, u32[]{:S(2)}, u32[]{:S(2)}) collective-permute-start(bf16[96,1536]{1,0:T(8,128)(2,1)} %collective-permute-done.18), channel_id=1, source_target_pairs={{0,8},{8,16},{16,24},{24,28},{28,20},{20,12},{12,4},{4,0},{1,9},{9... | collective-permute-start | bytes 884744 | tf_op jit(solution)/shard_map/ppermute | solution.py:44
  82.3 32.4 %collective-permute-start.28 = (bf16[96,1536]{1,0:T(8,128)(2,1)}, bf16[96,1536]{1,0:T(8,128)(2,1)}, u32[]{:S(2)}, u32[]{:S(2)}) collective-permute-start(bf16[96,1536]{1,0:T(8,128)(2,1)} %collective-permute-done.26), channel_id=1, source_target_pairs={{8,0},{16,8},{24,16},{28,24},{20,28},{12,20},{4,12},{0,4},{9,1},{1... | collective-permute-start | bytes 884744 | tf_op jit(solution)/shard_map/ppermute | solution.py:48
  82.3 32.3 %collective-permute-start.21 = (bf16[96,1536]{1,0:T(8,128)(2,1)}, bf16[96,1536]{1,0:T(8,128)(2,1)}, u32[]{:S(2)}, u32[]{:S(2)}) collective-permute-start(bf16[96,1536]{1,0:T(8,128)(2,1)} %collective-permute-done.19), channel_id=1, source_target_pairs={{8,0},{16,8},{24,16},{28,24},{20,28},{12,20},{4,12},{0,4},{9,1},{1... | collective-permute-start | bytes 884744 | tf_op jit(solution)/shard_map/ppermute | solution.py:48
  82.8 7.9 %collective-permute-start.6 = (bf16[96,1152]{1,0:T(8,128)(2,1)S(1)}, bf16[96,1152]{1,0:T(8,128)(2,1)S(1)}, u32[]{:S(2)}, u32[]{:S(2)}) collective-permute-start(bf16[96,1152]{1,0:T(8,128)(2,1)S(1)} %collective-permute-done.4), channel_id=1, source_target_pairs={{0,8},{8,16},{16,24},{24,28},{28,20},{20,12},{12,4},{4,0},{1,9},{9... | collective-permute-start | bytes 663560 | tf_op jit(solution)/shard_map/ppermute | solution.py:44
  106.0 10.6 %collective-permute-start.14 = (bf16[2,2,128,768]{3,2,1,0:T(8,128)(2,1)S(1)}, bf16[2,2,128,768]{3,2,1,0:T(8,128)(2,1)S(1)}, u32[]{:S(2)}, u32[]{:S(2)}) collective-permute-start(bf16[2,2,128,768]{3,2,1,0:T(8,128)(2,1)S(1)} %fusion.39), channel_id=1, source_target_pairs={{0,1},{1,0},{2,3},{3,2},{4,5},{5,4},{6,7},{7,6},{8,9},{9,8},{10,11... | collective-permute-start | bytes 2359304 | tf_op jit(solution)/shard_map/ppermute | solution.py:66
  107.8 16.7 %collective-permute-start.29 = (bf16[96,1536]{1,0:T(8,128)(2,1)}, bf16[96,1536]{1,0:T(8,128)(2,1)S(1)}, u32[]{:S(2)}, u32[]{:S(2)}) collective-permute-start(bf16[96,1536]{1,0:T(8,128)(2,1)} %collective-permute-done.27), channel_id=1, source_target_pairs={{0,8},{8,16},{16,24},{24,28},{28,20},{20,12},{12,4},{4,0},{1,9},{9... | collective-permute-start | bytes 884744 | tf_op jit(solution)/shard_map/ppermute | solution.py:44
  111.0 12.8 %collective-permute-start.22 = (bf16[96,1536]{1,0:T(8,128)(2,1)}, bf16[96,1536]{1,0:T(8,128)(2,1)S(1)}, u32[]{:S(2)}, u32[]{:S(2)}) collective-permute-start(bf16[96,1536]{1,0:T(8,128)(2,1)} %collective-permute-done.20), channel_id=1, source_target_pairs={{0,8},{8,16},{16,24},{24,28},{28,20},{20,12},{12,4},{4,0},{1,9},{9... | collective-permute-start | bytes 884744 | tf_op jit(solution)/shard_map/ppermute | solution.py:44
  116.8 11.0 %collective-permute-start.15 = (bf16[2,1,128,768]{3,2,1,0:T(8,128)(2,1)S(1)}, bf16[2,1,128,768]{3,2,1,0:T(8,128)(2,1)S(1)}, u32[]{:S(2)}, u32[]{:S(2)}) collective-permute-start(bf16[2,1,128,768]{3,2,1,0:T(8,128)(2,1)S(1)} %constant_dynamic-slice_fusion), channel_id=1, source_target_pairs={{0,2},{1,3},{2,0},{3,1},{4,6},{5,7},{6,4},{7,5},{8,10},{9,11},{10,... | collective-permute-start | bytes 1179656 | tf_op jit(solution)/shard_map/ppermute | solution.py:66
  164.4 2.4 collective-permute-start.30
  167.0 11.4 %collective-permute-start.31 = (bf16[2,1,128,768]{3,2,1,0:T(8,128)(2,1)S(1)}, bf16[2,1,128,768]{3,2,1,0:T(8,128)(2,1)S(1)}, u32[]{:S(2)}, u32[]{:S(2)}) collective-permute-start(bf16[2,1,128,768]{3,2,1,0:T(8,128)(2,1)S(1)} %constant_dynamic-slice_fusion.1), channel_id=1, source_target_pairs={{0,2},{1,3},{2,0},{3,1},{4,6},{5,7},{6,4},{7,5},{8,10},{9,11},{10,... | collective-permute-start | bytes 1179656 | tf_op jit(solution)/shard_map/ppermute | solution.py:66
  192.8 1.8 collective-permute-start.32
  194.7 7.2 %collective-permute-start.33 = (bf16[1,1,128,768]{3,2,1,0:T(8,128)(2,1)S(1)}, bf16[1,1,128,768]{3,2,1,0:T(8,128)(2,1)S(1)}, u32[]{:S(2)}, u32[]{:S(2)}) collective-permute-start(bf16[1,1,128,768]{3,2,1,0:T(8,128)(2,1)S(1)} %constant_dynamic-slice_fusion.2), channel_id=1, source_target_pairs={{0,2},{1,3},{2,0},{3,1},{4,6},{5,7},{6,4},{7,5},{8,10},{9,11},{10,... | collective-permute-start | bytes 589832 | tf_op jit(solution)/shard_map/ppermute | solution.py:66
  217.0 12.1 %all-to-all-start.1 = ((f32[8,47,128]{2,1,0:T(8,128)}), f32[8,47,128]{2,1,0:T(8,128)S(1)}, u32[]{:S(2)}, u32[]{:S(2)}) async-start(f32[8,47,128]{2,1,0:T(8,128)} %broadcast_in_dim.38), calls=%async_computation.1 | async-start | bytes 393216 | tf_op jit(solution)/shard_map/all_to_all | solution.py:236
  220.4 12.1 %copy-start.18 = (bf16[512,768]{1,0:T(8,128)(2,1)S(1)}, bf16[512,768]{1,0:T(8,128)(2,1)}, u32[]{:S(2)}) copy-start(bf16[512,768]{1,0:T(8,128)(2,1)} %copy-done.17) | copy-start | bytes 2359300
  229.1 15.0 %all-to-all-start.2 = ((bf16[8,96,192]{1,2,0:T(8,128)(2,1)}), bf16[8,96,192]{1,2,0:T(8,128)(2,1)S(1)}, u32[]{:S(2)}, u32[]{:S(2)}) async-start(bf16[8,96,192]{1,2,0:T(8,128)(2,1)} %copy.177), calls=%async_computation.2 | async-start | bytes 786432 | tf_op jit(solution)/shard_map/all_to_all | solution.py:224
  235.6 12.9 %copy-start.16 = (bf16[512,768]{1,0:T(8,128)(2,1)S(1)}, bf16[512,768]{1,0:T(8,128)(2,1)}, u32[]{:S(2)}) copy-start(bf16[512,768]{1,0:T(8,128)(2,1)} %copy-done.15) | copy-start | bytes 2359300
  244.9 32.0 %all-to-all-start.4 = ((bf16[8,96,768]{2,1,0:T(8,128)(2,1)}), bf16[8,96,768]{2,1,0:T(8,128)(2,1)S(1)}, u32[]{:S(2)}, u32[]{:S(2)}) async-start(bf16[8,96,768]{2,1,0:T(8,128)(2,1)} %bitcast.61), calls=%async_computation.4 | async-start | bytes 2359296 | tf_op jit(solution)/shard_map/all_to_all | solution.py:224
  276.9 35.9 %all-to-all-start.3 = ((bf16[8,96,768]{2,1,0:T(8,128)(2,1)}), bf16[8,96,768]{2,1,0:T(8,128)(2,1)S(1)}, u32[]{:S(2)}, u32[]{:S(2)}) async-start(bf16[8,96,768]{2,1,0:T(8,128)(2,1)} %bitcast.59), calls=%async_computation.3 | async-start | bytes 2359296 | tf_op jit(solution)/shard_map/all_to_all | solution.py:224
  280.4 18.1 %copy-start.6 = (bf16[768,1152]{1,0:T(8,128)(2,1)S(1)}, bf16[768,1152]{1,0:T(8,128)(2,1)}, u32[]{:S(2)}) copy-start(bf16[768,1152]{1,0:T(8,128)(2,1)} %copy-done.5) | copy-start | bytes 5308420
  302.0 16.5 %collective-permute-start.34 = (bf16[1,2,128,768]{3,2,1,0:T(8,128)(2,1)}, bf16[1,2,128,768]{3,2,1,0:T(8,128)(2,1)}, u32[]{:S(2)}, u32[]{:S(2)}) collective-permute-start(bf16[1,2,128,768]{3,2,1,0:T(8,128)(2,1)} %dynamic-slice_bitcast_fusion), channel_id=1, source_target_pairs={{0,1},{1,0},{2,3},{3,2},{4,5},{5,4},{6,7},{7,6},{8,9},{9,8},{10,11... | collective-permute-start | bytes 1179656 | tf_op jit(solution)/shard_map/ppermute | solution.py:66
  312.7 30.7 %all-to-all-start = ((bf16[8,96,576]{2,1,0:T(8,128)(2,1)}), bf16[8,96,576]{2,1,0:T(8,128)(2,1)S(1)}, u32[]{:S(2)}, u32[]{:S(2)}) async-start(bf16[8,96,576]{2,1,0:T(8,128)(2,1)} %bitcast.51), calls=%async_computation | async-start | bytes 1966080 | tf_op jit(solution)/shard_map/all_to_all | solution.py:224
  319.9 6.9 %collective-permute-start.35 = (bf16[1,1,128,768]{3,2,1,0:T(8,128)(2,1)S(1)}, bf16[1,1,128,768]{3,2,1,0:T(8,128)(2,1)S(1)}, u32[]{:S(2)}, u32[]{:S(2)}) collective-permute-start(bf16[1,1,128,768]{3,2,1,0:T(8,128)(2,1)S(1)} %constant_dynamic-slice_fusion.3), channel_id=1, source_target_pairs={{0,2},{1,3},{2,0},{3,1},{4,6},{5,7},{6,4},{7,5},{8,10},{9,11},{10,... | collective-permute-start | bytes 589832 | tf_op jit(solution)/shard_map/ppermute | solution.py:66
  (48 other events, 208.8 us)

commit v2 on v1

v2 whole, which is shorter than its diff:
```python
import functools
import math

import jax
import jax.numpy as jnp
from jax import lax
from jax.experimental import pallas as pl
from jax.experimental.pallas import tpu as pltpu
from jax.sharding import PartitionSpec as P

HEAD = 64
SEQ = 256
EPSILON = 1e-06
SCALE = HEAD ** (-0.5)
BLOCKS = (0, 2, 1, 3)
OWNERS = (0, 2, 4, 6, 1, 3, 5, 7)
SNAKE = (0, 2, 4, 6, 7, 5, 3, 1)
EXTRA = 8
BF = jnp.bfloat16
F32 = jnp.float32
VMEM_LIMIT = 16 * 1024 * 1024
TILE = 256

NN = ((1,), (0,))
NT = ((1,), (1,))
TN = ((0,), (0,))


def dot(left, right, dims):
    return lax.dot_general(left, right, (dims, ((), ())), preferred_element_type=F32)


def xor_pairs(size, bit):
    return [(i, i ^ bit) for i in range(size)]


def call(body, name, outs, near, shards=(), scratch=(), any_outs=False):
    smem = [a.dtype == jnp.int32 for a in near]
    specs = [pl.BlockSpec(memory_space=pltpu.SMEM if s else pltpu.VMEM) for s in smem]
    specs = specs + [pl.BlockSpec(memory_space=pl.ANY)] * len(shards)
    out_space = pltpu.HBM if any_outs else pltpu.VMEM
    return pl.pallas_call(
        body,
        out_shape=[jax.ShapeDtypeStruct(shape, kind) for shape, kind in outs],
        in_specs=specs,
        out_specs=[pl.BlockSpec(memory_space=out_space)] * len(outs),
        scratch_shapes=list(scratch),
        name=name,
        compiler_params=pltpu.CompilerParams(vmem_limit_bytes=VMEM_LIMIT),
        cost_estimate=pl.CostEstimate(flops=1, bytes_accessed=1, transcendentals=0),
    )(*near, *shards)


def tiles(width, body):
    step = TILE if width % TILE == 0 else width

    def one(i, carry):
        body(pl.ds(pl.multiple_of(i * step, step), step))
        return carry

    lax.fori_loop(0, width // step, one, 0)


def after(value, *others):
    return lax.optimization_barrier((value, *others))[0]


class Ring:
    def __init__(self, shard, dp):
        self.near = dp == len(SNAKE)
        self.dp = dp
        self.front = [shard, shard]
        self.parts = [shard]
        self.steps = 0

    def step(self):
        if not self.near:
            if self.steps == 0:
                self.parts = [lax.all_gather(self.parts[0], "dp", axis=0, tiled=True)]
                self.front = [self.parts[0]] * 2
            self.steps += 1
            return
        if self.steps == self.dp // 2:
            return
        ahead = [(SNAKE[i], SNAKE[(i + 1) % self.dp]) for i in range(self.dp)]
        behind = [(b, a) for a, b in ahead]
        self.steps += 1
        self.front[0] = lax.ppermute(self.front[0], "dp", ahead)
        self.parts.append(self.front[0])
        if self.steps < self.dp // 2:
            self.front[1] = lax.ppermute(self.front[1], "dp", behind)
            self.parts.append(self.front[1])


def join(rings, *values):
    fronts = [front for ring in rings for front in ring.front]
    joined = lax.optimization_barrier((*values, *fronts))
    for i, ring in enumerate(rings):
        ring.front = list(joined[len(values) + 2 * i :][:2])
    return joined[0] if len(values) == 1 else joined[: len(values)]


def ring_owner(me, index):
    size = len(SNAKE)
    place = jnp.where(me % 2 == 0, me // 2, size - 1 - me // 2)
    step = (index + 1) // 2
    place = lax.rem(place + (size - step if index % 2 else step), size)
    return jnp.where(place < size // 2, 2 * place, 2 * (size - 1 - place) + 1)


def shard_copies(where, refs, whole, sems):
    rows = whole.shape[0] // len(refs)
    made = []
    for i, ref in enumerate(refs):
        owner = ring_owner(where[1], i) if len(refs) > 1 else 0
        start = pl.multiple_of(owner * rows, rows)
        made.append(pltpu.make_async_copy(ref, whole.at[pl.ds(start, rows), :], sems.at[i]))
    return made


def start_all(copies):
    for copy in copies:
        copy.start()


def wait_all(copies):
    for copy in copies:
        copy.wait()


def swap(block, tp, bit):
    return lax.ppermute(block, "tp", xor_pairs(tp, bit))


def sum_exchange(keep, send, tp, rings=(), meanwhile=()):
    quarter = keep.shape[0] // 2
    first = swap(send, tp, 1)
    if rings or meanwhile:
        first = join(rings, first, *meanwhile)
        first = first[0] if meanwhile else first
    for ring in rings:
        ring.step()
    onward = (keep[quarter:].astype(F32) + first[quarter:].astype(F32)).astype(BF)
    second = swap(onward, tp, 2)
    if rings:
        second = join(rings, second)
    for ring in rings:
        ring.step()
    return keep, first, second


def spread_rows(own, tp, rings=()):
    across, beside = swap(own, tp, 2), swap(own, tp, 1)
    if rings:
        across = join(rings, across)
    for ring in rings:
        ring.step()
    return own, across, beside, swap(across, tp, 1)


def summed(keep, first, second):
    quarter = second.shape[0]
    near = keep[0:quarter, :].astype(F32) + first[0:quarter, :].astype(F32)
    return near + second[...].astype(F32)


def halves(array, keep, send, cols=slice(None)):
    half = array.shape[0] // 2
    keep[:, cols] = array[:half].astype(BF)
    send[:, cols] = array[half:].astype(BF)


def mean_last(value):
    return jnp.mean(value, axis=-1, keepdims=True)


def norm_along(unit, inverse, along):
    shifted = along - mean_last(along)
    return inverse * (shifted - unit * mean_last(unit * shifted))


def sum_rows(value):
    return jnp.sum(value, axis=0, keepdims=True)


def split_sums(lines):
    width = lines[0].shape[-1]
    missing = EXTRA // 2 - sum(line.shape[0] for line in lines)
    blank = [jnp.zeros((missing, width), F32)] if missing else []
    whole = jnp.concatenate([*lines, *blank]) if len(lines) + missing > 1 else lines[0]
    rounded = whole.astype(BF).astype(F32)
    return jnp.concatenate([rounded, whole - rounded]).astype(BF)


def tree_sum(four):
    return (four[0] + four[1]) + (four[2] + four[3])


def joined_sums(block):
    return block[: EXTRA // 2].astype(F32) + block[EXTRA // 2 :].astype(F32)


def pair_rows(array, pair, quarter, cols):
    near, far = pair * quarter, (pair + 2) * quarter
    return jnp.concatenate([array[near : near + quarter, cols], array[far : far + quarter, cols]])


def put_pair(ref, pair, quarter, cols, value):
    near, far = pair * quarter, (pair + 2) * quarter
    ref[near : near + quarter, cols] = value[:quarter]
    ref[far : far + quarter, cols] = value[quarter:]


def positions(me, quarter):
    local = lax.broadcasted_iota(jnp.int32, (1, SEQ), 1)
    half = jnp.where(local < quarter, me % 2, 1 - me % 2)
    return half * quarter + lax.rem(local, quarter)


def attention_forward(count, cols, where, x_ref, params, *refs):
    shards, refs = refs[:count], refs[count:]
    rel, mixed, probs, context, keep, send, whole, sems = refs
    copies = shard_copies(where, shards, whole, sems)
    start_all(copies)
    me = where[0]
    quarter = x_ref.shape[0] // 4
    for i, block in enumerate(BLOCKS):
        start = pl.multiple_of((me ^ block) * quarter, quarter)
        rel[i * quarter : (i + 1) * quarter, :] = x_ref[pl.ds(start, quarter), :]
    wait_all(copies)
    for third in range(3):
        part = slice(third * cols, (third + 1) * cols)
        mixed[:, part] = (dot(rel[...], whole[:, part], NN) + params[0:1, part]).astype(BF)
    slots = positions(me, quarter)
    heads = cols // HEAD
    for pair in range(2):
        valid = slots < where[2 + ((me // 2) ^ pair)]
        for head in range(heads):
            query, key, value = [
                pair_rows(mixed, pair, quarter, slice(at, at + HEAD))
                for at in range(head * HEAD, 3 * cols, cols)
            ]
            scores = jnp.where(valid, dot(query, key, NT) * SCALE, jnp.float32(-1e30))
            expo = jnp.exp(scores - jnp.max(scores, axis=-1, keepdims=True))
            prob = expo / jnp.sum(expo, axis=-1, keepdims=True)
            probs[pair * heads + head] = prob
            result = dot(prob.astype(BF), value, NN).astype(BF)
            put_pair(context, pair, quarter, slice(head * HEAD, (head + 1) * HEAD), result)

    def project(cut):
        halves(dot(context[...], whole[cut, 3 * cols : 4 * cols], NT), keep, send, cut)

    tiles(keep.shape[1], project)


def attention_tangent(
    count, cols, where, rel, mixed, probs, context, whole, *refs
):
    tshards, refs = refs[:count], refs[count:]
    keep, send, twhole, sems, tmixed, tcontext = refs
    copies = shard_copies(where, tshards, twhole, sems)
    start_all(copies)
    wait_all(copies)
    me = where[0]
    quarter = rel.shape[0] // 4
    for third in range(3):
        part = slice(third * cols, (third + 1) * cols)
        tmixed[:, part] = dot(rel[...], twhole[:, part], NN).astype(BF)
    slots = positions(me, quarter)
    heads = cols // HEAD
    for pair in range(2):
        valid = slots < where[2 + ((me // 2) ^ pair)]
        for head in range(heads):
            columns = [slice(at, at + HEAD) for at in range(head * HEAD, 3 * cols, cols)]
            query, key, value = [pair_rows(mixed, pair, quarter, at) for at in columns]
            tquery, tkey, tvalue = [pair_rows(tmixed, pair, quarter, at) for at in columns]
            prob = probs[pair * heads + head]
            tscores = (dot(tquery, key, NT) + dot(query, tkey, NT)) * SCALE
            tscores = jnp.where(valid, tscores, jnp.float32(0.0))
            total = jnp.sum(tscores * prob, axis=-1, keepdims=True)
            tprob = (prob * (tscores - total)).astype(BF)
            result = dot(tprob, value, NN) + dot(prob.astype(BF), tvalue, NN)
            put_pair(
                tcontext, pair, quarter, slice(head * HEAD, (head + 1) * HEAD), result.astype(BF)
            )

    def project(cut):
        part = dot(tcontext[...], whole[cut, 3 * cols : 4 * cols], NT)
        part = part + dot(context[...], twhole[cut, 3 * cols : 4 * cols], NT)
        halves(part, keep, send, cut)

    tiles(keep.shape[1], project)


def first_norm(x_rel, keep, came, second, params, first, unit, inverse, low):
    own = second.shape[0]
    resid = x_rel[0:own, :].astype(F32) + summed(keep, came, second) + params[1:2, :]
    center = resid - mean_last(resid)
    inv = lax.rsqrt(mean_last(center * center) + EPSILON)
    whitened = center * inv
    unit[...] = whitened
    inverse[...] = jnp.broadcast_to(inv, inverse.shape)
    value = whitened * params[2:3, :] + params[3:4, :]
    first[...] = value
    low[...] = value.astype(BF)


def first_norm_tangent(keep, came, second, params, unit, inverse, tfirst, low):
    along = norm_along(unit[...], inverse[:, 0:1], summed(keep, came, second)) * params[2:3, :]
    tfirst[...] = along
    low[...] = along.astype(BF)


def collect(pieces, rel):
    quarter = rel.shape[0] // 4
    for i, piece in enumerate(pieces):
        rel[i * quarter : (i + 1) * quarter, :] = piece[0:quarter, :]


def feed_forward(count, hidden, where, params, *refs):
    pieces, refs = refs[:4], refs[4:]
    shards, refs = refs[:count], refs[count:]
    rel, active, slope, keep, send, whole, sems = refs
    copies = shard_copies(where, shards, whole, sems)
    start_all(copies)
    collect(pieces, rel)
    wait_all(copies)

    def up(cut):
        upper = dot(rel[...], whole[:, cut], NN) + params[4:5, cut]
        half = 0.5 + 0.5 * lax.erf(upper * (2.0 ** -0.5))
        active[:, cut] = (upper * half).astype(BF)
        bell = jnp.exp(-0.5 * upper * upper) * 0.3989422804014327
        slope[:, cut] = half + upper * bell

    tiles(hidden, up)

    def down(cut):
        halves(dot(active[...], whole[cut, hidden:], NT), keep, send, cut)

    tiles(keep.shape[1], down)


def feed_forward_tangent(count, hidden, where, *refs):
    pieces, (rel, active, slope, whole), refs = refs[:4], refs[4:8], refs[8:]
    tshards, refs = refs[:count], refs[count:]
    keep, send, twhole, sems, trel, tactive = refs
    copies = shard_copies(where, tshards, twhole, sems)
    start_all(copies)
    collect(pieces, trel)
    wait_all(copies)

    def up(cut):
        tupper = dot(trel[...], whole[:, cut], NN) + dot(rel[...], twhole[:, cut], NN)
        tactive[:, cut] = (slope[:, cut] * tupper).astype(BF)

    tiles(hidden, up)

    def down(cut):
        part = dot(tactive[...], whole[cut, hidden:], NT)
        part = part + dot(active[...], twhole[cut, hidden:], NT)
        halves(part, keep, send, cut)

    tiles(keep.shape[1], down)


def second_norm(
    where, keep, came, second, params, first, upstream,
    result, grad, low, unit, inverse,
):
    resid = first[...] + summed(keep, came, second) + params[5:6, :]
    center = resid - mean_last(resid)
    inv = lax.rsqrt(mean_last(center * center) + EPSILON)
    whitened = center * inv
    own = second.shape[0]
    unit[...] = whitened
    inverse[...] = jnp.broadcast_to(inv, inverse.shape)
    result[...] = (whitened * params[6:7, :] + params[7:8, :]).astype(BF)
    back = upstream[pl.ds(pl.multiple_of(where[0] * own, own), own), :].astype(F32)
    value = norm_along(whitened, inv, back * params[6:7, :])
    grad[...] = value
    low[0:own, :] = value.astype(BF)
    low[own:, :] = split_sums([sum_rows(value), sum_rows(back * whitened), sum_rows(back)])


def second_norm_tangent(keep, came, second, params, tfirst, unit, inverse, result):
    along = tfirst[...] + summed(keep, came, second)
    result[...] = (norm_along(unit[...], inverse[:, 0:1], along) * params[6:7, :]).astype(BF)


def first_norm_backward(
    keep, came, second, params, grad_two, unit, inverse, grad, low
):
    back = grad_two[...] + summed(keep, came, second)
    value = norm_along(unit[...], inverse[:, 0:1], back * params[2:3, :])
    own = second.shape[0]
    grad[...] = value
    low[0:own, :] = value.astype(BF)
    low[own:, :] = split_sums([sum_rows(value), sum_rows(back * unit[...]), sum_rows(back)])


def piece_sums(pieces):
    own = pieces[0].shape[0] - EXTRA
    return tree_sum([joined_sums(piece[own:, :]) for piece in pieces])


def feed_forward_backward(hidden, *refs):
    pieces, (slope, whole) = refs[:4], refs[4:6]
    rel, grad_upper, sums, keep, send = refs[6:]
    collect(pieces, rel)
    sums[...] = piece_sums(pieces)

    def down(cut):
        there = pl.ds(pl.multiple_of(cut.start + hidden, cut.size), cut.size)
        value = dot(rel[...], whole[:, there], NN) * slope[:, cut]
        sums[3:4, cut] = sum_rows(value)
        grad_upper[:, cut] = value.astype(BF)

    tiles(hidden, down)

    def up(cut):
        halves(dot(grad_upper[...], whole[cut, :hidden], NT), keep, send, cut)

    tiles(keep.shape[1], up)


def put_owned(where, step, targets, sums=None):
    if len(targets) == 1:
        targets[0][...] = step[...]
        return
    rows = step.shape[0] // len(OWNERS)
    extra = None if sums is None else split_sums([sums])
    for i, owner in enumerate(OWNERS):
        start = pl.multiple_of((where[1] ^ owner) * rows, rows)
        target = targets[i // 4]
        target[i % 4, 0:rows, :] = step[pl.ds(start, rows), :]
        if extra is not None:
            target[i % 4, rows:, :] = extra


def weight_gradient(summing, where, *refs):
    if summing:
        left, sums, right = refs[:3]
        refs = refs[3:]
    else:
        (right, left), refs, sums = refs[:2], refs[2:], None
    targets, step = refs[:-1], refs[-1]

    def one(cut):
        step[cut, :] = dot(left[:, cut], right[...], TN).astype(BF)

    tiles(left.shape[1], one)
    put_owned(where, step, targets, None if sums is None else sums[...])


def attention_backward(cols, *refs):
    pieces, (mixed, probs, whole) = refs[:4], refs[4:7]
    rel, grad, sums, keep, send, back = refs[7:]
    collect(pieces, rel)
    sums[...] = piece_sums(pieces)
    quarter = rel.shape[0] // 4
    back[...] = dot(rel[...], whole[:, 3 * cols : 4 * cols], NN).astype(BF)
    heads = cols // HEAD
    for pair in range(2):
        for head in range(heads):
            columns = [slice(at, at + HEAD) for at in range(head * HEAD, 3 * cols, cols)]
            query, key, value = [pair_rows(mixed, pair, quarter, at) for at in columns]
            prob = probs[pair * heads + head]
            grad_context = pair_rows(back, pair, quarter, columns[0])
            grad_value = dot(prob.astype(BF), grad_context, TN)
            grad_prob = dot(grad_context, value, NT)
            total = jnp.sum(grad_prob * prob, axis=-1, keepdims=True)
            grad_score = (prob * (grad_prob - total)).astype(BF)
            put_pair(grad, pair, quarter, columns[2], grad_value.astype(BF))
            grad_query = dot(grad_score, key, NN) * SCALE
            put_pair(grad, pair, quarter, columns[0], grad_query.astype(BF))
            grad_key = dot(grad_score, query, TN) * SCALE
            put_pair(grad, pair, quarter, columns[1], grad_key.astype(BF))

    def project(cut):
        halves(dot(grad[...], whole[cut, : 3 * cols], NT), keep, send, cut)

    tiles(keep.shape[1], project)


def attention_weights(paired, cols, where, rel, grad, sums, x_rel, context, *refs):
    targets, refs = (refs[:2], refs[2:]) if paired else (refs[:1], refs[1:])
    (step,) = refs[-1:]

    def one(cut):
        step[cut, : 3 * cols] = dot(x_rel[:, cut], grad[...], TN).astype(BF)
        step[cut, 3 * cols :] = dot(rel[:, cut], context[...], TN).astype(BF)

    tiles(x_rel.shape[1], one)
    mixed = sum_rows(grad[...].astype(F32))
    mixed = jnp.concatenate([mixed, jnp.zeros((1, cols), F32)], axis=1)
    lines = jnp.concatenate([sums[0:3, :], mixed])
    put_owned(where, step, targets, lines)
    if not paired:
        refs[0][...] = lines


def fold_shards(keep, came, *outs):
    rows = outs[0].shape[0]
    for i in range(4):
        total = keep[i, 0:rows, :].astype(F32) + came[i, 0:rows, :].astype(F32)
        if i == 0:
            outs[0][...] = total
        else:
            outs[i][0:rows, :] = total.astype(BF)
    if len(outs) > 4:
        sums = joined_sums(keep[0, rows:, :]) + joined_sums(came[0, rows:, :])
        rounded = split_sums([sums])
        outs[4][...] = joined_sums(rounded)
        for i in range(1, 4):
            outs[i][rows:, :] = rounded


def last_total(refs):
    rows = refs[0].shape[0]
    total = refs[0][...]
    for ref in refs[1:4]:
        total = total + ref[0:rows, :].astype(F32)
    return total


def last_sums(refs, outs):
    rows = refs[0].shape[0]
    sums = tree_sum([refs[4][...]] + [joined_sums(ref[rows:, :]) for ref in refs[1:4]])
    for i, out in enumerate(outs):
        out[...] = sums[i]


def finish_up(*refs):
    refs[4][...] = last_total(refs)


def finish_down(*refs):
    refs[5][...] = last_total(refs)
    last_sums(refs, refs[6:])


def finish_attention(cols, *refs):
    total = last_total(refs)
    for i in range(3):
        refs[5 + i][...] = total[:, i * cols : (i + 1) * cols]
    refs[8][...] = total[:, 3 * cols :].T
    last_sums(refs, refs[9:])


def last_sum(keep, came, second, grad_one, out):
    out[...] = (grad_one[...] + summed(keep, came, second)).astype(BF)


def place_rows(count, where, *refs):
    pieces, outs, sems = refs[: 4 * count], refs[4 * count : 5 * count], refs[5 * count]
    own = pieces[0].shape[0]
    copies = []
    for i, out in enumerate(outs):
        for j, block in enumerate(BLOCKS):
            start = pl.multiple_of((where[0] ^ block) * own, own)
            copies.append(
                pltpu.make_async_copy(
                    pieces[4 * i + j], out.at[pl.ds(start, own), :], sems.at[4 * i + j]
                )
            )
    start_all(copies)
    wait_all(copies)


def per_device(tp, dp, *arrays):
    (
        layer_input,
        pair_lengths,
        query_weight,
        query_bias,
        key_weight,
        value_weight,
        value_bias,
        out_weight,
        out_bias,
        first_gain,
        first_shift,
        up_weight,
        up_bias,
        down_weight,
        down_bias,
        second_gain,
        second_shift,
        out_grad,
        query_tangent,
        key_tangent,
        value_tangent,
        out_tangent,
        up_tangent,
        down_tangent,
    ) = arrays
    rows, width = layer_input.shape
    cols = query_weight.shape[1]
    hidden = up_weight.shape[1]
    heads = cols // HEAD
    own = rows // tp
    half = rows // 2
    shard = width // dp
    paired = dp == len(SNAKE)

    place = jnp.stack([lax.axis_index("tp"), lax.axis_index("dp")]).astype(jnp.int32)
    where = jnp.concatenate([place, pair_lengths])
    zeros = jnp.zeros((cols,), F32)
    params = jnp.concatenate(
        [query_bias, zeros, value_bias, zeros, out_bias, first_gain, first_shift]
        + [up_bias, down_bias, second_gain, second_shift]
    ).reshape(8, width)
    parts = [((half, width), BF), ((half, width), BF)]
    piece = ((own + EXTRA, width), BF)
    lines = ((EXTRA // 2, width), F32)
    full_own = ((own, width), F32)
    attn_rows = ((width, 4 * cols), BF)
    ff_rows = ((width, 2 * hidden), BF)

    def pack(first_one, *blocks):
        return jnp.concatenate([first_one, *blocks], 1)

    def arriving(count):
        return pltpu.SemaphoreType.DMA((count,))

    where, out_rows, tout_rows, params = join((), where, out_weight.T, out_tangent.T, params)
    attn = Ring(pack(query_weight, key_weight, value_weight, out_rows), dp)
    attn.step()
    early = attn.parts[-1]
    ff = Ring(pack(after(up_weight, early), down_weight.T), dp)
    tattn = Ring(pack(after(query_tangent, early), key_tangent, value_tangent, tout_rows), dp)
    tff = Ring(pack(after(up_tangent, early), down_tangent.T), dp)
    attn.step()
    join([attn, ff])
    attn.step()
    ff.step()
    attn.step()
    where = join([ff], where)
    ff.step()
    count = len(attn.parts)
    x_rel, mixed, probs, context, keep, send, attn_whole = call(
        functools.partial(attention_forward, count, cols),
        "attention_forward",
        [
            ((rows, width), BF),
            ((rows, 3 * cols), BF),
            ((2 * heads, SEQ, SEQ), F32),
            ((rows, cols), BF),
            *parts,
            attn_rows,
        ],
        (where, layer_input, params),
        attn.parts,
        [arriving(count)],
    )
    first, unit_one, inverse_one, first_low = call(
        first_norm,
        "first_norm",
        [full_own, full_own, ((own, 128), F32), ((own, width), BF)],
        (x_rel, *sum_exchange(keep, send, tp, [ff]), params),
    )
    pieces = spread_rows(first_low, tp, [ff])
    tattn.front = [after(tattn.front[0], pieces[1])] * 2
    tattn.step()
    first_rel, active, slope, keep, send, ff_whole = call(
        functools.partial(feed_forward, count, hidden),
        "feed_forward",
        [((rows, width), BF), ((rows, hidden), BF), ((rows, hidden), F32), *parts, ff_rows],
        (where, params, *pieces),
        ff.parts,
        [arriving(count)],
    )
    result, grad_two, grad_two_low, unit_two, inverse_two = call(
        second_norm,
        "second_norm",
        [((own, width), BF), full_own, piece, full_own, ((own, 128), F32)],
        (where, *sum_exchange(keep, send, tp, [tattn]), params, first, out_grad),
    )
    pieces = spread_rows(grad_two_low, tp, [tattn])
    tff.front = [after(tff.front[0], pieces[1])] * 2
    tff.step()
    grad_down, grad_upper, sums_up, keep, send = call(
        functools.partial(feed_forward_backward, hidden),
        "feed_forward_backward",
        [((rows, width), BF), ((rows, hidden), BF), lines, *parts],
        (*pieces, slope, ff_whole),
    )

    def weight_outs(total, sums):
        if paired:
            return [((4, shard + (EXTRA if sums else 0), total), BF)] * 2
        return [((width, total), BF)]

    def step_of(name, near, summing):
        return call(
            functools.partial(weight_gradient, summing),
            name,
            weight_outs(hidden, summing),
            (where, *near),
            (),
            [pltpu.VMEM((width, hidden), BF)],
        )

    def swap_shards(steps):
        return lax.ppermute(steps[1], "dp", xor_pairs(dp, 1)) if paired else steps[0]

    down_steps = step_of("down_weights", (grad_down, sums_up, active), True)
    up_steps = step_of("up_weights", (grad_upper, first_rel), False)
    down_came = swap_shards(down_steps)
    exchanged = sum_exchange(keep, send, tp, [tff], (down_steps[0],))
    grad_one, grad_one_low = call(
        first_norm_backward,
        "first_norm_backward",
        [full_own, piece],
        (*exchanged, after(params, up_steps[0]), grad_two, unit_one, inverse_one),
    )
    up_came = swap_shards(up_steps)
    pieces = spread_rows(grad_one_low, tp, [tff])
    tkeep, tsend = call(
        functools.partial(attention_tangent, count, cols),
        "attention_tangent",
        parts,
        (after(where, grad_one_low), x_rel, mixed, probs, context, attn_whole),
        tattn.parts,
        [pltpu.VMEM(*attn_rows), arriving(count)]
        + [pltpu.VMEM((rows, 3 * cols), BF), pltpu.VMEM((rows, cols), BF)],
    )
    grad_attn, grad_mixed, sums_one, keep, send = call(
        functools.partial(attention_backward, cols),
        "attention_backward",
        [((rows, width), BF), ((rows, 3 * cols), BF), lines, *parts],
        (*pieces[:3], after(pieces[3], down_came, tkeep), mixed, probs, attn_whole),
        (),
        [pltpu.VMEM((rows, cols), BF)],
    )
    last_steps = call(
        functools.partial(attention_weights, paired, cols),
        "attention_weights",
        weight_outs(4 * cols, True) + ([] if paired else [lines]),
        (where, grad_attn, grad_mixed, sums_one, x_rel, context),
        (),
        [pltpu.VMEM(*attn_rows)],
    )
    last_came = swap_shards(last_steps)
    exchanged = sum_exchange(keep, send, tp, (), (last_steps[0],))
    (grad_input,) = call(
        last_sum, "last_sum", [((own, width), BF)], (*exchanged, grad_one)
    )

    tfirst, tfirst_low = call(
        first_norm_tangent,
        "first_norm_tangent",
        [full_own, ((own, width), BF)],
        (*sum_exchange(tkeep, tsend, tp), params, unit_one, inverse_one),
    )
    tkeep, tsend = call(
        functools.partial(feed_forward_tangent, count, hidden),
        "feed_forward_tangent",
        parts,
        (
            after(where, last_steps[0]),
            *spread_rows(tfirst_low, tp),
            first_rel,
            active,
            slope,
            ff_whole,
        ),
        tff.parts,
        [pltpu.VMEM(*ff_rows), arriving(count)]
        + [pltpu.VMEM((rows, width), BF), pltpu.VMEM((rows, hidden), BF)],
    )
    (tresult,) = call(
        second_norm_tangent,
        "second_norm_tangent",
        [((own, width), BF)],
        (*sum_exchange(tkeep, tsend, tp), params, tfirst, unit_two, inverse_two),
    )

    def over_dp(kept, came, sums):
        total = kept.shape[2]
        going = ((kept.shape[1], total), BF)
        outs = [((shard, total), F32), going, going, going] + ([lines] if sums else [])
        own_shard, *onward = call(fold_shards, "fold_shards", outs, (kept, came))
        there = [lax.ppermute(onward[i], "dp", xor_pairs(dp, 2 * i + 2)) for i in range(3)]
        return (own_shard, *there, *onward[3:])

    vector = ((width,), F32)
    if paired:
        own_down, *sums_two = call(
            finish_down,
            "finish_down",
            [((shard, hidden), F32)] + [vector] * 4,
            over_dp(down_steps[0], down_came, True),
        )
        (own_up,) = call(
            finish_up, "finish_up", [((shard, hidden), F32)], over_dp(up_steps[0], up_came, False)
        )
        *own_mixed, own_out, bias_out, gain_one, shift_one, mixed_line = call(
            functools.partial(finish_attention, cols),
            "finish_attention",
            [((shard, cols), F32)] * 3 + [((cols, shard), F32)] + [vector] * 4,
            over_dp(last_steps[0], last_came, True),
        )
        sums_one = [bias_out, gain_one, shift_one, mixed_line]
    else:

        def all_summed(step):
            split = step.reshape(dp, shard, -1)
            came = lax.all_to_all(split, "dp", 0, 0, tiled=True)
            return jnp.sum(came.astype(F32), axis=0)

        own_down, own_up = all_summed(down_steps[0]), all_summed(up_steps[0])
        last = all_summed(last_steps[0])
        own_mixed = [last[:, i * cols : (i + 1) * cols] for i in range(3)]
        own_out = last[:, 3 * cols :].T
        sums_two = list(lax.psum(sums_up, "dp"))
        sums_one = list(lax.psum(last_steps[1], "dp"))

    def all_rows(*blocks):
        pieces = [piece for block in blocks for piece in spread_rows(block, tp)]
        return call(
            functools.partial(place_rows, len(blocks)),
            "place_rows",
            [((rows, width), BF)] * len(blocks),
            (where, *pieces),
            scratch=[arriving(4 * len(blocks))],
            any_outs=True,
        )

    whole_result, whole_tresult = all_rows(result, tresult)
    (whole_grad,) = all_rows(grad_input)
    mixed_sums = sums_one[3]
    return (
        whole_result,
        whole_grad,
        whole_tresult,
        own_mixed[0],
        mixed_sums[:cols],
        own_mixed[1],
        own_mixed[2],
        mixed_sums[2 * cols : 3 * cols],
        own_out,
        *sums_one[:3],
        own_up,
        sums_two[3],
        own_down.T,
        *sums_two[:3],
    )


def solution(mesh):
    wide, tall, col, row, full = P("dp", "tp"), P("tp", "dp"), P("tp"), P("dp", None), P()
    placed = (
        (row, P("dp"), wide, col, wide, wide, col, tall, full, full, full, wide, col, tall)
        + (full, full, full, row, wide, wide, wide, tall, wide, tall)
    )
    results = (row, row, row, wide, col, wide, wide, col, tall, full, full, full)
    results = results + (wide, col, tall, full, full, full)
    tp, dp = mesh.shape["tp"], mesh.shape["dp"]

    def body(*arrays):
        return per_device(tp, dp, *arrays)

    return jax.shard_map(
        body, mesh=mesh, in_specs=placed, out_specs=results, check_vma=False
    )
```

time: 349 us -> 231 us (0.66)
  blocking collectives: 66.5 us -> 0 us
  local copies, waits for them, and re-layouts: 57.4 us -> 3.35 us
  matrix products: 43.8 us -> 0 us
  Pallas kernels: 0 us -> 41.7 us
  waiting for transfers between devices: 98.1 us -> 118 us
  between operations: 11.3 us -> 1.21 us
  other arithmetic: 8.69 us -> 3.1 us
    ppermute x36 -> x73, waiting for transfers between devices: 51 us -> 118 us  [the longest x16 54.2 us: step(): self.front[0] = lax.ppermute(self.front[0], 'dp', ahead)]
    all_gather x8 -> x0, blocking collectives: 66.5 us -> none  [the longest x3 26.9 us: all_rows(): return lax.all_gather(block, 'tp', axis=0, tiled=True)]
    all_to_all x5 -> x0, waiting for transfers between devices: 47 us -> none  [the longest x4 40 us: spread(): came = lax.all_to_all(split, 'dp', 0, 0, tiled=True)]
    dot_general x26 -> x0, matrix products: 41.9 us -> none  [the longest x17 35.7 us: dot(): lax.dot_general(left, right, (dims, ((), ())), preferred_element_type=F32)]
    pallas_call x0 -> x23, Pallas kernels: none -> 41.7 us  [call(): pl.pallas_call(body, out_shape=[jax.ShapeDtypeStruct(shape, kind) for sha...]
    dynamic_update_slice x30 -> x0, local copies, waits for them, and re-layouts: 32.2 us -> none  [the longest x16 16.2 us: gather_rows(): whole = lax.dynamic_update_slice(whole, one, (owner * rows, 0))]
    ppermute x36 -> x73, starting transfers between devices: 41.4 us -> 63 us  [the longest x33 17.5 us: swap(): return lax.ppermute(block, 'tp', xor_pairs(tp, bit))]
    all_to_all x5 -> x0, starting transfers between devices: 19.8 us -> none  [the longest x4 16.4 us: spread(): came = lax.all_to_all(split, 'dp', 0, 0, tiled=True)]
  transfers between devices with their start and end apart: 41 -> 73, of which waited for: 17 -> 35; matrix products, arithmetic and copies ran while one was open for 20% -> 1% of each run, Pallas kernels for 0% -> 9%
where the time goes in v2:
time: 231 us; the launch traced here: 230 us
  waiting for transfers between devices  118 us (51%)
  starting transfers between devices  63 us (27%)
  Pallas kernels  41.7 us (18%)
  local copies, waits for them, and re-layouts  3.35 us (1%)
  other arithmetic  3.1 us (1%)
    ppermute x16, waiting for transfers between devices, step(): self.front[0] = lax.ppermute(self.front[0], 'dp', ahead)  54.2 us
    pallas_call x23, Pallas kernels, call(): pl.pallas_call(body, out_shape=[jax.ShapeDtypeStruct(shape, kind) for sha...  41.7 us
    ppermute x9, waiting for transfers between devices, over_dp(): lax.ppermute(onward[i], 'dp', xor_pairs(dp, 2 * i + 2))  24.1 us
    ppermute x33, starting transfers between devices, swap(): return lax.ppermute(block, 'tp', xor_pairs(tp, bit))  17.5 us
    ppermute x33, waiting for transfers between devices, swap(): return lax.ppermute(block, 'tp', xor_pairs(tp, bit))  17.2 us
    ppermute x12, starting transfers between devices, step(): self.front[1] = lax.ppermute(self.front[1], 'dp', behind)  15.6 us
    ppermute x9, starting transfers between devices, over_dp(): lax.ppermute(onward[i], 'dp', xor_pairs(dp, 2 * i + 2))  14 us
    ppermute x16, starting transfers between devices, step(): self.front[0] = lax.ppermute(self.front[0], 'dp', ahead)  12.5 us
  transfers between devices with their start and end apart: 73, of which 35 were waited for; matrix products, arithmetic and copies ran while one was open for 1% of the time, Pallas kernels for 9%

profile of v2, /device:TPU:0, one launch (start us, length us, event | category | flops | bytes accessed | tf_op | source)
XLA Modules:
  0.0 230.2 jit_solution(10876919910638424265)
XLA Ops:
  5.1 3.0 %collective-permute-start.2 = (bf16[96,768]{1,0:T(8,128)(2,1)S(1)}, bf16[96,768]{1,0:T(8,128)(2,1)S(1)}, u32[]{:S(2)}, u32[]{:S(2)}) collective-permute-start(bf16[96,768]{1,0:T(8,128)(2,1)S(1)} %pad_maximum_fusion.2.refs_0_), channel_id=1, source_target_pairs={{8,0},{16,8},{24,16},{28,24},{20,28},{12,20},{4,12},{0,4},{9,1},{1... | collective-permute-start | bytes 442376 | tf_op jit(solution)/shard_map/ppermute | solution.py:91
  8.3 3.8 %collective-permute-done.2.refs_2_ = bf16[96,768]{1,0:T(8,128)(2,1)S(1)} collective-permute-done((bf16[96,768]{1,0:T(8,128)(2,1)S(1)}, bf16[96,768]{1,0:T(8,128)(2,1)S(1)}, u32[]{:S(2)}, u32[]{:S(2)}) %collective-permute-start.2) | collective-permute-done | bytes 147488 | tf_op jit(solution)/shard_map/ppermute | solution.py:91
  12.1 1.7 collective-permute-start.3
  15.1 2.1 collective-permute-done.3.refs_4_
  17.2 1.7 collective-permute-done.1.refs_3_
  19.2 1.7 collective-permute-start.5
  21.3 1.7 collective-permute-start.7
  22.9 6.3 %collective-permute-done.6.refs_5_ = bf16[96,768]{1,0:T(8,128)(2,1)S(1)} collective-permute-done((bf16[96,768]{1,0:T(8,128)(2,1)S(1)}, bf16[96,768]{1,0:T(8,128)(2,1)S(1)}, u32[]{:S(2)}, u32[]{:S(2)}) %collective-permute-start.6) | collective-permute-done | bytes 147488 | tf_op jit(solution)/shard_map/ppermute | solution.py:88
  29.6 4.8 %collective-permute-done.8.refs_7_ = bf16[96,768]{1,0:T(8,128)(2,1)S(1)} collective-permute-done((bf16[96,768]{1,0:T(8,128)(2,1)S(1)}, bf16[96,768]{1,0:T(8,128)(2,1)S(1)}, u32[]{:S(2)}, u32[]{:S(2)}) %collective-permute-start.8) | collective-permute-done | bytes 147488 | tf_op jit(solution)/shard_map/ppermute | solution.py:88
  34.3 5.9 %attention_forward.1 = (bf16[512,768]{1,0:T(8,128)(2,1)S(1)}, bf16[512,576]{1,0:T(8,128)(2,1)S(1)}, f32[6,256,256]{2,1,0:T(8,128)S(1)}, bf16[512,192]{1,0:T(8,12...) custom-call(s32[4]{0:T(128)S(1)} %pad_add_fusion.where, ...), custom_call_target="tpu_custom_call" | custom-call | flops 1 | bytes 1 | tf_op jit(solution)/shard_map/attention_forward/pallas_call | solution.py:42
  40.8 1.7 collective-permute-start.11
  42.4 7.3 %collective-permute-done.10.refs_7_ = bf16[96,1536]{1,0:T(8,128)(2,1)S(1)} collective-permute-done((bf16[96,1536]{1,0:T(8,128)(2,1)S(1)}, bf16[96,1536]{1,0:T(8,128)(2,1)S(1)}, u32[]{:S(2)}, u32[]{:S(2)}) %collective-permute-start.10) | collective-permute-done | bytes 294944 | tf_op jit(solution)/shard_map/ppermute | solution.py:88
  49.9 1.7 collective-permute-start.13
  51.9 1.6 collective-permute-start.12
  53.5 4.3 %collective-permute-done.12.second = bf16[128,768]{1,0:T(8,128)(2,1)S(1)} collective-permute-done((bf16[128,768]{1,0:T(8,128)(2,1)S(1)}, bf16[128,768]{1,0:T(8,128)(2,1)S(1)}, u32[]{:S(2)}, u32[]{:S(2)}) %collective-permute-start.12) | collective-permute-done | bytes 196640 | tf_op jit(solution)/shard_map/ppermute | solution.py:132
  59.6 1.6 collective-permute-start.16
  61.5 1.6 collective-permute-start.15
  63.1 4.1 %collective-permute-done.15.refs_1_ = bf16[128,768]{1,0:T(8,128)(2,1)S(1)} collective-permute-done((bf16[128,768]{1,0:T(8,128)(2,1)S(1)}, bf16[128,768]{1,0:T(8,128)(2,1)S(1)}, u32[]{:S(2)}, u32[]{:S(2)}) %collective-permute-start.15) | collective-permute-done | bytes 196640 | tf_op jit(solution)/shard_map/ppermute | solution.py:132
  68.7 3.9 %feed_forward.1 = (bf16[512,768]{1,0:T(8,128)(2,1)S(1)}, bf16[512,768]{1,0:T(8,128)(2,1)S(1)}, f32[512,768]{1,0:T(8,128)S(1)}, bf16[256,768]{1,0:T(8,128)(2,1)S(...) custom-call(s32[4]{0:T(128)S(1)} %pad_add_fusion.where, f32[8,768]{1,0:T(8,128)S(1)} %reshape.39.params, ...), custom_call_target="tpu_custom_call" | custom-call | flops 1 | bytes 1 | tf_op jit(solution)/shard_map/feed_forward/pallas_call | solution.py:42
  72.9 1.6 collective-permute-start.20
  75.0 4.1 %collective-permute-done.20.refs_1_ = bf16[96,768]{1,0:T(8,128)(2,1)S(1)} collective-permute-done((bf16[96,768]{1,0:T(8,128)(2,1)S(1)}, bf16[96,768]{1,0:T(8,128)(2,1)S(1)}, u32[]{:S(2)}, u32[]{:S(2)}) %collective-permute-start.20) | collective-permute-done | bytes 147488 | tf_op jit(solution)/shard_map/ppermute | solution.py:88
  80.4 1.6 collective-permute-start.22
  84.0 3.1 %collective-permute-done.23.refs_3_ = bf16[96,768]{1,0:T(8,128)(2,1)S(1)} collective-permute-done((bf16[96,768]{1,0:T(8,128)(2,1)S(1)}, bf16[96,768]{1,0:T(8,128)(2,1)S(1)}, u32[]{:S(2)}, u32[]{:S(2)}) %collective-permute-start.23) | collective-permute-done | bytes 147488 | tf_op jit(solution)/shard_map/ppermute | solution.py:88
  92.3 3.1 %collective-permute-done.29.refs_5_ = bf16[96,768]{1,0:T(8,128)(2,1)S(1)} collective-permute-done((bf16[96,768]{1,0:T(8,128)(2,1)S(1)}, bf16[96,768]{1,0:T(8,128)(2,1)S(1)}, u32[]{:S(2)}, u32[]{:S(2)}) %collective-permute-start.29) | collective-permute-done | bytes 147488 | tf_op jit(solution)/shard_map/ppermute | solution.py:88
  97.8 2.4 %feed_forward_backward.1 = (bf16[512,768]{1,0:T(8,128)(2,1)S(1)}, bf16[512,768]{1,0:T(8,128)(2,1)S(1)}, f32[4,768]{1,0:T(4,128)S(1)}, bf16[256,768]{1,0:T(8,128)(2,1)S(1)}, bf16[256,768]{1,0:T(8,128)(2,1)S(1)}) custom-call(bf16[136,768]{1,0:T(8,128)(2,1)S(1)} %get-tuple-element.168.refs_0_, bf16[136,768]{1,0:T(8,128)(2,1)S(1)} %collective-permute-done.28.refs_1_, ...), custom_call_target="tpu_custom_call" | custom-call | flops 1 | bytes 1 | tf_op jit(solution)/shard_map/feed_forward_backward/pallas_call | solution.py:42
  102.6 1.9 down_weights.1
  104.4 5.4 %collective-permute-done.34.refs_9_ = bf16[96,1536]{1,0:T(8,128)(2,1)S(1)} collective-permute-done((bf16[96,1536]{1,0:T(8,128)(2,1)S(1)}, bf16[96,1536]{1,0:T(8,128)(2,1)S(1)}, u32[]{:S(2)}, u32[]{:S(2)}) %collective-permute-start.34) | collective-permute-done | bytes 294944 | tf_op jit(solution)/shard_map/ppermute | solution.py:88
  112.4 1.6 collective-permute-start.36
  114.6 1.9 up_weights.1
  116.5 1.7 collective-permute-done.36.second
  118.1 1.9 collective-permute-done.37.refs_11_
  121.6 5.7 %attention_tangent.1 = (bf16[256,768]{1,0:T(8,128)(2,1)S(1)}, bf16[256,768]{1,0:T(8,128)(2,1)S(1)}) custom-call(s32[4]{0:T(128)S(1)} %pad_add_fusion.where, bf16[512,768]{1,0:T(8,128)(2,1)S(1)} %get-tuple-element.145.x_rel.rel, bf16[512,576]{1,0:T(8,128)(2,1)S(1)} %get-tuple-element.199.mixed.refs_4_, f32[6,256,256]{2,1,0:T(8,128)S(1)} %get-tuple-element.200.probs.refs_5_, ...), custom_call_target="tpu_custom_call" | custom-call | flops 1 | bytes 1 | tf_op jit(solution)/shard_map/attention_tangent/pallas_call | solution.py:42
  133.0 3.8 %collective-permute-done.39.refs_1_ = bf16[136,768]{1,0:T(8,128)(2,1)S(1)} collective-permute-done((bf16[136,768]{1,0:T(8,128)(2,1)S(1)}, bf16[136,768]{1,0:T(8,128)(2,1)S(1)}, u32[]{:S(2)}, u32[]{:S(2)}) %collective-permute-start.39) | collective-permute-done | bytes 208928 | tf_op jit(solution)/shard_map/ppermute | solution.py:132
  136.8 13.8 %collective-permute-done.40.refs_13_ = bf16[96,1536]{1,0:T(8,128)(2,1)S(1)} collective-permute-done((bf16[96,1536]{1,0:T(8,128)(2,1)S(1)}, bf16[96,1536]{1,0:T(8,128)(2,1)S(1)}, u32[]{:S(2)}, u32[]{:S(2)}) %collective-permute-start.40) | collective-permute-done | bytes 294944 | tf_op jit(solution)/shard_map/ppermute | solution.py:88
  151.4 1.6 collective-permute-start.48
  153.0 4.5 %attention_backward.1 = (bf16[512,768]{1,0:T(8,128)(2,1)S(1)}, bf16[512,576]{1,0:T(8,128)(2,1)S(1)}, f32[4,768]{1,0:T(4,128)S(1)}, bf16[256,768]{1,0:T(8,128)(2,1)S(1)}, bf16[256,768]{1,0:T(8,128)(2,1)S(1)}) custom-call(bf16[136,768]{1,0:T(8,128)(2,1)S(1)} %get-tuple-element.193.refs_0_, bf16[136,768]{1,0:T(8,128)(2,1)S(1)} %collective-permute-done.39.refs_1_, ...), custom_call_target="tpu_custom_call" | custom-call | flops 1 | bytes 1 | tf_op jit(solution)/shard_map/attention_backward/pallas_call | solution.py:42
  158.3 2.3 %attention_weights.1 = (bf16[4,104,768]{2,1,0:T(8,128)(2,1)S(1)}, bf16[4,104,768]{2,1,0:T(8,128)(2,1)S(1)}) custom-call(s32[4]{0:T(128)S(1)} %pad_add_fusion.where, bf16[512,768]{1,0:T(8,128)(2,1)S(1)} %get-tuple-element.206.rel, bf16[512,576]{1,0:T(8,128)(2,1)S(1)} %get-tuple-element.207.grad, f32[4,768]{1,0:T(4,128)S(1)} %get-tuple-element.208.sums, ...), custom_call_target="tpu_custom_call" | custom-call | flops 1 | bytes 1 | tf_op jit(solution)/shard_map/attention_weights/pallas_call | solution.py:42
  161.6 4.8 %feed_forward_tangent.1 = (bf16[256,768]{1,0:T(8,128)(2,1)S(1)}, bf16[256,768]{1,0:T(8,128)(2,1)S(1)}) custom-call(s32[4]{0:T(128)S(1)} %pad_add_fusion.where, bf16[128,768]{1,0:T(8,128)(2,1)S(1)} %get-tuple-element.212.refs_0_, bf16[128,768]{1,0:T(8,128)(2,1)S(1)} %collective-permute-done.48.refs_1_, bf16[128,768]{1,0:T(8,128)(2,1)S(1)} %collective-permute-done.49.refs_2_, ...), custom_call_target="tpu_custom_call" | custom-call | flops 1 | bytes 1 | tf_op jit(solution)/shard_map/feed_forward_tangent/pallas_call | solution.py:42
  171.8 10.9 %collective-permute-done.66.came = bf16[4,96,768]{2,1,0:T(8,128)(2,1)S(1)} collective-permute-done((bf16[4,96,768]{2,1,0:T(8,128)(2,1)S(1)}, bf16[4,96,768]{2,1,0:T(8,128)(2,1)S(1)}, u32[]{:S(2)}, u32[]{:S(2)}) %collective-permute-start.66) | collective-permute-done | bytes 589856 | tf_op jit(solution)/shard_map/ppermute | solution.py:706
  184.9 2.4 %collective-permute-start.69 = (bf16[96,768]{1,0:T(8,128)(2,1)S(1)}, bf16[96,768]{1,0:T(8,128)(2,1)S(1)}, u32[]{:S(2)}, u32[]{:S(2)}) collective-permute-start(bf16[96,768]{1,0:T(8,128)(2,1)S(1)} %get-tuple-element.243), channel_id=1, source_target_pairs={{0,24},{4,28},{8,16},{12,20},{16,8},{20,12},{24,0},{28,4},{1,25},{... | collective-permute-start | bytes 442376 | tf_op jit(solution)/shard_map/ppermute | solution.py:785
  187.4 2.3 %collective-permute-done.67.refs_1_ = bf16[96,768]{1,0:T(8,128)(2,1)S(1)} collective-permute-done((bf16[96,768]{1,0:T(8,128)(2,1)S(1)}, bf16[96,768]{1,0:T(8,128)(2,1)S(1)}, u32[]{:S(2)}, u32[]{:S(2)}) %collective-permute-start.67) | collective-permute-done | bytes 147488 | tf_op jit(solution)/shard_map/ppermute | solution.py:785
  190.1 6.7 %collective-permute-done.68.refs_2_ = bf16[96,768]{1,0:T(8,128)(2,1)S(1)} collective-permute-done((bf16[96,768]{1,0:T(8,128)(2,1)S(1)}, bf16[96,768]{1,0:T(8,128)(2,1)S(1)}, u32[]{:S(2)}, u32[]{:S(2)}) %collective-permute-start.68) | collective-permute-done | bytes 147488 | tf_op jit(solution)/shard_map/ppermute | solution.py:785
  196.9 2.0 collective-permute-start.71
  198.8 2.9 %collective-permute-start.72 = (bf16[104,768]{1,0:T(8,128)(2,1)S(1)}, bf16[104,768]{1,0:T(8,128)(2,1)S(1)}, u32[]{:S(2)}, u32[]{:S(2)}) collective-permute-start(bf16[104,768]{1,0:T(8,128)(2,1)S(1)} %get-tuple-element.247), channel_id=1, source_target_pairs={{0,24},{4,28},{8,16},{12,20},{16,8},{20,12},{24,0},{28,4},{1,25},{... | collective-permute-start | bytes 479240 | tf_op jit(solution)/shard_map/ppermute | solution.py:785
  203.4 7.1 %collective-permute-done.71.refs_2_ = bf16[104,768]{1,0:T(8,128)(2,1)S(1)} collective-permute-done((bf16[104,768]{1,0:T(8,128)(2,1)S(1)}, bf16[104,768]{1,0:T(8,128)(2,1)S(1)}, u32[]{:S(2)}, u32[]{:S(2)}) %collective-permute-start.71) | collective-permute-done | bytes 159776 | tf_op jit(solution)/shard_map/ppermute | solution.py:785
  210.5 3.1 %collective-permute-start.64 = (bf16[104,768]{1,0:T(8,128)(2,1)S(1)}, bf16[104,768]{1,0:T(8,128)(2,1)S(1)}, u32[]{:S(2)}, u32[]{:S(2)}) collective-permute-start(bf16[104,768]{1,0:T(8,128)(2,1)S(1)} %get-tuple-element.228), channel_id=1, source_target_pairs={{0,16},{4,20},{8,24},{12,28},{16,0},{20,4},{24,8},{28,12},{1,17},{... | collective-permute-start | bytes 479240 | tf_op jit(solution)/shard_map/ppermute | solution.py:785
  217.6 6.8 %collective-permute-done.64.refs_2_ = bf16[104,768]{1,0:T(8,128)(2,1)S(1)} collective-permute-done((bf16[104,768]{1,0:T(8,128)(2,1)S(1)}, bf16[104,768]{1,0:T(8,128)(2,1)S(1)}, u32[]{:S(2)}, u32[]{:S(2)}) %collective-permute-start.64) | collective-permute-done | bytes 159776 | tf_op jit(solution)/shard_map/ppermute | solution.py:785
  228.3 1.7 place_rows.2
  (152 shorter events, 55.9 us)
Async XLA Ops:
  5.1 6.9 %collective-permute-start.2 = (bf16[96,768]{1,0:T(8,128)(2,1)S(1)}, bf16[96,768]{1,0:T(8,128)(2,1)S(1)}, u32[]{:S(2)}, u32[]{:S(2)}) collective-permute-start(bf16[96,768]{1,0:T(8,128)(2,1)S(1)} %pad_maximum_fusion.2.refs_0_), channel_id=1, source_target_pairs={{8,0},{16,8},{24,16},{28,24},{20,28},{12,20},{4,12},{0,4},{9,1},{1... | collective-permute-start | bytes 442376 | tf_op jit(solution)/shard_map/ppermute | solution.py:91
  18.9 10.7 %collective-permute-start.4 = (bf16[96,1536]{1,0:T(8,128)(2,1)S(1)}, bf16[96,1536]{1,0:T(8,128)(2,1)S(1)}, u32[]{:S(2)}, u32[]{:S(2)}) collective-permute-start(bf16[96,1536]{1,0:T(8,128)(2,1)S(1)} %pad_maximum_fusion.refs_4_), channel_id=1, source_target_pairs={{0,8},{8,16},{16,24},{24,28},{28,20},{20,12},{12,4},{4,0},{1,9},{9... | collective-permute-start | bytes 884744 | tf_op jit(solution)/shard_map/ppermute | solution.py:88
  19.2 10.3 %collective-permute-start.5 = (bf16[96,1536]{1,0:T(8,128)(2,1)S(1)}, bf16[96,1536]{1,0:T(8,128)(2,1)S(1)}, u32[]{:S(2)}, u32[]{:S(2)}) collective-permute-start(bf16[96,1536]{1,0:T(8,128)(2,1)S(1)} %pad_maximum_fusion.refs_4_), channel_id=1, source_target_pairs={{8,0},{16,8},{24,16},{28,24},{20,28},{12,20},{4,12},{0,4},{9,1},{1... | collective-permute-start | bytes 884744 | tf_op jit(solution)/shard_map/ppermute | solution.py:91
  20.9 8.3 %collective-permute-start.6 = (bf16[96,768]{1,0:T(8,128)(2,1)S(1)}, bf16[96,768]{1,0:T(8,128)(2,1)S(1)}, u32[]{:S(2)}, u32[]{:S(2)}) collective-permute-start(bf16[96,768]{1,0:T(8,128)(2,1)S(1)} %collective-permute-done.1.refs_3_), channel_id=1, source_target_pairs={{0,8},{8,16},{16,24},{24,28},{28,20},{20,12},{12,4},{4,0},{1,9},{9... | collective-permute-start | bytes 442376 | tf_op jit(solution)/shard_map/ppermute | solution.py:88
  21.3 8.3 %collective-permute-start.7 = (bf16[96,768]{1,0:T(8,128)(2,1)S(1)}, bf16[96,768]{1,0:T(8,128)(2,1)S(1)}, u32[]{:S(2)}, u32[]{:S(2)}) collective-permute-start(bf16[96,768]{1,0:T(8,128)(2,1)S(1)} %collective-permute-done.3.refs_4_), channel_id=1, source_target_pairs={{8,0},{16,8},{24,16},{28,24},{20,28},{12,20},{4,12},{0,4},{9,1},{1... | collective-permute-start | bytes 442376 | tf_op jit(solution)/shard_map/ppermute | solution.py:91
  40.3 9.6 %collective-permute-start.9 = (bf16[256,768]{1,0:T(8,128)(2,1)S(1)}, bf16[256,768]{1,0:T(8,128)(2,1)S(1)}, u32[]{:S(2)}, u32[]{:S(2)}) collective-permute-start(bf16[256,768]{1,0:T(8,128)(2,1)S(1)} %get-tuple-element.147), channel_id=1, source_target_pairs={{0,1},{1,0},{2,3},{3,2},{4,5},{5,4},{6,7},{7,6},{8,9},{9,8},{10,11... | collective-permute-start | bytes 1179656 | tf_op jit(solution)/shard_map/ppermute | solution.py:132
  40.4 9.4 %collective-permute-start.10 = (bf16[96,1536]{1,0:T(8,128)(2,1)S(1)}, bf16[96,1536]{1,0:T(8,128)(2,1)S(1)}, u32[]{:S(2)}, u32[]{:S(2)}) collective-permute-start(bf16[96,1536]{1,0:T(8,128)(2,1)S(1)} %collective-permute-done.4.refs_5_), channel_id=1, source_target_pairs={{0,8},{8,16},{16,24},{24,28},{28,20},{20,12},{12,4},{4,0},{1,9},{9... | collective-permute-start | bytes 884744 | tf_op jit(solution)/shard_map/ppermute | solution.py:88
  40.8 9.1 %collective-permute-start.11 = (bf16[96,1536]{1,0:T(8,128)(2,1)S(1)}, bf16[96,1536]{1,0:T(8,128)(2,1)S(1)}, u32[]{:S(2)}, u32[]{:S(2)}) collective-permute-start(bf16[96,1536]{1,0:T(8,128)(2,1)S(1)} %collective-permute-done.5.refs_6_), channel_id=1, source_target_pairs={{8,0},{16,8},{24,16},{28,24},{20,28},{12,20},{4,12},{0,4},{9,1},{1... | collective-permute-start | bytes 884744 | tf_op jit(solution)/shard_map/ppermute | solution.py:91
  49.9 8.5 %collective-permute-start.13 = (bf16[96,1536]{1,0:T(8,128)(2,1)S(1)}, bf16[96,1536]{1,0:T(8,128)(2,1)S(1)}, u32[]{:S(2)}, u32[]{:S(2)}) collective-permute-start(bf16[96,1536]{1,0:T(8,128)(2,1)S(1)} %collective-permute-done.10.refs_7_), channel_id=1, source_target_pairs={{0,8},{8,16},{16,24},{24,28},{28,20},{20,12},{12,4},{4,0},{1,9},{9... | collective-permute-start | bytes 884744 | tf_op jit(solution)/shard_map/ppermute | solution.py:88
  51.6 8.0 %collective-permute-start.14 = (bf16[96,1536]{1,0:T(8,128)(2,1)S(1)}, bf16[96,1536]{1,0:T(8,128)(2,1)S(1)}, u32[]{:S(2)}, u32[]{:S(2)}) collective-permute-start(bf16[96,1536]{1,0:T(8,128)(2,1)S(1)} %collective-permute-done.11.refs_8_), channel_id=1, source_target_pairs={{8,0},{16,8},{24,16},{28,24},{20,28},{12,20},{4,12},{0,4},{9,1},{1... | collective-permute-start | bytes 884744 | tf_op jit(solution)/shard_map/ppermute | solution.py:91
  51.9 5.9 %collective-permute-start.12 = (bf16[128,768]{1,0:T(8,128)(2,1)S(1)}, bf16[128,768]{1,0:T(8,128)(2,1)S(1)}, u32[]{:S(2)}, u32[]{:S(2)}) collective-permute-start(bf16[128,768]{1,0:T(8,128)(2,1)S(1)} %add_convert_fusion.5), channel_id=1, source_target_pairs={{0,2},{1,3},{2,0},{3,1},{4,6},{5,7},{6,4},{7,5},{8,10},{9,11},{10,... | collective-permute-start | bytes 589832 | tf_op jit(solution)/shard_map/ppermute | solution.py:132
  59.6 7.7 %collective-permute-start.16 = (bf16[96,1536]{1,0:T(8,128)(2,1)S(1)}, bf16[96,1536]{1,0:T(8,128)(2,1)S(1)}, u32[]{:S(2)}, u32[]{:S(2)}) collective-permute-start(bf16[96,1536]{1,0:T(8,128)(2,1)S(1)} %collective-permute-done.13.refs_9_), channel_id=1, source_target_pairs={{0,8},{8,16},{16,24},{24,28},{28,20},{20,12},{12,4},{4,0},{1,9},{9... | collective-permute-start | bytes 884744 | tf_op jit(solution)/shard_map/ppermute | solution.py:88
  72.6 7.8 %collective-permute-start.19 = (bf16[256,768]{1,0:T(8,128)(2,1)S(1)}, bf16[256,768]{1,0:T(8,128)(2,1)S(1)}, u32[]{:S(2)}, u32[]{:S(2)}) collective-permute-start(bf16[256,768]{1,0:T(8,128)(2,1)S(1)} %get-tuple-element.158), channel_id=1, source_target_pairs={{0,1},{1,0},{2,3},{3,2},{4,5},{5,4},{6,7},{7,6},{8,9},{9,8},{10,11... | collective-permute-start | bytes 1179656 | tf_op jit(solution)/shard_map/ppermute | solution.py:132
  72.9 6.2 %collective-permute-start.20 = (bf16[96,768]{1,0:T(8,128)(2,1)S(1)}, bf16[96,768]{1,0:T(8,128)(2,1)S(1)}, u32[]{:S(2)}, u32[]{:S(2)}) collective-permute-start(bf16[96,768]{1,0:T(8,128)(2,1)S(1)} %pad_maximum_fusion.3.refs_0_), channel_id=1, source_target_pairs={{0,8},{8,16},{16,24},{24,28},{28,20},{20,12},{12,4},{4,0},{1,9},{9... | collective-permute-start | bytes 442376 | tf_op jit(solution)/shard_map/ppermute | solution.py:88
  74.5 5.8 %collective-permute-start.21 = (bf16[96,768]{1,0:T(8,128)(2,1)S(1)}, bf16[96,768]{1,0:T(8,128)(2,1)S(1)}, u32[]{:S(2)}, u32[]{:S(2)}) collective-permute-start(bf16[96,768]{1,0:T(8,128)(2,1)S(1)} %pad_maximum_fusion.3.refs_0_), channel_id=1, source_target_pairs={{8,0},{16,8},{24,16},{28,24},{20,28},{12,20},{4,12},{0,4},{9,1},{1... | collective-permute-start | bytes 442376 | tf_op jit(solution)/shard_map/ppermute | solution.py:91
  80.4 8.2 %collective-permute-start.22 = (bf16[128,768]{1,0:T(8,128)(2,1)S(1)}, bf16[128,768]{1,0:T(8,128)(2,1)S(1)}, u32[]{:S(2)}, u32[]{:S(2)}) collective-permute-start(bf16[128,768]{1,0:T(8,128)(2,1)S(1)} %add_convert_fusion.4), channel_id=1, source_target_pairs={{0,2},{1,3},{2,0},{3,1},{4,6},{5,7},{6,4},{7,5},{8,10},{9,11},{10,... | collective-permute-start | bytes 589832 | tf_op jit(solution)/shard_map/ppermute | solution.py:132
  89.7 6.7 %collective-permute-start.28 = (bf16[136,768]{1,0:T(8,128)(2,1)S(1)}, bf16[136,768]{1,0:T(8,128)(2,1)S(1)}, u32[]{:S(2)}, u32[]{:S(2)}) collective-permute-start(bf16[136,768]{1,0:T(8,128)(2,1)S(1)} %get-tuple-element.168.refs_0_), channel_id=1, source_target_pairs={{0,2},{1,3},{2,0},{3,1},{4,6},{5,7},{6,4},{7,5},{8,10},{9,11},{10,... | collective-permute-start | bytes 626696 | tf_op jit(solution)/shard_map/ppermute | solution.py:132
  100.3 10.1 %collective-permute-start.33 = (bf16[256,768]{1,0:T(8,128)(2,1)S(1)}, bf16[256,768]{1,0:T(8,128)(2,1)S(1)}, u32[]{:S(2)}, u32[]{:S(2)}) collective-permute-start(bf16[256,768]{1,0:T(8,128)(2,1)S(1)} %get-tuple-element.175), channel_id=1, source_target_pairs={{0,1},{1,0},{2,3},{3,2},{4,5},{5,4},{6,7},{7,6},{8,9},{9,8},{10,11... | collective-permute-start | bytes 1179656 | tf_op jit(solution)/shard_map/ppermute | solution.py:132
  100.5 9.3 %collective-permute-start.34 = (bf16[96,1536]{1,0:T(8,128)(2,1)S(1)}, bf16[96,1536]{1,0:T(8,128)(2,1)S(1)}, u32[]{:S(2)}, u32[]{:S(2)}) collective-permute-start(bf16[96,1536]{1,0:T(8,128)(2,1)S(1)} %pad_maximum_fusion.1.refs_8_), channel_id=1, source_target_pairs={{0,8},{8,16},{16,24},{24,28},{28,20},{20,12},{12,4},{4,0},{1,9},{9... | collective-permute-start | bytes 884744 | tf_op jit(solution)/shard_map/ppermute | solution.py:88
  101.3 9.0 %collective-permute-start.35 = (bf16[96,1536]{1,0:T(8,128)(2,1)S(1)}, bf16[96,1536]{1,0:T(8,128)(2,1)S(1)}, u32[]{:S(2)}, u32[]{:S(2)}) collective-permute-start(bf16[96,1536]{1,0:T(8,128)(2,1)S(1)} %pad_maximum_fusion.1.refs_8_), channel_id=1, source_target_pairs={{8,0},{16,8},{24,16},{28,24},{20,28},{12,20},{4,12},{0,4},{9,1},{1... | collective-permute-start | bytes 884744 | tf_op jit(solution)/shard_map/ppermute | solution.py:91
  110.3 9.7 %collective-permute-start.37 = (bf16[96,1536]{1,0:T(8,128)(2,1)S(1)}, bf16[96,1536]{1,0:T(8,128)(2,1)S(1)}, u32[]{:S(2)}, u32[]{:S(2)}) collective-permute-start(bf16[96,1536]{1,0:T(8,128)(2,1)S(1)} %collective-permute-done.34.refs_9_), channel_id=1, source_target_pairs={{0,8},{8,16},{16,24},{24,28},{28,20},{20,12},{12,4},{4,0},{1,9},{9... | collective-permute-start | bytes 884744 | tf_op jit(solution)/shard_map/ppermute | solution.py:88
  110.9 9.2 %collective-permute-start.38 = (bf16[96,1536]{1,0:T(8,128)(2,1)S(1)}, bf16[96,1536]{1,0:T(8,128)(2,1)S(1)}, u32[]{:S(2)}, u32[]{:S(2)}) collective-permute-start(bf16[96,1536]{1,0:T(8,128)(2,1)S(1)} %collective-permute-done.35.refs_10_), channel_id=1, source_target_pairs={{8,0},{16,8},{24,16},{28,24},{20,28},{12,20},{4,12},{0,4},{9,1},{1... | collective-permute-start | bytes 884744 | tf_op jit(solution)/shard_map/ppermute | solution.py:91
  114.0 7.6 %collective-permute-start.45 = (bf16[96,768]{1,0:T(8,128)(2,1)S(1)}, bf16[96,768]{1,0:T(8,128)(2,1)S(1)}, u32[]{:S(2)}, u32[]{:S(2)}) collective-permute-start(bf16[96,768]{1,0:T(8,128)(2,1)S(1)} %collective-permute-done.29.refs_5_), channel_id=1, source_target_pairs={{0,8},{8,16},{16,24},{24,28},{28,20},{20,12},{12,4},{4,0},{1,9},{9... | collective-permute-start | bytes 442376 | tf_op jit(solution)/shard_map/ppermute | solution.py:88
  127.5 25.5 %collective-permute-start.44 = (bf16[4,104,768]{2,1,0:T(8,128)(2,1)S(1)}, bf16[4,104,768]{2,1,0:T(8,128)(2,1)S(1)}, u32[]{:S(2)}, u32[]{:S(2)}) collective-permute-start(bf16[4,104,768]{2,1,0:T(8,128)(2,1)S(1)} %get-tuple-element.197), channel_id=1, source_target_pairs={{0,4},{4,0},{8,12},{12,8},{16,20},{20,16},{24,28},{28,24},{1,5},{5... | collective-permute-start | bytes 1916936 | tf_op jit(solution)/shard_map/ppermute | solution.py:706
  128.8 8.0 %collective-permute-start.39 = (bf16[136,768]{1,0:T(8,128)(2,1)S(1)}, bf16[136,768]{1,0:T(8,128)(2,1)S(1)}, u32[]{:S(2)}, u32[]{:S(2)}) collective-permute-start(bf16[136,768]{1,0:T(8,128)(2,1)S(1)} %get-tuple-element.193.refs_0_), channel_id=1, source_target_pairs={{0,2},{1,3},{2,0},{3,1},{4,6},{5,7},{6,4},{7,5},{8,10},{9,11},{10,... | collective-permute-start | bytes 626696 | tf_op jit(solution)/shard_map/ppermute | solution.py:132
  130.3 20.3 %collective-permute-start.40 = (bf16[96,1536]{1,0:T(8,128)(2,1)S(1)}, bf16[96,1536]{1,0:T(8,128)(2,1)S(1)}, u32[]{:S(2)}, u32[]{:S(2)}) collective-permute-start(bf16[96,1536]{1,0:T(8,128)(2,1)S(1)} %collective-permute-done.37.refs_11_), channel_id=1, source_target_pairs={{0,8},{8,16},{16,24},{24,28},{28,20},{20,12},{12,4},{4,0},{1,9},{9... | collective-permute-start | bytes 884744 | tf_op jit(solution)/shard_map/ppermute | solution.py:88
  131.4 19.2 %collective-permute-start.41 = (bf16[96,1536]{1,0:T(8,128)(2,1)S(1)}, bf16[96,1536]{1,0:T(8,128)(2,1)S(1)}, u32[]{:S(2)}, u32[]{:S(2)}) collective-permute-start(bf16[96,1536]{1,0:T(8,128)(2,1)S(1)} %collective-permute-done.38.refs_12_), channel_id=1, source_target_pairs={{8,0},{16,8},{24,16},{28,24},{20,28},{12,20},{4,12},{0,4},{9,1},{1... | collective-permute-start | bytes 884744 | tf_op jit(solution)/shard_map/ppermute | solution.py:91
  132.4 18.7 %collective-permute-start.47 = (bf16[128,768]{1,0:T(8,128)(2,1)S(1)}, bf16[128,768]{1,0:T(8,128)(2,1)S(1)}, u32[]{:S(2)}, u32[]{:S(2)}) collective-permute-start(bf16[128,768]{1,0:T(8,128)(2,1)S(1)} %add_convert_fusion.2), channel_id=1, source_target_pairs={{0,2},{1,3},{2,0},{3,1},{4,6},{5,7},{6,4},{7,5},{8,10},{9,11},{10,... | collective-permute-start | bytes 589832 | tf_op jit(solution)/shard_map/ppermute | solution.py:132
  151.4 6.9 %collective-permute-start.48 = (bf16[128,768]{1,0:T(8,128)(2,1)S(1)}, bf16[128,768]{1,0:T(8,128)(2,1)S(1)}, u32[]{:S(2)}, u32[]{:S(2)}) collective-permute-start(bf16[128,768]{1,0:T(8,128)(2,1)S(1)} %get-tuple-element.212.refs_0_), channel_id=1, source_target_pairs={{0,2},{1,3},{2,0},{3,1},{4,6},{5,7},{6,4},{7,5},{8,10},{9,11},{10,... | collective-permute-start | bytes 589832 | tf_op jit(solution)/shard_map/ppermute | solution.py:132
  153.0 8.6 %collective-permute-start.51 = (bf16[96,1536]{1,0:T(8,128)(2,1)S(1)}, bf16[96,1536]{1,0:T(8,128)(2,1)S(1)}, u32[]{:S(2)}, u32[]{:S(2)}) collective-permute-start(bf16[96,1536]{1,0:T(8,128)(2,1)S(1)} %collective-permute-done.40.refs_13_), channel_id=1, source_target_pairs={{0,8},{8,16},{16,24},{24,28},{28,20},{20,12},{12,4},{4,0},{1,9},{9... | collective-permute-start | bytes 884744 | tf_op jit(solution)/shard_map/ppermute | solution.py:88
  157.5 12.1 %collective-permute-start.57 = (bf16[256,768]{1,0:T(8,128)(2,1)S(1)}, bf16[256,768]{1,0:T(8,128)(2,1)S(1)}, u32[]{:S(2)}, u32[]{:S(2)}) collective-permute-start(bf16[256,768]{1,0:T(8,128)(2,1)S(1)} %get-tuple-element.221), channel_id=1, source_target_pairs={{0,1},{1,0},{2,3},{3,2},{4,5},{5,4},{6,7},{7,6},{8,9},{9,8},{10,11... | collective-permute-start | bytes 1179656 | tf_op jit(solution)/shard_map/ppermute | solution.py:132
  166.5 16.2 %collective-permute-start.66 = (bf16[4,96,768]{2,1,0:T(8,128)(2,1)S(1)}, bf16[4,96,768]{2,1,0:T(8,128)(2,1)S(1)}, u32[]{:S(2)}, u32[]{:S(2)}) collective-permute-start(bf16[4,96,768]{2,1,0:T(8,128)(2,1)S(1)} %get-tuple-element.239), channel_id=1, source_target_pairs={{0,4},{4,0},{8,12},{12,8},{16,20},{20,16},{24,28},{28,24},{1,5},{5... | collective-permute-start | bytes 1769480 | tf_op jit(solution)/shard_map/ppermute | solution.py:706
  167.8 15.5 %collective-permute-start.25 = (bf16[128,768]{1,0:T(8,128)(2,1)S(1)}, bf16[128,768]{1,0:T(8,128)(2,1)S(1)}, u32[]{:S(2)}, u32[]{:S(2)}) collective-permute-start(bf16[128,768]{1,0:T(8,128)(2,1)S(1)} %get-tuple-element.167.refs_0_), channel_id=1, source_target_pairs={{0,2},{1,3},{2,0},{3,1},{4,6},{5,7},{6,4},{7,5},{8,10},{9,11},{10,... | collective-permute-start | bytes 589832 | tf_op jit(solution)/shard_map/ppermute | solution.py:132
  168.8 33.6 %collective-permute-start.62 = (bf16[4,104,768]{2,1,0:T(8,128)(2,1)S(1)}, bf16[4,104,768]{2,1,0:T(8,128)(2,1)S(1)}, u32[]{:S(2)}, u32[]{:S(2)}) collective-permute-start(bf16[4,104,768]{2,1,0:T(8,128)(2,1)S(1)} %get-tuple-element.225), channel_id=1, source_target_pairs={{0,4},{4,0},{8,12},{12,8},{16,20},{20,16},{24,28},{28,24},{1,5},{5... | collective-permute-start | bytes 1916936 | tf_op jit(solution)/shard_map/ppermute | solution.py:706
  169.6 15.3 %collective-permute-start.58 = (bf16[128,768]{1,0:T(8,128)(2,1)S(1)}, bf16[128,768]{1,0:T(8,128)(2,1)S(1)}, u32[]{:S(2)}, u32[]{:S(2)}) collective-permute-start(bf16[128,768]{1,0:T(8,128)(2,1)S(1)} %add_convert_fusion), channel_id=1, source_target_pairs={{0,2},{1,3},{2,0},{3,1},{4,6},{5,7},{6,4},{7,5},{8,10},{9,11},{10,... | collective-permute-start | bytes 589832 | tf_op jit(solution)/shard_map/ppermute | solution.py:132
  170.8 28.0 %collective-permute-start.53 = (bf16[128,768]{1,0:T(8,128)(2,1)S(1)}, bf16[128,768]{1,0:T(8,128)(2,1)S(1)}, u32[]{:S(2)}, u32[]{:S(2)}) collective-permute-start(bf16[128,768]{1,0:T(8,128)(2,1)S(1)} %add_convert_fusion.1), channel_id=1, source_target_pairs={{0,2},{1,3},{2,0},{3,1},{4,6},{5,7},{6,4},{7,5},{8,10},{9,11},{10,... | collective-permute-start | bytes 589832 | tf_op jit(solution)/shard_map/ppermute | solution.py:132
  182.9 6.9 %collective-permute-start.67 = (bf16[96,768]{1,0:T(8,128)(2,1)S(1)}, bf16[96,768]{1,0:T(8,128)(2,1)S(1)}, u32[]{:S(2)}, u32[]{:S(2)}) collective-permute-start(bf16[96,768]{1,0:T(8,128)(2,1)S(1)} %get-tuple-element.241), channel_id=1, source_target_pairs={{0,8},{4,12},{8,0},{12,4},{16,24},{20,28},{24,16},{28,20},{1,9},{5... | collective-permute-start | bytes 442376 | tf_op jit(solution)/shard_map/ppermute | solution.py:785
  183.4 13.5 %collective-permute-start.68 = (bf16[96,768]{1,0:T(8,128)(2,1)S(1)}, bf16[96,768]{1,0:T(8,128)(2,1)S(1)}, u32[]{:S(2)}, u32[]{:S(2)}) collective-permute-start(bf16[96,768]{1,0:T(8,128)(2,1)S(1)} %get-tuple-element.242), channel_id=1, source_target_pairs={{0,16},{4,20},{8,24},{12,28},{16,0},{20,4},{24,8},{28,12},{1,17},{... | collective-permute-start | bytes 442376 | tf_op jit(solution)/shard_map/ppermute | solution.py:785
  184.9 11.9 %collective-permute-start.69 = (bf16[96,768]{1,0:T(8,128)(2,1)S(1)}, bf16[96,768]{1,0:T(8,128)(2,1)S(1)}, u32[]{:S(2)}, u32[]{:S(2)}) collective-permute-start(bf16[96,768]{1,0:T(8,128)(2,1)S(1)} %get-tuple-element.243), channel_id=1, source_target_pairs={{0,24},{4,28},{8,16},{12,20},{16,8},{20,12},{24,0},{28,4},{1,25},{... | collective-permute-start | bytes 442376 | tf_op jit(solution)/shard_map/ppermute | solution.py:785
  189.7 23.9 %collective-permute-start.59 = (bf16[128,768]{1,0:T(8,128)(2,1)S(1)}, bf16[128,768]{1,0:T(8,128)(2,1)S(1)}, u32[]{:S(2)}, u32[]{:S(2)}) collective-permute-start(bf16[128,768]{1,0:T(8,128)(2,1)S(1)} %last_sum.1.refs_0_), channel_id=1, source_target_pairs={{0,2},{1,3},{2,0},{3,1},{4,6},{5,7},{6,4},{7,5},{8,10},{9,11},{10,... | collective-permute-start | bytes 589832 | tf_op jit(solution)/shard_map/ppermute | solution.py:132
  196.9 13.6 %collective-permute-start.71 = (bf16[104,768]{1,0:T(8,128)(2,1)S(1)}, bf16[104,768]{1,0:T(8,128)(2,1)S(1)}, u32[]{:S(2)}, u32[]{:S(2)}) collective-permute-start(bf16[104,768]{1,0:T(8,128)(2,1)S(1)} %get-tuple-element.246), channel_id=1, source_target_pairs={{0,16},{4,20},{8,24},{12,28},{16,0},{20,4},{24,8},{28,12},{1,17},{... | collective-permute-start | bytes 479240 | tf_op jit(solution)/shard_map/ppermute | solution.py:785
  198.8 11.6 %collective-permute-start.72 = (bf16[104,768]{1,0:T(8,128)(2,1)S(1)}, bf16[104,768]{1,0:T(8,128)(2,1)S(1)}, u32[]{:S(2)}, u32[]{:S(2)}) collective-permute-start(bf16[104,768]{1,0:T(8,128)(2,1)S(1)} %get-tuple-element.247), channel_id=1, source_target_pairs={{0,24},{4,28},{8,16},{12,20},{16,8},{20,12},{24,0},{28,4},{1,25},{... | collective-permute-start | bytes 479240 | tf_op jit(solution)/shard_map/ppermute | solution.py:785
  202.3 23.4 %collective-permute-start.60 = (bf16[128,768]{1,0:T(8,128)(2,1)S(1)}, bf16[128,768]{1,0:T(8,128)(2,1)S(1)}, u32[]{:S(2)}, u32[]{:S(2)}) collective-permute-start(bf16[128,768]{1,0:T(8,128)(2,1)S(1)} %last_sum.1.refs_0_), channel_id=1, source_target_pairs={{0,1},{1,0},{2,3},{3,2},{4,5},{5,4},{6,7},{7,6},{8,9},{9,8},{10,11... | collective-permute-start | bytes 589832 | tf_op jit(solution)/shard_map/ppermute | solution.py:132
  202.4 23.4 %collective-permute-start.54 = (bf16[128,768]{1,0:T(8,128)(2,1)S(1)}, bf16[128,768]{1,0:T(8,128)(2,1)S(1)}, u32[]{:S(2)}, u32[]{:S(2)}) collective-permute-start(bf16[128,768]{1,0:T(8,128)(2,1)S(1)} %second_norm_tangent.1.refs_4_), channel_id=1, source_target_pairs={{0,2},{1,3},{2,0},{3,1},{4,6},{5,7},{6,4},{7,5},{8,10},{9,11},{10,... | collective-permute-start | bytes 589832 | tf_op jit(solution)/shard_map/ppermute | solution.py:132
  210.5 7.1 %collective-permute-start.63 = (bf16[104,768]{1,0:T(8,128)(2,1)S(1)}, bf16[104,768]{1,0:T(8,128)(2,1)S(1)}, u32[]{:S(2)}, u32[]{:S(2)}) collective-permute-start(bf16[104,768]{1,0:T(8,128)(2,1)S(1)} %get-tuple-element.227), channel_id=1, source_target_pairs={{0,8},{4,12},{8,0},{12,4},{16,24},{20,28},{24,16},{28,20},{1,9},{5... | collective-permute-start | bytes 479240 | tf_op jit(solution)/shard_map/ppermute | solution.py:785
  210.5 13.9 %collective-permute-start.64 = (bf16[104,768]{1,0:T(8,128)(2,1)S(1)}, bf16[104,768]{1,0:T(8,128)(2,1)S(1)}, u32[]{:S(2)}, u32[]{:S(2)}) collective-permute-start(bf16[104,768]{1,0:T(8,128)(2,1)S(1)} %get-tuple-element.228), channel_id=1, source_target_pairs={{0,16},{4,20},{8,24},{12,28},{16,0},{20,4},{24,8},{28,12},{1,17},{... | collective-permute-start | bytes 479240 | tf_op jit(solution)/shard_map/ppermute | solution.py:785
  213.6 10.8 %collective-permute-start.65 = (bf16[104,768]{1,0:T(8,128)(2,1)S(1)}, bf16[104,768]{1,0:T(8,128)(2,1)S(1)}, u32[]{:S(2)}, u32[]{:S(2)}) collective-permute-start(bf16[104,768]{1,0:T(8,128)(2,1)S(1)} %get-tuple-element.229), channel_id=1, source_target_pairs={{0,24},{4,28},{8,16},{12,20},{16,8},{20,12},{24,0},{28,4},{1,25},{... | collective-permute-start | bytes 479240 | tf_op jit(solution)/shard_map/ppermute | solution.py:785
  217.6 10.7 %collective-permute-start.26 = (bf16[128,768]{1,0:T(8,128)(2,1)S(1)}, bf16[128,768]{1,0:T(8,128)(2,1)S(1)}, u32[]{:S(2)}, u32[]{:S(2)}) collective-permute-start(bf16[128,768]{1,0:T(8,128)(2,1)S(1)} %get-tuple-element.167.refs_0_), channel_id=1, source_target_pairs={{0,1},{1,0},{2,3},{3,2},{4,5},{5,4},{6,7},{7,6},{8,9},{9,8},{10,11... | collective-permute-start | bytes 589832 | tf_op jit(solution)/shard_map/ppermute | solution.py:132
  (32 other events, 202.9 us)

commit v3 on v2

--- a/solution.py
+++ b/solution.py
@@ -13,7 +13,8 @@
 EPSILON = 1e-06
 SCALE = HEAD ** (-0.5)
 BLOCKS = (0, 2, 1, 3)
-OWNERS = (0, 2, 4, 6, 1, 3, 5, 7)
+FF_GROUPS = ((2,), (3,), (1,), (0,))
+LAST_GROUPS = ((2, 3), (1, 0))
 SNAKE = (0, 2, 4, 6, 7, 5, 3, 1)
 EXTRA = 8
 BF = jnp.bfloat16
@@ -39,7 +40,7 @@
     specs = [pl.BlockSpec(memory_space=pltpu.SMEM if s else pltpu.VMEM) for s in smem]
     specs = specs + [pl.BlockSpec(memory_space=pl.ANY)] * len(shards)
     out_space = pltpu.HBM if any_outs else pltpu.VMEM
-    return pl.pallas_call(
+    return list(pl.pallas_call(
         body,
         out_shape=[jax.ShapeDtypeStruct(shape, kind) for shape, kind in outs],
         in_specs=specs,
@@ -48,7 +49,7 @@
         name=name,
         compiler_params=pltpu.CompilerParams(vmem_limit_bytes=VMEM_LIMIT),
         cost_estimate=pl.CostEstimate(flops=1, bytes_accessed=1, transcendentals=0),
-    )(*near, *shards)
+    )(*near, *shards))
 
 
 def tiles(width, body):
@@ -108,6 +109,17 @@
     return jnp.where(place < size // 2, 2 * place, 2 * (size - 1 - place) + 1)
 
 
+def join_lists(*values):
+    counts = [len(value) if isinstance(value, list) else 1 for value in values]
+    flat = [v for value in values for v in (value if isinstance(value, list) else [value])]
+    joined = list(lax.optimization_barrier(tuple(flat)))
+    results = []
+    for value, count in zip(values, counts):
+        taken, joined = joined[:count], joined[count:]
+        results.append(taken if isinstance(value, list) else taken[0])
+    return results
+
+
 def shard_copies(where, refs, whole, sems):
     rows = whole.shape[0] // len(refs)
     made = []
@@ -132,30 +144,21 @@
     return lax.ppermute(block, "tp", xor_pairs(tp, bit))
 
 
-def sum_exchange(keep, send, tp, rings=(), meanwhile=()):
+def onward_sum(keep, first):
     quarter = keep.shape[0] // 2
+    return (keep[quarter:].astype(F32) + first[quarter:].astype(F32)).astype(BF)
+
+
+def sum_exchange(keep, send, tp):
     first = swap(send, tp, 1)
-    if rings or meanwhile:
-        first = join(rings, first, *meanwhile)
-        first = first[0] if meanwhile else first
-    for ring in rings:
-        ring.step()
-    onward = (keep[quarter:].astype(F32) + first[quarter:].astype(F32)).astype(BF)
-    second = swap(onward, tp, 2)
-    if rings:
-        second = join(rings, second)
-    for ring in rings:
-        ring.step()
-    return keep, first, second
+    return keep, first, swap(onward_sum(keep, first), tp, 2)
 
 
 def spread_rows(own, tp, rings=()):
     across, beside = swap(own, tp, 2), swap(own, tp, 1)
     if rings:
         across = join(rings, across)
-    for ring in rings:
-        ring.step()
-    return own, across, beside, swap(across, tp, 1)
+    return [own, across, beside, swap(across, tp, 1)]
 
 
 def summed(keep, first, second):
@@ -254,18 +257,14 @@
 
 
 def attention_tangent(
-    count, cols, where, rel, mixed, probs, context, whole, *refs
+    cols, at, where, rel, mixed, probs, context, whole, along, keep, send, tmixed, tcontext
 ):
-    tshards, refs = refs[:count], refs[count:]
-    keep, send, twhole, sems, tmixed, tcontext = refs
-    copies = shard_copies(where, tshards, twhole, sems)
-    start_all(copies)
-    wait_all(copies)
     me = where[0]
     quarter = rel.shape[0] // 4
     for third in range(3):
         part = slice(third * cols, (third + 1) * cols)
-        tmixed[:, part] = dot(rel[...], twhole[:, part], NN).astype(BF)
+        there = slice(at + third * cols, at + (third + 1) * cols)
+        tmixed[:, part] = dot(rel[...], along[:, there], NN).astype(BF)
     slots = positions(me, quarter)
     heads = cols // HEAD
     for pair in range(2):
@@ -286,7 +285,7 @@
 
     def project(cut):
         part = dot(tcontext[...], whole[cut, 3 * cols : 4 * cols], NT)
-        part = part + dot(context[...], twhole[cut, 3 * cols : 4 * cols], NT)
+        part = part + dot(context[...], along[cut, at + 3 * cols : at + 4 * cols], NT)
         halves(part, keep, send, cut)
 
     tiles(keep.shape[1], project)
@@ -311,6 +310,14 @@
     low[...] = along.astype(BF)
 
 
+def pack_weights(*refs):
+    at, out = 0, refs[-1]
+    for ref in refs[:-2]:
+        out[:, at : at + ref.shape[1]] = ref[...]
+        at = at + ref.shape[1]
+    out[:, at:] = refs[-2][...].astype(F32).T.astype(BF)
+
+
 def collect(pieces, rel):
     quarter = rel.shape[0] // 4
     for i, piece in enumerate(pieces):
@@ -336,7 +343,7 @@
     tiles(hidden, up)
 
     def down(cut):
-        halves(dot(active[...], whole[cut, hidden:], NT), keep, send, cut)
+        halves(dot(active[...], whole[cut, hidden : 2 * hidden], NT), keep, send, cut)
 
     tiles(keep.shape[1], down)
 
@@ -357,7 +364,7 @@
     tiles(hidden, up)
 
     def down(cut):
-        part = dot(tactive[...], whole[cut, hidden:], NT)
+        part = dot(tactive[...], whole[cut, hidden : 2 * hidden], NT)
         part = part + dot(active[...], twhole[cut, hidden:], NT)
         halves(part, keep, send, cut)
 
@@ -424,33 +431,38 @@
     tiles(keep.shape[1], up)
 
 
-def put_owned(where, step, targets, sums=None):
+def put_owned(groups, where, step, targets, sums):
     if len(targets) == 1:
         targets[0][...] = step[...]
         return
-    rows = step.shape[0] // len(OWNERS)
-    extra = None if sums is None else split_sums([sums])
-    for i, owner in enumerate(OWNERS):
+    rows = step.shape[0] // 8
+    spare = step.shape[1] - sums.shape[1]
+    if spare:
+        sums = jnp.concatenate([sums, jnp.zeros((EXTRA // 2, spare), F32)], axis=1)
+    extra = split_sums([sums])
+
+    def put(target, at, owner):
         start = pl.multiple_of((where[1] ^ owner) * rows, rows)
-        target = targets[i // 4]
-        target[i % 4, 0:rows, :] = step[pl.ds(start, rows), :]
-        if extra is not None:
-            target[i % 4, rows:, :] = extra
-
-
-def weight_gradient(summing, where, *refs):
-    if summing:
-        left, sums, right = refs[:3]
-        refs = refs[3:]
-    else:
-        (right, left), refs, sums = refs[:2], refs[2:], None
+        target[at, 0:rows, :] = step[pl.ds(start, rows), :]
+        target[at, rows:, :] = extra
+
+    for z in range(4):
+        put(targets[0], z, 2 * z)
+    for target, group in zip(targets[1:], groups):
+        for at, z in enumerate(group):
+            put(target, at, 2 * z + 1)
+
+
+def feed_forward_weights(where, rel, active, first, grad_upper, sums, *refs):
     targets, step = refs[:-1], refs[-1]
+    hidden = active.shape[1]
 
     def one(cut):
-        step[cut, :] = dot(left[:, cut], right[...], TN).astype(BF)
-
-    tiles(left.shape[1], one)
-    put_owned(where, step, targets, None if sums is None else sums[...])
+        step[cut, :hidden] = dot(rel[:, cut], active[...], TN).astype(BF)
+        step[cut, hidden:] = dot(first[:, cut], grad_upper[...], TN).astype(BF)
+
+    tiles(rel.shape[1], one)
+    put_owned(FF_GROUPS, where, step, targets, sums[...])
 
 
 def attention_backward(cols, *refs):
@@ -484,7 +496,8 @@
 
 
 def attention_weights(paired, cols, where, rel, grad, sums, x_rel, context, *refs):
-    targets, refs = (refs[:2], refs[2:]) if paired else (refs[:1], refs[1:])
+    count = 1 + len(LAST_GROUPS) if paired else 1
+    targets, refs = refs[:count], refs[count:]
     (step,) = refs[-1:]
 
     def one(cut):
@@ -495,25 +508,25 @@
     mixed = sum_rows(grad[...].astype(F32))
     mixed = jnp.concatenate([mixed, jnp.zeros((1, cols), F32)], axis=1)
     lines = jnp.concatenate([sums[0:3, :], mixed])
-    put_owned(where, step, targets, lines)
+    put_owned(LAST_GROUPS, where, step, targets, lines)
     if not paired:
         refs[0][...] = lines
 
 
-def fold_shards(keep, came, *outs):
-    rows = outs[0].shape[0]
-    for i in range(4):
-        total = keep[i, 0:rows, :].astype(F32) + came[i, 0:rows, :].astype(F32)
-        if i == 0:
-            outs[0][...] = total
+def fold_shards(group, keep, came, *outs):
+    outs = list(outs)
+    for at, z in enumerate(group):
+        out = outs.pop(0)
+        rows = keep.shape[1] - EXTRA
+        total = keep[z, 0:rows, :].astype(F32) + came[at, 0:rows, :].astype(F32)
+        sums = joined_sums(keep[z, rows:, :]) + joined_sums(came[at, rows:, :])
+        rounded = split_sums([sums])
+        if z == 0:
+            out[...] = total
+            outs.pop(0)[...] = joined_sums(rounded)
         else:
-            outs[i][0:rows, :] = total.astype(BF)
-    if len(outs) > 4:
-        sums = joined_sums(keep[0, rows:, :]) + joined_sums(came[0, rows:, :])
-        rounded = split_sums([sums])
-        outs[4][...] = joined_sums(rounded)
-        for i in range(1, 4):
-            outs[i][rows:, :] = rounded
+            out[0:rows, :] = total.astype(BF)
+            out[rows:, :] = rounded
 
 
 def last_total(refs):
@@ -528,16 +541,14 @@
     rows = refs[0].shape[0]
     sums = tree_sum([refs[4][...]] + [joined_sums(ref[rows:, :]) for ref in refs[1:4]])
     for i, out in enumerate(outs):
-        out[...] = sums[i]
-
-
-def finish_up(*refs):
-    refs[4][...] = last_total(refs)
-
-
-def finish_down(*refs):
-    refs[5][...] = last_total(refs)
-    last_sums(refs, refs[6:])
+        out[...] = sums[i, : out.shape[0]]
+
+
+def finish_feed_forward(hidden, *refs):
+    total = last_total(refs)
+    refs[5][...] = total[:, :hidden]
+    refs[6][...] = total[:, hidden:]
+    last_sums(refs, refs[7:])
 
 
 def finish_attention(cols, *refs):
@@ -616,7 +627,8 @@
     lines = ((EXTRA // 2, width), F32)
     full_own = ((own, width), F32)
     attn_rows = ((width, 4 * cols), BF)
-    ff_rows = ((width, 2 * hidden), BF)
+    ff_rows = ((width, 2 * hidden + 4 * cols), BF)
+    tff_rows = ((width, 2 * hidden), BF)
 
     def pack(first_one, *blocks):
         return jnp.concatenate([first_one, *blocks], 1)
@@ -624,19 +636,26 @@
     def arriving(count):
         return pltpu.SemaphoreType.DMA((count,))
 
-    where, out_rows, tout_rows, params = join((), where, out_weight.T, out_tangent.T, params)
+    where, out_rows, params = join((), where, out_weight.T, params)
     attn = Ring(pack(query_weight, key_weight, value_weight, out_rows), dp)
     attn.step()
     early = attn.parts[-1]
-    ff = Ring(pack(after(up_weight, early), down_weight.T), dp)
-    tattn = Ring(pack(after(query_tangent, early), key_tangent, value_tangent, tout_rows), dp)
+    tangents = (query_tangent, key_tangent, value_tangent)
+    group = call(
+        pack_weights,
+        "pack_weights",
+        [((shard, 2 * hidden + 4 * cols), BF)],
+        (after(up_weight, early), down_weight.T, *tangents, out_tangent),
+    )
+    ff = Ring(group[0], dp)
     tff = Ring(pack(after(up_tangent, early), down_tangent.T), dp)
     attn.step()
     join([attn, ff])
     attn.step()
     ff.step()
+    join([attn, ff])
     attn.step()
-    where = join([ff], where)
+    where, attn.parts[-1] = join([ff], where, attn.parts[-1])
     ff.step()
     count = len(attn.parts)
     x_rel, mixed, probs, context, keep, send, attn_whole = call(
@@ -654,15 +673,19 @@
         attn.parts,
         [arriving(count)],
     )
+    keep, send = join([ff], keep, send)
+    ff.step()
     first, unit_one, inverse_one, first_low = call(
         first_norm,
         "first_norm",
         [full_own, full_own, ((own, 128), F32), ((own, width), BF)],
-        (x_rel, *sum_exchange(keep, send, tp, [ff]), params),
-    )
+        (x_rel, *sum_exchange(keep, send, tp), params),
+    )
+    first_low = join([ff], first_low)
+    ff.step()
     pieces = spread_rows(first_low, tp, [ff])
-    tattn.front = [after(tattn.front[0], pieces[1])] * 2
-    tattn.step()
+    pieces[3] = join([tff], pieces[3])
+    tff.step()
     first_rel, active, slope, keep, send, ff_whole = call(
         functools.partial(feed_forward, count, hidden),
         "feed_forward",
@@ -671,14 +694,30 @@
         ff.parts,
         [arriving(count)],
     )
+    keep, send = join([tff], keep, send)
+    tff.step()
+    keep, first_came, second = sum_exchange(keep, send, tp)
+    tkeep, tsend = call(
+        functools.partial(attention_tangent, cols, 2 * hidden),
+        "attention_tangent",
+        parts,
+        (after(where, keep), x_rel, mixed, probs, context, attn_whole, ff_whole),
+        (),
+        [pltpu.VMEM((rows, 3 * cols), BF), pltpu.VMEM((rows, cols), BF)],
+    )
+    second, tkeep, tsend = join([tff], second, tkeep, tsend)
+    tff.step()
     result, grad_two, grad_two_low, unit_two, inverse_two = call(
         second_norm,
         "second_norm",
         [((own, width), BF), full_own, piece, full_own, ((own, 128), F32)],
-        (where, *sum_exchange(keep, send, tp, [tattn]), params, first, out_grad),
-    )
-    pieces = spread_rows(grad_two_low, tp, [tattn])
-    tff.front = [after(tff.front[0], pieces[1])] * 2
+        (where, keep, first_came, second, params, first, out_grad),
+    )
+    pieces = spread_rows(grad_two_low, tp)
+    tfirst_came = swap(tsend, tp, 1)
+    pieces[1], tfirst_came = join([], pieces[1], tfirst_came)
+    tsecond = swap(onward_sum(tkeep, tfirst_came), tp, 2)
+    pieces[3] = join([tff], pieces[3])
     tff.step()
     grad_down, grad_upper, sums_up, keep, send = call(
         functools.partial(feed_forward_backward, hidden),
@@ -686,123 +725,157 @@
         [((rows, width), BF), ((rows, hidden), BF), lines, *parts],
         (*pieces, slope, ff_whole),
     )
-
-    def weight_outs(total, sums):
+    result_pieces = spread_rows(result, tp)
+    keep, send, grad_down, grad_upper, result_pieces[1] = join(
+        [], keep, send, grad_down, grad_upper, result_pieces[1]
+    )
+
+    def weight_outs(total, groups):
         if paired:
-            return [((4, shard + (EXTRA if sums else 0), total), BF)] * 2
+            counts = [4] + [len(group) for group in groups]
+            return [((count, shard + EXTRA, total), BF) for count in counts]
         return [((width, total), BF)]
 
-    def step_of(name, near, summing):
-        return call(
-            functools.partial(weight_gradient, summing),
-            name,
-            weight_outs(hidden, summing),
-            (where, *near),
-            (),
-            [pltpu.VMEM((width, hidden), BF)],
-        )
-
-    def swap_shards(steps):
-        return lax.ppermute(steps[1], "dp", xor_pairs(dp, 1)) if paired else steps[0]
-
-    down_steps = step_of("down_weights", (grad_down, sums_up, active), True)
-    up_steps = step_of("up_weights", (grad_upper, first_rel), False)
-    down_came = swap_shards(down_steps)
-    exchanged = sum_exchange(keep, send, tp, [tff], (down_steps[0],))
+    def swap_shards(steps, index):
+        return lax.ppermute(steps[1 + index], "dp", xor_pairs(dp, 1)) if paired else steps[0]
+
+    def fold(steps, came, group):
+        if not paired:
+            return came
+        total = came.shape[2]
+        outs = []
+        for z in group:
+            if z == 0:
+                outs = outs + [((shard, total), F32), ((EXTRA // 2, total), F32)]
+            else:
+                outs.append(((shard + EXTRA, total), BF))
+        return call(functools.partial(fold_shards, group), "fold_shards", outs, (steps[0], came))
+
+    def send_on(folded, group):
+        if not paired:
+            return folded
+        moved = [
+            lax.ppermute(value, "dp", xor_pairs(dp, 2 * z)) for value, z in zip(folded, group) if z
+        ]
+        return moved + folded[len(moved) :]
+
+    first_came = swap(send, tp, 1)
+    second = swap(onward_sum(keep, first_came), tp, 2)
+    ff_steps = call(
+        feed_forward_weights,
+        "feed_forward_weights",
+        weight_outs(2 * hidden, FF_GROUPS),
+        (where, grad_down, active, first_rel, after(grad_upper, first_came), sums_up),
+        (),
+        [pltpu.VMEM((width, 2 * hidden), BF)],
+    )
+    tfirst, tfirst_low = call(
+        first_norm_tangent,
+        "first_norm_tangent",
+        [full_own, ((own, width), BF)],
+        (tkeep, tfirst_came, tsecond, after(params, ff_steps[0]), unit_one, inverse_one),
+    )
+    second, ff_steps, tff.front, tfirst_low, result_pieces = join_lists(
+        second, ff_steps, tff.front, tfirst_low, result_pieces
+    )
+    tff.step()
     grad_one, grad_one_low = call(
         first_norm_backward,
         "first_norm_backward",
         [full_own, piece],
-        (*exchanged, after(params, up_steps[0]), grad_two, unit_one, inverse_one),
-    )
-    up_came = swap_shards(up_steps)
-    pieces = spread_rows(grad_one_low, tp, [tff])
-    tkeep, tsend = call(
-        functools.partial(attention_tangent, count, cols),
-        "attention_tangent",
-        parts,
-        (after(where, grad_one_low), x_rel, mixed, probs, context, attn_whole),
-        tattn.parts,
-        [pltpu.VMEM(*attn_rows), arriving(count)]
-        + [pltpu.VMEM((rows, 3 * cols), BF), pltpu.VMEM((rows, cols), BF)],
-    )
+        (keep, first_came, second, params, grad_two, unit_one, inverse_one),
+    )
+    pieces = spread_rows(grad_one_low, tp)
+    tpieces = spread_rows(tfirst_low, tp)
+    ff_two = swap_shards(ff_steps, 0)
+    pieces[3], ff_two, ff_steps = join_lists(pieces[3], ff_two, ff_steps)
+    ff_three = swap_shards(ff_steps, 1)
+    ff_two = fold(ff_steps, ff_two, FF_GROUPS[0])
+    pieces[3], ff_two = join_lists(pieces[3], ff_two)
+    ff_two = send_on(ff_two, FF_GROUPS[0])
     grad_attn, grad_mixed, sums_one, keep, send = call(
         functools.partial(attention_backward, cols),
         "attention_backward",
         [((rows, width), BF), ((rows, 3 * cols), BF), lines, *parts],
-        (*pieces[:3], after(pieces[3], down_came, tkeep), mixed, probs, attn_whole),
+        (*pieces, mixed, probs, attn_whole),
         (),
         [pltpu.VMEM((rows, cols), BF)],
     )
+    keep, send, ff_three, tpieces[1] = join([], keep, send, ff_three, tpieces[1])
+    ff_one = swap_shards(ff_steps, 2)
+    first_came = swap(send, tp, 1)
     last_steps = call(
         functools.partial(attention_weights, paired, cols),
         "attention_weights",
-        weight_outs(4 * cols, True) + ([] if paired else [lines]),
+        weight_outs(4 * cols, LAST_GROUPS) + ([] if paired else [lines]),
         (where, grad_attn, grad_mixed, sums_one, x_rel, context),
         (),
         [pltpu.VMEM(*attn_rows)],
     )
-    last_came = swap_shards(last_steps)
-    exchanged = sum_exchange(keep, send, tp, (), (last_steps[0],))
-    (grad_input,) = call(
-        last_sum, "last_sum", [((own, width), BF)], (*exchanged, grad_one)
-    )
-
-    tfirst, tfirst_low = call(
-        first_norm_tangent,
-        "first_norm_tangent",
-        [full_own, ((own, width), BF)],
-        (*sum_exchange(tkeep, tsend, tp), params, unit_one, inverse_one),
-    )
+    ff_three = fold(ff_steps, ff_three, FF_GROUPS[1])
+    first_came, last_steps, tpieces[3], ff_three, ff_steps = join_lists(
+        first_came, last_steps, tpieces[3], ff_three, ff_steps
+    )
+    ff_zero = swap_shards(ff_steps, 3)
+    second = swap(onward_sum(keep, first_came), tp, 2)
+    last_near = swap_shards(last_steps, 0)
+    ff_three = send_on(ff_three, FF_GROUPS[1])
     tkeep, tsend = call(
         functools.partial(feed_forward_tangent, count, hidden),
         "feed_forward_tangent",
         parts,
-        (
-            after(where, last_steps[0]),
-            *spread_rows(tfirst_low, tp),
-            first_rel,
-            active,
-            slope,
-            ff_whole,
-        ),
+        (after(where, last_steps[0]), *tpieces, first_rel, active, slope, ff_whole),
         tff.parts,
-        [pltpu.VMEM(*ff_rows), arriving(count)]
+        [pltpu.VMEM(*tff_rows), arriving(count)]
         + [pltpu.VMEM((rows, width), BF), pltpu.VMEM((rows, hidden), BF)],
     )
+    second, tkeep, tsend, last_near, ff_one, ff_two, last_steps = join_lists(
+        second, tkeep, tsend, last_near, ff_one, ff_two, last_steps
+    )
+    last_far = swap_shards(last_steps, 1)
+    tfirst_came = swap(tsend, tp, 1)
+    ff_one = send_on(fold(ff_steps, ff_one, FF_GROUPS[2]), FF_GROUPS[2])
+    (grad_input,) = call(
+        last_sum, "last_sum", [((own, width), BF)], (keep, first_came, second, grad_one)
+    )
+    pieces = spread_rows(grad_input, tp)
+    tsecond = swap(onward_sum(tkeep, tfirst_came), tp, 2)
+    last_near = send_on(fold(last_steps, last_near, LAST_GROUPS[0]), LAST_GROUPS[0])
+    pieces[1], last_far, tsecond, ff_three = join_lists(pieces[1], last_far, tsecond, ff_three)
+    last_far = send_on(fold(last_steps, last_far, LAST_GROUPS[1]), LAST_GROUPS[1])
     (tresult,) = call(
         second_norm_tangent,
         "second_norm_tangent",
         [((own, width), BF)],
-        (*sum_exchange(tkeep, tsend, tp), params, tfirst, unit_two, inverse_two),
-    )
-
-    def over_dp(kept, came, sums):
-        total = kept.shape[2]
-        going = ((kept.shape[1], total), BF)
-        outs = [((shard, total), F32), going, going, going] + ([lines] if sums else [])
-        own_shard, *onward = call(fold_shards, "fold_shards", outs, (kept, came))
-        there = [lax.ppermute(onward[i], "dp", xor_pairs(dp, 2 * i + 2)) for i in range(3)]
-        return (own_shard, *there, *onward[3:])
+        (tkeep, tfirst_came, tsecond, params, tfirst, unit_two, inverse_two),
+    )
+    tresult, last_near = join_lists(tresult, last_near)
+    tresult_pieces = spread_rows(tresult, tp)
+    ff_zero = fold(ff_steps, ff_zero, FF_GROUPS[3])
+    if paired:
+        ff_folded = [ff_zero[0], ff_one[0], ff_two[0], ff_three[0], ff_zero[1]]
+        last_folded = [last_far[1], last_far[0], *last_near, last_far[2]]
+    else:
+        ff_folded, last_folded = [ff_zero], [last_far]
+
+    def finish(body, name, outs, folded):
+        return call(body, name, outs, folded)
 
     vector = ((width,), F32)
     if paired:
-        own_down, *sums_two = call(
-            finish_down,
-            "finish_down",
-            [((shard, hidden), F32)] + [vector] * 4,
-            over_dp(down_steps[0], down_came, True),
+        own_down, own_up, *sums_two = finish(
+            functools.partial(finish_feed_forward, hidden),
+            "finish_feed_forward",
+            [((shard, hidden), F32)] * 2 + [vector] * 4,
+            ff_folded,
         )
-        (own_up,) = call(
-            finish_up, "finish_up", [((shard, hidden), F32)], over_dp(up_steps[0], up_came, False)
-        )
-        *own_mixed, own_out, bias_out, gain_one, shift_one, mixed_line = call(
+        *own_mixed, own_out, bias_out, gain_one, shift_one, mixed_sums = finish(
             functools.partial(finish_attention, cols),
             "finish_attention",
             [((shard, cols), F32)] * 3 + [((cols, shard), F32)] + [vector] * 4,
-            over_dp(last_steps[0], last_came, True),
+            last_folded,
         )
-        sums_one = [bias_out, gain_one, shift_one, mixed_line]
+        sums_one = [bias_out, gain_one, shift_one]
     else:
 
         def all_summed(step):
@@ -810,27 +883,26 @@
             came = lax.all_to_all(split, "dp", 0, 0, tiled=True)
             return jnp.sum(came.astype(F32), axis=0)
 
-        own_down, own_up = all_summed(down_steps[0]), all_summed(up_steps[0])
-        last = all_summed(last_steps[0])
+        own_ff = all_summed(ff_folded[0])
+        own_down, own_up = own_ff[:, :hidden], own_ff[:, hidden:]
+        last = all_summed(last_folded[0])
         own_mixed = [last[:, i * cols : (i + 1) * cols] for i in range(3)]
         own_out = last[:, 3 * cols :].T
         sums_two = list(lax.psum(sums_up, "dp"))
-        sums_one = list(lax.psum(last_steps[1], "dp"))
-
-    def all_rows(*blocks):
-        pieces = [piece for block in blocks for piece in spread_rows(block, tp)]
+        *sums_one, mixed_sums = list(lax.psum(last_steps[1], "dp"))
+
+    def all_rows(*spread):
         return call(
-            functools.partial(place_rows, len(blocks)),
+            functools.partial(place_rows, len(spread)),
             "place_rows",
-            [((rows, width), BF)] * len(blocks),
-            (where, *pieces),
-            scratch=[arriving(4 * len(blocks))],
+            [((rows, width), BF)] * len(spread),
+            (where, *[piece for pieces in spread for piece in pieces]),
+            scratch=[arriving(4 * len(spread))],
             any_outs=True,
         )
 
-    whole_result, whole_tresult = all_rows(result, tresult)
-    (whole_grad,) = all_rows(grad_input)
-    mixed_sums = sums_one[3]
+    whole_result, whole_grad = all_rows(result_pieces, pieces)
+    (whole_tresult,) = all_rows(tresult_pieces)
     return (
         whole_result,
         whole_grad,
@@ -841,7 +913,7 @@
         own_mixed[2],
         mixed_sums[2 * cols : 3 * cols],
         own_out,
-        *sums_one[:3],
+        *sums_one,
         own_up,
         sums_two[3],
         own_down.T,

time: 231 us -> 208 us (0.900)
  waiting for transfers between devices: 118 us -> 103 us
  starting transfers between devices: 63 us -> 53.9 us
  local copies, waits for them, and re-layouts: 3.35 us -> 7.45 us
    ppermute x16 -> x12, waiting for transfers between devices: 54.2 us -> 27.5 us  [step(): self.front[0] = lax.ppermute(self.front[0], 'dp', ahead)]
    ppermute x33, waiting for transfers between devices: 17.2 us -> 27.7 us  [swap(): return lax.ppermute(block, 'tp', xor_pairs(tp, bit))]
    ppermute x12 -> x9, starting transfers between devices: 15.6 us -> 7.25 us  [step(): self.front[1] = lax.ppermute(self.front[1], 'dp', behind)]
    ppermute x12, starting transfers between devices: 17.3 us -> 11.9 us  [the longest x6 6.44 us: send_on(): lax.ppermute(value, 'dp', xor_pairs(dp, 2 * z))]
    ppermute x16 -> x12, starting transfers between devices: 12.5 us -> 17 us  [step(): self.front[0] = lax.ppermute(self.front[0], 'dp', ahead)]
    unnamed x16 -> x21, local copies, waits for them, and re-layouts: 1.81 us -> 5.92 us
    pallas_call x23 -> x25, Pallas kernels: 41.7 us -> 40 us  [call(): pl.pallas_call(body, out_shape=[jax.ShapeDtypeStruct(shape, kind) for sha...]
    ppermute x12 -> x9, waiting for transfers between devices: 11.5 us -> 10.5 us  [step(): self.front[1] = lax.ppermute(self.front[1], 'dp', behind)]
  transfers between devices with their start and end apart: 73 -> 66, of which waited for: 35 -> 37; matrix products, arithmetic and copies ran while one was open for 1% -> 0% of each run, Pallas kernels for 9% -> 18%
where the time goes in v3:
time: 208 us; the launch traced here: 207 us
  waiting for transfers between devices  103 us (50%)
  starting transfers between devices  53.9 us (26%)
  Pallas kernels  40 us (19%)
  local copies, waits for them, and re-layouts  7.45 us (4%)
    pallas_call x25, Pallas kernels, call(): pl.pallas_call(body, out_shape=[jax.ShapeDtypeStruct(shape, kind) for sha...  40 us
    ppermute x6, waiting for transfers between devices, send_on(): lax.ppermute(value, 'dp', xor_pairs(dp, 2 * z))  33.1 us
    ppermute x33, waiting for transfers between devices, swap(): return lax.ppermute(block, 'tp', xor_pairs(tp, bit))  27.7 us
    ppermute x12, waiting for transfers between devices, step(): self.front[0] = lax.ppermute(self.front[0], 'dp', ahead)  27.5 us
    ppermute x33, starting transfers between devices, swap(): return lax.ppermute(block, 'tp', xor_pairs(tp, bit))  17.8 us
    ppermute x12, starting transfers between devices, step(): self.front[0] = lax.ppermute(self.front[0], 'dp', ahead)  17 us
    ppermute x9, waiting for transfers between devices, step(): self.front[1] = lax.ppermute(self.front[1], 'dp', behind)  10.5 us
    ppermute x9, starting transfers between devices, step(): self.front[1] = lax.ppermute(self.front[1], 'dp', behind)  7.25 us
  transfers between devices with their start and end apart: 66, of which 37 were waited for; matrix products, arithmetic and copies ran while one was open for 0% of the time, Pallas kernels for 18%

profile of v3, /device:TPU:0, one launch (start us, length us, event | category | flops | bytes accessed | tf_op | source)
XLA Modules:
  0.0 207.4 jit_solution(4746183898492501454)
XLA Ops:
  4.2 3.0 %collective-permute-start.2 = (bf16[96,768]{1,0:T(8,128)(2,1)S(1)}, bf16[96,768]{1,0:T(8,128)(2,1)S(1)}, u32[]{:S(2)}, u32[]{:S(2)}) collective-permute-start(bf16[96,768]{1,0:T(8,128)(2,1)S(1)} %pad_maximum_fusion.1.refs_0_), channel_id=1, source_target_pairs={{8,0},{16,8},{24,16},{28,24},{20,28},{12,20},{4,12},{0,4},{9,1},{1... | collective-permute-start | bytes 442376 | tf_op jit(solution)/shard_map/ppermute | solution.py:92
  7.4 3.8 %collective-permute-done.2.refs_2_ = bf16[96,768]{1,0:T(8,128)(2,1)S(1)} collective-permute-done((bf16[96,768]{1,0:T(8,128)(2,1)S(1)}, bf16[96,768]{1,0:T(8,128)(2,1)S(1)}, u32[]{:S(2)}, u32[]{:S(2)}) %collective-permute-start.2) | collective-permute-done | bytes 147488 | tf_op jit(solution)/shard_map/ppermute | solution.py:92
  11.2 1.7 collective-permute-start.3
  18.4 1.8 collective-permute-start.6
  20.5 1.7 collective-permute-start.4
  22.5 9.9 %collective-permute-done.4.refs_5_ = bf16[96,768]{1,0:T(8,128)(2,1)S(1)} collective-permute-done((bf16[96,768]{1,0:T(8,128)(2,1)S(1)}, bf16[96,768]{1,0:T(8,128)(2,1)S(1)}, u32[]{:S(2)}, u32[]{:S(2)}) %collective-permute-start.4) | collective-permute-done | bytes 147488 | tf_op jit(solution)/shard_map/ppermute | solution.py:89
  33.5 1.6 collective-permute-start.8
  35.1 4.3 %collective-permute-done.8.refs_7_ = bf16[96,768]{1,0:T(8,128)(2,1)S(1)} collective-permute-done((bf16[96,768]{1,0:T(8,128)(2,1)S(1)}, bf16[96,768]{1,0:T(8,128)(2,1)S(1)}, u32[]{:S(2)}, u32[]{:S(2)}) %collective-permute-start.8) | collective-permute-done | bytes 147488 | tf_op jit(solution)/shard_map/ppermute | solution.py:89
  39.4 2.1 %collective-permute-start.9 = (bf16[96,2304]{1,0:T(8,128)(2,1)S(1)}, bf16[96,2304]{1,0:T(8,128)(2,1)S(1)}, u32[]{:S(2)}, u32[]{:S(2)}) collective-permute-start(bf16[96,2304]{1,0:T(8,128)(2,1)S(1)} %collective-permute-done.6.refs_5_), channel_id=1, source_target_pairs={{0,8},{8,16},{16,24},{24,28},{28,20},{20,12},{12,4},{4,0},{1,9},{9... | collective-permute-start | bytes 1327112 | tf_op jit(solution)/shard_map/ppermute | solution.py:89
  41.5 5.9 %attention_forward.1 = (bf16[512,768]{1,0:T(8,128)(2,1)S(1)}, bf16[512,576]{1,0:T(8,128)(2,1)S(1)}, f32[6,256,256]{2,1,0:T(8,128)S(1)}, bf16[512,192]{1,0:T(8,12...) custom-call(s32[4]{0:T(128)S(1)} %pad_add_fusion.where, ...), custom_call_target="tpu_custom_call" | custom-call | flops 1 | bytes 1 | tf_op jit(solution)/shard_map/attention_forward/pallas_call | solution.py:43
  48.2 1.7 collective-permute-start.13
  50.3 1.6 collective-permute-start.12
  51.8 5.3 %collective-permute-done.12.second = bf16[128,768]{1,0:T(8,128)(2,1)S(1)} collective-permute-done((bf16[128,768]{1,0:T(8,128)(2,1)S(1)}, bf16[128,768]{1,0:T(8,128)(2,1)S(1)}, u32[]{:S(2)}, u32[]{:S(2)}) %collective-permute-start.12) | collective-permute-done | bytes 196640 | tf_op jit(solution)/shard_map/ppermute | solution.py:144
  57.4 3.3 %collective-permute-done.13.refs_9_ = bf16[96,2304]{1,0:T(8,128)(2,1)S(1)} collective-permute-done((bf16[96,2304]{1,0:T(8,128)(2,1)S(1)}, bf16[96,2304]{1,0:T(8,128)(2,1)S(1)}, u32[]{:S(2)}, u32[]{:S(2)}) %collective-permute-start.13) | collective-permute-done | bytes 442400 | tf_op jit(solution)/shard_map/ppermute | solution.py:89
  60.8 1.7 collective-permute-done.14.refs_10_
  62.4 1.7 collective-permute-start.16
  64.2 1.5 collective-permute-start.15
  65.7 4.4 %collective-permute-done.15.refs_1_ = bf16[128,768]{1,0:T(8,128)(2,1)S(1)} collective-permute-done((bf16[128,768]{1,0:T(8,128)(2,1)S(1)}, bf16[128,768]{1,0:T(8,128)(2,1)S(1)}, u32[]{:S(2)}, u32[]{:S(2)}) %collective-permute-start.15) | collective-permute-done | bytes 196640 | tf_op jit(solution)/shard_map/ppermute | solution.py:144
  70.1 4.1 %collective-permute-done.16.refs_11_ = bf16[96,2304]{1,0:T(8,128)(2,1)S(1)} collective-permute-done((bf16[96,2304]{1,0:T(8,128)(2,1)S(1)}, bf16[96,2304]{1,0:T(8,128)(2,1)S(1)}, u32[]{:S(2)}, u32[]{:S(2)}) %collective-permute-start.16) | collective-permute-done | bytes 442400 | tf_op jit(solution)/shard_map/ppermute | solution.py:89
  77.7 1.4 collective-permute-done.17.refs_2_
  79.1 5.5 %feed_forward.1 = (bf16[512,768]{1,0:T(8,128)(2,1)S(1)}, bf16[512,768]{1,0:T(8,128)(2,1)S(1)}, f32[512,768]{1,0:T(8,128)S(1)}, bf16[256,768]{1,0:T(8,128)(2,1)S(...) custom-call(s32[4]{0:T(128)S(1)} %pad_add_fusion.where, f32[8,768]{1,0:T(8,128)S(1)} %reshape.39.params, ...), custom_call_target="tpu_custom_call" | custom-call | flops 1 | bytes 1 | tf_op jit(solution)/shard_map/feed_forward/pallas_call | solution.py:43
  85.9 1.6 collective-permute-start.23
  88.0 1.6 collective-permute-start.22
  89.5 4.1 %attention_tangent.1 = (bf16[256,768]{1,0:T(8,128)(2,1)S(1)}, bf16[256,768]{1,0:T(8,128)(2,1)S(1)}) custom-call(s32[4]{0:T(128)S(1)} %pad_add_fusion.where, bf16[512,768]{1,0:T(8,128)(2,1)S(1)} %get-tuple-element.196.x_rel.rel, bf16[512,576]{1,0:T(8,128)(2,1)S(1)} %get-tuple-element.218.mixed.refs_4_, f32[6,256,256]{2,1,0:T(8,128)S(1)} %get-tuple-element.219.probs.refs_5_, ...), custom_call_target="tpu_custom_call" | custom-call | flops 1 | bytes 1 | tf_op jit(solution)/shard_map/attention_tangent/pallas_call | solution.py:43
  93.6 1.7 collective-permute-done.23.refs_11_
  97.6 1.6 collective-permute-start.25
  101.2 4.0 %collective-permute-done.25.refs_1_ = bf16[136,768]{1,0:T(8,128)(2,1)S(1)} collective-permute-done((bf16[136,768]{1,0:T(8,128)(2,1)S(1)}, bf16[136,768]{1,0:T(8,128)(2,1)S(1)}, u32[]{:S(2)}, u32[]{:S(2)}) %collective-permute-start.25) | collective-permute-done | bytes 208928 | tf_op jit(solution)/shard_map/ppermute | solution.py:144
  105.8 1.5 collective-permute-start.31
  109.4 2.5 %feed_forward_backward.1 = (bf16[512,768]{1,0:T(8,128)(2,1)S(1)}, bf16[512,768]{1,0:T(8,128)(2,1)S(1)}, f32[4,768]{1,0:T(4,128)S(1)}, bf16[256,768]{1,0:T(8,128)(2,1)S(1)}, bf16[256,768]{1,0:T(8,128)(2,1)S(1)}) custom-call(bf16[136,768]{1,0:T(8,128)(2,1)S(1)} %get-tuple-element.229.refs_0_, bf16[136,768]{1,0:T(8,128)(2,1)S(1)} %collective-permute-done.25.refs_1_, ...), custom_call_target="tpu_custom_call" | custom-call | flops 1 | bytes 1 | tf_op jit(solution)/shard_map/feed_forward_backward/pallas_call | solution.py:43
  113.1 1.6 collective-permute-start.35
  116.7 2.5 %feed_forward_weights.1 = (bf16[4,104,1536]{2,1,0:T(8,128)(2,1)S(1)}, bf16[1,104,1536]{2,1,0:T(8,128)(2,1)S(1)}, bf16[1,104,1536]{2,1,0:T(8,128)(2,1)S(1)}, bf16...) custom-call(s32[4]{0:T(128)S(1)} %pad_add_fusion.where, bf16[512,768]{1,0:T(8,128)(2,1)S(1)} %get-tuple-element.243.rel, ...), custom_call_target="tpu_custom_call" | custom-call | flops 1 | bytes 1 | tf_op jit(solution)/shard_map/feed_forward_weights/pallas_call | solution.py:43
  119.3 1.6 collective-permute-done.35.second
  121.2 2.7 %collective-permute-done.34.refs_15_ = bf16[96,1536]{1,0:T(8,128)(2,1)S(1)} collective-permute-done((bf16[96,1536]{1,0:T(8,128)(2,1)S(1)}, bf16[96,1536]{1,0:T(8,128)(2,1)S(1)}, u32[]{:S(2)}, u32[]{:S(2)}) %collective-permute-start.34) | collective-permute-done | bytes 294944 | tf_op jit(solution)/shard_map/ppermute | solution.py:89
  125.1 1.6 collective-permute-start.38
  127.2 4.8 %collective-permute-done.38.refs_1_ = bf16[136,768]{1,0:T(8,128)(2,1)S(1)} collective-permute-done((bf16[136,768]{1,0:T(8,128)(2,1)S(1)}, bf16[136,768]{1,0:T(8,128)(2,1)S(1)}, u32[]{:S(2)}, u32[]{:S(2)}) %collective-permute-start.38) | collective-permute-done | bytes 208928 | tf_op jit(solution)/shard_map/ppermute | solution.py:144
  132.0 3.6 %collective-permute-done.41.came = bf16[1,104,1536]{2,1,0:T(8,128)(2,1)S(1)} collective-permute-done((bf16[1,104,1536]{2,1,0:T(8,128)(2,1)S(1)}, bf16[1,104,1536]{2,1,0:T(8,128)(2,1)S(1)}, u32[]{:S(2)}, u32[]{:S(2)}) %collective-permute-start.41) | collective-permute-done | bytes 319520 | tf_op jit(solution)/shard_map/ppermute | solution.py:740
  137.5 4.5 %attention_backward.1 = (bf16[512,768]{1,0:T(8,128)(2,1)S(1)}, bf16[512,576]{1,0:T(8,128)(2,1)S(1)}, f32[4,768]{1,0:T(4,128)S(1)}, bf16[256,768]{1,0:T(8,128)(2,1)S(1)}, bf16[256,768]{1,0:T(8,128)(2,1)S(1)}) custom-call(bf16[136,768]{1,0:T(8,128)(2,1)S(1)} %get-tuple-element.268.refs_0_, bf16[136,768]{1,0:T(8,128)(2,1)S(1)} %collective-permute-done.38.refs_1_, ...), custom_call_target="tpu_custom_call" | custom-call | flops 1 | bytes 1 | tf_op jit(solution)/shard_map/attention_backward/pallas_call | solution.py:43
  146.9 2.3 %attention_weights.1 = (bf16[4,104,768]{2,1,0:T(8,128)(2,1)S(1)}, bf16[2,104,768]{2,1,0:T(8,128)(2,1)S(1)}, bf16[2,104,768]{2,1,0:T(8,128)(2,1)S(1)}) custom-call(s32[4]{0:T(128)S(1)} %pad_add_fusion.where, bf16[512,768]{1,0:T(8,128)(2,1)S(1)} %get-tuple-element.284.rel, bf16[512,576]{1,0:T(8,128)(2,1)S(1)} %get-tuple-element.285.grad, ...), custom_call_target="tpu_custom_call" | custom-call | flops 1 | bytes 1 | tf_op jit(solution)/shard_map/attention_weights/pallas_call | solution.py:43
  151.1 4.8 %feed_forward_tangent.1 = (bf16[256,768]{1,0:T(8,128)(2,1)S(1)}, bf16[256,768]{1,0:T(8,128)(2,1)S(1)}) custom-call(s32[4]{0:T(128)S(1)} %pad_add_fusion.where, bf16[128,768]{1,0:T(8,128)(2,1)S(1)} %get-tuple-element.281.refs_0_, bf16[128,768]{1,0:T(8,128)(2,1)S(1)} %collective-permute-done.43.refs_1_, bf16[128,768]{1,0:T(8,128)(2,1)S(1)} %collective-permute-done.47.refs_2_, ...), custom_call_target="tpu_custom_call" | custom-call | flops 1 | bytes 1 | tf_op jit(solution)/shard_map/feed_forward_tangent/pallas_call | solution.py:43
  155.9 5.8 %collective-permute-done.50.refs_2_ = bf16[104,1536]{1,0:T(8,128)(2,1)S(1)} collective-permute-done((bf16[104,1536]{1,0:T(8,128)(2,1)S(1)}, bf16[104,1536]{1,0:T(8,128)(2,1)S(1)}, u32[]{:S(2)}, u32[]{:S(2)}) %collective-permute-start.50) | collective-permute-done | bytes 319520 | tf_op jit(solution)/shard_map/ppermute | solution.py:758
  162.0 2.3 %collective-permute-start.55 = (bf16[104,1536]{1,0:T(8,128)(2,1)S(1)}, bf16[104,1536]{1,0:T(8,128)(2,1)S(1)}, u32[]{:S(2)}, u32[]{:S(2)}) collective-permute-start(bf16[104,1536]{1,0:T(8,128)(2,1)S(1)} %fold_shards.7), channel_id=1, source_target_pairs={{0,24},{4,28},{8,16},{12,20},{16,8},{20,12},{24,0},{28,4},{1,25},{... | collective-permute-start | bytes 958472 | tf_op jit(solution)/shard_map/ppermute | solution.py:758
  167.8 6.5 %collective-permute-done.55.refs_3_ = bf16[104,1536]{1,0:T(8,128)(2,1)S(1)} collective-permute-done((bf16[104,1536]{1,0:T(8,128)(2,1)S(1)}, bf16[104,1536]{1,0:T(8,128)(2,1)S(1)}, u32[]{:S(2)}, u32[]{:S(2)}) %collective-permute-start.55) | collective-permute-done | bytes 319520 | tf_op jit(solution)/shard_map/ppermute | solution.py:758
  175.2 10.4 %collective-permute-done.58.refs_2_ = bf16[104,768]{1,0:T(8,128)(2,1)S(1)} collective-permute-done((bf16[104,768]{1,0:T(8,128)(2,1)S(1)}, bf16[104,768]{1,0:T(8,128)(2,1)S(1)}, u32[]{:S(2)}, u32[]{:S(2)}) %collective-permute-start.58) | collective-permute-done | bytes 159776 | tf_op jit(solution)/shard_map/ppermute | solution.py:758
  185.6 2.5 %collective-permute-start.59 = (bf16[104,768]{1,0:T(8,128)(2,1)S(1)}, bf16[104,768]{1,0:T(8,128)(2,1)S(1)}, u32[]{:S(2)}, u32[]{:S(2)}) collective-permute-start(bf16[104,768]{1,0:T(8,128)(2,1)S(1)} %get-tuple-element.319), channel_id=1, source_target_pairs={{0,24},{4,28},{8,16},{12,20},{16,8},{20,12},{24,0},{28,4},{1,25},{... | collective-permute-start | bytes 479240 | tf_op jit(solution)/shard_map/ppermute | solution.py:758
  189.1 5.3 %collective-permute-done.59.refs_3_ = bf16[104,768]{1,0:T(8,128)(2,1)S(1)} collective-permute-done((bf16[104,768]{1,0:T(8,128)(2,1)S(1)}, bf16[104,768]{1,0:T(8,128)(2,1)S(1)}, u32[]{:S(2)}, u32[]{:S(2)}) %collective-permute-start.59) | collective-permute-done | bytes 159776 | tf_op jit(solution)/shard_map/ppermute | solution.py:758
  195.7 4.5 %collective-permute-done.65.refs_1_ = bf16[104,1536]{1,0:T(8,128)(2,1)S(1)} collective-permute-done((bf16[104,1536]{1,0:T(8,128)(2,1)S(1)}, bf16[104,1536]{1,0:T(8,128)(2,1)S(1)}, u32[]{:S(2)}, u32[]{:S(2)}) %collective-permute-start.65) | collective-permute-done | bytes 319520 | tf_op jit(solution)/shard_map/ppermute | solution.py:758
  201.1 1.7 place_rows.2
  205.8 1.4 place_rows.3
  (143 shorter events, 49.4 us)
Async XLA Ops:
  4.2 6.9 %collective-permute-start.2 = (bf16[96,768]{1,0:T(8,128)(2,1)S(1)}, bf16[96,768]{1,0:T(8,128)(2,1)S(1)}, u32[]{:S(2)}, u32[]{:S(2)}) collective-permute-start(bf16[96,768]{1,0:T(8,128)(2,1)S(1)} %pad_maximum_fusion.1.refs_0_), channel_id=1, source_target_pairs={{8,0},{16,8},{24,16},{28,24},{20,28},{12,20},{4,12},{0,4},{9,1},{1... | collective-permute-start | bytes 442376 | tf_op jit(solution)/shard_map/ppermute | solution.py:92
  11.2 7.2 %collective-permute-start.3 = (bf16[96,768]{1,0:T(8,128)(2,1)S(1)}, bf16[96,768]{1,0:T(8,128)(2,1)S(1)}, u32[]{:S(2)}, u32[]{:S(2)}) collective-permute-start(bf16[96,768]{1,0:T(8,128)(2,1)S(1)} %collective-permute-done.2.refs_2_), channel_id=1, source_target_pairs={{8,0},{16,8},{24,16},{28,24},{20,28},{12,20},{4,12},{0,4},{9,1},{1... | collective-permute-start | bytes 442376 | tf_op jit(solution)/shard_map/ppermute | solution.py:92
  18.4 15.2 %collective-permute-start.6 = (bf16[96,2304]{1,0:T(8,128)(2,1)S(1)}, bf16[96,2304]{1,0:T(8,128)(2,1)S(1)}, u32[]{:S(2)}, u32[]{:S(2)}) collective-permute-start(bf16[96,2304]{1,0:T(8,128)(2,1)S(1)} %pack_weights.1.refs_4_), channel_id=1, source_target_pairs={{0,8},{8,16},{16,24},{24,28},{28,20},{20,12},{12,4},{4,0},{1,9},{9... | collective-permute-start | bytes 1327112 | tf_op jit(solution)/shard_map/ppermute | solution.py:89
  20.2 13.4 %collective-permute-start.7 = (bf16[96,2304]{1,0:T(8,128)(2,1)S(1)}, bf16[96,2304]{1,0:T(8,128)(2,1)S(1)}, u32[]{:S(2)}, u32[]{:S(2)}) collective-permute-start(bf16[96,2304]{1,0:T(8,128)(2,1)S(1)} %pack_weights.1.refs_4_), channel_id=1, source_target_pairs={{8,0},{16,8},{24,16},{28,24},{20,28},{12,20},{4,12},{0,4},{9,1},{1... | collective-permute-start | bytes 1327112 | tf_op jit(solution)/shard_map/ppermute | solution.py:92
  20.5 11.9 %collective-permute-start.4 = (bf16[96,768]{1,0:T(8,128)(2,1)S(1)}, bf16[96,768]{1,0:T(8,128)(2,1)S(1)}, u32[]{:S(2)}, u32[]{:S(2)}) collective-permute-start(bf16[96,768]{1,0:T(8,128)(2,1)S(1)} %collective-permute-done.1.refs_3_), channel_id=1, source_target_pairs={{0,8},{8,16},{16,24},{24,28},{28,20},{20,12},{12,4},{4,0},{1,9},{9... | collective-permute-start | bytes 442376 | tf_op jit(solution)/shard_map/ppermute | solution.py:89
  22.2 11.3 %collective-permute-start.5 = (bf16[96,768]{1,0:T(8,128)(2,1)S(1)}, bf16[96,768]{1,0:T(8,128)(2,1)S(1)}, u32[]{:S(2)}, u32[]{:S(2)}) collective-permute-start(bf16[96,768]{1,0:T(8,128)(2,1)S(1)} %collective-permute-done.3.refs_4_), channel_id=1, source_target_pairs={{8,0},{16,8},{24,16},{28,24},{20,28},{12,20},{4,12},{0,4},{9,1},{1... | collective-permute-start | bytes 442376 | tf_op jit(solution)/shard_map/ppermute | solution.py:92
  39.4 8.4 %collective-permute-start.10 = (bf16[96,2304]{1,0:T(8,128)(2,1)S(1)}, bf16[96,2304]{1,0:T(8,128)(2,1)S(1)}, u32[]{:S(2)}, u32[]{:S(2)}) collective-permute-start(bf16[96,2304]{1,0:T(8,128)(2,1)S(1)} %collective-permute-done.7.refs_6_), channel_id=1, source_target_pairs={{8,0},{16,8},{24,16},{28,24},{20,28},{12,20},{4,12},{0,4},{9,1},{1... | collective-permute-start | bytes 1327112 | tf_op jit(solution)/shard_map/ppermute | solution.py:92
  39.4 8.7 %collective-permute-start.9 = (bf16[96,2304]{1,0:T(8,128)(2,1)S(1)}, bf16[96,2304]{1,0:T(8,128)(2,1)S(1)}, u32[]{:S(2)}, u32[]{:S(2)}) collective-permute-start(bf16[96,2304]{1,0:T(8,128)(2,1)S(1)} %collective-permute-done.6.refs_5_), channel_id=1, source_target_pairs={{0,8},{8,16},{16,24},{24,28},{28,20},{20,12},{12,4},{4,0},{1,9},{9... | collective-permute-start | bytes 1327112 | tf_op jit(solution)/shard_map/ppermute | solution.py:89
  48.2 12.6 %collective-permute-start.13 = (bf16[96,2304]{1,0:T(8,128)(2,1)S(1)}, bf16[96,2304]{1,0:T(8,128)(2,1)S(1)}, u32[]{:S(2)}, u32[]{:S(2)}) collective-permute-start(bf16[96,2304]{1,0:T(8,128)(2,1)S(1)} %collective-permute-done.9.refs_7_), channel_id=1, source_target_pairs={{0,8},{8,16},{16,24},{24,28},{28,20},{20,12},{12,4},{4,0},{1,9},{9... | collective-permute-start | bytes 1327112 | tf_op jit(solution)/shard_map/ppermute | solution.py:89
  49.8 12.6 %collective-permute-start.14 = (bf16[96,2304]{1,0:T(8,128)(2,1)S(1)}, bf16[96,2304]{1,0:T(8,128)(2,1)S(1)}, u32[]{:S(2)}, u32[]{:S(2)}) collective-permute-start(bf16[96,2304]{1,0:T(8,128)(2,1)S(1)} %collective-permute-done.10.refs_8_), channel_id=1, source_target_pairs={{8,0},{16,8},{24,16},{28,24},{20,28},{12,20},{4,12},{0,4},{9,1},{1... | collective-permute-start | bytes 1327112 | tf_op jit(solution)/shard_map/ppermute | solution.py:92
  50.3 6.9 %collective-permute-start.12 = (bf16[128,768]{1,0:T(8,128)(2,1)S(1)}, bf16[128,768]{1,0:T(8,128)(2,1)S(1)}, u32[]{:S(2)}, u32[]{:S(2)}) collective-permute-start(bf16[128,768]{1,0:T(8,128)(2,1)S(1)} %add_convert_fusion.5), channel_id=1, source_target_pairs={{0,2},{1,3},{2,0},{3,1},{4,6},{5,7},{6,4},{7,5},{8,10},{9,11},{10,... | collective-permute-start | bytes 589832 | tf_op jit(solution)/shard_map/ppermute | solution.py:144
  62.4 11.8 %collective-permute-start.16 = (bf16[96,2304]{1,0:T(8,128)(2,1)S(1)}, bf16[96,2304]{1,0:T(8,128)(2,1)S(1)}, u32[]{:S(2)}, u32[]{:S(2)}) collective-permute-start(bf16[96,2304]{1,0:T(8,128)(2,1)S(1)} %collective-permute-done.13.refs_9_), channel_id=1, source_target_pairs={{0,8},{8,16},{16,24},{24,28},{28,20},{20,12},{12,4},{4,0},{1,9},{9... | collective-permute-start | bytes 1327112 | tf_op jit(solution)/shard_map/ppermute | solution.py:89
  75.7 9.1 %collective-permute-start.19 = (bf16[96,1536]{1,0:T(8,128)(2,1)S(1)}, bf16[96,1536]{1,0:T(8,128)(2,1)S(1)}, u32[]{:S(2)}, u32[]{:S(2)}) collective-permute-start(bf16[96,1536]{1,0:T(8,128)(2,1)S(1)} %pad_maximum_fusion.refs_8_), channel_id=1, source_target_pairs={{0,8},{8,16},{16,24},{24,28},{28,20},{20,12},{12,4},{4,0},{1,9},{9... | collective-permute-start | bytes 884744 | tf_op jit(solution)/shard_map/ppermute | solution.py:89
  77.1 8.8 %collective-permute-start.20 = (bf16[96,1536]{1,0:T(8,128)(2,1)S(1)}, bf16[96,1536]{1,0:T(8,128)(2,1)S(1)}, u32[]{:S(2)}, u32[]{:S(2)}) collective-permute-start(bf16[96,1536]{1,0:T(8,128)(2,1)S(1)} %pad_maximum_fusion.refs_8_), channel_id=1, source_target_pairs={{8,0},{16,8},{24,16},{28,24},{20,28},{12,20},{4,12},{0,4},{9,1},{1... | collective-permute-start | bytes 884744 | tf_op jit(solution)/shard_map/ppermute | solution.py:92
  85.9 9.4 %collective-permute-start.23 = (bf16[96,1536]{1,0:T(8,128)(2,1)S(1)}, bf16[96,1536]{1,0:T(8,128)(2,1)S(1)}, u32[]{:S(2)}, u32[]{:S(2)}) collective-permute-start(bf16[96,1536]{1,0:T(8,128)(2,1)S(1)} %collective-permute-done.19.refs_9_), channel_id=1, source_target_pairs={{0,8},{8,16},{16,24},{24,28},{28,20},{20,12},{12,4},{4,0},{1,9},{9... | collective-permute-start | bytes 884744 | tf_op jit(solution)/shard_map/ppermute | solution.py:89
  87.4 9.1 %collective-permute-start.24 = (bf16[96,1536]{1,0:T(8,128)(2,1)S(1)}, bf16[96,1536]{1,0:T(8,128)(2,1)S(1)}, u32[]{:S(2)}, u32[]{:S(2)}) collective-permute-start(bf16[96,1536]{1,0:T(8,128)(2,1)S(1)} %collective-permute-done.20.refs_10_), channel_id=1, source_target_pairs={{8,0},{16,8},{24,16},{28,24},{20,28},{12,20},{4,12},{0,4},{9,1},{1... | collective-permute-start | bytes 884744 | tf_op jit(solution)/shard_map/ppermute | solution.py:92
  88.0 8.6 %collective-permute-start.22 = (bf16[128,768]{1,0:T(8,128)(2,1)S(1)}, bf16[128,768]{1,0:T(8,128)(2,1)S(1)}, u32[]{:S(2)}, u32[]{:S(2)}) collective-permute-start(bf16[128,768]{1,0:T(8,128)(2,1)S(1)} %add_convert_fusion.4), channel_id=1, source_target_pairs={{0,2},{1,3},{2,0},{3,1},{4,6},{5,7},{6,4},{7,5},{8,10},{9,11},{10,... | collective-permute-start | bytes 589832 | tf_op jit(solution)/shard_map/ppermute | solution.py:144
  96.6 9.2 %collective-permute-start.26 = (bf16[256,768]{1,0:T(8,128)(2,1)S(1)}, bf16[256,768]{1,0:T(8,128)(2,1)S(1)}, u32[]{:S(2)}, u32[]{:S(2)}) collective-permute-start(bf16[256,768]{1,0:T(8,128)(2,1)S(1)} %get-tuple-element.230), channel_id=1, source_target_pairs={{0,1},{1,0},{2,3},{3,2},{4,5},{5,4},{6,7},{7,6},{8,9},{9,8},{10,11... | collective-permute-start | bytes 1179656 | tf_op jit(solution)/shard_map/ppermute | solution.py:144
  97.6 7.6 %collective-permute-start.25 = (bf16[136,768]{1,0:T(8,128)(2,1)S(1)}, bf16[136,768]{1,0:T(8,128)(2,1)S(1)}, u32[]{:S(2)}, u32[]{:S(2)}) collective-permute-start(bf16[136,768]{1,0:T(8,128)(2,1)S(1)} %get-tuple-element.229.refs_0_), channel_id=1, source_target_pairs={{0,2},{1,3},{2,0},{3,1},{4,6},{5,7},{6,4},{7,5},{8,10},{9,11},{10,... | collective-permute-start | bytes 626696 | tf_op jit(solution)/shard_map/ppermute | solution.py:144
  99.2 9.1 %collective-permute-start.29 = (bf16[96,1536]{1,0:T(8,128)(2,1)S(1)}, bf16[96,1536]{1,0:T(8,128)(2,1)S(1)}, u32[]{:S(2)}, u32[]{:S(2)}) collective-permute-start(bf16[96,1536]{1,0:T(8,128)(2,1)S(1)} %collective-permute-done.23.refs_11_), channel_id=1, source_target_pairs={{0,8},{8,16},{16,24},{24,28},{28,20},{20,12},{12,4},{4,0},{1,9},{9... | collective-permute-start | bytes 884744 | tf_op jit(solution)/shard_map/ppermute | solution.py:89
  100.6 8.9 %collective-permute-start.30 = (bf16[96,1536]{1,0:T(8,128)(2,1)S(1)}, bf16[96,1536]{1,0:T(8,128)(2,1)S(1)}, u32[]{:S(2)}, u32[]{:S(2)}) collective-permute-start(bf16[96,1536]{1,0:T(8,128)(2,1)S(1)} %collective-permute-done.24.refs_12_), channel_id=1, source_target_pairs={{8,0},{16,8},{24,16},{28,24},{20,28},{12,20},{4,12},{0,4},{9,1},{1... | collective-permute-start | bytes 884744 | tf_op jit(solution)/shard_map/ppermute | solution.py:92
  105.8 6.8 %collective-permute-start.31 = (bf16[128,768]{1,0:T(8,128)(2,1)S(1)}, bf16[128,768]{1,0:T(8,128)(2,1)S(1)}, u32[]{:S(2)}, u32[]{:S(2)}) collective-permute-start(bf16[128,768]{1,0:T(8,128)(2,1)S(1)} %get-tuple-element.262.refs_0_), channel_id=1, source_target_pairs={{0,2},{1,3},{2,0},{3,1},{4,6},{5,7},{6,4},{7,5},{8,10},{9,11},{10,... | collective-permute-start | bytes 589832 | tf_op jit(solution)/shard_map/ppermute | solution.py:144
  112.6 8.6 %collective-permute-start.36 = (bf16[128,768]{1,0:T(8,128)(2,1)S(1)}, bf16[128,768]{1,0:T(8,128)(2,1)S(1)}, u32[]{:S(2)}, u32[]{:S(2)}) collective-permute-start(bf16[128,768]{1,0:T(8,128)(2,1)S(1)} %get-tuple-element.262.refs_0_), channel_id=1, source_target_pairs={{0,1},{1,0},{2,3},{3,2},{4,5},{5,4},{6,7},{7,6},{8,9},{9,8},{10,11... | collective-permute-start | bytes 589832 | tf_op jit(solution)/shard_map/ppermute | solution.py:144
  113.1 8.1 %collective-permute-start.37 = (bf16[128,768]{1,0:T(8,128)(2,1)S(1)}, bf16[128,768]{1,0:T(8,128)(2,1)S(1)}, u32[]{:S(2)}, u32[]{:S(2)}) collective-permute-start(bf16[128,768]{1,0:T(8,128)(2,1)S(1)} %collective-permute-done.31.refs_1_), channel_id=1, source_target_pairs={{0,1},{1,0},{2,3},{3,2},{4,5},{5,4},{6,7},{7,6},{8,9},{9,8},{10,11... | collective-permute-start | bytes 589832 | tf_op jit(solution)/shard_map/ppermute | solution.py:144
  113.1 7.8 %collective-permute-start.35 = (bf16[128,768]{1,0:T(8,128)(2,1)S(1)}, bf16[128,768]{1,0:T(8,128)(2,1)S(1)}, u32[]{:S(2)}, u32[]{:S(2)}) collective-permute-start(bf16[128,768]{1,0:T(8,128)(2,1)S(1)} %add_convert_fusion.2), channel_id=1, source_target_pairs={{0,2},{1,3},{2,0},{3,1},{4,6},{5,7},{6,4},{7,5},{8,10},{9,11},{10,... | collective-permute-start | bytes 589832 | tf_op jit(solution)/shard_map/ppermute | solution.py:144
  114.7 9.1 %collective-permute-start.34 = (bf16[96,1536]{1,0:T(8,128)(2,1)S(1)}, bf16[96,1536]{1,0:T(8,128)(2,1)S(1)}, u32[]{:S(2)}, u32[]{:S(2)}) collective-permute-start(bf16[96,1536]{1,0:T(8,128)(2,1)S(1)} %collective-permute-done.29.refs_13_), channel_id=1, source_target_pairs={{0,8},{8,16},{16,24},{24,28},{28,20},{20,12},{12,4},{4,0},{1,9},{9... | collective-permute-start | bytes 884744 | tf_op jit(solution)/shard_map/ppermute | solution.py:89
  116.2 8.6 %collective-permute-start.33 = (bf16[128,768]{1,0:T(8,128)(2,1)S(1)}, bf16[128,768]{1,0:T(8,128)(2,1)S(1)}, u32[]{:S(2)}, u32[]{:S(2)}) collective-permute-start(bf16[128,768]{1,0:T(8,128)(2,1)S(1)} %add_convert_fusion.3), channel_id=1, source_target_pairs={{0,2},{1,3},{2,0},{3,1},{4,6},{5,7},{6,4},{7,5},{8,10},{9,11},{10,... | collective-permute-start | bytes 589832 | tf_op jit(solution)/shard_map/ppermute | solution.py:144
  125.1 6.9 %collective-permute-start.38 = (bf16[136,768]{1,0:T(8,128)(2,1)S(1)}, bf16[136,768]{1,0:T(8,128)(2,1)S(1)}, u32[]{:S(2)}, u32[]{:S(2)}) collective-permute-start(bf16[136,768]{1,0:T(8,128)(2,1)S(1)} %get-tuple-element.268.refs_0_), channel_id=1, source_target_pairs={{0,2},{1,3},{2,0},{3,1},{4,6},{5,7},{6,4},{7,5},{8,10},{9,11},{10,... | collective-permute-start | bytes 626696 | tf_op jit(solution)/shard_map/ppermute | solution.py:144
  126.7 8.9 %collective-permute-start.41 = (bf16[1,104,1536]{2,1,0:T(8,128)(2,1)S(1)}, bf16[1,104,1536]{2,1,0:T(8,128)(2,1)S(1)}, u32[]{:S(2)}, u32[]{:S(2)}) collective-permute-start(bf16[1,104,1536]{2,1,0:T(8,128)(2,1)S(1)} %get-tuple-element.269), channel_id=1, source_target_pairs={{0,4},{4,0},{8,12},{12,8},{16,20},{20,16},{24,28},{28,24},{1,5},{5... | collective-permute-start | bytes 958472 | tf_op jit(solution)/shard_map/ppermute | solution.py:740
  135.6 8.0 %collective-permute-start.42 = (bf16[1,104,1536]{2,1,0:T(8,128)(2,1)S(1)}, bf16[1,104,1536]{2,1,0:T(8,128)(2,1)S(1)}, u32[]{:S(2)}, u32[]{:S(2)}) collective-permute-start(bf16[1,104,1536]{2,1,0:T(8,128)(2,1)S(1)} %get-tuple-element.280), channel_id=1, source_target_pairs={{0,4},{4,0},{8,12},{12,8},{16,20},{20,16},{24,28},{28,24},{1,5},{5... | collective-permute-start | bytes 958472 | tf_op jit(solution)/shard_map/ppermute | solution.py:740
  136.1 7.3 %collective-permute-start.43 = (bf16[128,768]{1,0:T(8,128)(2,1)S(1)}, bf16[128,768]{1,0:T(8,128)(2,1)S(1)}, u32[]{:S(2)}, u32[]{:S(2)}) collective-permute-start(bf16[128,768]{1,0:T(8,128)(2,1)S(1)} %get-tuple-element.281.refs_0_), channel_id=1, source_target_pairs={{0,2},{1,3},{2,0},{3,1},{4,6},{5,7},{6,4},{7,5},{8,10},{9,11},{10,... | collective-permute-start | bytes 589832 | tf_op jit(solution)/shard_map/ppermute | solution.py:144
  144.1 7.1 %collective-permute-start.47 = (bf16[128,768]{1,0:T(8,128)(2,1)S(1)}, bf16[128,768]{1,0:T(8,128)(2,1)S(1)}, u32[]{:S(2)}, u32[]{:S(2)}) collective-permute-start(bf16[128,768]{1,0:T(8,128)(2,1)S(1)} %get-tuple-element.281.refs_0_), channel_id=1, source_target_pairs={{0,1},{1,0},{2,3},{3,2},{4,5},{5,4},{6,7},{7,6},{8,9},{9,8},{10,11... | collective-permute-start | bytes 589832 | tf_op jit(solution)/shard_map/ppermute | solution.py:144
  144.1 17.7 %collective-permute-start.50 = (bf16[104,1536]{1,0:T(8,128)(2,1)S(1)}, bf16[104,1536]{1,0:T(8,128)(2,1)S(1)}, u32[]{:S(2)}, u32[]{:S(2)}) collective-permute-start(bf16[104,1536]{1,0:T(8,128)(2,1)S(1)} %fold_shards.6), channel_id=1, source_target_pairs={{0,16},{4,20},{8,24},{12,28},{16,0},{20,4},{24,8},{28,12},{1,17},{... | collective-permute-start | bytes 958472 | tf_op jit(solution)/shard_map/ppermute | solution.py:758
  145.5 16.3 %collective-permute-start.49 = (bf16[1,104,1536]{2,1,0:T(8,128)(2,1)S(1)}, bf16[1,104,1536]{2,1,0:T(8,128)(2,1)S(1)}, u32[]{:S(2)}, u32[]{:S(2)}) collective-permute-start(bf16[1,104,1536]{2,1,0:T(8,128)(2,1)S(1)} %get-tuple-element.291), channel_id=1, source_target_pairs={{0,4},{4,0},{8,12},{12,8},{16,20},{20,16},{24,28},{28,24},{1,5},{5... | collective-permute-start | bytes 958472 | tf_op jit(solution)/shard_map/ppermute | solution.py:740
  149.3 12.7 %collective-permute-start.48 = (bf16[2,104,768]{2,1,0:T(8,128)(2,1)S(1)}, bf16[2,104,768]{2,1,0:T(8,128)(2,1)S(1)}, u32[]{:S(2)}, u32[]{:S(2)}) collective-permute-start(bf16[2,104,768]{2,1,0:T(8,128)(2,1)S(1)} %get-tuple-element.300), channel_id=1, source_target_pairs={{0,4},{4,0},{8,12},{12,8},{16,20},{20,16},{24,28},{28,24},{1,5},{5... | collective-permute-start | bytes 958472 | tf_op jit(solution)/shard_map/ppermute | solution.py:740
  150.1 11.7 %collective-permute-start.46 = (bf16[128,768]{1,0:T(8,128)(2,1)S(1)}, bf16[128,768]{1,0:T(8,128)(2,1)S(1)}, u32[]{:S(2)}, u32[]{:S(2)}) collective-permute-start(bf16[128,768]{1,0:T(8,128)(2,1)S(1)} %add_convert_fusion.1), channel_id=1, source_target_pairs={{0,2},{1,3},{2,0},{3,1},{4,6},{5,7},{6,4},{7,5},{8,10},{9,11},{10,... | collective-permute-start | bytes 589832 | tf_op jit(solution)/shard_map/ppermute | solution.py:144
  162.0 12.2 %collective-permute-start.55 = (bf16[104,1536]{1,0:T(8,128)(2,1)S(1)}, bf16[104,1536]{1,0:T(8,128)(2,1)S(1)}, u32[]{:S(2)}, u32[]{:S(2)}) collective-permute-start(bf16[104,1536]{1,0:T(8,128)(2,1)S(1)} %fold_shards.7), channel_id=1, source_target_pairs={{0,24},{4,28},{8,16},{12,20},{16,8},{20,12},{24,0},{28,4},{1,25},{... | collective-permute-start | bytes 958472 | tf_op jit(solution)/shard_map/ppermute | solution.py:758
  164.4 31.1 %collective-permute-start.64 = (bf16[1,104,1536]{2,1,0:T(8,128)(2,1)S(1)}, bf16[1,104,1536]{2,1,0:T(8,128)(2,1)S(1)}, u32[]{:S(2)}, u32[]{:S(2)}) collective-permute-start(bf16[1,104,1536]{2,1,0:T(8,128)(2,1)S(1)} %get-tuple-element.336), channel_id=1, source_target_pairs={{0,4},{4,0},{8,12},{12,8},{16,20},{20,16},{24,28},{28,24},{1,5},{5... | collective-permute-start | bytes 958472 | tf_op jit(solution)/shard_map/ppermute | solution.py:740
  165.9 22.3 %collective-permute-start.51 = (bf16[128,768]{1,0:T(8,128)(2,1)S(1)}, bf16[128,768]{1,0:T(8,128)(2,1)S(1)}, u32[]{:S(2)}, u32[]{:S(2)}) collective-permute-start(bf16[128,768]{1,0:T(8,128)(2,1)S(1)} %last_sum.1.refs_4_), channel_id=1, source_target_pairs={{0,2},{1,3},{2,0},{3,1},{4,6},{5,7},{6,4},{7,5},{8,10},{9,11},{10,... | collective-permute-start | bytes 589832 | tf_op jit(solution)/shard_map/ppermute | solution.py:144
  166.4 21.8 %collective-permute-start.52 = (bf16[2,104,768]{2,1,0:T(8,128)(2,1)S(1)}, bf16[2,104,768]{2,1,0:T(8,128)(2,1)S(1)}, u32[]{:S(2)}, u32[]{:S(2)}) collective-permute-start(bf16[2,104,768]{2,1,0:T(8,128)(2,1)S(1)} %get-tuple-element.305), channel_id=1, source_target_pairs={{0,4},{4,0},{8,12},{12,8},{16,20},{20,16},{24,28},{28,24},{1,5},{5... | collective-permute-start | bytes 958472 | tf_op jit(solution)/shard_map/ppermute | solution.py:740
  167.7 17.9 %collective-permute-start.58 = (bf16[104,768]{1,0:T(8,128)(2,1)S(1)}, bf16[104,768]{1,0:T(8,128)(2,1)S(1)}, u32[]{:S(2)}, u32[]{:S(2)}) collective-permute-start(bf16[104,768]{1,0:T(8,128)(2,1)S(1)} %get-tuple-element.318), channel_id=1, source_target_pairs={{0,16},{4,20},{8,24},{12,28},{16,0},{20,4},{24,8},{28,12},{1,17},{... | collective-permute-start | bytes 479240 | tf_op jit(solution)/shard_map/ppermute | solution.py:758
  174.3 14.1 %collective-permute-start.54 = (bf16[128,768]{1,0:T(8,128)(2,1)S(1)}, bf16[128,768]{1,0:T(8,128)(2,1)S(1)}, u32[]{:S(2)}, u32[]{:S(2)}) collective-permute-start(bf16[128,768]{1,0:T(8,128)(2,1)S(1)} %add_convert_fusion), channel_id=1, source_target_pairs={{0,2},{1,3},{2,0},{3,1},{4,6},{5,7},{6,4},{7,5},{8,10},{9,11},{10,... | collective-permute-start | bytes 589832 | tf_op jit(solution)/shard_map/ppermute | solution.py:144
  185.6 8.8 %collective-permute-start.59 = (bf16[104,768]{1,0:T(8,128)(2,1)S(1)}, bf16[104,768]{1,0:T(8,128)(2,1)S(1)}, u32[]{:S(2)}, u32[]{:S(2)}) collective-permute-start(bf16[104,768]{1,0:T(8,128)(2,1)S(1)} %get-tuple-element.319), channel_id=1, source_target_pairs={{0,24},{4,28},{8,16},{12,20},{16,8},{20,12},{24,0},{28,4},{1,25},{... | collective-permute-start | bytes 479240 | tf_op jit(solution)/shard_map/ppermute | solution.py:758
  188.2 12.0 %collective-permute-start.65 = (bf16[104,1536]{1,0:T(8,128)(2,1)S(1)}, bf16[104,1536]{1,0:T(8,128)(2,1)S(1)}, u32[]{:S(2)}, u32[]{:S(2)}) collective-permute-start(bf16[104,1536]{1,0:T(8,128)(2,1)S(1)} %fold_shards.11), channel_id=1, source_target_pairs={{0,8},{4,12},{8,0},{12,4},{16,24},{20,28},{24,16},{28,20},{1,9},{5... | collective-permute-start | bytes 958472 | tf_op jit(solution)/shard_map/ppermute | solution.py:758
  188.3 12.8 %collective-permute-start.56 = (bf16[128,768]{1,0:T(8,128)(2,1)S(1)}, bf16[128,768]{1,0:T(8,128)(2,1)S(1)}, u32[]{:S(2)}, u32[]{:S(2)}) collective-permute-start(bf16[128,768]{1,0:T(8,128)(2,1)S(1)} %last_sum.1.refs_4_), channel_id=1, source_target_pairs={{0,1},{1,0},{2,3},{3,2},{4,5},{5,4},{6,7},{7,6},{8,9},{9,8},{10,11... | collective-permute-start | bytes 589832 | tf_op jit(solution)/shard_map/ppermute | solution.py:144
  188.4 12.7 %collective-permute-start.57 = (bf16[128,768]{1,0:T(8,128)(2,1)S(1)}, bf16[128,768]{1,0:T(8,128)(2,1)S(1)}, u32[]{:S(2)}, u32[]{:S(2)}) collective-permute-start(bf16[128,768]{1,0:T(8,128)(2,1)S(1)} %collective-permute-done.51.refs_5_), channel_id=1, source_target_pairs={{0,1},{1,0},{2,3},{3,2},{4,5},{5,4},{6,7},{7,6},{8,9},{9,8},{10,11... | collective-permute-start | bytes 589832 | tf_op jit(solution)/shard_map/ppermute | solution.py:144
  194.4 10.0 %collective-permute-start.60 = (bf16[128,768]{1,0:T(8,128)(2,1)S(1)}, bf16[128,768]{1,0:T(8,128)(2,1)S(1)}, u32[]{:S(2)}, u32[]{:S(2)}) collective-permute-start(bf16[128,768]{1,0:T(8,128)(2,1)S(1)} %second_norm_tangent.1.refs_0_), channel_id=1, source_target_pairs={{0,2},{1,3},{2,0},{3,1},{4,6},{5,7},{6,4},{7,5},{8,10},{9,11},{10,... | collective-permute-start | bytes 589832 | tf_op jit(solution)/shard_map/ppermute | solution.py:144
  195.5 8.0 %collective-permute-start.63 = (bf16[104,768]{1,0:T(8,128)(2,1)S(1)}, bf16[104,768]{1,0:T(8,128)(2,1)S(1)}, u32[]{:S(2)}, u32[]{:S(2)}) collective-permute-start(bf16[104,768]{1,0:T(8,128)(2,1)S(1)} %get-tuple-element.323), channel_id=1, source_target_pairs={{0,8},{4,12},{8,0},{12,4},{16,24},{20,28},{24,16},{28,20},{1,9},{5... | collective-permute-start | bytes 479240 | tf_op jit(solution)/shard_map/ppermute | solution.py:758
  (28 other events, 176.8 us)

commit v4 on v3

--- a/solution.py
+++ b/solution.py
@@ -19,6 +19,27 @@
 EXTRA = 8
 BF = jnp.bfloat16
 F32 = jnp.float32
+PLAN = {
+    "xf0": ("P1", "P4"),
+    "zf0": ("P4", "P7"),
+    "xf1": ("P4", "P7"),
+    "zf1": ("P6", "P9"),
+    "xf2": ("P2", "P7"),
+    "zf2": ("P7", None),
+    "xf3": ("P6b", "P12"),
+    "zf3": ("P11", None),
+    "xl0": ("P6", "P7"),
+    "zl0": ("P7", "P12"),
+    "xl1": ("P8", "P9"),
+    "zl1": ("P10", "P12"),
+    "r2": ("P1", "P5"),
+    "r3": ("P5", None),
+    "a0": ("P2", "P7"),
+    "a1": ("P4", "P7"),
+    "n": ("P6", None),
+    "h0": ("P6b", "P12"),
+    "h1": ("P7", "P13"),
+}
 VMEM_LIMIT = 16 * 1024 * 1024
 TILE = 256
 
@@ -99,6 +120,32 @@
     for i, ring in enumerate(rings):
         ring.front = list(joined[len(values) + 2 * i :][:2])
     return joined[0] if len(values) == 1 else joined[: len(values)]
+
+
+class Flow:
+    def __init__(self):
+        self.makers, self.values = {}, {}
+
+    def add(self, name, maker, needs, send):
+        self.makers[name] = (maker, needs, send)
+
+    def value_of(self, name):
+        return self.values[name]
+
+    def point(self, name, *values):
+        start = [key for key in PLAN if PLAN[key][0] == name and key in self.makers]
+        due = [key for key in PLAN if PLAN[key][1] == name and key in self.values]
+        inputs = {}
+        for key in start:
+            maker, needs, _ = self.makers[key]
+            inputs[key] = maker(*[self.values[need] for need in needs])
+        results = join_lists(*values, *[inputs[key] for key in start], *[self.values[key] for key in due])
+        count = len(values)
+        for key, value in zip(due, results[count + len(start) :]):
+            self.values[key] = value
+        for key, value in zip(start, results[count : count + len(start)]):
+            self.values[key] = self.makers[key][2](value)
+        return results[0] if count == 1 else results[:count]
 
 
 def ring_owner(me, index):
@@ -257,14 +304,18 @@
 
 
 def attention_tangent(
-    cols, at, where, rel, mixed, probs, context, whole, along, keep, send, tmixed, tcontext
+    count, cols, where, rel, mixed, probs, context, whole, *refs
 ):
+    tshards, refs = refs[:count], refs[count:]
+    keep, send, twhole, sems, tmixed, tcontext = refs
+    copies = shard_copies(where, tshards, twhole, sems)
+    start_all(copies)
+    wait_all(copies)
     me = where[0]
     quarter = rel.shape[0] // 4
     for third in range(3):
         part = slice(third * cols, (third + 1) * cols)
-        there = slice(at + third * cols, at + (third + 1) * cols)
-        tmixed[:, part] = dot(rel[...], along[:, there], NN).astype(BF)
+        tmixed[:, part] = dot(rel[...], twhole[:, part], NN).astype(BF)
     slots = positions(me, quarter)
     heads = cols // HEAD
     for pair in range(2):
@@ -285,7 +336,7 @@
 
     def project(cut):
         part = dot(tcontext[...], whole[cut, 3 * cols : 4 * cols], NT)
-        part = part + dot(context[...], along[cut, at + 3 * cols : at + 4 * cols], NT)
+        part = part + dot(context[...], twhole[cut, 3 * cols : 4 * cols], NT)
         halves(part, keep, send, cut)
 
     tiles(keep.shape[1], project)
@@ -537,18 +588,18 @@
     return total
 
 
-def last_sums(refs, outs):
+def last_sums(refs, outs, places):
     rows = refs[0].shape[0]
     sums = tree_sum([refs[4][...]] + [joined_sums(ref[rows:, :]) for ref in refs[1:4]])
-    for i, out in enumerate(outs):
-        out[...] = sums[i, : out.shape[0]]
+    for out, (line, start) in zip(outs, places):
+        out[...] = sums[line, start : start + out.shape[0]]
 
 
 def finish_feed_forward(hidden, *refs):
     total = last_total(refs)
     refs[5][...] = total[:, :hidden]
     refs[6][...] = total[:, hidden:]
-    last_sums(refs, refs[7:])
+    last_sums(refs, refs[7:], [(i, 0) for i in range(4)])
 
 
 def finish_attention(cols, *refs):
@@ -556,7 +607,7 @@
     for i in range(3):
         refs[5 + i][...] = total[:, i * cols : (i + 1) * cols]
     refs[8][...] = total[:, 3 * cols :].T
-    last_sums(refs, refs[9:])
+    last_sums(refs, refs[9:], [(0, 0), (1, 0), (2, 0), (3, 0), (3, 2 * cols)])
 
 
 def last_sum(keep, came, second, grad_one, out):
@@ -627,8 +678,8 @@
     lines = ((EXTRA // 2, width), F32)
     full_own = ((own, width), F32)
     attn_rows = ((width, 4 * cols), BF)
-    ff_rows = ((width, 2 * hidden + 4 * cols), BF)
-    tff_rows = ((width, 2 * hidden), BF)
+    ff_rows = ((width, 2 * hidden), BF)
+    tff_rows = ff_rows
 
     def pack(first_one, *blocks):
         return jnp.concatenate([first_one, *blocks], 1)
@@ -640,14 +691,14 @@
     attn = Ring(pack(query_weight, key_weight, value_weight, out_rows), dp)
     attn.step()
     early = attn.parts[-1]
-    tangents = (query_tangent, key_tangent, value_tangent)
+    ff = Ring(pack(after(up_weight, early), down_weight.T), dp)
     group = call(
         pack_weights,
         "pack_weights",
-        [((shard, 2 * hidden + 4 * cols), BF)],
-        (after(up_weight, early), down_weight.T, *tangents, out_tangent),
-    )
-    ff = Ring(group[0], dp)
+        [((shard, 4 * cols), BF)],
+        (after(query_tangent, early), key_tangent, value_tangent, out_tangent),
+    )
+    tattn = Ring(group[0], dp)
     tff = Ring(pack(after(up_tangent, early), down_tangent.T), dp)
     attn.step()
     join([attn, ff])
@@ -683,9 +734,8 @@
     )
     first_low = join([ff], first_low)
     ff.step()
-    pieces = spread_rows(first_low, tp, [ff])
-    pieces[3] = join([tff], pieces[3])
-    tff.step()
+    pieces = spread_rows(first_low, tp, [ff, tattn])
+    tattn.step()
     first_rel, active, slope, keep, send, ff_whole = call(
         functools.partial(feed_forward, count, hidden),
         "feed_forward",
@@ -694,31 +744,21 @@
         ff.parts,
         [arriving(count)],
     )
-    keep, send = join([tff], keep, send)
-    tff.step()
+    keep, send = join([tattn], keep, send)
+    tattn.step()
     keep, first_came, second = sum_exchange(keep, send, tp)
-    tkeep, tsend = call(
-        functools.partial(attention_tangent, cols, 2 * hidden),
-        "attention_tangent",
-        parts,
-        (after(where, keep), x_rel, mixed, probs, context, attn_whole, ff_whole),
-        (),
-        [pltpu.VMEM((rows, 3 * cols), BF), pltpu.VMEM((rows, cols), BF)],
-    )
-    second, tkeep, tsend = join([tff], second, tkeep, tsend)
-    tff.step()
+    second = join([tattn], second)
+    tattn.step()
     result, grad_two, grad_two_low, unit_two, inverse_two = call(
         second_norm,
         "second_norm",
         [((own, width), BF), full_own, piece, full_own, ((own, 128), F32)],
         (where, keep, first_came, second, params, first, out_grad),
     )
-    pieces = spread_rows(grad_two_low, tp)
-    tfirst_came = swap(tsend, tp, 1)
-    pieces[1], tfirst_came = join([], pieces[1], tfirst_came)
-    tsecond = swap(onward_sum(tkeep, tfirst_came), tp, 2)
-    pieces[3] = join([tff], pieces[3])
+    grad_two_low = join([tff], grad_two_low)
     tff.step()
+    pieces = spread_rows(grad_two_low, tp, [tattn])
+    tattn.step()
     grad_down, grad_upper, sums_up, keep, send = call(
         functools.partial(feed_forward_backward, hidden),
         "feed_forward_backward",
@@ -727,17 +767,15 @@
     )
     result_pieces = spread_rows(result, tp)
     keep, send, grad_down, grad_upper, result_pieces[1] = join(
-        [], keep, send, grad_down, grad_upper, result_pieces[1]
-    )
+        [tff, tattn], keep, send, grad_down, grad_upper, result_pieces[1]
+    )
+    tff.step()
 
     def weight_outs(total, groups):
         if paired:
             counts = [4] + [len(group) for group in groups]
             return [((count, shard + EXTRA, total), BF) for count in counts]
         return [((width, total), BF)]
-
-    def swap_shards(steps, index):
-        return lax.ppermute(steps[1 + index], "dp", xor_pairs(dp, 1)) if paired else steps[0]
 
     def fold(steps, came, group):
         if not paired:
@@ -751,13 +789,53 @@
                 outs.append(((shard + EXTRA, total), BF))
         return call(functools.partial(fold_shards, group), "fold_shards", outs, (steps[0], came))
 
-    def send_on(folded, group):
-        if not paired:
-            return folded
-        moved = [
-            lax.ppermute(value, "dp", xor_pairs(dp, 2 * z)) for value, z in zip(folded, group) if z
-        ]
-        return moved + folded[len(moved) :]
+    flow = Flow()
+
+    def x_swap(value):
+        return lax.ppermute(value, "dp", xor_pairs(dp, 1)) if paired else value
+
+    def z_moves(group):
+        def move(values):
+            if not paired:
+                return values
+            moved = [
+                lax.ppermute(value, "dp", xor_pairs(dp, 2 * z)) for value, z in zip(values, group) if z
+            ]
+            return moved + values[len(moved) :]
+
+        return move
+
+    def add_shards(prefix, steps, groups):
+        for index, group in enumerate(groups):
+            key = prefix + str(index)
+            source = steps[1 + index] if paired else steps[0]
+            flow.add("x" + key, lambda source=source: source, (), x_swap)
+
+            def folded(came, group=group):
+                return fold(steps, came, group)
+
+            flow.add("z" + key, folded, ("x" + key,), z_moves(group))
+
+    def ring_step(values):
+        tff.front = values
+        tff.step()
+        return tff.front
+
+    flow.values["r1"] = tff.front
+    for index in (2, 3):
+        flow.add(f"r{index}", lambda front: front, (f"r{index - 1}",), ring_step)
+    flow.add("a0", lambda: tsend, (), lambda value: swap(value, tp, 1))
+    flow.add("a1", lambda came: onward_sum(tkeep, came), ("a0",), lambda value: swap(value, tp, 2))
+
+    def norm_tangent(*_):
+        return call(
+            first_norm_tangent,
+            "first_norm_tangent",
+            [full_own, ((own, width), BF)],
+            (tkeep, flow.values["a0"], flow.values["a1"], params, unit_one, inverse_one),
+        )
+
+    flow.add("n", norm_tangent, ("a1",), lambda values: values)
 
     first_came = swap(send, tp, 1)
     second = swap(onward_sum(keep, first_came), tp, 2)
@@ -769,30 +847,29 @@
         (),
         [pltpu.VMEM((width, 2 * hidden), BF)],
     )
-    tfirst, tfirst_low = call(
-        first_norm_tangent,
-        "first_norm_tangent",
-        [full_own, ((own, width), BF)],
-        (tkeep, tfirst_came, tsecond, after(params, ff_steps[0]), unit_one, inverse_one),
-    )
-    second, ff_steps, tff.front, tfirst_low, result_pieces = join_lists(
-        second, ff_steps, tff.front, tfirst_low, result_pieces
-    )
-    tff.step()
+    add_shards("f", ff_steps, FF_GROUPS)
+    flow.point("P0", ff_steps[0])
+    tkeep, tsend = call(
+        functools.partial(attention_tangent, count, cols),
+        "attention_tangent",
+        parts,
+        (after(where, ff_steps[0]), x_rel, mixed, probs, context, attn_whole),
+        tattn.parts,
+        [pltpu.VMEM(*attn_rows), arriving(count)]
+        + [pltpu.VMEM((rows, 3 * cols), BF), pltpu.VMEM((rows, cols), BF)],
+    )
+    second, tkeep, tsend, result_pieces = flow.point("P1", second, tkeep, tsend, result_pieces)
     grad_one, grad_one_low = call(
         first_norm_backward,
         "first_norm_backward",
         [full_own, piece],
         (keep, first_came, second, params, grad_two, unit_one, inverse_one),
     )
-    pieces = spread_rows(grad_one_low, tp)
-    tpieces = spread_rows(tfirst_low, tp)
-    ff_two = swap_shards(ff_steps, 0)
-    pieces[3], ff_two, ff_steps = join_lists(pieces[3], ff_two, ff_steps)
-    ff_three = swap_shards(ff_steps, 1)
-    ff_two = fold(ff_steps, ff_two, FF_GROUPS[0])
-    pieces[3], ff_two = join_lists(pieces[3], ff_two)
-    ff_two = send_on(ff_two, FF_GROUPS[0])
+    grad_one_low = flow.point("P2", grad_one_low)
+    across, beside = swap(grad_one_low, tp, 2), swap(grad_one_low, tp, 1)
+    across = flow.point("P3", across)
+    pieces = [grad_one_low, across, beside, swap(across, tp, 1)]
+    pieces[3] = flow.point("P4", pieces[3])
     grad_attn, grad_mixed, sums_one, keep, send = call(
         functools.partial(attention_backward, cols),
         "attention_backward",
@@ -801,8 +878,7 @@
         (),
         [pltpu.VMEM((rows, cols), BF)],
     )
-    keep, send, ff_three, tpieces[1] = join([], keep, send, ff_three, tpieces[1])
-    ff_one = swap_shards(ff_steps, 2)
+    keep, send = flow.point("P5", keep, send)
     first_came = swap(send, tp, 1)
     last_steps = call(
         functools.partial(attention_weights, paired, cols),
@@ -812,51 +888,59 @@
         (),
         [pltpu.VMEM(*attn_rows)],
     )
-    ff_three = fold(ff_steps, ff_three, FF_GROUPS[1])
-    first_came, last_steps, tpieces[3], ff_three, ff_steps = join_lists(
-        first_came, last_steps, tpieces[3], ff_three, ff_steps
-    )
-    ff_zero = swap_shards(ff_steps, 3)
+    add_shards("l", last_steps, LAST_GROUPS)
+    first_came = flow.point("P6", first_came)
+    tfirst, tfirst_low = flow.value_of("n")
+    flow.add("h0", lambda: tfirst_low, (), lambda value: [swap(value, tp, 2), swap(value, tp, 1)])
+    flow.add("h1", lambda both: both[0], ("h0",), lambda value: swap(value, tp, 1))
+    first_came = flow.point("P6b", first_came)
     second = swap(onward_sum(keep, first_came), tp, 2)
-    last_near = swap_shards(last_steps, 0)
-    ff_three = send_on(ff_three, FF_GROUPS[1])
+    second = flow.point("P7", second)
+    (grad_input,) = call(
+        last_sum, "last_sum", [((own, width), BF)], (keep, first_came, second, grad_one)
+    )
+    grad_input = flow.point("P8", grad_input)
+    across, beside = swap(grad_input, tp, 2), swap(grad_input, tp, 1)
     tkeep, tsend = call(
         functools.partial(feed_forward_tangent, count, hidden),
         "feed_forward_tangent",
         parts,
-        (after(where, last_steps[0]), *tpieces, first_rel, active, slope, ff_whole),
+        (where, tfirst_low, *flow.value_of("h0"), flow.value_of("h1"), first_rel, active, slope, ff_whole),
         tff.parts,
         [pltpu.VMEM(*tff_rows), arriving(count)]
         + [pltpu.VMEM((rows, width), BF), pltpu.VMEM((rows, hidden), BF)],
     )
-    second, tkeep, tsend, last_near, ff_one, ff_two, last_steps = join_lists(
-        second, tkeep, tsend, last_near, ff_one, ff_two, last_steps
-    )
-    last_far = swap_shards(last_steps, 1)
+    across, tkeep, tsend = flow.point("P9", across, tkeep, tsend)
+    pieces = [grad_input, across, beside, swap(across, tp, 1)]
     tfirst_came = swap(tsend, tp, 1)
-    ff_one = send_on(fold(ff_steps, ff_one, FF_GROUPS[2]), FF_GROUPS[2])
-    (grad_input,) = call(
-        last_sum, "last_sum", [((own, width), BF)], (keep, first_came, second, grad_one)
-    )
-    pieces = spread_rows(grad_input, tp)
+    tfirst_came = flow.point("P10", tfirst_came)
     tsecond = swap(onward_sum(tkeep, tfirst_came), tp, 2)
-    last_near = send_on(fold(last_steps, last_near, LAST_GROUPS[0]), LAST_GROUPS[0])
-    pieces[1], last_far, tsecond, ff_three = join_lists(pieces[1], last_far, tsecond, ff_three)
-    last_far = send_on(fold(last_steps, last_far, LAST_GROUPS[1]), LAST_GROUPS[1])
+    tsecond = flow.point("P11", tsecond)
     (tresult,) = call(
         second_norm_tangent,
         "second_norm_tangent",
         [((own, width), BF)],
         (tkeep, tfirst_came, tsecond, params, tfirst, unit_two, inverse_two),
     )
-    tresult, last_near = join_lists(tresult, last_near)
-    tresult_pieces = spread_rows(tresult, tp)
-    ff_zero = fold(ff_steps, ff_zero, FF_GROUPS[3])
-    if paired:
-        ff_folded = [ff_zero[0], ff_one[0], ff_two[0], ff_three[0], ff_zero[1]]
-        last_folded = [last_far[1], last_far[0], *last_near, last_far[2]]
-    else:
-        ff_folded, last_folded = [ff_zero], [last_far]
+    tresult = flow.point("P12", tresult)
+    across, beside = swap(tresult, tp, 2), swap(tresult, tp, 1)
+    across = flow.point("P13", across)
+    tresult_pieces = [tresult, across, beside, swap(across, tp, 1)]
+
+    def gathered(prefix, groups):
+        found = {}
+        for index, group in enumerate(groups):
+            values = flow.value_of("z" + prefix + str(index))
+            if not paired:
+                return [values]
+            at = 0
+            for z in [z for z in group if z]:
+                found[z], at = values[at], at + 1
+            if 0 in group:
+                found[0], found[4] = values[at], values[at + 1]
+        return [found[i] for i in range(5)]
+
+    ff_folded, last_folded = gathered("f", FF_GROUPS), gathered("l", LAST_GROUPS)
 
     def finish(body, name, outs, folded):
         return call(body, name, outs, folded)
@@ -869,10 +953,13 @@
             [((shard, hidden), F32)] * 2 + [vector] * 4,
             ff_folded,
         )
-        *own_mixed, own_out, bias_out, gain_one, shift_one, mixed_sums = finish(
+        *own_mixed, own_out, bias_out, gain_one, shift_one, bias_query, bias_value = finish(
             functools.partial(finish_attention, cols),
             "finish_attention",
-            [((shard, cols), F32)] * 3 + [((cols, shard), F32)] + [vector] * 4,
+            [((shard, cols), F32)] * 3
+            + [((cols, shard), F32)]
+            + [vector] * 3
+            + [((cols,), F32)] * 2,
             last_folded,
         )
         sums_one = [bias_out, gain_one, shift_one]
@@ -890,6 +977,7 @@
         own_out = last[:, 3 * cols :].T
         sums_two = list(lax.psum(sums_up, "dp"))
         *sums_one, mixed_sums = list(lax.psum(last_steps[1], "dp"))
+        bias_query, bias_value = mixed_sums[:cols], mixed_sums[2 * cols : 3 * cols]
 
     def all_rows(*spread):
         return call(
@@ -908,10 +996,10 @@
         whole_grad,
         whole_tresult,
         own_mixed[0],
-        mixed_sums[:cols],
+        bias_query,
         own_mixed[1],
         own_mixed[2],
-        mixed_sums[2 * cols : 3 * cols],
+        bias_value,
         own_out,
         *sums_one,
         own_up,

time: 208 us -> 194 us (0.933)
  waiting for transfers between devices: 103 us -> 85.7 us
  starting transfers between devices: 53.9 us -> 62 us
  local copies, waits for them, and re-layouts: 7.45 us -> 1.9 us
    ppermute x12, waiting for transfers between devices: 37.1 us -> 27.8 us  [the longest x6 16.7 us: x_swap(): return lax.ppermute(value, 'dp', xor_pairs(dp, 1)) if paired else value]
    ppermute x12 -> x16, waiting for transfers between devices: 27.5 us -> 20.9 us  [step(): self.front[0] = lax.ppermute(self.front[0], 'dp', ahead)]
    ppermute x9 -> x12, starting transfers between devices: 7.25 us -> 12.3 us  [step(): self.front[1] = lax.ppermute(self.front[1], 'dp', behind)]
    unnamed x21 -> x17, local copies, waits for them, and re-layouts: 5.92 us -> 0.93 us
    ppermute x12, starting transfers between devices: 11.9 us -> 16.1 us  [the longest x6 12 us: move(): lax.ppermute(value, 'dp', xor_pairs(dp, 2 * z))]
    ppermute x33, waiting for transfers between devices: 27.7 us -> 23.9 us  [swap(): return lax.ppermute(block, 'tp', xor_pairs(tp, bit))]
    ppermute x9 -> x12, waiting for transfers between devices: 10.5 us -> 13.1 us  [step(): self.front[1] = lax.ppermute(self.front[1], 'dp', behind)]
    ppermute x33, starting transfers between devices: 17.8 us -> 15.6 us  [swap(): return lax.ppermute(block, 'tp', xor_pairs(tp, bit))]
  transfers between devices with their start and end apart: 66 -> 73, of which waited for: 37 -> 35; matrix products, arithmetic and copies ran while one was open for 0% -> 1% of each run, Pallas kernels for 18% -> 20%
where the time goes in v4:
time: 194 us
  waiting for transfers between devices  85.7 us (44%)
  starting transfers between devices  62 us (32%)
  Pallas kernels  40.2 us (21%)
  other arithmetic  3.01 us (2%)
    pallas_call x25, Pallas kernels, call(): pl.pallas_call(body, out_shape=[jax.ShapeDtypeStruct(shape, kind) for sha...  40.2 us
    ppermute x33, waiting for transfers between devices, swap(): return lax.ppermute(block, 'tp', xor_pairs(tp, bit))  23.9 us
    ppermute x16, waiting for transfers between devices, step(): self.front[0] = lax.ppermute(self.front[0], 'dp', ahead)  20.9 us
    ppermute x16, starting transfers between devices, step(): self.front[0] = lax.ppermute(self.front[0], 'dp', ahead)  18 us
    ppermute x6, waiting for transfers between devices, x_swap(): return lax.ppermute(value, 'dp', xor_pairs(dp, 1)) if paired else value  16.7 us
    ppermute x33, starting transfers between devices, swap(): return lax.ppermute(block, 'tp', xor_pairs(tp, bit))  15.6 us
    ppermute x12, waiting for transfers between devices, step(): self.front[1] = lax.ppermute(self.front[1], 'dp', behind)  13.1 us
    ppermute x12, starting transfers between devices, step(): self.front[1] = lax.ppermute(self.front[1], 'dp', behind)  12.3 us
  transfers between devices with their start and end apart: 73, of which 35 were waited for; matrix products, arithmetic and copies ran while one was open for 1% of the time, Pallas kernels for 20%

profile of v4, /device:TPU:0, one launch (start us, length us, event | category | flops | bytes accessed | tf_op | source)
XLA Modules:
  0.0 194.1 jit_solution(4293113789940199682)
XLA Ops:
  4.2 3.0 %collective-permute-start.2 = (bf16[96,768]{1,0:T(8,128)(2,1)S(1)}, bf16[96,768]{1,0:T(8,128)(2,1)S(1)}, u32[]{:S(2)}, u32[]{:S(2)}) collective-permute-start(bf16[96,768]{1,0:T(8,128)(2,1)S(1)} %pad_maximum_fusion.2.refs_0_), channel_id=1, source_target_pairs={{8,0},{16,8},{24,16},{28,24},{20,28},{12,20},{4,12},{0,4},{9,1},{1... | collective-permute-start | bytes 442376 | tf_op jit(solution)/shard_map/ppermute | solution.py:113
  7.4 3.8 %collective-permute-done.2.refs_2_ = bf16[96,768]{1,0:T(8,128)(2,1)S(1)} collective-permute-done((bf16[96,768]{1,0:T(8,128)(2,1)S(1)}, bf16[96,768]{1,0:T(8,128)(2,1)S(1)}, u32[]{:S(2)}, u32[]{:S(2)}) %collective-permute-start.2) | collective-permute-done | bytes 147488 | tf_op jit(solution)/shard_map/ppermute | solution.py:113
  11.2 1.7 collective-permute-start.3
  14.2 2.1 %collective-permute-done.3.refs_4_ = bf16[96,768]{1,0:T(8,128)(2,1)S(1)} collective-permute-done((bf16[96,768]{1,0:T(8,128)(2,1)S(1)}, bf16[96,768]{1,0:T(8,128)(2,1)S(1)}, u32[]{:S(2)}, u32[]{:S(2)}) %collective-permute-start.3) | collective-permute-done | bytes 147488 | tf_op jit(solution)/shard_map/ppermute | solution.py:113
  16.3 1.7 collective-permute-done.1.refs_3_
  18.3 1.7 collective-permute-start.7
  20.4 1.7 collective-permute-start.5
  22.0 6.2 %collective-permute-done.4.refs_5_ = bf16[96,768]{1,0:T(8,128)(2,1)S(1)} collective-permute-done((bf16[96,768]{1,0:T(8,128)(2,1)S(1)}, bf16[96,768]{1,0:T(8,128)(2,1)S(1)}, u32[]{:S(2)}, u32[]{:S(2)}) %collective-permute-start.4) | collective-permute-done | bytes 147488 | tf_op jit(solution)/shard_map/ppermute | solution.py:110
  29.4 4.3 %collective-permute-done.8.refs_7_ = bf16[96,768]{1,0:T(8,128)(2,1)S(1)} collective-permute-done((bf16[96,768]{1,0:T(8,128)(2,1)S(1)}, bf16[96,768]{1,0:T(8,128)(2,1)S(1)}, u32[]{:S(2)}, u32[]{:S(2)}) %collective-permute-start.8) | collective-permute-done | bytes 147488 | tf_op jit(solution)/shard_map/ppermute | solution.py:110
  33.7 1.6 collective-permute-start.10
  35.7 5.9 %attention_forward.1 = (bf16[512,768]{1,0:T(8,128)(2,1)S(1)}, bf16[512,576]{1,0:T(8,128)(2,1)S(1)}, f32[6,256,256]{2,1,0:T(8,128)S(1)}, bf16[512,192]{1,0:T(8,12...) custom-call(s32[4]{0:T(128)S(1)} %pad_add_fusion.where, ...), custom_call_target="tpu_custom_call" | custom-call | flops 1 | bytes 1 | tf_op jit(solution)/shard_map/attention_forward/pallas_call | solution.py:64
  42.0 1.8 collective-permute-start.13
  44.1 1.6 collective-permute-start.12
  45.6 5.3 %collective-permute-done.12.second = bf16[128,768]{1,0:T(8,128)(2,1)S(1)} collective-permute-done((bf16[128,768]{1,0:T(8,128)(2,1)S(1)}, bf16[128,768]{1,0:T(8,128)(2,1)S(1)}, u32[]{:S(2)}, u32[]{:S(2)}) %collective-permute-start.12) | collective-permute-done | bytes 196640 | tf_op jit(solution)/shard_map/ppermute | solution.py:191
  51.5 1.6 collective-permute-done.14.refs_10_
  53.1 1.7 collective-permute-start.16
  56.7 4.0 %collective-permute-done.15.refs_1_ = bf16[128,768]{1,0:T(8,128)(2,1)S(1)} collective-permute-done((bf16[128,768]{1,0:T(8,128)(2,1)S(1)}, bf16[128,768]{1,0:T(8,128)(2,1)S(1)}, u32[]{:S(2)}, u32[]{:S(2)}) %collective-permute-start.15) | collective-permute-done | bytes 196640 | tf_op jit(solution)/shard_map/ppermute | solution.py:191
  63.7 3.9 %feed_forward.1 = (bf16[512,768]{1,0:T(8,128)(2,1)S(1)}, bf16[512,768]{1,0:T(8,128)(2,1)S(1)}, f32[512,768]{1,0:T(8,128)S(1)}, bf16[256,768]{1,0:T(8,128)(2,1)S(...) custom-call(s32[4]{0:T(128)S(1)} %pad_add_fusion.where, f32[8,768]{1,0:T(8,128)S(1)} %reshape.39.params, ...), custom_call_target="tpu_custom_call" | custom-call | flops 1 | bytes 1 | tf_op jit(solution)/shard_map/feed_forward/pallas_call | solution.py:64
  69.1 1.7 collective-permute-done.21.came
  70.9 1.6 collective-permute-start.22
  72.5 1.6 collective-permute-start.23
  74.5 3.6 %collective-permute-done.23.refs_3_ = bf16[96,768]{1,0:T(8,128)(2,1)S(1)} collective-permute-done((bf16[96,768]{1,0:T(8,128)(2,1)S(1)}, bf16[96,768]{1,0:T(8,128)(2,1)S(1)}, u32[]{:S(2)}, u32[]{:S(2)}) %collective-permute-start.23) | collective-permute-done | bytes 147488 | tf_op jit(solution)/shard_map/ppermute | solution.py:110
  79.4 1.7 collective-permute-start.26
  83.1 1.7 collective-permute-start.31
  85.1 3.1 %collective-permute-done.27.refs_6_ = bf16[96,768]{1,0:T(8,128)(2,1)S(1)} collective-permute-done((bf16[96,768]{1,0:T(8,128)(2,1)S(1)}, bf16[96,768]{1,0:T(8,128)(2,1)S(1)}, u32[]{:S(2)}, u32[]{:S(2)}) %collective-permute-start.27) | collective-permute-done | bytes 147488 | tf_op jit(solution)/shard_map/ppermute | solution.py:113
  90.4 2.4 %feed_forward_backward.1 = (bf16[512,768]{1,0:T(8,128)(2,1)S(1)}, bf16[512,768]{1,0:T(8,128)(2,1)S(1)}, f32[4,768]{1,0:T(4,128)S(1)}, bf16[256,768]{1,0:T(8,128)(2,1)S(1)}, bf16[256,768]{1,0:T(8,128)(2,1)S(1)}) custom-call(bf16[136,768]{1,0:T(8,128)(2,1)S(1)} %get-tuple-element.231.refs_0_, bf16[136,768]{1,0:T(8,128)(2,1)S(1)} %collective-permute-done.25.refs_1_, ...), custom_call_target="tpu_custom_call" | custom-call | flops 1 | bytes 1 | tf_op jit(solution)/shard_map/feed_forward_backward/pallas_call | solution.py:64
  92.9 2.6 %collective-permute-done.30.refs_1_ = bf16[128,768]{1,0:T(8,128)(2,1)S(1)} collective-permute-done((bf16[128,768]{1,0:T(8,128)(2,1)S(1)}, bf16[128,768]{1,0:T(8,128)(2,1)S(1)}, u32[]{:S(2)}, u32[]{:S(2)}) %collective-permute-start.30) | collective-permute-done | bytes 196640 | tf_op jit(solution)/shard_map/ppermute | solution.py:191
  96.2 1.7 collective-permute-start.38
  99.8 2.5 %feed_forward_weights.1 = (bf16[4,104,1536]{2,1,0:T(8,128)(2,1)S(1)}, bf16[1,104,1536]{2,1,0:T(8,128)(2,1)S(1)}, bf16[1,104,1536]{2,1,0:T(8,128)(2,1)S(1)}, bf16...) custom-call(s32[4]{0:T(128)S(1)} %pad_add_fusion.where, bf16[512,768]{1,0:T(8,128)(2,1)S(1)} %get-tuple-element.247.rel, ...), custom_call_target="tpu_custom_call" | custom-call | flops 1 | bytes 1 | tf_op jit(solution)/shard_map/feed_forward_weights/pallas_call | solution.py:64
  102.3 5.7 %attention_tangent.1 = (bf16[256,768]{1,0:T(8,128)(2,1)S(1)}, bf16[256,768]{1,0:T(8,128)(2,1)S(1)}) custom-call(s32[4]{0:T(128)S(1)} %pad_add_fusion.where, bf16[512,768]{1,0:T(8,128)(2,1)S(1)} %get-tuple-element.205.x_rel.rel, bf16[512,576]{1,0:T(8,128)(2,1)S(1)} %get-tuple-element.255.mixed.refs_4_, f32[6,256,256]{2,1,0:T(8,128)S(1)} %get-tuple-element.256.probs.refs_5_, ...), custom_call_target="tpu_custom_call" | custom-call | flops 1 | bytes 1 | tf_op jit(solution)/shard_map/attention_tangent/pallas_call | solution.py:64
  111.7 4.7 %collective-permute-done.40.refs_1_ = bf16[136,768]{1,0:T(8,128)(2,1)S(1)} collective-permute-done((bf16[136,768]{1,0:T(8,128)(2,1)S(1)}, bf16[136,768]{1,0:T(8,128)(2,1)S(1)}, u32[]{:S(2)}, u32[]{:S(2)}) %collective-permute-start.40) | collective-permute-done | bytes 208928 | tf_op jit(solution)/shard_map/ppermute | solution.py:191
  116.4 2.7 %collective-permute-done.43.came = bf16[1,104,1536]{2,1,0:T(8,128)(2,1)S(1)} collective-permute-done((bf16[1,104,1536]{2,1,0:T(8,128)(2,1)S(1)}, bf16[1,104,1536]{2,1,0:T(8,128)(2,1)S(1)}, u32[]{:S(2)}, u32[]{:S(2)}) %collective-permute-start.43) | collective-permute-done | bytes 319520 | tf_op jit(solution)/shard_map/ppermute | solution.py:795
  120.5 4.5 %attention_backward.1 = (bf16[512,768]{1,0:T(8,128)(2,1)S(1)}, bf16[512,576]{1,0:T(8,128)(2,1)S(1)}, f32[4,768]{1,0:T(4,128)S(1)}, bf16[256,768]{1,0:T(8,128)(2,1)S(1)}, bf16[256,768]{1,0:T(8,128)(2,1)S(1)}) custom-call(bf16[136,768]{1,0:T(8,128)(2,1)S(1)} %get-tuple-element.276.refs_0_, bf16[136,768]{1,0:T(8,128)(2,1)S(1)} %collective-permute-done.40.refs_1_, ...), custom_call_target="tpu_custom_call" | custom-call | flops 1 | bytes 1 | tf_op jit(solution)/shard_map/attention_backward/pallas_call | solution.py:64
  126.1 1.6 collective-permute-start.51
  127.8 1.8 collective-permute-start.54
  129.5 2.3 %attention_weights.1 = (bf16[4,104,768]{2,1,0:T(8,128)(2,1)S(1)}, bf16[2,104,768]{2,1,0:T(8,128)(2,1)S(1)}, bf16[2,104,768]{2,1,0:T(8,128)(2,1)S(1)}) custom-call(s32[4]{0:T(128)S(1)} %pad_add_fusion.where, bf16[512,768]{1,0:T(8,128)(2,1)S(1)} %get-tuple-element.289.rel, bf16[512,576]{1,0:T(8,128)(2,1)S(1)} %get-tuple-element.290.grad, ...), custom_call_target="tpu_custom_call" | custom-call | flops 1 | bytes 1 | tf_op jit(solution)/shard_map/attention_weights/pallas_call | solution.py:64
  132.8 2.7 %collective-permute-done.48.came = bf16[1,104,1536]{2,1,0:T(8,128)(2,1)S(1)} collective-permute-done((bf16[1,104,1536]{2,1,0:T(8,128)(2,1)S(1)}, bf16[1,104,1536]{2,1,0:T(8,128)(2,1)S(1)}, u32[]{:S(2)}, u32[]{:S(2)}) %collective-permute-start.48) | collective-permute-done | bytes 319520 | tf_op jit(solution)/shard_map/ppermute | solution.py:795
  138.3 4.1 %collective-permute-done.51.came = bf16[1,104,1536]{2,1,0:T(8,128)(2,1)S(1)} collective-permute-done((bf16[1,104,1536]{2,1,0:T(8,128)(2,1)S(1)}, bf16[1,104,1536]{2,1,0:T(8,128)(2,1)S(1)}, u32[]{:S(2)}, u32[]{:S(2)}) %collective-permute-start.51) | collective-permute-done | bytes 319520 | tf_op jit(solution)/shard_map/ppermute | solution.py:795
  143.8 5.4 %collective-permute-done.52.came = bf16[2,104,768]{2,1,0:T(8,128)(2,1)S(1)} collective-permute-done((bf16[2,104,768]{2,1,0:T(8,128)(2,1)S(1)}, bf16[2,104,768]{2,1,0:T(8,128)(2,1)S(1)}, u32[]{:S(2)}, u32[]{:S(2)}) %collective-permute-start.52) | collective-permute-done | bytes 319520 | tf_op jit(solution)/shard_map/ppermute | solution.py:795
  152.4 3.2 %collective-permute-done.58.refs_15_ = bf16[96,1536]{1,0:T(8,128)(2,1)S(1)} collective-permute-done((bf16[96,1536]{1,0:T(8,128)(2,1)S(1)}, bf16[96,1536]{1,0:T(8,128)(2,1)S(1)}, u32[]{:S(2)}, u32[]{:S(2)}) %collective-permute-start.58) | collective-permute-done | bytes 294944 | tf_op jit(solution)/shard_map/ppermute | solution.py:110
  156.1 4.8 %feed_forward_tangent.1 = (bf16[256,768]{1,0:T(8,128)(2,1)S(1)}, bf16[256,768]{1,0:T(8,128)(2,1)S(1)}) custom-call(s32[4]{0:T(128)S(1)} %pad_add_fusion.where, bf16[128,768]{1,0:T(8,128)(2,1)S(1)} %get-tuple-element.305.refs_0_, bf16[128,768]{1,0:T(8,128)(2,1)S(1)} %collective-permute-done.53.refs_1_, bf16[128,768]{1,0:T(8,128)(2,1)S(1)} %collective-permute-done.56.refs_2_, ...), custom_call_target="tpu_custom_call" | custom-call | flops 1 | bytes 1 | tf_op jit(solution)/shard_map/feed_forward_tangent/pallas_call | solution.py:64
  162.0 1.6 collective-permute-done.63.came
  164.4 4.5 %collective-permute-start.66 = (bf16[104,768]{1,0:T(8,128)(2,1)S(1)}, bf16[104,768]{1,0:T(8,128)(2,1)S(1)}, u32[]{:S(2)}, u32[]{:S(2)}) collective-permute-start(bf16[104,768]{1,0:T(8,128)(2,1)S(1)} %get-tuple-element.334), channel_id=1, source_target_pairs={{0,16},{4,20},{8,24},{12,28},{16,0},{20,4},{24,8},{28,12},{1,17},{... | collective-permute-start | bytes 479240 | tf_op jit(solution)/shard_map/ppermute | solution.py:802
  168.9 1.7 collective-permute-start.67
  172.2 8.5 %collective-permute-done.66.refs_2_ = bf16[104,768]{1,0:T(8,128)(2,1)S(1)} collective-permute-done((bf16[104,768]{1,0:T(8,128)(2,1)S(1)}, bf16[104,768]{1,0:T(8,128)(2,1)S(1)}, u32[]{:S(2)}, u32[]{:S(2)}) %collective-permute-start.66) | collective-permute-done | bytes 159776 | tf_op jit(solution)/shard_map/ppermute | solution.py:802
  182.2 2.7 %collective-permute-start.72 = (bf16[104,1536]{1,0:T(8,128)(2,1)S(1)}, bf16[104,1536]{1,0:T(8,128)(2,1)S(1)}, u32[]{:S(2)}, u32[]{:S(2)}) collective-permute-start(bf16[104,1536]{1,0:T(8,128)(2,1)S(1)} %fold_shards.8), channel_id=1, source_target_pairs={{0,8},{4,12},{8,0},{12,4},{16,24},{20,28},{24,16},{28,20},{1,9},{5... | collective-permute-start | bytes 958472 | tf_op jit(solution)/shard_map/ppermute | solution.py:802
  186.9 1.7 place_rows.2
  189.5 2.1 %collective-permute-done.72.refs_1_ = bf16[104,1536]{1,0:T(8,128)(2,1)S(1)} collective-permute-done((bf16[104,1536]{1,0:T(8,128)(2,1)S(1)}, bf16[104,1536]{1,0:T(8,128)(2,1)S(1)}, u32[]{:S(2)}, u32[]{:S(2)}) %collective-permute-start.72) | collective-permute-done | bytes 319520 | tf_op jit(solution)/shard_map/ppermute | solution.py:802
  (153 shorter events, 48.7 us)
Async XLA Ops:
  4.2 6.9 %collective-permute-start.2 = (bf16[96,768]{1,0:T(8,128)(2,1)S(1)}, bf16[96,768]{1,0:T(8,128)(2,1)S(1)}, u32[]{:S(2)}, u32[]{:S(2)}) collective-permute-start(bf16[96,768]{1,0:T(8,128)(2,1)S(1)} %pad_maximum_fusion.2.refs_0_), channel_id=1, source_target_pairs={{8,0},{16,8},{24,16},{28,24},{20,28},{12,20},{4,12},{0,4},{9,1},{1... | collective-permute-start | bytes 442376 | tf_op jit(solution)/shard_map/ppermute | solution.py:113
  18.0 10.3 %collective-permute-start.6 = (bf16[96,1536]{1,0:T(8,128)(2,1)S(1)}, bf16[96,1536]{1,0:T(8,128)(2,1)S(1)}, u32[]{:S(2)}, u32[]{:S(2)}) collective-permute-start(bf16[96,1536]{1,0:T(8,128)(2,1)S(1)} %pad_maximum_fusion.refs_4_), channel_id=1, source_target_pairs={{0,8},{8,16},{16,24},{24,28},{28,20},{20,12},{12,4},{4,0},{1,9},{9... | collective-permute-start | bytes 884744 | tf_op jit(solution)/shard_map/ppermute | solution.py:110
  18.3 9.9 %collective-permute-start.7 = (bf16[96,1536]{1,0:T(8,128)(2,1)S(1)}, bf16[96,1536]{1,0:T(8,128)(2,1)S(1)}, u32[]{:S(2)}, u32[]{:S(2)}) collective-permute-start(bf16[96,1536]{1,0:T(8,128)(2,1)S(1)} %pad_maximum_fusion.refs_4_), channel_id=1, source_target_pairs={{8,0},{16,8},{24,16},{28,24},{20,28},{12,20},{4,12},{0,4},{9,1},{1... | collective-permute-start | bytes 884744 | tf_op jit(solution)/shard_map/ppermute | solution.py:113
  20.0 8.2 %collective-permute-start.4 = (bf16[96,768]{1,0:T(8,128)(2,1)S(1)}, bf16[96,768]{1,0:T(8,128)(2,1)S(1)}, u32[]{:S(2)}, u32[]{:S(2)}) collective-permute-start(bf16[96,768]{1,0:T(8,128)(2,1)S(1)} %collective-permute-done.1.refs_3_), channel_id=1, source_target_pairs={{0,8},{8,16},{16,24},{24,28},{28,20},{20,12},{12,4},{4,0},{1,9},{9... | collective-permute-start | bytes 442376 | tf_op jit(solution)/shard_map/ppermute | solution.py:110
  20.4 7.9 %collective-permute-start.5 = (bf16[96,768]{1,0:T(8,128)(2,1)S(1)}, bf16[96,768]{1,0:T(8,128)(2,1)S(1)}, u32[]{:S(2)}, u32[]{:S(2)}) collective-permute-start(bf16[96,768]{1,0:T(8,128)(2,1)S(1)} %collective-permute-done.3.refs_4_), channel_id=1, source_target_pairs={{8,0},{16,8},{24,16},{28,24},{20,28},{12,20},{4,12},{0,4},{9,1},{1... | collective-permute-start | bytes 442376 | tf_op jit(solution)/shard_map/ppermute | solution.py:113
  33.7 8.0 %collective-permute-start.10 = (bf16[96,1536]{1,0:T(8,128)(2,1)S(1)}, bf16[96,1536]{1,0:T(8,128)(2,1)S(1)}, u32[]{:S(2)}, u32[]{:S(2)}) collective-permute-start(bf16[96,1536]{1,0:T(8,128)(2,1)S(1)} %collective-permute-done.7.refs_6_), channel_id=1, source_target_pairs={{8,0},{16,8},{24,16},{28,24},{20,28},{12,20},{4,12},{0,4},{9,1},{1... | collective-permute-start | bytes 884744 | tf_op jit(solution)/shard_map/ppermute | solution.py:113
  35.3 6.7 %collective-permute-start.9 = (bf16[96,1536]{1,0:T(8,128)(2,1)S(1)}, bf16[96,1536]{1,0:T(8,128)(2,1)S(1)}, u32[]{:S(2)}, u32[]{:S(2)}) collective-permute-start(bf16[96,1536]{1,0:T(8,128)(2,1)S(1)} %collective-permute-done.6.refs_5_), channel_id=1, source_target_pairs={{0,8},{8,16},{16,24},{24,28},{28,20},{20,12},{12,4},{4,0},{1,9},{9... | collective-permute-start | bytes 884744 | tf_op jit(solution)/shard_map/ppermute | solution.py:110
  42.0 9.5 %collective-permute-start.13 = (bf16[96,1536]{1,0:T(8,128)(2,1)S(1)}, bf16[96,1536]{1,0:T(8,128)(2,1)S(1)}, u32[]{:S(2)}, u32[]{:S(2)}) collective-permute-start(bf16[96,1536]{1,0:T(8,128)(2,1)S(1)} %collective-permute-done.9.refs_7_), channel_id=1, source_target_pairs={{0,8},{8,16},{16,24},{24,28},{28,20},{20,12},{12,4},{4,0},{1,9},{9... | collective-permute-start | bytes 884744 | tf_op jit(solution)/shard_map/ppermute | solution.py:110
  43.8 9.3 %collective-permute-start.14 = (bf16[96,1536]{1,0:T(8,128)(2,1)S(1)}, bf16[96,1536]{1,0:T(8,128)(2,1)S(1)}, u32[]{:S(2)}, u32[]{:S(2)}) collective-permute-start(bf16[96,1536]{1,0:T(8,128)(2,1)S(1)} %collective-permute-done.10.refs_8_), channel_id=1, source_target_pairs={{8,0},{16,8},{24,16},{28,24},{20,28},{12,20},{4,12},{0,4},{9,1},{1... | collective-permute-start | bytes 884744 | tf_op jit(solution)/shard_map/ppermute | solution.py:113
  44.1 6.9 %collective-permute-start.12 = (bf16[128,768]{1,0:T(8,128)(2,1)S(1)}, bf16[128,768]{1,0:T(8,128)(2,1)S(1)}, u32[]{:S(2)}, u32[]{:S(2)}) collective-permute-start(bf16[128,768]{1,0:T(8,128)(2,1)S(1)} %add_convert_fusion.5), channel_id=1, source_target_pairs={{0,2},{1,3},{2,0},{3,1},{4,6},{5,7},{6,4},{7,5},{8,10},{9,11},{10,... | collective-permute-start | bytes 589832 | tf_op jit(solution)/shard_map/ppermute | solution.py:191
  53.1 8.5 %collective-permute-start.16 = (bf16[96,1536]{1,0:T(8,128)(2,1)S(1)}, bf16[96,1536]{1,0:T(8,128)(2,1)S(1)}, u32[]{:S(2)}, u32[]{:S(2)}) collective-permute-start(bf16[96,1536]{1,0:T(8,128)(2,1)S(1)} %collective-permute-done.13.refs_9_), channel_id=1, source_target_pairs={{0,8},{8,16},{16,24},{24,28},{28,20},{20,12},{12,4},{4,0},{1,9},{9... | collective-permute-start | bytes 884744 | tf_op jit(solution)/shard_map/ppermute | solution.py:110
  56.6 7.1 %collective-permute-start.17 = (bf16[128,768]{1,0:T(8,128)(2,1)S(1)}, bf16[128,768]{1,0:T(8,128)(2,1)S(1)}, u32[]{:S(2)}, u32[]{:S(2)}) collective-permute-start(bf16[128,768]{1,0:T(8,128)(2,1)S(1)} %get-tuple-element.215.refs_0_), channel_id=1, source_target_pairs={{0,1},{1,0},{2,3},{3,2},{4,5},{5,4},{6,7},{7,6},{8,9},{9,8},{10,11... | collective-permute-start | bytes 589832 | tf_op jit(solution)/shard_map/ppermute | solution.py:191
  61.7 6.3 %collective-permute-start.19 = (bf16[96,768]{1,0:T(8,128)(2,1)S(1)}, bf16[96,768]{1,0:T(8,128)(2,1)S(1)}, u32[]{:S(2)}, u32[]{:S(2)}) collective-permute-start(bf16[96,768]{1,0:T(8,128)(2,1)S(1)} %pack_weights.1.refs_0_), channel_id=1, source_target_pairs={{0,8},{8,16},{16,24},{24,28},{28,20},{20,12},{12,4},{4,0},{1,9},{9... | collective-permute-start | bytes 442376 | tf_op jit(solution)/shard_map/ppermute | solution.py:110
  63.1 6.0 %collective-permute-start.20 = (bf16[96,768]{1,0:T(8,128)(2,1)S(1)}, bf16[96,768]{1,0:T(8,128)(2,1)S(1)}, u32[]{:S(2)}, u32[]{:S(2)}) collective-permute-start(bf16[96,768]{1,0:T(8,128)(2,1)S(1)} %pack_weights.1.refs_0_), channel_id=1, source_target_pairs={{8,0},{16,8},{24,16},{28,24},{20,28},{12,20},{4,12},{0,4},{9,1},{1... | collective-permute-start | bytes 442376 | tf_op jit(solution)/shard_map/ppermute | solution.py:113
  70.9 8.5 %collective-permute-start.22 = (bf16[128,768]{1,0:T(8,128)(2,1)S(1)}, bf16[128,768]{1,0:T(8,128)(2,1)S(1)}, u32[]{:S(2)}, u32[]{:S(2)}) collective-permute-start(bf16[128,768]{1,0:T(8,128)(2,1)S(1)} %add_convert_fusion.4), channel_id=1, source_target_pairs={{0,2},{1,3},{2,0},{3,1},{4,6},{5,7},{6,4},{7,5},{8,10},{9,11},{10,... | collective-permute-start | bytes 589832 | tf_op jit(solution)/shard_map/ppermute | solution.py:191
  83.0 6.6 %collective-permute-start.28 = (bf16[136,768]{1,0:T(8,128)(2,1)S(1)}, bf16[136,768]{1,0:T(8,128)(2,1)S(1)}, u32[]{:S(2)}, u32[]{:S(2)}) collective-permute-start(bf16[136,768]{1,0:T(8,128)(2,1)S(1)} %get-tuple-element.231.refs_0_), channel_id=1, source_target_pairs={{0,1},{1,0},{2,3},{3,2},{4,5},{5,4},{6,7},{7,6},{8,9},{9,8},{10,11... | collective-permute-start | bytes 626696 | tf_op jit(solution)/shard_map/ppermute | solution.py:191
  83.1 12.4 %collective-permute-start.31 = (bf16[96,1536]{1,0:T(8,128)(2,1)S(1)}, bf16[96,1536]{1,0:T(8,128)(2,1)S(1)}, u32[]{:S(2)}, u32[]{:S(2)}) collective-permute-start(bf16[96,1536]{1,0:T(8,128)(2,1)S(1)} %pad_maximum_fusion.1.refs_8_), channel_id=1, source_target_pairs={{0,8},{8,16},{16,24},{24,28},{28,20},{20,12},{12,4},{4,0},{1,9},{9... | collective-permute-start | bytes 884744 | tf_op jit(solution)/shard_map/ppermute | solution.py:110
  84.8 10.7 %collective-permute-start.32 = (bf16[96,1536]{1,0:T(8,128)(2,1)S(1)}, bf16[96,1536]{1,0:T(8,128)(2,1)S(1)}, u32[]{:S(2)}, u32[]{:S(2)}) collective-permute-start(bf16[96,1536]{1,0:T(8,128)(2,1)S(1)} %pad_maximum_fusion.1.refs_8_), channel_id=1, source_target_pairs={{8,0},{16,8},{24,16},{28,24},{20,28},{12,20},{4,12},{0,4},{9,1},{1... | collective-permute-start | bytes 884744 | tf_op jit(solution)/shard_map/ppermute | solution.py:113
  88.1 7.3 %collective-permute-start.30 = (bf16[128,768]{1,0:T(8,128)(2,1)S(1)}, bf16[128,768]{1,0:T(8,128)(2,1)S(1)}, u32[]{:S(2)}, u32[]{:S(2)}) collective-permute-start(bf16[128,768]{1,0:T(8,128)(2,1)S(1)} %get-tuple-element.265.refs_0_), channel_id=1, source_target_pairs={{0,2},{1,3},{2,0},{3,1},{4,6},{5,7},{6,4},{7,5},{8,10},{9,11},{10,... | collective-permute-start | bytes 589832 | tf_op jit(solution)/shard_map/ppermute | solution.py:191
  89.7 6.0 %collective-permute-start.33 = (bf16[96,768]{1,0:T(8,128)(2,1)S(1)}, bf16[96,768]{1,0:T(8,128)(2,1)S(1)}, u32[]{:S(2)}, u32[]{:S(2)}) collective-permute-start(bf16[96,768]{1,0:T(8,128)(2,1)S(1)} %collective-permute-done.26.refs_5_), channel_id=1, source_target_pairs={{0,8},{8,16},{16,24},{24,28},{28,20},{20,12},{12,4},{4,0},{1,9},{9... | collective-permute-start | bytes 442376 | tf_op jit(solution)/shard_map/ppermute | solution.py:110
  95.7 12.4 %collective-permute-start.36 = (bf16[128,768]{1,0:T(8,128)(2,1)S(1)}, bf16[128,768]{1,0:T(8,128)(2,1)S(1)}, u32[]{:S(2)}, u32[]{:S(2)}) collective-permute-start(bf16[128,768]{1,0:T(8,128)(2,1)S(1)} %get-tuple-element.265.refs_0_), channel_id=1, source_target_pairs={{0,1},{1,0},{2,3},{3,2},{4,5},{5,4},{6,7},{7,6},{8,9},{9,8},{10,11... | collective-permute-start | bytes 589832 | tf_op jit(solution)/shard_map/ppermute | solution.py:191
  96.2 12.0 %collective-permute-start.37 = (bf16[128,768]{1,0:T(8,128)(2,1)S(1)}, bf16[128,768]{1,0:T(8,128)(2,1)S(1)}, u32[]{:S(2)}, u32[]{:S(2)}) collective-permute-start(bf16[128,768]{1,0:T(8,128)(2,1)S(1)} %collective-permute-done.30.refs_1_), channel_id=1, source_target_pairs={{0,1},{1,0},{2,3},{3,2},{4,5},{5,4},{6,7},{7,6},{8,9},{9,8},{10,11... | collective-permute-start | bytes 589832 | tf_op jit(solution)/shard_map/ppermute | solution.py:191
  96.2 12.0 %collective-permute-start.38 = (bf16[96,1536]{1,0:T(8,128)(2,1)S(1)}, bf16[96,1536]{1,0:T(8,128)(2,1)S(1)}, u32[]{:S(2)}, u32[]{:S(2)}) collective-permute-start(bf16[96,1536]{1,0:T(8,128)(2,1)S(1)} %collective-permute-done.31.refs_9_), channel_id=1, source_target_pairs={{0,8},{8,16},{16,24},{24,28},{28,20},{20,12},{12,4},{4,0},{1,9},{9... | collective-permute-start | bytes 884744 | tf_op jit(solution)/shard_map/ppermute | solution.py:110
  97.9 10.3 %collective-permute-start.39 = (bf16[96,1536]{1,0:T(8,128)(2,1)S(1)}, bf16[96,1536]{1,0:T(8,128)(2,1)S(1)}, u32[]{:S(2)}, u32[]{:S(2)}) collective-permute-start(bf16[96,1536]{1,0:T(8,128)(2,1)S(1)} %collective-permute-done.32.refs_10_), channel_id=1, source_target_pairs={{8,0},{16,8},{24,16},{28,24},{20,28},{12,20},{4,12},{0,4},{9,1},{1... | collective-permute-start | bytes 884744 | tf_op jit(solution)/shard_map/ppermute | solution.py:113
  98.2 9.9 %collective-permute-start.35 = (bf16[128,768]{1,0:T(8,128)(2,1)S(1)}, bf16[128,768]{1,0:T(8,128)(2,1)S(1)}, u32[]{:S(2)}, u32[]{:S(2)}) collective-permute-start(bf16[128,768]{1,0:T(8,128)(2,1)S(1)} %add_convert_fusion.3), channel_id=1, source_target_pairs={{0,2},{1,3},{2,0},{3,1},{4,6},{5,7},{6,4},{7,5},{8,10},{9,11},{10,... | collective-permute-start | bytes 589832 | tf_op jit(solution)/shard_map/ppermute | solution.py:191
  108.6 10.6 %collective-permute-start.44 = (bf16[256,768]{1,0:T(8,128)(2,1)S(1)}, bf16[256,768]{1,0:T(8,128)(2,1)S(1)}, u32[]{:S(2)}, u32[]{:S(2)}) collective-permute-start(bf16[256,768]{1,0:T(8,128)(2,1)S(1)} %get-tuple-element.280), channel_id=1, source_target_pairs={{0,1},{1,0},{2,3},{3,2},{4,5},{5,4},{6,7},{7,6},{8,9},{9,8},{10,11... | collective-permute-start | bytes 1179656 | tf_op jit(solution)/shard_map/ppermute | solution.py:191
  108.6 10.4 %collective-permute-start.43 = (bf16[1,104,1536]{2,1,0:T(8,128)(2,1)S(1)}, bf16[1,104,1536]{2,1,0:T(8,128)(2,1)S(1)}, u32[]{:S(2)}, u32[]{:S(2)}) collective-permute-start(bf16[1,104,1536]{2,1,0:T(8,128)(2,1)S(1)} %get-tuple-element.277), channel_id=1, source_target_pairs={{0,4},{4,0},{8,12},{12,8},{16,20},{20,16},{24,28},{28,24},{1,5},{5... | collective-permute-start | bytes 958472 | tf_op jit(solution)/shard_map/ppermute | solution.py:795
  109.1 7.2 %collective-permute-start.40 = (bf16[136,768]{1,0:T(8,128)(2,1)S(1)}, bf16[136,768]{1,0:T(8,128)(2,1)S(1)}, u32[]{:S(2)}, u32[]{:S(2)}) collective-permute-start(bf16[136,768]{1,0:T(8,128)(2,1)S(1)} %get-tuple-element.276.refs_0_), channel_id=1, source_target_pairs={{0,2},{1,3},{2,0},{3,1},{4,6},{5,7},{6,4},{7,5},{8,10},{9,11},{10,... | collective-permute-start | bytes 626696 | tf_op jit(solution)/shard_map/ppermute | solution.py:191
  109.6 15.3 %collective-permute-start.45 = (bf16[96,1536]{1,0:T(8,128)(2,1)S(1)}, bf16[96,1536]{1,0:T(8,128)(2,1)S(1)}, u32[]{:S(2)}, u32[]{:S(2)}) collective-permute-start(bf16[96,1536]{1,0:T(8,128)(2,1)S(1)} %collective-permute-done.38.refs_11_), channel_id=1, source_target_pairs={{0,8},{8,16},{16,24},{24,28},{28,20},{20,12},{12,4},{4,0},{1,9},{9... | collective-permute-start | bytes 884744 | tf_op jit(solution)/shard_map/ppermute | solution.py:110
  111.0 14.0 %collective-permute-start.46 = (bf16[96,1536]{1,0:T(8,128)(2,1)S(1)}, bf16[96,1536]{1,0:T(8,128)(2,1)S(1)}, u32[]{:S(2)}, u32[]{:S(2)}) collective-permute-start(bf16[96,1536]{1,0:T(8,128)(2,1)S(1)} %collective-permute-done.39.refs_12_), channel_id=1, source_target_pairs={{8,0},{16,8},{24,16},{28,24},{20,28},{12,20},{4,12},{0,4},{9,1},{1... | collective-permute-start | bytes 884744 | tf_op jit(solution)/shard_map/ppermute | solution.py:113
  125.0 10.7 %collective-permute-start.47 = (bf16[256,768]{1,0:T(8,128)(2,1)S(1)}, bf16[256,768]{1,0:T(8,128)(2,1)S(1)}, u32[]{:S(2)}, u32[]{:S(2)}) collective-permute-start(bf16[256,768]{1,0:T(8,128)(2,1)S(1)} %get-tuple-element.287), channel_id=1, source_target_pairs={{0,1},{1,0},{2,3},{3,2},{4,5},{5,4},{6,7},{7,6},{8,9},{9,8},{10,11... | collective-permute-start | bytes 1179656 | tf_op jit(solution)/shard_map/ppermute | solution.py:191
  125.2 10.4 %collective-permute-start.48 = (bf16[1,104,1536]{2,1,0:T(8,128)(2,1)S(1)}, bf16[1,104,1536]{2,1,0:T(8,128)(2,1)S(1)}, u32[]{:S(2)}, u32[]{:S(2)}) collective-permute-start(bf16[1,104,1536]{2,1,0:T(8,128)(2,1)S(1)} %get-tuple-element.288), channel_id=1, source_target_pairs={{0,4},{4,0},{8,12},{12,8},{16,20},{20,16},{24,28},{28,24},{1,5},{5... | collective-permute-start | bytes 958472 | tf_op jit(solution)/shard_map/ppermute | solution.py:795
  125.6 6.9 %collective-permute-start.49 = (bf16[128,768]{1,0:T(8,128)(2,1)S(1)}, bf16[128,768]{1,0:T(8,128)(2,1)S(1)}, u32[]{:S(2)}, u32[]{:S(2)}) collective-permute-start(bf16[128,768]{1,0:T(8,128)(2,1)S(1)} %add_convert_fusion.2), channel_id=1, source_target_pairs={{0,2},{1,3},{2,0},{3,1},{4,6},{5,7},{6,4},{7,5},{8,10},{9,11},{10,... | collective-permute-start | bytes 589832 | tf_op jit(solution)/shard_map/ppermute | solution.py:191
  126.1 16.3 %collective-permute-start.51 = (bf16[1,104,1536]{2,1,0:T(8,128)(2,1)S(1)}, bf16[1,104,1536]{2,1,0:T(8,128)(2,1)S(1)}, u32[]{:S(2)}, u32[]{:S(2)}) collective-permute-start(bf16[1,104,1536]{2,1,0:T(8,128)(2,1)S(1)} %get-tuple-element.300), channel_id=1, source_target_pairs={{0,4},{4,0},{8,12},{12,8},{16,20},{20,16},{24,28},{28,24},{1,5},{5... | collective-permute-start | bytes 958472 | tf_op jit(solution)/shard_map/ppermute | solution.py:795
  127.8 23.0 %collective-permute-start.54 = (bf16[104,1536]{1,0:T(8,128)(2,1)S(1)}, bf16[104,1536]{1,0:T(8,128)(2,1)S(1)}, u32[]{:S(2)}, u32[]{:S(2)}) collective-permute-start(bf16[104,1536]{1,0:T(8,128)(2,1)S(1)} %fold_shards.6), channel_id=1, source_target_pairs={{0,16},{4,20},{8,24},{12,28},{16,0},{20,4},{24,8},{28,12},{1,17},{... | collective-permute-start | bytes 958472 | tf_op jit(solution)/shard_map/ppermute | solution.py:802
  135.7 13.6 %collective-permute-start.52 = (bf16[2,104,768]{2,1,0:T(8,128)(2,1)S(1)}, bf16[2,104,768]{2,1,0:T(8,128)(2,1)S(1)}, u32[]{:S(2)}, u32[]{:S(2)}) collective-permute-start(bf16[2,104,768]{2,1,0:T(8,128)(2,1)S(1)} %get-tuple-element.302), channel_id=1, source_target_pairs={{0,4},{4,0},{8,12},{12,8},{16,20},{20,16},{24,28},{28,24},{1,5},{5... | collective-permute-start | bytes 958472 | tf_op jit(solution)/shard_map/ppermute | solution.py:795
  136.2 14.6 %collective-permute-start.50 = (bf16[128,768]{1,0:T(8,128)(2,1)S(1)}, bf16[128,768]{1,0:T(8,128)(2,1)S(1)}, u32[]{:S(2)}, u32[]{:S(2)}) collective-permute-start(bf16[128,768]{1,0:T(8,128)(2,1)S(1)} %add_convert_fusion.1), channel_id=1, source_target_pairs={{0,2},{1,3},{2,0},{3,1},{4,6},{5,7},{6,4},{7,5},{8,10},{9,11},{10,... | collective-permute-start | bytes 589832 | tf_op jit(solution)/shard_map/ppermute | solution.py:191
  136.8 14.0 %collective-permute-start.53 = (bf16[128,768]{1,0:T(8,128)(2,1)S(1)}, bf16[128,768]{1,0:T(8,128)(2,1)S(1)}, u32[]{:S(2)}, u32[]{:S(2)}) collective-permute-start(bf16[128,768]{1,0:T(8,128)(2,1)S(1)} %get-tuple-element.305.refs_0_), channel_id=1, source_target_pairs={{0,2},{1,3},{2,0},{3,1},{4,6},{5,7},{6,4},{7,5},{8,10},{9,11},{10,... | collective-permute-start | bytes 589832 | tf_op jit(solution)/shard_map/ppermute | solution.py:191
  142.4 13.2 %collective-permute-start.58 = (bf16[96,1536]{1,0:T(8,128)(2,1)S(1)}, bf16[96,1536]{1,0:T(8,128)(2,1)S(1)}, u32[]{:S(2)}, u32[]{:S(2)}) collective-permute-start(bf16[96,1536]{1,0:T(8,128)(2,1)S(1)} %collective-permute-done.45.refs_13_), channel_id=1, source_target_pairs={{0,8},{8,16},{16,24},{24,28},{28,20},{20,12},{12,4},{4,0},{1,9},{9... | collective-permute-start | bytes 884744 | tf_op jit(solution)/shard_map/ppermute | solution.py:110
  149.2 11.7 %collective-permute-start.59 = (bf16[104,1536]{1,0:T(8,128)(2,1)S(1)}, bf16[104,1536]{1,0:T(8,128)(2,1)S(1)}, u32[]{:S(2)}, u32[]{:S(2)}) collective-permute-start(bf16[104,1536]{1,0:T(8,128)(2,1)S(1)} %fold_shards.7), channel_id=1, source_target_pairs={{0,24},{4,28},{8,16},{12,20},{16,8},{20,12},{24,0},{28,4},{1,25},{... | collective-permute-start | bytes 958472 | tf_op jit(solution)/shard_map/ppermute | solution.py:802
  150.9 11.0 %collective-permute-start.60 = (bf16[2,104,768]{2,1,0:T(8,128)(2,1)S(1)}, bf16[2,104,768]{2,1,0:T(8,128)(2,1)S(1)}, u32[]{:S(2)}, u32[]{:S(2)}) collective-permute-start(bf16[2,104,768]{2,1,0:T(8,128)(2,1)S(1)} %get-tuple-element.316), channel_id=1, source_target_pairs={{0,4},{4,0},{8,12},{12,8},{16,20},{20,16},{24,28},{28,24},{1,5},{5... | collective-permute-start | bytes 958472 | tf_op jit(solution)/shard_map/ppermute | solution.py:795
  161.9 9.9 %collective-permute-start.65 = (bf16[1,104,1536]{2,1,0:T(8,128)(2,1)S(1)}, bf16[1,104,1536]{2,1,0:T(8,128)(2,1)S(1)}, u32[]{:S(2)}, u32[]{:S(2)}) collective-permute-start(bf16[1,104,1536]{2,1,0:T(8,128)(2,1)S(1)} %get-tuple-element.327), channel_id=1, source_target_pairs={{0,4},{4,0},{8,12},{12,8},{16,20},{20,16},{24,28},{28,24},{1,5},{5... | collective-permute-start | bytes 958472 | tf_op jit(solution)/shard_map/ppermute | solution.py:795
  163.6 8.3 %collective-permute-start.64 = (bf16[128,768]{1,0:T(8,128)(2,1)S(1)}, bf16[128,768]{1,0:T(8,128)(2,1)S(1)}, u32[]{:S(2)}, u32[]{:S(2)}) collective-permute-start(bf16[128,768]{1,0:T(8,128)(2,1)S(1)} %add_convert_fusion), channel_id=1, source_target_pairs={{0,2},{1,3},{2,0},{3,1},{4,6},{5,7},{6,4},{7,5},{8,10},{9,11},{10,... | collective-permute-start | bytes 589832 | tf_op jit(solution)/shard_map/ppermute | solution.py:191
  164.4 16.3 %collective-permute-start.66 = (bf16[104,768]{1,0:T(8,128)(2,1)S(1)}, bf16[104,768]{1,0:T(8,128)(2,1)S(1)}, u32[]{:S(2)}, u32[]{:S(2)}) collective-permute-start(bf16[104,768]{1,0:T(8,128)(2,1)S(1)} %get-tuple-element.334), channel_id=1, source_target_pairs={{0,16},{4,20},{8,24},{12,28},{16,0},{20,4},{24,8},{28,12},{1,17},{... | collective-permute-start | bytes 479240 | tf_op jit(solution)/shard_map/ppermute | solution.py:802
  168.9 11.8 %collective-permute-start.67 = (bf16[104,768]{1,0:T(8,128)(2,1)S(1)}, bf16[104,768]{1,0:T(8,128)(2,1)S(1)}, u32[]{:S(2)}, u32[]{:S(2)}) collective-permute-start(bf16[104,768]{1,0:T(8,128)(2,1)S(1)} %get-tuple-element.335), channel_id=1, source_target_pairs={{0,24},{4,28},{8,16},{12,20},{16,8},{20,12},{24,0},{28,4},{1,25},{... | collective-permute-start | bytes 479240 | tf_op jit(solution)/shard_map/ppermute | solution.py:802
  170.5 10.7 %collective-permute-start.68 = (bf16[104,768]{1,0:T(8,128)(2,1)S(1)}, bf16[104,768]{1,0:T(8,128)(2,1)S(1)}, u32[]{:S(2)}, u32[]{:S(2)}) collective-permute-start(bf16[104,768]{1,0:T(8,128)(2,1)S(1)} %get-tuple-element.336), channel_id=1, source_target_pairs={{0,8},{4,12},{8,0},{12,4},{16,24},{20,28},{24,16},{28,20},{1,9},{5... | collective-permute-start | bytes 479240 | tf_op jit(solution)/shard_map/ppermute | solution.py:802
  182.2 9.4 %collective-permute-start.72 = (bf16[104,1536]{1,0:T(8,128)(2,1)S(1)}, bf16[104,1536]{1,0:T(8,128)(2,1)S(1)}, u32[]{:S(2)}, u32[]{:S(2)}) collective-permute-start(bf16[104,1536]{1,0:T(8,128)(2,1)S(1)} %fold_shards.8), channel_id=1, source_target_pairs={{0,8},{4,12},{8,0},{12,4},{16,24},{20,28},{24,16},{28,20},{1,9},{5... | collective-permute-start | bytes 958472 | tf_op jit(solution)/shard_map/ppermute | solution.py:802
  185.4 7.1 %collective-permute-start.70 = (bf16[128,768]{1,0:T(8,128)(2,1)S(1)}, bf16[128,768]{1,0:T(8,128)(2,1)S(1)}, u32[]{:S(2)}, u32[]{:S(2)}) collective-permute-start(bf16[128,768]{1,0:T(8,128)(2,1)S(1)} %second_norm_tangent.1.refs_0_), channel_id=1, source_target_pairs={{0,1},{1,0},{2,3},{3,2},{4,5},{5,4},{6,7},{7,6},{8,9},{9,8},{10,11... | collective-permute-start | bytes 589832 | tf_op jit(solution)/shard_map/ppermute | solution.py:191
  (33 other events, 270.1 us)

commit v5 on v4

--- a/solution.py
+++ b/solution.py
@@ -23,7 +23,7 @@
     "xf0": ("P1", "P4"),
     "zf0": ("P4", "P7"),
     "xf1": ("P4", "P7"),
-    "zf1": ("P6", "P9"),
+    "zf1": ("P6b", "P9"),
     "xf2": ("P2", "P7"),
     "zf2": ("P7", None),
     "xf3": ("P6b", "P12"),
@@ -39,9 +39,10 @@
     "n": ("P6", None),
     "h0": ("P6b", "P12"),
     "h1": ("P7", "P13"),
+    "_c": ("f", "l"),
 }
 VMEM_LIMIT = 16 * 1024 * 1024
-TILE = 256
+TILE = 768
 
 NN = ((1,), (0,))
 NT = ((1,), (1,))
@@ -687,7 +688,7 @@
     def arriving(count):
         return pltpu.SemaphoreType.DMA((count,))
 
-    where, out_rows, params = join((), where, out_weight.T, params)
+    where, out_rows = join((), where, out_weight.T)
     attn = Ring(pack(query_weight, key_weight, value_weight, out_rows), dp)
     attn.step()
     early = attn.parts[-1]

time: 194 us -> 192 us (0.990)
  Pallas kernels: 40.2 us -> 34.7 us
  waiting for transfers between devices: 85.7 us -> 90.6 us
    pallas_call x25, Pallas kernels: 40.2 us -> 34.7 us  [call(): pl.pallas_call(body, out_shape=[jax.ShapeDtypeStruct(shape, kind) for sha...]
    ppermute x16, waiting for transfers between devices: 20.9 us -> 25.7 us  [step(): self.front[0] = lax.ppermute(self.front[0], 'dp', ahead)]
    ppermute x12, waiting for transfers between devices: 13.1 us -> 10.2 us  [step(): self.front[1] = lax.ppermute(self.front[1], 'dp', behind)]
    ppermute x16, starting transfers between devices: 18 us -> 15.6 us  [step(): self.front[0] = lax.ppermute(self.front[0], 'dp', ahead)]
    ppermute x6, starting transfers between devices: 12 us -> 9.8 us  [move(): lax.ppermute(value, 'dp', xor_pairs(dp, 2 * z))]
    ppermute x33, waiting for transfers between devices: 23.9 us -> 26.1 us  [swap(): return lax.ppermute(block, 'tp', xor_pairs(tp, bit))]
    ppermute x33, starting transfers between devices: 15.6 us -> 17.7 us  [swap(): return lax.ppermute(block, 'tp', xor_pairs(tp, bit))]
  transfers between devices with their start and end apart: 73 -> 73, of which waited for: 35 -> 35; matrix products, arithmetic and copies ran while one was open for 1% -> 1% of each run, Pallas kernels for 20% -> 17%
where the time goes in v5:
time: 192 us
  waiting for transfers between devices  90.6 us (47%)
  starting transfers between devices  60.6 us (32%)
  Pallas kernels  34.7 us (18%)
  other arithmetic  3.01 us (2%)
    pallas_call x25, Pallas kernels, call(): pl.pallas_call(body, out_shape=[jax.ShapeDtypeStruct(shape, kind) for sha...  34.7 us
    ppermute x33, waiting for transfers between devices, swap(): return lax.ppermute(block, 'tp', xor_pairs(tp, bit))  26.1 us
    ppermute x16, waiting for transfers between devices, step(): self.front[0] = lax.ppermute(self.front[0], 'dp', ahead)  25.7 us
    ppermute x6, waiting for transfers between devices, x_swap(): return lax.ppermute(value, 'dp', xor_pairs(dp, 1)) if paired else value  18 us
    ppermute x33, starting transfers between devices, swap(): return lax.ppermute(block, 'tp', xor_pairs(tp, bit))  17.7 us
    ppermute x16, starting transfers between devices, step(): self.front[0] = lax.ppermute(self.front[0], 'dp', ahead)  15.6 us
    ppermute x12, starting transfers between devices, step(): self.front[1] = lax.ppermute(self.front[1], 'dp', behind)  14.1 us
    ppermute x6, waiting for transfers between devices, move(): lax.ppermute(value, 'dp', xor_pairs(dp, 2 * z))  10.6 us
  transfers between devices with their start and end apart: 73, of which 35 were waited for; matrix products, arithmetic and copies ran while one was open for 1% of the time, Pallas kernels for 17%

profile of v5, /device:TPU:0, one launch (start us, length us, event | category | flops | bytes accessed | tf_op | source)
XLA Modules:
  0.0 192.1 jit_solution(9515616693998143786)
XLA Ops:
  3.3 3.0 %collective-permute-start.2 = (bf16[96,768]{1,0:T(8,128)(2,1)S(1)}, bf16[96,768]{1,0:T(8,128)(2,1)S(1)}, u32[]{:S(2)}, u32[]{:S(2)}) collective-permute-start(bf16[96,768]{1,0:T(8,128)(2,1)S(1)} %pad_maximum_fusion.2.refs_0_), channel_id=1, source_target_pairs={{8,0},{16,8},{24,16},{28,24},{20,28},{12,20},{4,12},{0,4},{9,1},{1... | collective-permute-start | bytes 442376 | tf_op jit(solution)/shard_map/ppermute | solution.py:114
  6.5 3.8 %collective-permute-done.2.refs_2_ = bf16[96,768]{1,0:T(8,128)(2,1)S(1)} collective-permute-done((bf16[96,768]{1,0:T(8,128)(2,1)S(1)}, bf16[96,768]{1,0:T(8,128)(2,1)S(1)}, u32[]{:S(2)}, u32[]{:S(2)}) %collective-permute-start.2) | collective-permute-done | bytes 147488 | tf_op jit(solution)/shard_map/ppermute | solution.py:114
  10.3 1.7 collective-permute-start.3
  13.3 3.8 %collective-permute-done.1.refs_3_ = bf16[96,768]{1,0:T(8,128)(2,1)S(1)} collective-permute-done((bf16[96,768]{1,0:T(8,128)(2,1)S(1)}, bf16[96,768]{1,0:T(8,128)(2,1)S(1)}, u32[]{:S(2)}, u32[]{:S(2)}) %collective-permute-start.1) | collective-permute-done | bytes 147488 | tf_op jit(solution)/shard_map/ppermute | solution.py:111
  17.4 1.7 collective-permute-start.7
  19.5 1.7 collective-permute-start.5
  21.1 6.2 %collective-permute-done.4.refs_5_ = bf16[96,768]{1,0:T(8,128)(2,1)S(1)} collective-permute-done((bf16[96,768]{1,0:T(8,128)(2,1)S(1)}, bf16[96,768]{1,0:T(8,128)(2,1)S(1)}, u32[]{:S(2)}, u32[]{:S(2)}) %collective-permute-start.4) | collective-permute-done | bytes 147488 | tf_op jit(solution)/shard_map/ppermute | solution.py:111
  28.5 5.6 %collective-permute-done.8.refs_7_ = bf16[96,768]{1,0:T(8,128)(2,1)S(1)} collective-permute-done((bf16[96,768]{1,0:T(8,128)(2,1)S(1)}, bf16[96,768]{1,0:T(8,128)(2,1)S(1)}, u32[]{:S(2)}, u32[]{:S(2)}) %collective-permute-start.8) | collective-permute-done | bytes 147488 | tf_op jit(solution)/shard_map/ppermute | solution.py:111
  37.0 5.1 %attention_forward.1 = (bf16[512,768]{1,0:T(8,128)(2,1)S(1)}, bf16[512,576]{1,0:T(8,128)(2,1)S(1)}, f32[6,256,256]{2,1,0:T(8,128)S(1)}, bf16[512,192]{1,0:T(8,12...) custom-call(s32[4]{0:T(128)S(1)} %pad_add_fusion.where, ...), custom_call_target="tpu_custom_call" | custom-call | flops 1 | bytes 1 | tf_op jit(solution)/shard_map/attention_forward/pallas_call | solution.py:65
  44.4 1.6 collective-permute-start.12
  46.0 5.2 %collective-permute-done.12.second = bf16[128,768]{1,0:T(8,128)(2,1)S(1)} collective-permute-done((bf16[128,768]{1,0:T(8,128)(2,1)S(1)}, bf16[128,768]{1,0:T(8,128)(2,1)S(1)}, u32[]{:S(2)}, u32[]{:S(2)}) %collective-permute-start.12) | collective-permute-done | bytes 196640 | tf_op jit(solution)/shard_map/ppermute | solution.py:192
  52.6 1.6 collective-permute-start.16
  54.3 1.5 collective-permute-start.15
  56.1 4.1 %collective-permute-done.15.refs_1_ = bf16[128,768]{1,0:T(8,128)(2,1)S(1)} collective-permute-done((bf16[128,768]{1,0:T(8,128)(2,1)S(1)}, bf16[128,768]{1,0:T(8,128)(2,1)S(1)}, u32[]{:S(2)}, u32[]{:S(2)}) %collective-permute-start.15) | collective-permute-done | bytes 196640 | tf_op jit(solution)/shard_map/ppermute | solution.py:192
  60.9 1.6 collective-permute-start.19
  63.0 3.2 %feed_forward.1 = (bf16[512,768]{1,0:T(8,128)(2,1)S(1)}, bf16[512,768]{1,0:T(8,128)(2,1)S(1)}, f32[512,768]{1,0:T(8,128)S(1)}, bf16[256,768]{1,0:T(8,128)(2,1)S(...) custom-call(s32[4]{0:T(128)S(1)} %pad_add_fusion.where, f32[8,768]{1,0:T(8,128)S(1)} %reshape.39.params, ...), custom_call_target="tpu_custom_call" | custom-call | flops 1 | bytes 1 | tf_op jit(solution)/shard_map/feed_forward/pallas_call | solution.py:65
  68.6 1.7 collective-permute-done.21.came
  70.3 1.6 collective-permute-start.22
  71.9 1.7 collective-permute-start.23
  73.9 3.6 %collective-permute-done.23.refs_3_ = bf16[96,768]{1,0:T(8,128)(2,1)S(1)} collective-permute-done((bf16[96,768]{1,0:T(8,128)(2,1)S(1)}, bf16[96,768]{1,0:T(8,128)(2,1)S(1)}, u32[]{:S(2)}, u32[]{:S(2)}) %collective-permute-start.23) | collective-permute-done | bytes 147488 | tf_op jit(solution)/shard_map/ppermute | solution.py:111
  77.5 1.4 collective-permute-done.24.refs_4_
  84.6 2.7 %collective-permute-done.27.refs_6_ = bf16[96,768]{1,0:T(8,128)(2,1)S(1)} collective-permute-done((bf16[96,768]{1,0:T(8,128)(2,1)S(1)}, bf16[96,768]{1,0:T(8,128)(2,1)S(1)}, u32[]{:S(2)}, u32[]{:S(2)}) %collective-permute-start.27) | collective-permute-done | bytes 147488 | tf_op jit(solution)/shard_map/ppermute | solution.py:114
  87.3 1.5 collective-permute-start.30
  89.6 1.5 feed_forward_backward.1
  91.2 3.4 %collective-permute-done.30.refs_1_ = bf16[128,768]{1,0:T(8,128)(2,1)S(1)} collective-permute-done((bf16[128,768]{1,0:T(8,128)(2,1)S(1)}, bf16[128,768]{1,0:T(8,128)(2,1)S(1)}, u32[]{:S(2)}, u32[]{:S(2)}) %collective-permute-start.30) | collective-permute-done | bytes 196640 | tf_op jit(solution)/shard_map/ppermute | solution.py:192
  97.8 1.6 collective-permute-start.35
  99.3 2.1 %feed_forward_weights.1 = (bf16[4,104,1536]{2,1,0:T(8,128)(2,1)S(1)}, bf16[1,104,1536]{2,1,0:T(8,128)(2,1)S(1)}, bf16[1,104,1536]{2,1,0:T(8,128)(2,1)S(1)}, bf16...) custom-call(s32[4]{0:T(128)S(1)} %pad_add_fusion.where, bf16[512,768]{1,0:T(8,128)(2,1)S(1)} %get-tuple-element.245.rel, ...), custom_call_target="tpu_custom_call" | custom-call | flops 1 | bytes 1 | tf_op jit(solution)/shard_map/feed_forward_weights/pallas_call | solution.py:65
  101.5 5.2 %attention_tangent.1 = (bf16[256,768]{1,0:T(8,128)(2,1)S(1)}, bf16[256,768]{1,0:T(8,128)(2,1)S(1)}) custom-call(s32[4]{0:T(128)S(1)} %pad_add_fusion.where, bf16[512,768]{1,0:T(8,128)(2,1)S(1)} %get-tuple-element.203.x_rel.rel, bf16[512,576]{1,0:T(8,128)(2,1)S(1)} %get-tuple-element.253.mixed.refs_4_, f32[6,256,256]{2,1,0:T(8,128)S(1)} %get-tuple-element.254.probs.refs_5_, ...), custom_call_target="tpu_custom_call" | custom-call | flops 1 | bytes 1 | tf_op jit(solution)/shard_map/attention_tangent/pallas_call | solution.py:65
  109.3 1.7 collective-permute-start.46
  110.9 3.9 %collective-permute-done.40.refs_1_ = bf16[136,768]{1,0:T(8,128)(2,1)S(1)} collective-permute-done((bf16[136,768]{1,0:T(8,128)(2,1)S(1)}, bf16[136,768]{1,0:T(8,128)(2,1)S(1)}, u32[]{:S(2)}, u32[]{:S(2)}) %collective-permute-start.40) | collective-permute-done | bytes 208928 | tf_op jit(solution)/shard_map/ppermute | solution.py:192
  114.9 2.8 %collective-permute-done.43.came = bf16[1,104,1536]{2,1,0:T(8,128)(2,1)S(1)} collective-permute-done((bf16[1,104,1536]{2,1,0:T(8,128)(2,1)S(1)}, bf16[1,104,1536]{2,1,0:T(8,128)(2,1)S(1)}, u32[]{:S(2)}, u32[]{:S(2)}) %collective-permute-start.43) | collective-permute-done | bytes 319520 | tf_op jit(solution)/shard_map/ppermute | solution.py:796
  119.1 3.9 %attention_backward.1 = (bf16[512,768]{1,0:T(8,128)(2,1)S(1)}, bf16[512,576]{1,0:T(8,128)(2,1)S(1)}, f32[4,768]{1,0:T(4,128)S(1)}, bf16[256,768]{1,0:T(8,128)(2,1)S(1)}, bf16[256,768]{1,0:T(8,128)(2,1)S(1)}) custom-call(bf16[136,768]{1,0:T(8,128)(2,1)S(1)} %get-tuple-element.274.refs_0_, bf16[136,768]{1,0:T(8,128)(2,1)S(1)} %collective-permute-done.40.refs_1_, ...), custom_call_target="tpu_custom_call" | custom-call | flops 1 | bytes 1 | tf_op jit(solution)/shard_map/attention_backward/pallas_call | solution.py:65
  127.3 1.7 attention_weights.1
  129.0 1.9 collective-permute-done.48.second
  131.2 2.7 %collective-permute-done.49.came = bf16[1,104,1536]{2,1,0:T(8,128)(2,1)S(1)} collective-permute-done((bf16[1,104,1536]{2,1,0:T(8,128)(2,1)S(1)}, bf16[1,104,1536]{2,1,0:T(8,128)(2,1)S(1)}, u32[]{:S(2)}, u32[]{:S(2)}) %collective-permute-start.49) | collective-permute-done | bytes 319520 | tf_op jit(solution)/shard_map/ppermute | solution.py:796
  136.5 4.2 %collective-permute-done.51.came = bf16[1,104,1536]{2,1,0:T(8,128)(2,1)S(1)} collective-permute-done((bf16[1,104,1536]{2,1,0:T(8,128)(2,1)S(1)}, bf16[1,104,1536]{2,1,0:T(8,128)(2,1)S(1)}, u32[]{:S(2)}, u32[]{:S(2)}) %collective-permute-start.51) | collective-permute-done | bytes 319520 | tf_op jit(solution)/shard_map/ppermute | solution.py:796
  141.5 6.0 %collective-permute-done.52.came = bf16[2,104,768]{2,1,0:T(8,128)(2,1)S(1)} collective-permute-done((bf16[2,104,768]{2,1,0:T(8,128)(2,1)S(1)}, bf16[2,104,768]{2,1,0:T(8,128)(2,1)S(1)}, u32[]{:S(2)}, u32[]{:S(2)}) %collective-permute-start.52) | collective-permute-done | bytes 319520 | tf_op jit(solution)/shard_map/ppermute | solution.py:796
  150.5 3.4 %collective-permute-done.58.refs_15_ = bf16[96,1536]{1,0:T(8,128)(2,1)S(1)} collective-permute-done((bf16[96,1536]{1,0:T(8,128)(2,1)S(1)}, bf16[96,1536]{1,0:T(8,128)(2,1)S(1)}, u32[]{:S(2)}, u32[]{:S(2)}) %collective-permute-start.58) | collective-permute-done | bytes 294944 | tf_op jit(solution)/shard_map/ppermute | solution.py:111
  154.8 3.8 %feed_forward_tangent.1 = (bf16[256,768]{1,0:T(8,128)(2,1)S(1)}, bf16[256,768]{1,0:T(8,128)(2,1)S(1)}) custom-call(s32[4]{0:T(128)S(1)} %pad_add_fusion.where, bf16[128,768]{1,0:T(8,128)(2,1)S(1)} %get-tuple-element.303.refs_0_, bf16[128,768]{1,0:T(8,128)(2,1)S(1)} %collective-permute-done.53.refs_1_, bf16[128,768]{1,0:T(8,128)(2,1)S(1)} %collective-permute-done.56.refs_2_, ...), custom_call_target="tpu_custom_call" | custom-call | flops 1 | bytes 1 | tf_op jit(solution)/shard_map/feed_forward_tangent/pallas_call | solution.py:65
  160.4 1.6 collective-permute-done.63.came
  163.1 3.9 %collective-permute-start.66 = (bf16[104,768]{1,0:T(8,128)(2,1)S(1)}, bf16[104,768]{1,0:T(8,128)(2,1)S(1)}, u32[]{:S(2)}, u32[]{:S(2)}) collective-permute-start(bf16[104,768]{1,0:T(8,128)(2,1)S(1)} %get-tuple-element.332), channel_id=1, source_target_pairs={{0,16},{4,20},{8,24},{12,28},{16,0},{20,4},{24,8},{28,12},{1,17},{... | collective-permute-start | bytes 479240 | tf_op jit(solution)/shard_map/ppermute | solution.py:803
  168.2 2.0 %collective-permute-done.65.came = bf16[1,104,1536]{2,1,0:T(8,128)(2,1)S(1)} collective-permute-done((bf16[1,104,1536]{2,1,0:T(8,128)(2,1)S(1)}, bf16[1,104,1536]{2,1,0:T(8,128)(2,1)S(1)}, u32[]{:S(2)}, u32[]{:S(2)}) %collective-permute-start.65) | collective-permute-done | bytes 319520 | tf_op jit(solution)/shard_map/ppermute | solution.py:796
  170.7 8.1 %collective-permute-done.66.refs_2_ = bf16[104,768]{1,0:T(8,128)(2,1)S(1)} collective-permute-done((bf16[104,768]{1,0:T(8,128)(2,1)S(1)}, bf16[104,768]{1,0:T(8,128)(2,1)S(1)}, u32[]{:S(2)}, u32[]{:S(2)}) %collective-permute-start.66) | collective-permute-done | bytes 159776 | tf_op jit(solution)/shard_map/ppermute | solution.py:803
  180.2 2.7 %collective-permute-start.72 = (bf16[104,1536]{1,0:T(8,128)(2,1)S(1)}, bf16[104,1536]{1,0:T(8,128)(2,1)S(1)}, u32[]{:S(2)}, u32[]{:S(2)}) collective-permute-start(bf16[104,1536]{1,0:T(8,128)(2,1)S(1)} %fold_shards.8), channel_id=1, source_target_pairs={{0,8},{4,12},{8,0},{12,4},{16,24},{20,28},{24,16},{28,20},{1,9},{5... | collective-permute-start | bytes 958472 | tf_op jit(solution)/shard_map/ppermute | solution.py:803
  183.4 1.6 collective-permute-done.69.refs_1_
  185.0 1.7 place_rows.2
  187.6 2.0 %collective-permute-done.72.refs_1_ = bf16[104,1536]{1,0:T(8,128)(2,1)S(1)} collective-permute-done((bf16[104,1536]{1,0:T(8,128)(2,1)S(1)}, bf16[104,1536]{1,0:T(8,128)(2,1)S(1)}, u32[]{:S(2)}, u32[]{:S(2)}) %collective-permute-start.72) | collective-permute-done | bytes 319520 | tf_op jit(solution)/shard_map/ppermute | solution.py:803
  190.5 1.5 place_rows.3
  (153 shorter events, 50.4 us)
Async XLA Ops:
  3.3 6.9 %collective-permute-start.2 = (bf16[96,768]{1,0:T(8,128)(2,1)S(1)}, bf16[96,768]{1,0:T(8,128)(2,1)S(1)}, u32[]{:S(2)}, u32[]{:S(2)}) collective-permute-start(bf16[96,768]{1,0:T(8,128)(2,1)S(1)} %pad_maximum_fusion.2.refs_0_), channel_id=1, source_target_pairs={{8,0},{16,8},{24,16},{28,24},{20,28},{12,20},{4,12},{0,4},{9,1},{1... | collective-permute-start | bytes 442376 | tf_op jit(solution)/shard_map/ppermute | solution.py:114
  10.3 6.8 %collective-permute-start.3 = (bf16[96,768]{1,0:T(8,128)(2,1)S(1)}, bf16[96,768]{1,0:T(8,128)(2,1)S(1)}, u32[]{:S(2)}, u32[]{:S(2)}) collective-permute-start(bf16[96,768]{1,0:T(8,128)(2,1)S(1)} %collective-permute-done.2.refs_2_), channel_id=1, source_target_pairs={{8,0},{16,8},{24,16},{28,24},{20,28},{12,20},{4,12},{0,4},{9,1},{1... | collective-permute-start | bytes 442376 | tf_op jit(solution)/shard_map/ppermute | solution.py:114
  17.1 10.3 %collective-permute-start.6 = (bf16[96,1536]{1,0:T(8,128)(2,1)S(1)}, bf16[96,1536]{1,0:T(8,128)(2,1)S(1)}, u32[]{:S(2)}, u32[]{:S(2)}) collective-permute-start(bf16[96,1536]{1,0:T(8,128)(2,1)S(1)} %pad_maximum_fusion.refs_4_), channel_id=1, source_target_pairs={{0,8},{8,16},{16,24},{24,28},{28,20},{20,12},{12,4},{4,0},{1,9},{9... | collective-permute-start | bytes 884744 | tf_op jit(solution)/shard_map/ppermute | solution.py:111
  17.4 9.9 %collective-permute-start.7 = (bf16[96,1536]{1,0:T(8,128)(2,1)S(1)}, bf16[96,1536]{1,0:T(8,128)(2,1)S(1)}, u32[]{:S(2)}, u32[]{:S(2)}) collective-permute-start(bf16[96,1536]{1,0:T(8,128)(2,1)S(1)} %pad_maximum_fusion.refs_4_), channel_id=1, source_target_pairs={{8,0},{16,8},{24,16},{28,24},{20,28},{12,20},{4,12},{0,4},{9,1},{1... | collective-permute-start | bytes 884744 | tf_op jit(solution)/shard_map/ppermute | solution.py:114
  19.1 8.2 %collective-permute-start.4 = (bf16[96,768]{1,0:T(8,128)(2,1)S(1)}, bf16[96,768]{1,0:T(8,128)(2,1)S(1)}, u32[]{:S(2)}, u32[]{:S(2)}) collective-permute-start(bf16[96,768]{1,0:T(8,128)(2,1)S(1)} %collective-permute-done.1.refs_3_), channel_id=1, source_target_pairs={{0,8},{8,16},{16,24},{24,28},{28,20},{20,12},{12,4},{4,0},{1,9},{9... | collective-permute-start | bytes 442376 | tf_op jit(solution)/shard_map/ppermute | solution.py:111
  19.5 7.9 %collective-permute-start.5 = (bf16[96,768]{1,0:T(8,128)(2,1)S(1)}, bf16[96,768]{1,0:T(8,128)(2,1)S(1)}, u32[]{:S(2)}, u32[]{:S(2)}) collective-permute-start(bf16[96,768]{1,0:T(8,128)(2,1)S(1)} %collective-permute-done.3.refs_4_), channel_id=1, source_target_pairs={{8,0},{16,8},{24,16},{28,24},{20,28},{12,20},{4,12},{0,4},{9,1},{1... | collective-permute-start | bytes 442376 | tf_op jit(solution)/shard_map/ppermute | solution.py:114
  27.3 6.8 %collective-permute-start.8 = (bf16[96,768]{1,0:T(8,128)(2,1)S(1)}, bf16[96,768]{1,0:T(8,128)(2,1)S(1)}, u32[]{:S(2)}, u32[]{:S(2)}) collective-permute-start(bf16[96,768]{1,0:T(8,128)(2,1)S(1)} %collective-permute-done.4.refs_5_), channel_id=1, source_target_pairs={{0,8},{8,16},{16,24},{24,28},{28,20},{20,12},{12,4},{4,0},{1,9},{9... | collective-permute-start | bytes 442376 | tf_op jit(solution)/shard_map/ppermute | solution.py:111
  34.1 8.1 %collective-permute-start.9 = (bf16[96,1536]{1,0:T(8,128)(2,1)S(1)}, bf16[96,1536]{1,0:T(8,128)(2,1)S(1)}, u32[]{:S(2)}, u32[]{:S(2)}) collective-permute-start(bf16[96,1536]{1,0:T(8,128)(2,1)S(1)} %collective-permute-done.6.refs_5_), channel_id=1, source_target_pairs={{0,8},{8,16},{16,24},{24,28},{28,20},{20,12},{12,4},{4,0},{1,9},{9... | collective-permute-start | bytes 884744 | tf_op jit(solution)/shard_map/ppermute | solution.py:111
  35.2 7.0 %collective-permute-start.10 = (bf16[96,1536]{1,0:T(8,128)(2,1)S(1)}, bf16[96,1536]{1,0:T(8,128)(2,1)S(1)}, u32[]{:S(2)}, u32[]{:S(2)}) collective-permute-start(bf16[96,1536]{1,0:T(8,128)(2,1)S(1)} %collective-permute-done.7.refs_6_), channel_id=1, source_target_pairs={{8,0},{16,8},{24,16},{28,24},{20,28},{12,20},{4,12},{0,4},{9,1},{1... | collective-permute-start | bytes 884744 | tf_op jit(solution)/shard_map/ppermute | solution.py:114
  42.3 9.4 %collective-permute-start.13 = (bf16[96,1536]{1,0:T(8,128)(2,1)S(1)}, bf16[96,1536]{1,0:T(8,128)(2,1)S(1)}, u32[]{:S(2)}, u32[]{:S(2)}) collective-permute-start(bf16[96,1536]{1,0:T(8,128)(2,1)S(1)} %collective-permute-done.9.refs_7_), channel_id=1, source_target_pairs={{0,8},{8,16},{16,24},{24,28},{28,20},{20,12},{12,4},{4,0},{1,9},{9... | collective-permute-start | bytes 884744 | tf_op jit(solution)/shard_map/ppermute | solution.py:111
  43.5 9.1 %collective-permute-start.14 = (bf16[96,1536]{1,0:T(8,128)(2,1)S(1)}, bf16[96,1536]{1,0:T(8,128)(2,1)S(1)}, u32[]{:S(2)}, u32[]{:S(2)}) collective-permute-start(bf16[96,1536]{1,0:T(8,128)(2,1)S(1)} %collective-permute-done.10.refs_8_), channel_id=1, source_target_pairs={{8,0},{16,8},{24,16},{28,24},{20,28},{12,20},{4,12},{0,4},{9,1},{1... | collective-permute-start | bytes 884744 | tf_op jit(solution)/shard_map/ppermute | solution.py:114
  44.4 6.8 %collective-permute-start.12 = (bf16[128,768]{1,0:T(8,128)(2,1)S(1)}, bf16[128,768]{1,0:T(8,128)(2,1)S(1)}, u32[]{:S(2)}, u32[]{:S(2)}) collective-permute-start(bf16[128,768]{1,0:T(8,128)(2,1)S(1)} %add_convert_fusion.5), channel_id=1, source_target_pairs={{0,2},{1,3},{2,0},{3,1},{4,6},{5,7},{6,4},{7,5},{8,10},{9,11},{10,... | collective-permute-start | bytes 589832 | tf_op jit(solution)/shard_map/ppermute | solution.py:192
  52.6 8.3 %collective-permute-start.16 = (bf16[96,1536]{1,0:T(8,128)(2,1)S(1)}, bf16[96,1536]{1,0:T(8,128)(2,1)S(1)}, u32[]{:S(2)}, u32[]{:S(2)}) collective-permute-start(bf16[96,1536]{1,0:T(8,128)(2,1)S(1)} %collective-permute-done.13.refs_9_), channel_id=1, source_target_pairs={{0,8},{8,16},{16,24},{24,28},{28,20},{20,12},{12,4},{4,0},{1,9},{9... | collective-permute-start | bytes 884744 | tf_op jit(solution)/shard_map/ppermute | solution.py:111
  56.0 7.0 %collective-permute-start.17 = (bf16[128,768]{1,0:T(8,128)(2,1)S(1)}, bf16[128,768]{1,0:T(8,128)(2,1)S(1)}, u32[]{:S(2)}, u32[]{:S(2)}) collective-permute-start(bf16[128,768]{1,0:T(8,128)(2,1)S(1)} %get-tuple-element.213.refs_0_), channel_id=1, source_target_pairs={{0,1},{1,0},{2,3},{3,2},{4,5},{5,4},{6,7},{7,6},{8,9},{9,8},{10,11... | collective-permute-start | bytes 589832 | tf_op jit(solution)/shard_map/ppermute | solution.py:192
  70.3 8.6 %collective-permute-start.22 = (bf16[128,768]{1,0:T(8,128)(2,1)S(1)}, bf16[128,768]{1,0:T(8,128)(2,1)S(1)}, u32[]{:S(2)}, u32[]{:S(2)}) collective-permute-start(bf16[128,768]{1,0:T(8,128)(2,1)S(1)} %add_convert_fusion.4), channel_id=1, source_target_pairs={{0,2},{1,3},{2,0},{3,1},{4,6},{5,7},{6,4},{7,5},{8,10},{9,11},{10,... | collective-permute-start | bytes 589832 | tf_op jit(solution)/shard_map/ppermute | solution.py:192
  82.6 6.3 %collective-permute-start.28 = (bf16[136,768]{1,0:T(8,128)(2,1)S(1)}, bf16[136,768]{1,0:T(8,128)(2,1)S(1)}, u32[]{:S(2)}, u32[]{:S(2)}) collective-permute-start(bf16[136,768]{1,0:T(8,128)(2,1)S(1)} %get-tuple-element.229.refs_0_), channel_id=1, source_target_pairs={{0,1},{1,0},{2,3},{3,2},{4,5},{5,4},{6,7},{7,6},{8,9},{9,8},{10,11... | collective-permute-start | bytes 626696 | tf_op jit(solution)/shard_map/ppermute | solution.py:192
  82.6 12.1 %collective-permute-start.31 = (bf16[96,1536]{1,0:T(8,128)(2,1)S(1)}, bf16[96,1536]{1,0:T(8,128)(2,1)S(1)}, u32[]{:S(2)}, u32[]{:S(2)}) collective-permute-start(bf16[96,1536]{1,0:T(8,128)(2,1)S(1)} %pad_maximum_fusion.1.refs_8_), channel_id=1, source_target_pairs={{0,8},{8,16},{16,24},{24,28},{28,20},{20,12},{12,4},{4,0},{1,9},{9... | collective-permute-start | bytes 884744 | tf_op jit(solution)/shard_map/ppermute | solution.py:111
  84.1 10.6 %collective-permute-start.32 = (bf16[96,1536]{1,0:T(8,128)(2,1)S(1)}, bf16[96,1536]{1,0:T(8,128)(2,1)S(1)}, u32[]{:S(2)}, u32[]{:S(2)}) collective-permute-start(bf16[96,1536]{1,0:T(8,128)(2,1)S(1)} %pad_maximum_fusion.1.refs_8_), channel_id=1, source_target_pairs={{8,0},{16,8},{24,16},{28,24},{20,28},{12,20},{4,12},{0,4},{9,1},{1... | collective-permute-start | bytes 884744 | tf_op jit(solution)/shard_map/ppermute | solution.py:114
  87.3 7.3 %collective-permute-start.30 = (bf16[128,768]{1,0:T(8,128)(2,1)S(1)}, bf16[128,768]{1,0:T(8,128)(2,1)S(1)}, u32[]{:S(2)}, u32[]{:S(2)}) collective-permute-start(bf16[128,768]{1,0:T(8,128)(2,1)S(1)} %get-tuple-element.263.refs_0_), channel_id=1, source_target_pairs={{0,2},{1,3},{2,0},{3,1},{4,6},{5,7},{6,4},{7,5},{8,10},{9,11},{10,... | collective-permute-start | bytes 589832 | tf_op jit(solution)/shard_map/ppermute | solution.py:192
  88.8 6.3 %collective-permute-start.33 = (bf16[96,768]{1,0:T(8,128)(2,1)S(1)}, bf16[96,768]{1,0:T(8,128)(2,1)S(1)}, u32[]{:S(2)}, u32[]{:S(2)}) collective-permute-start(bf16[96,768]{1,0:T(8,128)(2,1)S(1)} %collective-permute-done.26.refs_5_), channel_id=1, source_target_pairs={{0,8},{8,16},{16,24},{24,28},{28,20},{20,12},{12,4},{4,0},{1,9},{9... | collective-permute-start | bytes 442376 | tf_op jit(solution)/shard_map/ppermute | solution.py:111
  95.2 11.5 %collective-permute-start.36 = (bf16[128,768]{1,0:T(8,128)(2,1)S(1)}, bf16[128,768]{1,0:T(8,128)(2,1)S(1)}, u32[]{:S(2)}, u32[]{:S(2)}) collective-permute-start(bf16[128,768]{1,0:T(8,128)(2,1)S(1)} %get-tuple-element.263.refs_0_), channel_id=1, source_target_pairs={{0,1},{1,0},{2,3},{3,2},{4,5},{5,4},{6,7},{7,6},{8,9},{9,8},{10,11... | collective-permute-start | bytes 589832 | tf_op jit(solution)/shard_map/ppermute | solution.py:192
  95.7 11.0 %collective-permute-start.37 = (bf16[128,768]{1,0:T(8,128)(2,1)S(1)}, bf16[128,768]{1,0:T(8,128)(2,1)S(1)}, u32[]{:S(2)}, u32[]{:S(2)}) collective-permute-start(bf16[128,768]{1,0:T(8,128)(2,1)S(1)} %collective-permute-done.30.refs_1_), channel_id=1, source_target_pairs={{0,1},{1,0},{2,3},{3,2},{4,5},{5,4},{6,7},{7,6},{8,9},{9,8},{10,11... | collective-permute-start | bytes 589832 | tf_op jit(solution)/shard_map/ppermute | solution.py:192
  95.7 11.0 %collective-permute-start.38 = (bf16[96,1536]{1,0:T(8,128)(2,1)S(1)}, bf16[96,1536]{1,0:T(8,128)(2,1)S(1)}, u32[]{:S(2)}, u32[]{:S(2)}) collective-permute-start(bf16[96,1536]{1,0:T(8,128)(2,1)S(1)} %collective-permute-done.31.refs_9_), channel_id=1, source_target_pairs={{0,8},{8,16},{16,24},{24,28},{28,20},{20,12},{12,4},{4,0},{1,9},{9... | collective-permute-start | bytes 884744 | tf_op jit(solution)/shard_map/ppermute | solution.py:111
  97.0 9.7 %collective-permute-start.39 = (bf16[96,1536]{1,0:T(8,128)(2,1)S(1)}, bf16[96,1536]{1,0:T(8,128)(2,1)S(1)}, u32[]{:S(2)}, u32[]{:S(2)}) collective-permute-start(bf16[96,1536]{1,0:T(8,128)(2,1)S(1)} %collective-permute-done.32.refs_10_), channel_id=1, source_target_pairs={{8,0},{16,8},{24,16},{28,24},{20,28},{12,20},{4,12},{0,4},{9,1},{1... | collective-permute-start | bytes 884744 | tf_op jit(solution)/shard_map/ppermute | solution.py:114
  97.8 9.0 %collective-permute-start.35 = (bf16[128,768]{1,0:T(8,128)(2,1)S(1)}, bf16[128,768]{1,0:T(8,128)(2,1)S(1)}, u32[]{:S(2)}, u32[]{:S(2)}) collective-permute-start(bf16[128,768]{1,0:T(8,128)(2,1)S(1)} %add_convert_fusion.3), channel_id=1, source_target_pairs={{0,2},{1,3},{2,0},{3,1},{4,6},{5,7},{6,4},{7,5},{8,10},{9,11},{10,... | collective-permute-start | bytes 589832 | tf_op jit(solution)/shard_map/ppermute | solution.py:192
  107.1 10.6 %collective-permute-start.44 = (bf16[256,768]{1,0:T(8,128)(2,1)S(1)}, bf16[256,768]{1,0:T(8,128)(2,1)S(1)}, u32[]{:S(2)}, u32[]{:S(2)}) collective-permute-start(bf16[256,768]{1,0:T(8,128)(2,1)S(1)} %get-tuple-element.278), channel_id=1, source_target_pairs={{0,1},{1,0},{2,3},{3,2},{4,5},{5,4},{6,7},{7,6},{8,9},{9,8},{10,11... | collective-permute-start | bytes 1179656 | tf_op jit(solution)/shard_map/ppermute | solution.py:192
  107.2 10.4 %collective-permute-start.43 = (bf16[1,104,1536]{2,1,0:T(8,128)(2,1)S(1)}, bf16[1,104,1536]{2,1,0:T(8,128)(2,1)S(1)}, u32[]{:S(2)}, u32[]{:S(2)}) collective-permute-start(bf16[1,104,1536]{2,1,0:T(8,128)(2,1)S(1)} %get-tuple-element.275), channel_id=1, source_target_pairs={{0,4},{4,0},{8,12},{12,8},{16,20},{20,16},{24,28},{28,24},{1,5},{5... | collective-permute-start | bytes 958472 | tf_op jit(solution)/shard_map/ppermute | solution.py:796
  107.6 7.2 %collective-permute-start.40 = (bf16[136,768]{1,0:T(8,128)(2,1)S(1)}, bf16[136,768]{1,0:T(8,128)(2,1)S(1)}, u32[]{:S(2)}, u32[]{:S(2)}) collective-permute-start(bf16[136,768]{1,0:T(8,128)(2,1)S(1)} %get-tuple-element.274.refs_0_), channel_id=1, source_target_pairs={{0,2},{1,3},{2,0},{3,1},{4,6},{5,7},{6,4},{7,5},{8,10},{9,11},{10,... | collective-permute-start | bytes 626696 | tf_op jit(solution)/shard_map/ppermute | solution.py:192
  108.9 14.6 %collective-permute-start.45 = (bf16[96,1536]{1,0:T(8,128)(2,1)S(1)}, bf16[96,1536]{1,0:T(8,128)(2,1)S(1)}, u32[]{:S(2)}, u32[]{:S(2)}) collective-permute-start(bf16[96,1536]{1,0:T(8,128)(2,1)S(1)} %collective-permute-done.38.refs_11_), channel_id=1, source_target_pairs={{0,8},{8,16},{16,24},{24,28},{28,20},{20,12},{12,4},{4,0},{1,9},{9... | collective-permute-start | bytes 884744 | tf_op jit(solution)/shard_map/ppermute | solution.py:111
  109.3 14.2 %collective-permute-start.46 = (bf16[96,1536]{1,0:T(8,128)(2,1)S(1)}, bf16[96,1536]{1,0:T(8,128)(2,1)S(1)}, u32[]{:S(2)}, u32[]{:S(2)}) collective-permute-start(bf16[96,1536]{1,0:T(8,128)(2,1)S(1)} %collective-permute-done.39.refs_12_), channel_id=1, source_target_pairs={{8,0},{16,8},{24,16},{28,24},{20,28},{12,20},{4,12},{0,4},{9,1},{1... | collective-permute-start | bytes 884744 | tf_op jit(solution)/shard_map/ppermute | solution.py:114
  123.5 10.4 %collective-permute-start.47 = (bf16[256,768]{1,0:T(8,128)(2,1)S(1)}, bf16[256,768]{1,0:T(8,128)(2,1)S(1)}, u32[]{:S(2)}, u32[]{:S(2)}) collective-permute-start(bf16[256,768]{1,0:T(8,128)(2,1)S(1)} %get-tuple-element.285), channel_id=1, source_target_pairs={{0,1},{1,0},{2,3},{3,2},{4,5},{5,4},{6,7},{7,6},{8,9},{9,8},{10,11... | collective-permute-start | bytes 1179656 | tf_op jit(solution)/shard_map/ppermute | solution.py:192
  123.5 10.3 %collective-permute-start.49 = (bf16[1,104,1536]{2,1,0:T(8,128)(2,1)S(1)}, bf16[1,104,1536]{2,1,0:T(8,128)(2,1)S(1)}, u32[]{:S(2)}, u32[]{:S(2)}) collective-permute-start(bf16[1,104,1536]{2,1,0:T(8,128)(2,1)S(1)} %get-tuple-element.294), channel_id=1, source_target_pairs={{0,4},{4,0},{8,12},{12,8},{16,20},{20,16},{24,28},{28,24},{1,5},{5... | collective-permute-start | bytes 958472 | tf_op jit(solution)/shard_map/ppermute | solution.py:796
  123.8 7.0 %collective-permute-start.48 = (bf16[128,768]{1,0:T(8,128)(2,1)S(1)}, bf16[128,768]{1,0:T(8,128)(2,1)S(1)}, u32[]{:S(2)}, u32[]{:S(2)}) collective-permute-start(bf16[128,768]{1,0:T(8,128)(2,1)S(1)} %add_convert_fusion.2), channel_id=1, source_target_pairs={{0,2},{1,3},{2,0},{3,1},{4,6},{5,7},{6,4},{7,5},{8,10},{9,11},{10,... | collective-permute-start | bytes 589832 | tf_op jit(solution)/shard_map/ppermute | solution.py:192
  125.1 15.5 %collective-permute-start.51 = (bf16[1,104,1536]{2,1,0:T(8,128)(2,1)S(1)}, bf16[1,104,1536]{2,1,0:T(8,128)(2,1)S(1)}, u32[]{:S(2)}, u32[]{:S(2)}) collective-permute-start(bf16[1,104,1536]{2,1,0:T(8,128)(2,1)S(1)} %get-tuple-element.298), channel_id=1, source_target_pairs={{0,4},{4,0},{8,12},{12,8},{16,20},{20,16},{24,28},{28,24},{1,5},{5... | collective-permute-start | bytes 958472 | tf_op jit(solution)/shard_map/ppermute | solution.py:796
  126.5 22.4 %collective-permute-start.54 = (bf16[104,1536]{1,0:T(8,128)(2,1)S(1)}, bf16[104,1536]{1,0:T(8,128)(2,1)S(1)}, u32[]{:S(2)}, u32[]{:S(2)}) collective-permute-start(bf16[104,1536]{1,0:T(8,128)(2,1)S(1)} %fold_shards.6), channel_id=1, source_target_pairs={{0,16},{4,20},{8,24},{12,28},{16,0},{20,4},{24,8},{28,12},{1,17},{... | collective-permute-start | bytes 958472 | tf_op jit(solution)/shard_map/ppermute | solution.py:803
  133.9 13.6 %collective-permute-start.52 = (bf16[2,104,768]{2,1,0:T(8,128)(2,1)S(1)}, bf16[2,104,768]{2,1,0:T(8,128)(2,1)S(1)}, u32[]{:S(2)}, u32[]{:S(2)}) collective-permute-start(bf16[2,104,768]{2,1,0:T(8,128)(2,1)S(1)} %get-tuple-element.300), channel_id=1, source_target_pairs={{0,4},{4,0},{8,12},{12,8},{16,20},{20,16},{24,28},{28,24},{1,5},{5... | collective-permute-start | bytes 958472 | tf_op jit(solution)/shard_map/ppermute | solution.py:796
  134.4 14.5 %collective-permute-start.50 = (bf16[128,768]{1,0:T(8,128)(2,1)S(1)}, bf16[128,768]{1,0:T(8,128)(2,1)S(1)}, u32[]{:S(2)}, u32[]{:S(2)}) collective-permute-start(bf16[128,768]{1,0:T(8,128)(2,1)S(1)} %add_convert_fusion.1), channel_id=1, source_target_pairs={{0,2},{1,3},{2,0},{3,1},{4,6},{5,7},{6,4},{7,5},{8,10},{9,11},{10,... | collective-permute-start | bytes 589832 | tf_op jit(solution)/shard_map/ppermute | solution.py:192
  135.7 13.2 %collective-permute-start.53 = (bf16[128,768]{1,0:T(8,128)(2,1)S(1)}, bf16[128,768]{1,0:T(8,128)(2,1)S(1)}, u32[]{:S(2)}, u32[]{:S(2)}) collective-permute-start(bf16[128,768]{1,0:T(8,128)(2,1)S(1)} %get-tuple-element.303.refs_0_), channel_id=1, source_target_pairs={{0,2},{1,3},{2,0},{3,1},{4,6},{5,7},{6,4},{7,5},{8,10},{9,11},{10,... | collective-permute-start | bytes 589832 | tf_op jit(solution)/shard_map/ppermute | solution.py:192
  140.7 13.2 %collective-permute-start.58 = (bf16[96,1536]{1,0:T(8,128)(2,1)S(1)}, bf16[96,1536]{1,0:T(8,128)(2,1)S(1)}, u32[]{:S(2)}, u32[]{:S(2)}) collective-permute-start(bf16[96,1536]{1,0:T(8,128)(2,1)S(1)} %collective-permute-done.45.refs_13_), channel_id=1, source_target_pairs={{0,8},{8,16},{16,24},{24,28},{28,20},{20,12},{12,4},{4,0},{1,9},{9... | collective-permute-start | bytes 884744 | tf_op jit(solution)/shard_map/ppermute | solution.py:111
  147.5 11.2 %collective-permute-start.59 = (bf16[104,1536]{1,0:T(8,128)(2,1)S(1)}, bf16[104,1536]{1,0:T(8,128)(2,1)S(1)}, u32[]{:S(2)}, u32[]{:S(2)}) collective-permute-start(bf16[104,1536]{1,0:T(8,128)(2,1)S(1)} %fold_shards.7), channel_id=1, source_target_pairs={{0,24},{4,28},{8,16},{12,20},{16,8},{20,12},{24,0},{28,4},{1,25},{... | collective-permute-start | bytes 958472 | tf_op jit(solution)/shard_map/ppermute | solution.py:803
  149.0 11.3 %collective-permute-start.60 = (bf16[2,104,768]{2,1,0:T(8,128)(2,1)S(1)}, bf16[2,104,768]{2,1,0:T(8,128)(2,1)S(1)}, u32[]{:S(2)}, u32[]{:S(2)}) collective-permute-start(bf16[2,104,768]{2,1,0:T(8,128)(2,1)S(1)} %get-tuple-element.314), channel_id=1, source_target_pairs={{0,4},{4,0},{8,12},{12,8},{16,20},{20,16},{24,28},{28,24},{1,5},{5... | collective-permute-start | bytes 958472 | tf_op jit(solution)/shard_map/ppermute | solution.py:796
  160.3 9.9 %collective-permute-start.65 = (bf16[1,104,1536]{2,1,0:T(8,128)(2,1)S(1)}, bf16[1,104,1536]{2,1,0:T(8,128)(2,1)S(1)}, u32[]{:S(2)}, u32[]{:S(2)}) collective-permute-start(bf16[1,104,1536]{2,1,0:T(8,128)(2,1)S(1)} %get-tuple-element.325), channel_id=1, source_target_pairs={{0,4},{4,0},{8,12},{12,8},{16,20},{20,16},{24,28},{28,24},{1,5},{5... | collective-permute-start | bytes 958472 | tf_op jit(solution)/shard_map/ppermute | solution.py:796
  162.1 8.3 %collective-permute-start.64 = (bf16[128,768]{1,0:T(8,128)(2,1)S(1)}, bf16[128,768]{1,0:T(8,128)(2,1)S(1)}, u32[]{:S(2)}, u32[]{:S(2)}) collective-permute-start(bf16[128,768]{1,0:T(8,128)(2,1)S(1)} %add_convert_fusion), channel_id=1, source_target_pairs={{0,2},{1,3},{2,0},{3,1},{4,6},{5,7},{6,4},{7,5},{8,10},{9,11},{10,... | collective-permute-start | bytes 589832 | tf_op jit(solution)/shard_map/ppermute | solution.py:192
  163.1 15.7 %collective-permute-start.66 = (bf16[104,768]{1,0:T(8,128)(2,1)S(1)}, bf16[104,768]{1,0:T(8,128)(2,1)S(1)}, u32[]{:S(2)}, u32[]{:S(2)}) collective-permute-start(bf16[104,768]{1,0:T(8,128)(2,1)S(1)} %get-tuple-element.332), channel_id=1, source_target_pairs={{0,16},{4,20},{8,24},{12,28},{16,0},{20,4},{24,8},{28,12},{1,17},{... | collective-permute-start | bytes 479240 | tf_op jit(solution)/shard_map/ppermute | solution.py:803
  167.0 11.8 %collective-permute-start.67 = (bf16[104,768]{1,0:T(8,128)(2,1)S(1)}, bf16[104,768]{1,0:T(8,128)(2,1)S(1)}, u32[]{:S(2)}, u32[]{:S(2)}) collective-permute-start(bf16[104,768]{1,0:T(8,128)(2,1)S(1)} %get-tuple-element.333), channel_id=1, source_target_pairs={{0,24},{4,28},{8,16},{12,20},{16,8},{20,12},{24,0},{28,4},{1,25},{... | collective-permute-start | bytes 479240 | tf_op jit(solution)/shard_map/ppermute | solution.py:803
  168.2 11.1 %collective-permute-start.68 = (bf16[104,768]{1,0:T(8,128)(2,1)S(1)}, bf16[104,768]{1,0:T(8,128)(2,1)S(1)}, u32[]{:S(2)}, u32[]{:S(2)}) collective-permute-start(bf16[104,768]{1,0:T(8,128)(2,1)S(1)} %get-tuple-element.334), channel_id=1, source_target_pairs={{0,8},{4,12},{8,0},{12,4},{16,24},{20,28},{24,16},{28,20},{1,9},{5... | collective-permute-start | bytes 479240 | tf_op jit(solution)/shard_map/ppermute | solution.py:803
  180.2 9.4 %collective-permute-start.72 = (bf16[104,1536]{1,0:T(8,128)(2,1)S(1)}, bf16[104,1536]{1,0:T(8,128)(2,1)S(1)}, u32[]{:S(2)}, u32[]{:S(2)}) collective-permute-start(bf16[104,1536]{1,0:T(8,128)(2,1)S(1)} %fold_shards.8), channel_id=1, source_target_pairs={{0,8},{4,12},{8,0},{12,4},{16,24},{20,28},{24,16},{28,20},{1,9},{5... | collective-permute-start | bytes 958472 | tf_op jit(solution)/shard_map/ppermute | solution.py:803
  183.4 7.1 %collective-permute-start.70 = (bf16[128,768]{1,0:T(8,128)(2,1)S(1)}, bf16[128,768]{1,0:T(8,128)(2,1)S(1)}, u32[]{:S(2)}, u32[]{:S(2)}) collective-permute-start(bf16[128,768]{1,0:T(8,128)(2,1)S(1)} %second_norm_tangent.1.refs_0_), channel_id=1, source_target_pairs={{0,1},{1,0},{2,3},{3,2},{4,5},{5,4},{6,7},{7,6},{8,9},{9,8},{10,11... | collective-permute-start | bytes 589832 | tf_op jit(solution)/shard_map/ppermute | solution.py:192
  (33 other events, 269.9 us)

commit v6 on v5

--- a/solution.py
+++ b/solution.py
@@ -293,7 +293,7 @@
             ]
             scores = jnp.where(valid, dot(query, key, NT) * SCALE, jnp.float32(-1e30))
             expo = jnp.exp(scores - jnp.max(scores, axis=-1, keepdims=True))
-            prob = expo / jnp.sum(expo, axis=-1, keepdims=True)
+            prob = expo * (1.0 / jnp.sum(expo, axis=-1, keepdims=True))
             probs[pair * heads + head] = prob
             result = dot(prob.astype(BF), value, NN).astype(BF)
             put_pair(context, pair, quarter, slice(head * HEAD, (head + 1) * HEAD), result)

time: 192 us -> 192 us (level)
  no operation moved by 1% of the time
where the time goes in v6:
time: 192 us
  waiting for transfers between devices  90.6 us (47%)
  starting transfers between devices  60.6 us (32%)
  Pallas kernels  34.7 us (18%)
  other arithmetic  3.01 us (2%)
    pallas_call x25, Pallas kernels, call(): pl.pallas_call(body, out_shape=[jax.ShapeDtypeStruct(shape, kind) for sha...  34.7 us
    ppermute x33, waiting for transfers between devices, swap(): return lax.ppermute(block, 'tp', xor_pairs(tp, bit))  26.1 us
    ppermute x16, waiting for transfers between devices, step(): self.front[0] = lax.ppermute(self.front[0], 'dp', ahead)  25.7 us
    ppermute x6, waiting for transfers between devices, x_swap(): return lax.ppermute(value, 'dp', xor_pairs(dp, 1)) if paired else value  18 us
    ppermute x33, starting transfers between devices, swap(): return lax.ppermute(block, 'tp', xor_pairs(tp, bit))  17.7 us
    ppermute x16, starting transfers between devices, step(): self.front[0] = lax.ppermute(self.front[0], 'dp', ahead)  15.6 us
    ppermute x12, starting transfers between devices, step(): self.front[1] = lax.ppermute(self.front[1], 'dp', behind)  14.1 us
    ppermute x6, waiting for transfers between devices, move(): lax.ppermute(value, 'dp', xor_pairs(dp, 2 * z))  10.6 us
  transfers between devices with their start and end apart: 73, of which 35 were waited for; matrix products, arithmetic and copies ran while one was open for 1% of the time, Pallas kernels for 17%

profile of v6, /device:TPU:0, one launch (start us, length us, event | category | flops | bytes accessed | tf_op | source)
XLA Modules:
  0.0 192.1 jit_solution(9515616693998143786)
XLA Ops:
  3.3 3.0 %collective-permute-start.2 = (bf16[96,768]{1,0:T(8,128)(2,1)S(1)}, bf16[96,768]{1,0:T(8,128)(2,1)S(1)}, u32[]{:S(2)}, u32[]{:S(2)}) collective-permute-start(bf16[96,768]{1,0:T(8,128)(2,1)S(1)} %pad_maximum_fusion.2.refs_0_), channel_id=1, source_target_pairs={{8,0},{16,8},{24,16},{28,24},{20,28},{12,20},{4,12},{0,4},{9,1},{1... | collective-permute-start | bytes 442376 | tf_op jit(solution)/shard_map/ppermute | solution.py:114
  6.5 3.8 %collective-permute-done.2.refs_2_ = bf16[96,768]{1,0:T(8,128)(2,1)S(1)} collective-permute-done((bf16[96,768]{1,0:T(8,128)(2,1)S(1)}, bf16[96,768]{1,0:T(8,128)(2,1)S(1)}, u32[]{:S(2)}, u32[]{:S(2)}) %collective-permute-start.2) | collective-permute-done | bytes 147488 | tf_op jit(solution)/shard_map/ppermute | solution.py:114
  10.3 1.7 collective-permute-start.3
  13.3 3.8 %collective-permute-done.1.refs_3_ = bf16[96,768]{1,0:T(8,128)(2,1)S(1)} collective-permute-done((bf16[96,768]{1,0:T(8,128)(2,1)S(1)}, bf16[96,768]{1,0:T(8,128)(2,1)S(1)}, u32[]{:S(2)}, u32[]{:S(2)}) %collective-permute-start.1) | collective-permute-done | bytes 147488 | tf_op jit(solution)/shard_map/ppermute | solution.py:111
  17.4 1.7 collective-permute-start.7
  19.5 1.7 collective-permute-start.5
  21.1 6.2 %collective-permute-done.4.refs_5_ = bf16[96,768]{1,0:T(8,128)(2,1)S(1)} collective-permute-done((bf16[96,768]{1,0:T(8,128)(2,1)S(1)}, bf16[96,768]{1,0:T(8,128)(2,1)S(1)}, u32[]{:S(2)}, u32[]{:S(2)}) %collective-permute-start.4) | collective-permute-done | bytes 147488 | tf_op jit(solution)/shard_map/ppermute | solution.py:111
  28.5 5.6 %collective-permute-done.8.refs_7_ = bf16[96,768]{1,0:T(8,128)(2,1)S(1)} collective-permute-done((bf16[96,768]{1,0:T(8,128)(2,1)S(1)}, bf16[96,768]{1,0:T(8,128)(2,1)S(1)}, u32[]{:S(2)}, u32[]{:S(2)}) %collective-permute-start.8) | collective-permute-done | bytes 147488 | tf_op jit(solution)/shard_map/ppermute | solution.py:111
  37.0 5.1 %attention_forward.1 = (bf16[512,768]{1,0:T(8,128)(2,1)S(1)}, bf16[512,576]{1,0:T(8,128)(2,1)S(1)}, f32[6,256,256]{2,1,0:T(8,128)S(1)}, bf16[512,192]{1,0:T(8,12...) custom-call(s32[4]{0:T(128)S(1)} %pad_add_fusion.where, ...), custom_call_target="tpu_custom_call" | custom-call | flops 1 | bytes 1 | tf_op jit(solution)/shard_map/attention_forward/pallas_call | solution.py:65
  44.4 1.6 collective-permute-start.12
  46.0 5.2 %collective-permute-done.12.second = bf16[128,768]{1,0:T(8,128)(2,1)S(1)} collective-permute-done((bf16[128,768]{1,0:T(8,128)(2,1)S(1)}, bf16[128,768]{1,0:T(8,128)(2,1)S(1)}, u32[]{:S(2)}, u32[]{:S(2)}) %collective-permute-start.12) | collective-permute-done | bytes 196640 | tf_op jit(solution)/shard_map/ppermute | solution.py:192
  52.6 1.6 collective-permute-start.16
  54.3 1.5 collective-permute-start.15
  56.1 4.1 %collective-permute-done.15.refs_1_ = bf16[128,768]{1,0:T(8,128)(2,1)S(1)} collective-permute-done((bf16[128,768]{1,0:T(8,128)(2,1)S(1)}, bf16[128,768]{1,0:T(8,128)(2,1)S(1)}, u32[]{:S(2)}, u32[]{:S(2)}) %collective-permute-start.15) | collective-permute-done | bytes 196640 | tf_op jit(solution)/shard_map/ppermute | solution.py:192
  60.9 1.6 collective-permute-start.19
  63.0 3.2 %feed_forward.1 = (bf16[512,768]{1,0:T(8,128)(2,1)S(1)}, bf16[512,768]{1,0:T(8,128)(2,1)S(1)}, f32[512,768]{1,0:T(8,128)S(1)}, bf16[256,768]{1,0:T(8,128)(2,1)S(...) custom-call(s32[4]{0:T(128)S(1)} %pad_add_fusion.where, f32[8,768]{1,0:T(8,128)S(1)} %reshape.39.params, ...), custom_call_target="tpu_custom_call" | custom-call | flops 1 | bytes 1 | tf_op jit(solution)/shard_map/feed_forward/pallas_call | solution.py:65
  68.6 1.7 collective-permute-done.21.came
  70.3 1.6 collective-permute-start.22
  71.9 1.7 collective-permute-start.23
  73.9 3.6 %collective-permute-done.23.refs_3_ = bf16[96,768]{1,0:T(8,128)(2,1)S(1)} collective-permute-done((bf16[96,768]{1,0:T(8,128)(2,1)S(1)}, bf16[96,768]{1,0:T(8,128)(2,1)S(1)}, u32[]{:S(2)}, u32[]{:S(2)}) %collective-permute-start.23) | collective-permute-done | bytes 147488 | tf_op jit(solution)/shard_map/ppermute | solution.py:111
  77.5 1.4 collective-permute-done.24.refs_4_
  84.6 2.7 %collective-permute-done.27.refs_6_ = bf16[96,768]{1,0:T(8,128)(2,1)S(1)} collective-permute-done((bf16[96,768]{1,0:T(8,128)(2,1)S(1)}, bf16[96,768]{1,0:T(8,128)(2,1)S(1)}, u32[]{:S(2)}, u32[]{:S(2)}) %collective-permute-start.27) | collective-permute-done | bytes 147488 | tf_op jit(solution)/shard_map/ppermute | solution.py:114
  87.3 1.5 collective-permute-start.30
  89.6 1.5 feed_forward_backward.1
  91.2 3.4 %collective-permute-done.30.refs_1_ = bf16[128,768]{1,0:T(8,128)(2,1)S(1)} collective-permute-done((bf16[128,768]{1,0:T(8,128)(2,1)S(1)}, bf16[128,768]{1,0:T(8,128)(2,1)S(1)}, u32[]{:S(2)}, u32[]{:S(2)}) %collective-permute-start.30) | collective-permute-done | bytes 196640 | tf_op jit(solution)/shard_map/ppermute | solution.py:192
  97.8 1.6 collective-permute-start.35
  99.3 2.1 %feed_forward_weights.1 = (bf16[4,104,1536]{2,1,0:T(8,128)(2,1)S(1)}, bf16[1,104,1536]{2,1,0:T(8,128)(2,1)S(1)}, bf16[1,104,1536]{2,1,0:T(8,128)(2,1)S(1)}, bf16...) custom-call(s32[4]{0:T(128)S(1)} %pad_add_fusion.where, bf16[512,768]{1,0:T(8,128)(2,1)S(1)} %get-tuple-element.245.rel, ...), custom_call_target="tpu_custom_call" | custom-call | flops 1 | bytes 1 | tf_op jit(solution)/shard_map/feed_forward_weights/pallas_call | solution.py:65
  101.5 5.2 %attention_tangent.1 = (bf16[256,768]{1,0:T(8,128)(2,1)S(1)}, bf16[256,768]{1,0:T(8,128)(2,1)S(1)}) custom-call(s32[4]{0:T(128)S(1)} %pad_add_fusion.where, bf16[512,768]{1,0:T(8,128)(2,1)S(1)} %get-tuple-element.203.x_rel.rel, bf16[512,576]{1,0:T(8,128)(2,1)S(1)} %get-tuple-element.253.mixed.refs_4_, f32[6,256,256]{2,1,0:T(8,128)S(1)} %get-tuple-element.254.probs.refs_5_, ...), custom_call_target="tpu_custom_call" | custom-call | flops 1 | bytes 1 | tf_op jit(solution)/shard_map/attention_tangent/pallas_call | solution.py:65
  109.3 1.7 collective-permute-start.46
  110.9 3.9 %collective-permute-done.40.refs_1_ = bf16[136,768]{1,0:T(8,128)(2,1)S(1)} collective-permute-done((bf16[136,768]{1,0:T(8,128)(2,1)S(1)}, bf16[136,768]{1,0:T(8,128)(2,1)S(1)}, u32[]{:S(2)}, u32[]{:S(2)}) %collective-permute-start.40) | collective-permute-done | bytes 208928 | tf_op jit(solution)/shard_map/ppermute | solution.py:192
  114.9 2.8 %collective-permute-done.43.came = bf16[1,104,1536]{2,1,0:T(8,128)(2,1)S(1)} collective-permute-done((bf16[1,104,1536]{2,1,0:T(8,128)(2,1)S(1)}, bf16[1,104,1536]{2,1,0:T(8,128)(2,1)S(1)}, u32[]{:S(2)}, u32[]{:S(2)}) %collective-permute-start.43) | collective-permute-done | bytes 319520 | tf_op jit(solution)/shard_map/ppermute | solution.py:796
  119.1 3.9 %attention_backward.1 = (bf16[512,768]{1,0:T(8,128)(2,1)S(1)}, bf16[512,576]{1,0:T(8,128)(2,1)S(1)}, f32[4,768]{1,0:T(4,128)S(1)}, bf16[256,768]{1,0:T(8,128)(2,1)S(1)}, bf16[256,768]{1,0:T(8,128)(2,1)S(1)}) custom-call(bf16[136,768]{1,0:T(8,128)(2,1)S(1)} %get-tuple-element.274.refs_0_, bf16[136,768]{1,0:T(8,128)(2,1)S(1)} %collective-permute-done.40.refs_1_, ...), custom_call_target="tpu_custom_call" | custom-call | flops 1 | bytes 1 | tf_op jit(solution)/shard_map/attention_backward/pallas_call | solution.py:65
  127.3 1.7 attention_weights.1
  129.0 1.9 collective-permute-done.48.second
  131.2 2.7 %collective-permute-done.49.came = bf16[1,104,1536]{2,1,0:T(8,128)(2,1)S(1)} collective-permute-done((bf16[1,104,1536]{2,1,0:T(8,128)(2,1)S(1)}, bf16[1,104,1536]{2,1,0:T(8,128)(2,1)S(1)}, u32[]{:S(2)}, u32[]{:S(2)}) %collective-permute-start.49) | collective-permute-done | bytes 319520 | tf_op jit(solution)/shard_map/ppermute | solution.py:796
  136.5 4.2 %collective-permute-done.51.came = bf16[1,104,1536]{2,1,0:T(8,128)(2,1)S(1)} collective-permute-done((bf16[1,104,1536]{2,1,0:T(8,128)(2,1)S(1)}, bf16[1,104,1536]{2,1,0:T(8,128)(2,1)S(1)}, u32[]{:S(2)}, u32[]{:S(2)}) %collective-permute-start.51) | collective-permute-done | bytes 319520 | tf_op jit(solution)/shard_map/ppermute | solution.py:796
  141.5 6.0 %collective-permute-done.52.came = bf16[2,104,768]{2,1,0:T(8,128)(2,1)S(1)} collective-permute-done((bf16[2,104,768]{2,1,0:T(8,128)(2,1)S(1)}, bf16[2,104,768]{2,1,0:T(8,128)(2,1)S(1)}, u32[]{:S(2)}, u32[]{:S(2)}) %collective-permute-start.52) | collective-permute-done | bytes 319520 | tf_op jit(solution)/shard_map/ppermute | solution.py:796
  150.5 3.4 %collective-permute-done.58.refs_15_ = bf16[96,1536]{1,0:T(8,128)(2,1)S(1)} collective-permute-done((bf16[96,1536]{1,0:T(8,128)(2,1)S(1)}, bf16[96,1536]{1,0:T(8,128)(2,1)S(1)}, u32[]{:S(2)}, u32[]{:S(2)}) %collective-permute-start.58) | collective-permute-done | bytes 294944 | tf_op jit(solution)/shard_map/ppermute | solution.py:111
  154.8 3.8 %feed_forward_tangent.1 = (bf16[256,768]{1,0:T(8,128)(2,1)S(1)}, bf16[256,768]{1,0:T(8,128)(2,1)S(1)}) custom-call(s32[4]{0:T(128)S(1)} %pad_add_fusion.where, bf16[128,768]{1,0:T(8,128)(2,1)S(1)} %get-tuple-element.303.refs_0_, bf16[128,768]{1,0:T(8,128)(2,1)S(1)} %collective-permute-done.53.refs_1_, bf16[128,768]{1,0:T(8,128)(2,1)S(1)} %collective-permute-done.56.refs_2_, ...), custom_call_target="tpu_custom_call" | custom-call | flops 1 | bytes 1 | tf_op jit(solution)/shard_map/feed_forward_tangent/pallas_call | solution.py:65
  160.4 1.6 collective-permute-done.63.came
  163.1 3.9 %collective-permute-start.66 = (bf16[104,768]{1,0:T(8,128)(2,1)S(1)}, bf16[104,768]{1,0:T(8,128)(2,1)S(1)}, u32[]{:S(2)}, u32[]{:S(2)}) collective-permute-start(bf16[104,768]{1,0:T(8,128)(2,1)S(1)} %get-tuple-element.332), channel_id=1, source_target_pairs={{0,16},{4,20},{8,24},{12,28},{16,0},{20,4},{24,8},{28,12},{1,17},{... | collective-permute-start | bytes 479240 | tf_op jit(solution)/shard_map/ppermute | solution.py:803
  168.2 2.0 %collective-permute-done.65.came = bf16[1,104,1536]{2,1,0:T(8,128)(2,1)S(1)} collective-permute-done((bf16[1,104,1536]{2,1,0:T(8,128)(2,1)S(1)}, bf16[1,104,1536]{2,1,0:T(8,128)(2,1)S(1)}, u32[]{:S(2)}, u32[]{:S(2)}) %collective-permute-start.65) | collective-permute-done | bytes 319520 | tf_op jit(solution)/shard_map/ppermute | solution.py:796
  170.7 8.1 %collective-permute-done.66.refs_2_ = bf16[104,768]{1,0:T(8,128)(2,1)S(1)} collective-permute-done((bf16[104,768]{1,0:T(8,128)(2,1)S(1)}, bf16[104,768]{1,0:T(8,128)(2,1)S(1)}, u32[]{:S(2)}, u32[]{:S(2)}) %collective-permute-start.66) | collective-permute-done | bytes 159776 | tf_op jit(solution)/shard_map/ppermute | solution.py:803
  180.2 2.7 %collective-permute-start.72 = (bf16[104,1536]{1,0:T(8,128)(2,1)S(1)}, bf16[104,1536]{1,0:T(8,128)(2,1)S(1)}, u32[]{:S(2)}, u32[]{:S(2)}) collective-permute-start(bf16[104,1536]{1,0:T(8,128)(2,1)S(1)} %fold_shards.8), channel_id=1, source_target_pairs={{0,8},{4,12},{8,0},{12,4},{16,24},{20,28},{24,16},{28,20},{1,9},{5... | collective-permute-start | bytes 958472 | tf_op jit(solution)/shard_map/ppermute | solution.py:803
  183.4 1.6 collective-permute-done.69.refs_1_
  185.0 1.7 place_rows.2
  187.6 2.0 %collective-permute-done.72.refs_1_ = bf16[104,1536]{1,0:T(8,128)(2,1)S(1)} collective-permute-done((bf16[104,1536]{1,0:T(8,128)(2,1)S(1)}, bf16[104,1536]{1,0:T(8,128)(2,1)S(1)}, u32[]{:S(2)}, u32[]{:S(2)}) %collective-permute-start.72) | collective-permute-done | bytes 319520 | tf_op jit(solution)/shard_map/ppermute | solution.py:803
  190.5 1.5 place_rows.3
  (153 shorter events, 50.4 us)
Async XLA Ops:
  3.3 6.9 %collective-permute-start.2 = (bf16[96,768]{1,0:T(8,128)(2,1)S(1)}, bf16[96,768]{1,0:T(8,128)(2,1)S(1)}, u32[]{:S(2)}, u32[]{:S(2)}) collective-permute-start(bf16[96,768]{1,0:T(8,128)(2,1)S(1)} %pad_maximum_fusion.2.refs_0_), channel_id=1, source_target_pairs={{8,0},{16,8},{24,16},{28,24},{20,28},{12,20},{4,12},{0,4},{9,1},{1... | collective-permute-start | bytes 442376 | tf_op jit(solution)/shard_map/ppermute | solution.py:114
  10.3 6.8 %collective-permute-start.3 = (bf16[96,768]{1,0:T(8,128)(2,1)S(1)}, bf16[96,768]{1,0:T(8,128)(2,1)S(1)}, u32[]{:S(2)}, u32[]{:S(2)}) collective-permute-start(bf16[96,768]{1,0:T(8,128)(2,1)S(1)} %collective-permute-done.2.refs_2_), channel_id=1, source_target_pairs={{8,0},{16,8},{24,16},{28,24},{20,28},{12,20},{4,12},{0,4},{9,1},{1... | collective-permute-start | bytes 442376 | tf_op jit(solution)/shard_map/ppermute | solution.py:114
  17.1 10.3 %collective-permute-start.6 = (bf16[96,1536]{1,0:T(8,128)(2,1)S(1)}, bf16[96,1536]{1,0:T(8,128)(2,1)S(1)}, u32[]{:S(2)}, u32[]{:S(2)}) collective-permute-start(bf16[96,1536]{1,0:T(8,128)(2,1)S(1)} %pad_maximum_fusion.refs_4_), channel_id=1, source_target_pairs={{0,8},{8,16},{16,24},{24,28},{28,20},{20,12},{12,4},{4,0},{1,9},{9... | collective-permute-start | bytes 884744 | tf_op jit(solution)/shard_map/ppermute | solution.py:111
  17.4 9.9 %collective-permute-start.7 = (bf16[96,1536]{1,0:T(8,128)(2,1)S(1)}, bf16[96,1536]{1,0:T(8,128)(2,1)S(1)}, u32[]{:S(2)}, u32[]{:S(2)}) collective-permute-start(bf16[96,1536]{1,0:T(8,128)(2,1)S(1)} %pad_maximum_fusion.refs_4_), channel_id=1, source_target_pairs={{8,0},{16,8},{24,16},{28,24},{20,28},{12,20},{4,12},{0,4},{9,1},{1... | collective-permute-start | bytes 884744 | tf_op jit(solution)/shard_map/ppermute | solution.py:114
  19.1 8.2 %collective-permute-start.4 = (bf16[96,768]{1,0:T(8,128)(2,1)S(1)}, bf16[96,768]{1,0:T(8,128)(2,1)S(1)}, u32[]{:S(2)}, u32[]{:S(2)}) collective-permute-start(bf16[96,768]{1,0:T(8,128)(2,1)S(1)} %collective-permute-done.1.refs_3_), channel_id=1, source_target_pairs={{0,8},{8,16},{16,24},{24,28},{28,20},{20,12},{12,4},{4,0},{1,9},{9... | collective-permute-start | bytes 442376 | tf_op jit(solution)/shard_map/ppermute | solution.py:111
  19.5 7.9 %collective-permute-start.5 = (bf16[96,768]{1,0:T(8,128)(2,1)S(1)}, bf16[96,768]{1,0:T(8,128)(2,1)S(1)}, u32[]{:S(2)}, u32[]{:S(2)}) collective-permute-start(bf16[96,768]{1,0:T(8,128)(2,1)S(1)} %collective-permute-done.3.refs_4_), channel_id=1, source_target_pairs={{8,0},{16,8},{24,16},{28,24},{20,28},{12,20},{4,12},{0,4},{9,1},{1... | collective-permute-start | bytes 442376 | tf_op jit(solution)/shard_map/ppermute | solution.py:114
  27.3 6.8 %collective-permute-start.8 = (bf16[96,768]{1,0:T(8,128)(2,1)S(1)}, bf16[96,768]{1,0:T(8,128)(2,1)S(1)}, u32[]{:S(2)}, u32[]{:S(2)}) collective-permute-start(bf16[96,768]{1,0:T(8,128)(2,1)S(1)} %collective-permute-done.4.refs_5_), channel_id=1, source_target_pairs={{0,8},{8,16},{16,24},{24,28},{28,20},{20,12},{12,4},{4,0},{1,9},{9... | collective-permute-start | bytes 442376 | tf_op jit(solution)/shard_map/ppermute | solution.py:111
  34.1 8.1 %collective-permute-start.9 = (bf16[96,1536]{1,0:T(8,128)(2,1)S(1)}, bf16[96,1536]{1,0:T(8,128)(2,1)S(1)}, u32[]{:S(2)}, u32[]{:S(2)}) collective-permute-start(bf16[96,1536]{1,0:T(8,128)(2,1)S(1)} %collective-permute-done.6.refs_5_), channel_id=1, source_target_pairs={{0,8},{8,16},{16,24},{24,28},{28,20},{20,12},{12,4},{4,0},{1,9},{9... | collective-permute-start | bytes 884744 | tf_op jit(solution)/shard_map/ppermute | solution.py:111
  35.2 7.0 %collective-permute-start.10 = (bf16[96,1536]{1,0:T(8,128)(2,1)S(1)}, bf16[96,1536]{1,0:T(8,128)(2,1)S(1)}, u32[]{:S(2)}, u32[]{:S(2)}) collective-permute-start(bf16[96,1536]{1,0:T(8,128)(2,1)S(1)} %collective-permute-done.7.refs_6_), channel_id=1, source_target_pairs={{8,0},{16,8},{24,16},{28,24},{20,28},{12,20},{4,12},{0,4},{9,1},{1... | collective-permute-start | bytes 884744 | tf_op jit(solution)/shard_map/ppermute | solution.py:114
  42.3 9.4 %collective-permute-start.13 = (bf16[96,1536]{1,0:T(8,128)(2,1)S(1)}, bf16[96,1536]{1,0:T(8,128)(2,1)S(1)}, u32[]{:S(2)}, u32[]{:S(2)}) collective-permute-start(bf16[96,1536]{1,0:T(8,128)(2,1)S(1)} %collective-permute-done.9.refs_7_), channel_id=1, source_target_pairs={{0,8},{8,16},{16,24},{24,28},{28,20},{20,12},{12,4},{4,0},{1,9},{9... | collective-permute-start | bytes 884744 | tf_op jit(solution)/shard_map/ppermute | solution.py:111
  43.5 9.1 %collective-permute-start.14 = (bf16[96,1536]{1,0:T(8,128)(2,1)S(1)}, bf16[96,1536]{1,0:T(8,128)(2,1)S(1)}, u32[]{:S(2)}, u32[]{:S(2)}) collective-permute-start(bf16[96,1536]{1,0:T(8,128)(2,1)S(1)} %collective-permute-done.10.refs_8_), channel_id=1, source_target_pairs={{8,0},{16,8},{24,16},{28,24},{20,28},{12,20},{4,12},{0,4},{9,1},{1... | collective-permute-start | bytes 884744 | tf_op jit(solution)/shard_map/ppermute | solution.py:114
  44.4 6.8 %collective-permute-start.12 = (bf16[128,768]{1,0:T(8,128)(2,1)S(1)}, bf16[128,768]{1,0:T(8,128)(2,1)S(1)}, u32[]{:S(2)}, u32[]{:S(2)}) collective-permute-start(bf16[128,768]{1,0:T(8,128)(2,1)S(1)} %add_convert_fusion.5), channel_id=1, source_target_pairs={{0,2},{1,3},{2,0},{3,1},{4,6},{5,7},{6,4},{7,5},{8,10},{9,11},{10,... | collective-permute-start | bytes 589832 | tf_op jit(solution)/shard_map/ppermute | solution.py:192
  52.6 8.3 %collective-permute-start.16 = (bf16[96,1536]{1,0:T(8,128)(2,1)S(1)}, bf16[96,1536]{1,0:T(8,128)(2,1)S(1)}, u32[]{:S(2)}, u32[]{:S(2)}) collective-permute-start(bf16[96,1536]{1,0:T(8,128)(2,1)S(1)} %collective-permute-done.13.refs_9_), channel_id=1, source_target_pairs={{0,8},{8,16},{16,24},{24,28},{28,20},{20,12},{12,4},{4,0},{1,9},{9... | collective-permute-start | bytes 884744 | tf_op jit(solution)/shard_map/ppermute | solution.py:111
  56.0 7.0 %collective-permute-start.17 = (bf16[128,768]{1,0:T(8,128)(2,1)S(1)}, bf16[128,768]{1,0:T(8,128)(2,1)S(1)}, u32[]{:S(2)}, u32[]{:S(2)}) collective-permute-start(bf16[128,768]{1,0:T(8,128)(2,1)S(1)} %get-tuple-element.213.refs_0_), channel_id=1, source_target_pairs={{0,1},{1,0},{2,3},{3,2},{4,5},{5,4},{6,7},{7,6},{8,9},{9,8},{10,11... | collective-permute-start | bytes 589832 | tf_op jit(solution)/shard_map/ppermute | solution.py:192
  70.3 8.6 %collective-permute-start.22 = (bf16[128,768]{1,0:T(8,128)(2,1)S(1)}, bf16[128,768]{1,0:T(8,128)(2,1)S(1)}, u32[]{:S(2)}, u32[]{:S(2)}) collective-permute-start(bf16[128,768]{1,0:T(8,128)(2,1)S(1)} %add_convert_fusion.4), channel_id=1, source_target_pairs={{0,2},{1,3},{2,0},{3,1},{4,6},{5,7},{6,4},{7,5},{8,10},{9,11},{10,... | collective-permute-start | bytes 589832 | tf_op jit(solution)/shard_map/ppermute | solution.py:192
  82.6 6.3 %collective-permute-start.28 = (bf16[136,768]{1,0:T(8,128)(2,1)S(1)}, bf16[136,768]{1,0:T(8,128)(2,1)S(1)}, u32[]{:S(2)}, u32[]{:S(2)}) collective-permute-start(bf16[136,768]{1,0:T(8,128)(2,1)S(1)} %get-tuple-element.229.refs_0_), channel_id=1, source_target_pairs={{0,1},{1,0},{2,3},{3,2},{4,5},{5,4},{6,7},{7,6},{8,9},{9,8},{10,11... | collective-permute-start | bytes 626696 | tf_op jit(solution)/shard_map/ppermute | solution.py:192
  82.6 12.1 %collective-permute-start.31 = (bf16[96,1536]{1,0:T(8,128)(2,1)S(1)}, bf16[96,1536]{1,0:T(8,128)(2,1)S(1)}, u32[]{:S(2)}, u32[]{:S(2)}) collective-permute-start(bf16[96,1536]{1,0:T(8,128)(2,1)S(1)} %pad_maximum_fusion.1.refs_8_), channel_id=1, source_target_pairs={{0,8},{8,16},{16,24},{24,28},{28,20},{20,12},{12,4},{4,0},{1,9},{9... | collective-permute-start | bytes 884744 | tf_op jit(solution)/shard_map/ppermute | solution.py:111
  84.1 10.6 %collective-permute-start.32 = (bf16[96,1536]{1,0:T(8,128)(2,1)S(1)}, bf16[96,1536]{1,0:T(8,128)(2,1)S(1)}, u32[]{:S(2)}, u32[]{:S(2)}) collective-permute-start(bf16[96,1536]{1,0:T(8,128)(2,1)S(1)} %pad_maximum_fusion.1.refs_8_), channel_id=1, source_target_pairs={{8,0},{16,8},{24,16},{28,24},{20,28},{12,20},{4,12},{0,4},{9,1},{1... | collective-permute-start | bytes 884744 | tf_op jit(solution)/shard_map/ppermute | solution.py:114
  87.3 7.3 %collective-permute-start.30 = (bf16[128,768]{1,0:T(8,128)(2,1)S(1)}, bf16[128,768]{1,0:T(8,128)(2,1)S(1)}, u32[]{:S(2)}, u32[]{:S(2)}) collective-permute-start(bf16[128,768]{1,0:T(8,128)(2,1)S(1)} %get-tuple-element.263.refs_0_), channel_id=1, source_target_pairs={{0,2},{1,3},{2,0},{3,1},{4,6},{5,7},{6,4},{7,5},{8,10},{9,11},{10,... | collective-permute-start | bytes 589832 | tf_op jit(solution)/shard_map/ppermute | solution.py:192
  88.8 6.3 %collective-permute-start.33 = (bf16[96,768]{1,0:T(8,128)(2,1)S(1)}, bf16[96,768]{1,0:T(8,128)(2,1)S(1)}, u32[]{:S(2)}, u32[]{:S(2)}) collective-permute-start(bf16[96,768]{1,0:T(8,128)(2,1)S(1)} %collective-permute-done.26.refs_5_), channel_id=1, source_target_pairs={{0,8},{8,16},{16,24},{24,28},{28,20},{20,12},{12,4},{4,0},{1,9},{9... | collective-permute-start | bytes 442376 | tf_op jit(solution)/shard_map/ppermute | solution.py:111
  95.2 11.5 %collective-permute-start.36 = (bf16[128,768]{1,0:T(8,128)(2,1)S(1)}, bf16[128,768]{1,0:T(8,128)(2,1)S(1)}, u32[]{:S(2)}, u32[]{:S(2)}) collective-permute-start(bf16[128,768]{1,0:T(8,128)(2,1)S(1)} %get-tuple-element.263.refs_0_), channel_id=1, source_target_pairs={{0,1},{1,0},{2,3},{3,2},{4,5},{5,4},{6,7},{7,6},{8,9},{9,8},{10,11... | collective-permute-start | bytes 589832 | tf_op jit(solution)/shard_map/ppermute | solution.py:192
  95.7 11.0 %collective-permute-start.37 = (bf16[128,768]{1,0:T(8,128)(2,1)S(1)}, bf16[128,768]{1,0:T(8,128)(2,1)S(1)}, u32[]{:S(2)}, u32[]{:S(2)}) collective-permute-start(bf16[128,768]{1,0:T(8,128)(2,1)S(1)} %collective-permute-done.30.refs_1_), channel_id=1, source_target_pairs={{0,1},{1,0},{2,3},{3,2},{4,5},{5,4},{6,7},{7,6},{8,9},{9,8},{10,11... | collective-permute-start | bytes 589832 | tf_op jit(solution)/shard_map/ppermute | solution.py:192
  95.7 11.0 %collective-permute-start.38 = (bf16[96,1536]{1,0:T(8,128)(2,1)S(1)}, bf16[96,1536]{1,0:T(8,128)(2,1)S(1)}, u32[]{:S(2)}, u32[]{:S(2)}) collective-permute-start(bf16[96,1536]{1,0:T(8,128)(2,1)S(1)} %collective-permute-done.31.refs_9_), channel_id=1, source_target_pairs={{0,8},{8,16},{16,24},{24,28},{28,20},{20,12},{12,4},{4,0},{1,9},{9... | collective-permute-start | bytes 884744 | tf_op jit(solution)/shard_map/ppermute | solution.py:111
  97.0 9.7 %collective-permute-start.39 = (bf16[96,1536]{1,0:T(8,128)(2,1)S(1)}, bf16[96,1536]{1,0:T(8,128)(2,1)S(1)}, u32[]{:S(2)}, u32[]{:S(2)}) collective-permute-start(bf16[96,1536]{1,0:T(8,128)(2,1)S(1)} %collective-permute-done.32.refs_10_), channel_id=1, source_target_pairs={{8,0},{16,8},{24,16},{28,24},{20,28},{12,20},{4,12},{0,4},{9,1},{1... | collective-permute-start | bytes 884744 | tf_op jit(solution)/shard_map/ppermute | solution.py:114
  97.8 9.0 %collective-permute-start.35 = (bf16[128,768]{1,0:T(8,128)(2,1)S(1)}, bf16[128,768]{1,0:T(8,128)(2,1)S(1)}, u32[]{:S(2)}, u32[]{:S(2)}) collective-permute-start(bf16[128,768]{1,0:T(8,128)(2,1)S(1)} %add_convert_fusion.3), channel_id=1, source_target_pairs={{0,2},{1,3},{2,0},{3,1},{4,6},{5,7},{6,4},{7,5},{8,10},{9,11},{10,... | collective-permute-start | bytes 589832 | tf_op jit(solution)/shard_map/ppermute | solution.py:192
  107.1 10.6 %collective-permute-start.44 = (bf16[256,768]{1,0:T(8,128)(2,1)S(1)}, bf16[256,768]{1,0:T(8,128)(2,1)S(1)}, u32[]{:S(2)}, u32[]{:S(2)}) collective-permute-start(bf16[256,768]{1,0:T(8,128)(2,1)S(1)} %get-tuple-element.278), channel_id=1, source_target_pairs={{0,1},{1,0},{2,3},{3,2},{4,5},{5,4},{6,7},{7,6},{8,9},{9,8},{10,11... | collective-permute-start | bytes 1179656 | tf_op jit(solution)/shard_map/ppermute | solution.py:192
  107.2 10.4 %collective-permute-start.43 = (bf16[1,104,1536]{2,1,0:T(8,128)(2,1)S(1)}, bf16[1,104,1536]{2,1,0:T(8,128)(2,1)S(1)}, u32[]{:S(2)}, u32[]{:S(2)}) collective-permute-start(bf16[1,104,1536]{2,1,0:T(8,128)(2,1)S(1)} %get-tuple-element.275), channel_id=1, source_target_pairs={{0,4},{4,0},{8,12},{12,8},{16,20},{20,16},{24,28},{28,24},{1,5},{5... | collective-permute-start | bytes 958472 | tf_op jit(solution)/shard_map/ppermute | solution.py:796
  107.6 7.2 %collective-permute-start.40 = (bf16[136,768]{1,0:T(8,128)(2,1)S(1)}, bf16[136,768]{1,0:T(8,128)(2,1)S(1)}, u32[]{:S(2)}, u32[]{:S(2)}) collective-permute-start(bf16[136,768]{1,0:T(8,128)(2,1)S(1)} %get-tuple-element.274.refs_0_), channel_id=1, source_target_pairs={{0,2},{1,3},{2,0},{3,1},{4,6},{5,7},{6,4},{7,5},{8,10},{9,11},{10,... | collective-permute-start | bytes 626696 | tf_op jit(solution)/shard_map/ppermute | solution.py:192
  108.9 14.6 %collective-permute-start.45 = (bf16[96,1536]{1,0:T(8,128)(2,1)S(1)}, bf16[96,1536]{1,0:T(8,128)(2,1)S(1)}, u32[]{:S(2)}, u32[]{:S(2)}) collective-permute-start(bf16[96,1536]{1,0:T(8,128)(2,1)S(1)} %collective-permute-done.38.refs_11_), channel_id=1, source_target_pairs={{0,8},{8,16},{16,24},{24,28},{28,20},{20,12},{12,4},{4,0},{1,9},{9... | collective-permute-start | bytes 884744 | tf_op jit(solution)/shard_map/ppermute | solution.py:111
  109.3 14.2 %collective-permute-start.46 = (bf16[96,1536]{1,0:T(8,128)(2,1)S(1)}, bf16[96,1536]{1,0:T(8,128)(2,1)S(1)}, u32[]{:S(2)}, u32[]{:S(2)}) collective-permute-start(bf16[96,1536]{1,0:T(8,128)(2,1)S(1)} %collective-permute-done.39.refs_12_), channel_id=1, source_target_pairs={{8,0},{16,8},{24,16},{28,24},{20,28},{12,20},{4,12},{0,4},{9,1},{1... | collective-permute-start | bytes 884744 | tf_op jit(solution)/shard_map/ppermute | solution.py:114
  123.5 10.4 %collective-permute-start.47 = (bf16[256,768]{1,0:T(8,128)(2,1)S(1)}, bf16[256,768]{1,0:T(8,128)(2,1)S(1)}, u32[]{:S(2)}, u32[]{:S(2)}) collective-permute-start(bf16[256,768]{1,0:T(8,128)(2,1)S(1)} %get-tuple-element.285), channel_id=1, source_target_pairs={{0,1},{1,0},{2,3},{3,2},{4,5},{5,4},{6,7},{7,6},{8,9},{9,8},{10,11... | collective-permute-start | bytes 1179656 | tf_op jit(solution)/shard_map/ppermute | solution.py:192
  123.5 10.3 %collective-permute-start.49 = (bf16[1,104,1536]{2,1,0:T(8,128)(2,1)S(1)}, bf16[1,104,1536]{2,1,0:T(8,128)(2,1)S(1)}, u32[]{:S(2)}, u32[]{:S(2)}) collective-permute-start(bf16[1,104,1536]{2,1,0:T(8,128)(2,1)S(1)} %get-tuple-element.294), channel_id=1, source_target_pairs={{0,4},{4,0},{8,12},{12,8},{16,20},{20,16},{24,28},{28,24},{1,5},{5... | collective-permute-start | bytes 958472 | tf_op jit(solution)/shard_map/ppermute | solution.py:796
  123.8 7.0 %collective-permute-start.48 = (bf16[128,768]{1,0:T(8,128)(2,1)S(1)}, bf16[128,768]{1,0:T(8,128)(2,1)S(1)}, u32[]{:S(2)}, u32[]{:S(2)}) collective-permute-start(bf16[128,768]{1,0:T(8,128)(2,1)S(1)} %add_convert_fusion.2), channel_id=1, source_target_pairs={{0,2},{1,3},{2,0},{3,1},{4,6},{5,7},{6,4},{7,5},{8,10},{9,11},{10,... | collective-permute-start | bytes 589832 | tf_op jit(solution)/shard_map/ppermute | solution.py:192
  125.1 15.5 %collective-permute-start.51 = (bf16[1,104,1536]{2,1,0:T(8,128)(2,1)S(1)}, bf16[1,104,1536]{2,1,0:T(8,128)(2,1)S(1)}, u32[]{:S(2)}, u32[]{:S(2)}) collective-permute-start(bf16[1,104,1536]{2,1,0:T(8,128)(2,1)S(1)} %get-tuple-element.298), channel_id=1, source_target_pairs={{0,4},{4,0},{8,12},{12,8},{16,20},{20,16},{24,28},{28,24},{1,5},{5... | collective-permute-start | bytes 958472 | tf_op jit(solution)/shard_map/ppermute | solution.py:796
  126.5 22.4 %collective-permute-start.54 = (bf16[104,1536]{1,0:T(8,128)(2,1)S(1)}, bf16[104,1536]{1,0:T(8,128)(2,1)S(1)}, u32[]{:S(2)}, u32[]{:S(2)}) collective-permute-start(bf16[104,1536]{1,0:T(8,128)(2,1)S(1)} %fold_shards.6), channel_id=1, source_target_pairs={{0,16},{4,20},{8,24},{12,28},{16,0},{20,4},{24,8},{28,12},{1,17},{... | collective-permute-start | bytes 958472 | tf_op jit(solution)/shard_map/ppermute | solution.py:803
  133.9 13.6 %collective-permute-start.52 = (bf16[2,104,768]{2,1,0:T(8,128)(2,1)S(1)}, bf16[2,104,768]{2,1,0:T(8,128)(2,1)S(1)}, u32[]{:S(2)}, u32[]{:S(2)}) collective-permute-start(bf16[2,104,768]{2,1,0:T(8,128)(2,1)S(1)} %get-tuple-element.300), channel_id=1, source_target_pairs={{0,4},{4,0},{8,12},{12,8},{16,20},{20,16},{24,28},{28,24},{1,5},{5... | collective-permute-start | bytes 958472 | tf_op jit(solution)/shard_map/ppermute | solution.py:796
  134.4 14.5 %collective-permute-start.50 = (bf16[128,768]{1,0:T(8,128)(2,1)S(1)}, bf16[128,768]{1,0:T(8,128)(2,1)S(1)}, u32[]{:S(2)}, u32[]{:S(2)}) collective-permute-start(bf16[128,768]{1,0:T(8,128)(2,1)S(1)} %add_convert_fusion.1), channel_id=1, source_target_pairs={{0,2},{1,3},{2,0},{3,1},{4,6},{5,7},{6,4},{7,5},{8,10},{9,11},{10,... | collective-permute-start | bytes 589832 | tf_op jit(solution)/shard_map/ppermute | solution.py:192
  135.7 13.2 %collective-permute-start.53 = (bf16[128,768]{1,0:T(8,128)(2,1)S(1)}, bf16[128,768]{1,0:T(8,128)(2,1)S(1)}, u32[]{:S(2)}, u32[]{:S(2)}) collective-permute-start(bf16[128,768]{1,0:T(8,128)(2,1)S(1)} %get-tuple-element.303.refs_0_), channel_id=1, source_target_pairs={{0,2},{1,3},{2,0},{3,1},{4,6},{5,7},{6,4},{7,5},{8,10},{9,11},{10,... | collective-permute-start | bytes 589832 | tf_op jit(solution)/shard_map/ppermute | solution.py:192
  140.7 13.2 %collective-permute-start.58 = (bf16[96,1536]{1,0:T(8,128)(2,1)S(1)}, bf16[96,1536]{1,0:T(8,128)(2,1)S(1)}, u32[]{:S(2)}, u32[]{:S(2)}) collective-permute-start(bf16[96,1536]{1,0:T(8,128)(2,1)S(1)} %collective-permute-done.45.refs_13_), channel_id=1, source_target_pairs={{0,8},{8,16},{16,24},{24,28},{28,20},{20,12},{12,4},{4,0},{1,9},{9... | collective-permute-start | bytes 884744 | tf_op jit(solution)/shard_map/ppermute | solution.py:111
  147.5 11.2 %collective-permute-start.59 = (bf16[104,1536]{1,0:T(8,128)(2,1)S(1)}, bf16[104,1536]{1,0:T(8,128)(2,1)S(1)}, u32[]{:S(2)}, u32[]{:S(2)}) collective-permute-start(bf16[104,1536]{1,0:T(8,128)(2,1)S(1)} %fold_shards.7), channel_id=1, source_target_pairs={{0,24},{4,28},{8,16},{12,20},{16,8},{20,12},{24,0},{28,4},{1,25},{... | collective-permute-start | bytes 958472 | tf_op jit(solution)/shard_map/ppermute | solution.py:803
  149.0 11.3 %collective-permute-start.60 = (bf16[2,104,768]{2,1,0:T(8,128)(2,1)S(1)}, bf16[2,104,768]{2,1,0:T(8,128)(2,1)S(1)}, u32[]{:S(2)}, u32[]{:S(2)}) collective-permute-start(bf16[2,104,768]{2,1,0:T(8,128)(2,1)S(1)} %get-tuple-element.314), channel_id=1, source_target_pairs={{0,4},{4,0},{8,12},{12,8},{16,20},{20,16},{24,28},{28,24},{1,5},{5... | collective-permute-start | bytes 958472 | tf_op jit(solution)/shard_map/ppermute | solution.py:796
  160.3 9.9 %collective-permute-start.65 = (bf16[1,104,1536]{2,1,0:T(8,128)(2,1)S(1)}, bf16[1,104,1536]{2,1,0:T(8,128)(2,1)S(1)}, u32[]{:S(2)}, u32[]{:S(2)}) collective-permute-start(bf16[1,104,1536]{2,1,0:T(8,128)(2,1)S(1)} %get-tuple-element.325), channel_id=1, source_target_pairs={{0,4},{4,0},{8,12},{12,8},{16,20},{20,16},{24,28},{28,24},{1,5},{5... | collective-permute-start | bytes 958472 | tf_op jit(solution)/shard_map/ppermute | solution.py:796
  162.1 8.3 %collective-permute-start.64 = (bf16[128,768]{1,0:T(8,128)(2,1)S(1)}, bf16[128,768]{1,0:T(8,128)(2,1)S(1)}, u32[]{:S(2)}, u32[]{:S(2)}) collective-permute-start(bf16[128,768]{1,0:T(8,128)(2,1)S(1)} %add_convert_fusion), channel_id=1, source_target_pairs={{0,2},{1,3},{2,0},{3,1},{4,6},{5,7},{6,4},{7,5},{8,10},{9,11},{10,... | collective-permute-start | bytes 589832 | tf_op jit(solution)/shard_map/ppermute | solution.py:192
  163.1 15.7 %collective-permute-start.66 = (bf16[104,768]{1,0:T(8,128)(2,1)S(1)}, bf16[104,768]{1,0:T(8,128)(2,1)S(1)}, u32[]{:S(2)}, u32[]{:S(2)}) collective-permute-start(bf16[104,768]{1,0:T(8,128)(2,1)S(1)} %get-tuple-element.332), channel_id=1, source_target_pairs={{0,16},{4,20},{8,24},{12,28},{16,0},{20,4},{24,8},{28,12},{1,17},{... | collective-permute-start | bytes 479240 | tf_op jit(solution)/shard_map/ppermute | solution.py:803
  167.0 11.8 %collective-permute-start.67 = (bf16[104,768]{1,0:T(8,128)(2,1)S(1)}, bf16[104,768]{1,0:T(8,128)(2,1)S(1)}, u32[]{:S(2)}, u32[]{:S(2)}) collective-permute-start(bf16[104,768]{1,0:T(8,128)(2,1)S(1)} %get-tuple-element.333), channel_id=1, source_target_pairs={{0,24},{4,28},{8,16},{12,20},{16,8},{20,12},{24,0},{28,4},{1,25},{... | collective-permute-start | bytes 479240 | tf_op jit(solution)/shard_map/ppermute | solution.py:803
  168.2 11.1 %collective-permute-start.68 = (bf16[104,768]{1,0:T(8,128)(2,1)S(1)}, bf16[104,768]{1,0:T(8,128)(2,1)S(1)}, u32[]{:S(2)}, u32[]{:S(2)}) collective-permute-start(bf16[104,768]{1,0:T(8,128)(2,1)S(1)} %get-tuple-element.334), channel_id=1, source_target_pairs={{0,8},{4,12},{8,0},{12,4},{16,24},{20,28},{24,16},{28,20},{1,9},{5... | collective-permute-start | bytes 479240 | tf_op jit(solution)/shard_map/ppermute | solution.py:803
  180.2 9.4 %collective-permute-start.72 = (bf16[104,1536]{1,0:T(8,128)(2,1)S(1)}, bf16[104,1536]{1,0:T(8,128)(2,1)S(1)}, u32[]{:S(2)}, u32[]{:S(2)}) collective-permute-start(bf16[104,1536]{1,0:T(8,128)(2,1)S(1)} %fold_shards.8), channel_id=1, source_target_pairs={{0,8},{4,12},{8,0},{12,4},{16,24},{20,28},{24,16},{28,20},{1,9},{5... | collective-permute-start | bytes 958472 | tf_op jit(solution)/shard_map/ppermute | solution.py:803
  183.4 7.1 %collective-permute-start.70 = (bf16[128,768]{1,0:T(8,128)(2,1)S(1)}, bf16[128,768]{1,0:T(8,128)(2,1)S(1)}, u32[]{:S(2)}, u32[]{:S(2)}) collective-permute-start(bf16[128,768]{1,0:T(8,128)(2,1)S(1)} %second_norm_tangent.1.refs_0_), channel_id=1, source_target_pairs={{0,1},{1,0},{2,3},{3,2},{4,5},{5,4},{6,7},{7,6},{8,9},{9,8},{10,11... | collective-permute-start | bytes 589832 | tf_op jit(solution)/shard_map/ppermute | solution.py:192
  (33 other events, 269.9 us)
